TPU v7x, 32 devices: a whole 2x2x4 slice. The times are simulated.
32 devices in a mesh: batch: 2 (over y), blk: 8 (over z, core), head: 2 (over x).
Axes of the slice: x: 2, y: 2, z: 4, core: 2. Of those that a mesh axis runs over, the one named last changes fastest.
Arguments:
- layer_input: bfloat16 [8, 4096, 768], P('batch', ('blk', 'head')), may hold values from -6 to 6
- lengths: int32 [8], P('batch'), may hold values from 1024 to 4096, as said below
- cotangent: bfloat16 [8, 4096, 768], P('batch', ('blk', 'head')), may hold values from -6 to 6
- w_query: bfloat16 [768, 768], P(('batch', 'blk', 'head')), may hold values from -0.3125 to 0.3125
- b_query: bfloat16 [768], P(('batch', 'blk', 'head')), may hold values from -3 to 3
- w_key: bfloat16 [768, 768], P(('batch', 'blk', 'head')), may hold values from -0.3125 to 0.3125
- w_value: bfloat16 [768, 768], P(('batch', 'blk', 'head')), may hold values from -0.21875 to 0.21875
- b_value: bfloat16 [768], P(('batch', 'blk', 'head')), may hold values from -0.59765625 to 0.59765625
- w_attn_out: bfloat16 [768, 768], P(('batch', 'blk', 'head')), may hold values from -1.5 to 1.5
- b_attn_out: bfloat16 [768], P(('batch', 'blk', 'head')), may hold values from -2 to 2
- norm1_gain: bfloat16 [768], P(('batch', 'blk', 'head')), may hold values from 0.5 to 1.5
- norm1_bias: bfloat16 [768], P(('batch', 'blk', 'head')), may hold values from -2 to 2
- w_inner: bfloat16 [768, 3072], P(('batch', 'blk', 'head')), may hold values from -0.21875 to 0.21875
- b_inner: bfloat16 [3072], P(('batch', 'blk', 'head')), may hold values from -2 to 2
- w_outer: bfloat16 [3072, 768], P(('batch', 'blk', 'head')), may hold values from -0.109375 to 0.109375
- b_outer: bfloat16 [768], P(('batch', 'blk', 'head')), may hold values from -2 to 2
- norm2_gain: bfloat16 [768], P(('batch', 'blk', 'head')), may hold values from 0.5 to 1.5
- norm2_bias: bfloat16 [768], P(('batch', 'blk', 'head')), may hold values from -2 to 2
Outputs:
- output: bfloat16 [8, 4096, 768], P('batch', ('blk', 'head'))
- input_grad: bfloat16 [8, 4096, 768], P('batch', ('blk', 'head'))
- grad_w_query: float32 [768, 768], P(('batch', 'blk', 'head'))
- grad_b_query: float32 [768], P(('batch', 'blk', 'head'))
- grad_w_key: float32 [768, 768], P(('batch', 'blk', 'head'))
- grad_w_value: float32 [768, 768], P(('batch', 'blk', 'head'))
- grad_b_value: float32 [768], P(('batch', 'blk', 'head'))
- grad_w_attn_out: float32 [768, 768], P(('batch', 'blk', 'head'))
- grad_b_attn_out: float32 [768], P(('batch', 'blk', 'head'))
- grad_norm1_gain: float32 [768], P(('batch', 'blk', 'head'))
- grad_norm1_bias: float32 [768], P(('batch', 'blk', 'head'))
- grad_w_inner: float32 [768, 3072], P(('batch', 'blk', 'head'))
- grad_b_inner: float32 [3072], P(('batch', 'blk', 'head'))
- grad_w_outer: float32 [3072, 768], P(('batch', 'blk', 'head'))
- grad_b_outer: float32 [768], P(('batch', 'blk', 'head'))
- grad_norm2_gain: float32 [768], P(('batch', 'blk', 'head'))
- grad_norm2_bias: float32 [768], P(('batch', 'blk', 'head'))
Inputs may be any that keep to these rules, and one draw needn't show every extreme that they name: `lengths`: each sequence's number of valid positions; later positions are padding. In every draw some sequence has exactly 4096 and some exactly 1024.
All inputs are finite; a program needn't handle non-finite values.
Results may differ from a plain program's by a relative error of at most 0.03.
Values may be sent and summed in bfloat16 or wider, within the bound.
No kernel may reach another device: no remote copies, remote signals or barrier semaphores. Data moves between devices by JAX's collectives and lax.ppermute only.
A program may use at most 120 MiB of HBM per device.

v0:
```python
import math

import jax
import jax.numpy as jnp
from jax import lax
from jax.sharding import PartitionSpec as P

HEADS = 12
MICRO = 4


NEG_BIG = -1e30
EPSILON = 1e-06


def for_sending(array):
    return jax.tree.map(lambda a: a.astype(jnp.bfloat16) if a.dtype == jnp.float32 else a, array)


def shifted(block, axis, distance):
    devices = range(lax.axis_size(axis))
    route = [((i - distance) % len(devices), i) for i in devices]
    return lax.ppermute(block, axis, route)


def norm_apply(residue, gain_row, shift_row):
    center = jnp.mean(residue, axis=-1, keepdims=True)
    centred = residue - center
    spread = jnp.mean(centred * centred, axis=-1, keepdims=True)
    return centred * lax.rsqrt(spread + EPSILON) * gain_row + shift_row


def gelu_exact(pre_act):
    return jax.nn.gelu(pre_act, approximate=False)


def matmul(left_op, right_op):
    return jnp.dot(left_op, right_op, preferred_element_type=jnp.float32)


def contract_rows(left_op, right_op):
    return lax.dot_general(
        left_op, right_op, (((0,), (0,)), ((), ())), preferred_element_type=jnp.float32
    )


def contract_cols(left_op, right_op):
    return lax.dot_general(
        left_op, right_op, (((1,), (1,)), ((), ())), preferred_element_type=jnp.float32
    )


def split_heads(packed, head_count):
    return packed.reshape(
        packed.shape[0], packed.shape[1], head_count, packed.shape[2] // head_count
    )


def key_mask(seq_lengths, key_start, key_count):
    key_places = key_start + jnp.arange(key_count, dtype=jnp.int32)
    return (key_places[None, :] < seq_lengths[:, None])[:, None, None, :]


def attend_block(
    run_state, queries, key_block, value_block, key_start, seq_lengths, head_count, score_scale
):
    run_max, run_sum, run_acc = run_state
    key_valid = key_mask(seq_lengths, key_start, key_block.shape[1])
    scores = (
        jnp.einsum(
            "sqhd,skhd->shqk",
            queries,
            split_heads(key_block, head_count),
            preferred_element_type=jnp.float32,
        )
        * score_scale
    )
    scores = jnp.where(key_valid, scores, NEG_BIG)
    new_max = jnp.maximum(run_max, jnp.max(scores, axis=-1))
    rescale = jnp.exp(run_max - new_max)
    weights = jnp.where(key_valid, jnp.exp(scores - new_max[..., None]), 0.0)
    new_sum = run_sum * rescale + jnp.sum(weights, axis=-1)
    summed = jnp.einsum(
        "shqk,skhd->sqhd",
        weights.astype(jnp.bfloat16),
        split_heads(value_block, head_count),
        preferred_element_type=jnp.float32,
    )
    new_acc = run_acc * jnp.transpose(rescale, (0, 2, 1))[..., None] + summed
    return (new_max, new_sum, new_acc)


def attend_piece(run_state, queries, key_piece, value_piece, seq_lengths, head_count, score_scale):
    piece_rows = key_piece.shape[1]
    block_rows = min(piece_rows, queries.shape[1])

    def one_block(carry_state, block_index):
        offset = block_index * block_rows
        key_block = lax.dynamic_slice_in_dim(key_piece, offset, block_rows, 1)
        value_block = lax.dynamic_slice_in_dim(value_piece, offset, block_rows, 1)
        return (
            attend_block(
                carry_state,
                queries,
                key_block,
                value_block,
                offset,
                seq_lengths,
                head_count,
                score_scale,
            ),
            None,
        )

    final_state, unused = lax.scan(
        one_block, run_state, jnp.arange(piece_rows // block_rows, dtype=jnp.int32)
    )
    return final_state


def block_grads(
    queries,
    grads_out,
    log_sums,
    deltas,
    key_block,
    value_block,
    key_start,
    seq_lengths,
    head_count,
    score_scale,
):
    key_valid = key_mask(seq_lengths, key_start, key_block.shape[1])
    query_heads = split_heads(queries, head_count)
    grad_heads = split_heads(grads_out, head_count)
    key_heads = split_heads(key_block, head_count)
    value_heads = split_heads(value_block, head_count)
    scores = (
        jnp.einsum("sqhd,skhd->shqk", query_heads, key_heads, preferred_element_type=jnp.float32)
        * score_scale
    )
    weights = jnp.where(key_valid, jnp.exp(scores - log_sums[..., None]), 0.0)
    grad_values = jnp.einsum(
        "shqk,sqhd->skhd",
        weights.astype(jnp.bfloat16),
        grad_heads,
        preferred_element_type=jnp.float32,
    )
    grad_weights = jnp.einsum(
        "sqhd,skhd->shqk", grad_heads, value_heads, preferred_element_type=jnp.float32
    )
    grad_scores = (weights * (grad_weights - deltas[..., None])).astype(jnp.bfloat16)
    grad_queries = (
        jnp.einsum("shqk,skhd->sqhd", grad_scores, key_heads, preferred_element_type=jnp.float32)
        * score_scale
    )
    grad_keys = (
        jnp.einsum("shqk,sqhd->skhd", grad_scores, query_heads, preferred_element_type=jnp.float32)
        * score_scale
    )
    return (
        grad_queries.reshape(queries.shape),
        grad_keys.reshape(key_block.shape),
        grad_values.reshape(value_block.shape),
    )


def local(
    layer_input,
    lengths,
    cotangent,
    w_query,
    b_query,
    w_key,
    w_value,
    b_value,
    w_attn_out,
    b_attn_out,
    norm1_gain,
    norm1_bias,
    w_inner,
    b_inner,
    w_outer,
    b_outer,
    norm2_gain,
    norm2_bias,
):
    local_shards = (
        w_query,
        b_query,
        w_key,
        w_value,
        b_value,
        w_attn_out,
        b_attn_out,
        norm1_gain,
        norm1_bias,
        w_inner,
        b_inner,
        w_outer,
        b_outer,
        norm2_gain,
        norm2_bias,
    )
    seq_here, rows_here, width = layer_input.shape
    seq_step = seq_here // MICRO
    head_count = HEADS // lax.axis_size("head")
    score_scale = 1.0 / math.sqrt(width // HEADS)
    cycle_size = lax.axis_size("blk")
    cycle_place = lax.axis_index("blk")
    first_row = (cycle_place * lax.axis_size("head") + lax.axis_index("head")) * rows_here
    row_places = first_row + jnp.arange(rows_here, dtype=jnp.int32)
    totals = ()
    outputs_list = []
    input_list = []
    for micro_index in range(MICRO):
        gathered = (
            lax.all_gather(local_shards[0], ("batch", "blk", "head"), axis=0, tiled=True),
            lax.all_gather(local_shards[1], ("batch", "blk", "head"), axis=0, tiled=True),
            lax.all_gather(local_shards[2], ("batch", "blk", "head"), axis=0, tiled=True),
            lax.all_gather(local_shards[3], ("batch", "blk", "head"), axis=0, tiled=True),
            lax.all_gather(local_shards[4], ("batch", "blk", "head"), axis=0, tiled=True),
            lax.all_gather(local_shards[5], ("batch", "blk", "head"), axis=0, tiled=True),
            lax.all_gather(local_shards[6], ("batch", "blk", "head"), axis=0, tiled=True),
            lax.all_gather(local_shards[7], ("batch", "blk", "head"), axis=0, tiled=True),
            lax.all_gather(local_shards[8], ("batch", "blk", "head"), axis=0, tiled=True),
            lax.all_gather(local_shards[9], ("batch", "blk", "head"), axis=0, tiled=True),
            lax.all_gather(local_shards[10], ("batch", "blk", "head"), axis=0, tiled=True),
            lax.all_gather(local_shards[11], ("batch", "blk", "head"), axis=0, tiled=True),
            lax.all_gather(local_shards[12], ("batch", "blk", "head"), axis=0, tiled=True),
            lax.all_gather(local_shards[13], ("batch", "blk", "head"), axis=0, tiled=True),
            lax.all_gather(local_shards[14], ("batch", "blk", "head"), axis=0, tiled=True),
        )
        if micro_index == 0:
            totals = tuple((jnp.zeros(member.shape, jnp.float32) for member in gathered))
        (
            weight_query,
            bias_query,
            weight_key,
            weight_value,
            bias_value,
            weight_out,
            bias_out,
            gain_first,
            shift_first,
            weight_inner,
            bias_inner,
            weight_outer,
            bias_outer,
            gain_second,
            shift_second,
        ) = gathered
        tokens = layer_input[micro_index * seq_step : (micro_index + 1) * seq_step]
        cot_rows = cotangent[micro_index * seq_step : (micro_index + 1) * seq_step]
        seq_lengths = lengths[micro_index * seq_step : (micro_index + 1) * seq_step]
        flat_rows = tokens.reshape(-1, width)
        queries = (
            (matmul(flat_rows, weight_query) + bias_query.astype(jnp.float32))
            .astype(jnp.bfloat16)
            .reshape(seq_step, rows_here, width)
        )
        keys_here = (
            matmul(flat_rows, weight_key).astype(jnp.bfloat16).reshape(seq_step, rows_here, width)
        )
        values_here = (
            (matmul(flat_rows, weight_value) + bias_value.astype(jnp.float32))
            .astype(jnp.bfloat16)
            .reshape(seq_step, rows_here, width)
        )
        query_side, key_side, value_side = (
            lax.all_to_all(queries, "head", split_axis=2, concat_axis=1, tiled=True),
            lax.all_to_all(keys_here, "head", split_axis=2, concat_axis=1, tiled=True),
            lax.all_to_all(values_here, "head", split_axis=2, concat_axis=1, tiled=True),
        )
        block_len = key_side.shape[1]
        query_four = split_heads(query_side, head_count)
        start_state = (
            jnp.full((seq_step, head_count, block_len), NEG_BIG, jnp.float32),
            jnp.zeros((seq_step, head_count, block_len), jnp.float32),
            jnp.zeros(query_four.shape, jnp.float32),
        )
        key_piece = lax.all_gather(key_side, "blk", axis=1, tiled=True)
        value_piece = lax.all_gather(value_side, "blk", axis=1, tiled=True)
        run_max, run_sum, run_acc = attend_piece(
            start_state, query_four, key_piece, value_piece, seq_lengths, head_count, score_scale
        )
        log_sums = run_max + jnp.log(run_sum)
        attended_side = (
            (run_acc / jnp.transpose(run_sum, (0, 2, 1))[..., None])
            .reshape(query_side.shape)
            .astype(jnp.bfloat16)
        )
        attended = lax.all_to_all(attended_side, "head", split_axis=1, concat_axis=2, tiled=True)
        attended_flat = attended.reshape(-1, width)
        branch = matmul(attended_flat, weight_out) + bias_out.astype(jnp.float32)
        normed1, back_first = jax.vjp(
            norm_apply,
            flat_rows.astype(jnp.float32) + branch,
            gain_first.astype(jnp.float32),
            shift_first.astype(jnp.float32),
        )
        normed_low = normed1.astype(jnp.bfloat16)
        inner_pre = matmul(normed_low, weight_inner) + bias_inner.astype(jnp.float32)
        active, back_gelu = jax.vjp(gelu_exact, inner_pre)
        active_low = active.astype(jnp.bfloat16)
        outer_out = matmul(active_low, weight_outer) + bias_outer.astype(jnp.float32)
        final_rows, back_second = jax.vjp(
            norm_apply,
            normed1 + outer_out,
            gain_second.astype(jnp.float32),
            shift_second.astype(jnp.float32),
        )
        outputs_list.append(final_rows.astype(jnp.bfloat16).reshape(seq_step, rows_here, width))
        row_keep = (row_places[None, :] < seq_lengths[:, None]).reshape(-1, 1)
        grad_final = jnp.where(row_keep, cot_rows.reshape(-1, width).astype(jnp.float32), 0.0)
        grad_resid2, grad_gain2, grad_shift2 = back_second(grad_final)
        grad_outer = grad_resid2.astype(jnp.bfloat16)
        grad_bias_outer = jnp.sum(grad_outer.astype(jnp.float32), axis=0)
        grad_weight_outer = contract_rows(active_low, grad_outer)
        (grad_inner_pre,) = back_gelu(contract_cols(grad_outer, weight_outer))
        grad_inner = grad_inner_pre.astype(jnp.bfloat16)
        grad_bias_inner = jnp.sum(grad_inner.astype(jnp.float32), axis=0)
        grad_weight_inner = contract_rows(normed_low, grad_inner)
        grad_normed1 = grad_resid2 + contract_cols(grad_inner, weight_inner)
        grad_resid1, grad_gain1, grad_shift1 = back_first(grad_normed1)
        grad_branch = grad_resid1.astype(jnp.bfloat16)
        grad_bias_out = jnp.sum(grad_branch.astype(jnp.float32), axis=0)
        grad_weight_out = contract_rows(attended_flat, grad_branch)
        grad_attended = (
            contract_cols(grad_branch, weight_out)
            .astype(jnp.bfloat16)
            .reshape(seq_step, rows_here, width)
        )
        grad_side = lax.all_to_all(grad_attended, "head", split_axis=2, concat_axis=1, tiled=True)
        deltas = jnp.einsum(
            "sqhd,sqhd->shq",
            split_heads(grad_side, head_count),
            split_heads(attended_side, head_count),
            preferred_element_type=jnp.float32,
        )

        def cycle_keys(cycle_step, carry):
            key_pair, grad_pair, grad_query_acc = carry
            source = (cycle_place - cycle_step) % cycle_size
            key_start = source * block_len
            pair_in = key_pair
            grads_in = grad_pair
            query_acc = grad_query_acc
            grad_q, grad_k, grad_v = block_grads(
                query_side,
                grad_side,
                log_sums,
                deltas,
                pair_in[0],
                pair_in[1],
                key_start,
                seq_lengths,
                head_count,
                score_scale,
            )
            key_pair = pair_in
            grad_pair = (grads_in[0] + grad_k, grads_in[1] + grad_v)
            grad_query_acc = query_acc + grad_q
            key_pair = jax.tree.map(
                lambda part, own: part.astype(own.dtype),
                shifted(for_sending(key_pair), "blk", 1),
                key_pair,
            )
            grad_pair = (
                shifted(grad_pair[0].astype(jnp.bfloat16), "blk", 1).astype(jnp.float32),
                shifted(grad_pair[1].astype(jnp.bfloat16), "blk", 1).astype(jnp.float32),
            )
            return (key_pair, grad_pair, grad_query_acc)

        zero_side = jnp.zeros(key_side.shape, jnp.float32)
        cycle_out = lax.fori_loop(
            0,
            cycle_size,
            cycle_keys,
            (
                (key_side, value_side),
                (zero_side, zero_side),
                jnp.zeros(query_side.shape, jnp.float32),
            ),
        )
        grad_query_side = cycle_out[2]
        grad_key_side = cycle_out[1][0]
        grad_value_side = cycle_out[1][1]
        grad_queries, grad_keys, grad_values = (
            lax.all_to_all(
                grad_query_side.astype(jnp.bfloat16),
                "head",
                split_axis=1,
                concat_axis=2,
                tiled=True,
            ),
            lax.all_to_all(
                grad_key_side.astype(jnp.bfloat16), "head", split_axis=1, concat_axis=2, tiled=True
            ),
            lax.all_to_all(
                grad_value_side.astype(jnp.bfloat16),
                "head",
                split_axis=1,
                concat_axis=2,
                tiled=True,
            ),
        )
        grad_queries = grad_queries.reshape(-1, width)
        grad_keys = grad_keys.reshape(-1, width)
        grad_values = grad_values.reshape(-1, width)
        grad_input = (
            grad_resid1
            + contract_cols(grad_queries, weight_query)
            + contract_cols(grad_keys, weight_key)
            + contract_cols(grad_values, weight_value)
        )
        input_list.append(grad_input.astype(jnp.bfloat16).reshape(seq_step, rows_here, width))
        micro_grads = (
            contract_rows(flat_rows, grad_queries),
            jnp.sum(grad_queries.astype(jnp.float32), axis=0),
            contract_rows(flat_rows, grad_keys),
            contract_rows(flat_rows, grad_values),
            jnp.sum(grad_values.astype(jnp.float32), axis=0),
            grad_weight_out,
            grad_bias_out,
            grad_gain1,
            grad_shift1,
            grad_weight_inner,
            grad_bias_inner,
            grad_weight_outer,
            grad_bias_outer,
            grad_gain2,
            grad_shift2,
        )
        totals = tuple(
            (total_item + micro_item for total_item, micro_item in zip(totals, micro_grads))
        )
    owned = lax.psum_scatter(totals, ("batch", "blk", "head"), scatter_dimension=0, tiled=True)
    return (jnp.concatenate(outputs_list, axis=0), jnp.concatenate(input_list, axis=0)) + tuple(
        owned
    )


def solution(mesh):
    placed = (
        P("batch", ("blk", "head"), None),
        P("batch"),
        P("batch", ("blk", "head"), None),
        P(("batch", "blk", "head"), None),
        P(("batch", "blk", "head")),
        P(("batch", "blk", "head"), None),
        P(("batch", "blk", "head"), None),
        P(("batch", "blk", "head")),
        P(("batch", "blk", "head"), None),
        P(("batch", "blk", "head")),
        P(("batch", "blk", "head")),
        P(("batch", "blk", "head")),
        P(("batch", "blk", "head"), None),
        P(("batch", "blk", "head")),
        P(("batch", "blk", "head"), None),
        P(("batch", "blk", "head")),
        P(("batch", "blk", "head")),
        P(("batch", "blk", "head")),
    )
    return jax.shard_map(
        local,
        mesh=mesh,
        in_specs=placed,
        out_specs=(
            P("batch", ("blk", "head"), None),
            P("batch", ("blk", "head"), None),
            P(("batch", "blk", "head"), None),
            P(("batch", "blk", "head")),
            P(("batch", "blk", "head"), None),
            P(("batch", "blk", "head"), None),
            P(("batch", "blk", "head")),
            P(("batch", "blk", "head"), None),
            P(("batch", "blk", "head")),
            P(("batch", "blk", "head")),
            P(("batch", "blk", "head")),
            P(("batch", "blk", "head"), None),
            P(("batch", "blk", "head")),
            P(("batch", "blk", "head"), None),
            P(("batch", "blk", "head")),
            P(("batch", "blk", "head")),
            P(("batch", "blk", "head")),
        ),
        check_vma=False,
    )
```

profile of v0, /device:TPU:0, one launch (start us, length us, event | category | flops | bytes accessed | tf_op | source)
XLA Modules:
  0.0 2741.2 jit_solution(13891205155294647793)
XLA Ops:
  9.5 58.4 %all-gather.15.cloned.1.call-done = bf16[768,768]{1,0:T(8,128)(2,1)} async-done(((bf16[24,768]{1,0:T(8,128)(2,1)}), bf16[768,768]{1,0:T(8,128)(2,1)}) %all-gather.15.cloned.1.call-update) | async-done | bytes 1179664 | tf_op jit(solution)/shard_map/all_gather | solution.py:220
  74.2 10.0 all_to_all.528
  87.7 39.0 %all-reduce.19 = (bf16[3072]{0:T(1024)(128)(2,1)}, bf16[768]{0:T(1024)(128)(2,1)}, bf16[768]{0:T(1024)(128)(2,1)S(1)}, bf16[768]{0:T(1024)(128)(2,1)}, bf16[768]...) all-reduce(bf16[3072]{0:T(1024)(128)(2,1)S(1)} %dynamic-update-slic, ...), channel_id=1, replica_groups=mesh['batch'=2,'blk'=8,'head'=2] {'batch','blk','head'}, use_global_device_ids=true, to_apply=%add.5 | all-reduce | flops 9216 | bytes 36864
  134.1 10.0 all_to_all.529
  156.7 9.0 all_to_all.530
  179.5 9.0 all_to_all.531
  200.9 9.0 all_to_all.532
  224.0 9.0 all_to_all.533
  245.5 9.0 all_to_all.534
  262.9 8.3 all_to_all.535
  365.0 147.9 %while.159 = (s32[]{:T(128)}, f32[1,6,512]{2,1,0:T(8,128)}, f32[1,6,512]{2,1,0:T(8,128)}, f32[1,512,6,64]{1,3,2,0:T(8,128)S(1)}, s32[8]{0:T(128)}, /*index=5*/s3...) while((s32[]{:T(128)}, f32[1,6,512]{2,1,0:T(8,128)}, ...), condition=%wide.region_27.28_spmd.clone, body=%wide.region_24.27_spmd.clone.sunk | while | flops 423709696 | bytes 25121092 | solution.py:115
  523.4 135.3 %while.158 = (s32[]{:T(128)}, f32[1,6,512]{2,1,0:T(8,128)S(1)}, f32[1,6,512]{2,1,0:T(8,128)S(1)}, f32[1,512,6,64]{1,3,2,0:T(8,128)}, s32[8]{0:T(128)S(1)}, /*ind...) while((s32[]{:T(128)}, f32[1,6,512]{2,1,0:T(8,128)S(1)}, ...), condition=%wide.region_19.20_spmd.clone, body=%wide.region_16.19_spmd.clone.sunk | while | flops 423709696 | bytes 24971480 | solution.py:115
  534.9 5.3 fusion.580
  551.6 5.5 fusion.580
  568.5 5.5 fusion.580
  585.4 5.5 fusion.580
  602.3 5.6 fusion.580
  619.2 5.6 fusion.580
  636.2 5.6 fusion.580
  653.2 5.5 fusion.580
  659.2 147.7 %while.157 = (s32[]{:T(128)}, f32[1,6,512]{2,1,0:T(8,128)}, f32[1,6,512]{2,1,0:T(8,128)}, f32[1,512,6,64]{1,3,2,0:T(8,128)S(1)}, s32[8]{0:T(128)}, /*index=5*/s3...) while((s32[]{:T(128)}, f32[1,6,512]{2,1,0:T(8,128)}, ...), condition=%wide.region_11.12_spmd.clone, body=%wide.region_8.11_spmd.clone.sunk | while | flops 423709696 | bytes 25121092 | solution.py:115
  807.1 127.7 %while.156 = (s32[]{:T(128)}, f32[1,6,512]{2,1,0:T(8,128)S(1)}, f32[1,6,512]{2,1,0:T(8,128)}, f32[1,512,6,64]{1,3,2,0:T(8,128)S(1)}, s32[8]{0:T(128)S(1)}, /*ind...) while((s32[]{:T(128)}, f32[1,6,512]{2,1,0:T(8,128)S(1)}, ...), condition=%wide.region_3.4_spmd.clone, body=%wide.region_0.3_spmd.clone.sunk | while | flops 423709696 | bytes 25069836 | solution.py:115
  956.3 7.3 all-to-all-done.11
  967.7 7.0 all-to-all-done.7
  996.6 11.8 multiply_convert_fusion.4
  1013.3 11.4 multiply_convert_fusion.6
  1026.5 8.1 multiply_convert_fusion.7
  1038.6 11.3 multiply_convert_fusion.5
  1056.0 5.8 convert_reduce_fusion
  1068.1 5.8 convert_reduce_fusion.1
  1075.3 5.9 convert_reduce_fusion.2
  1187.0 219.1 %while.163 = (s32[]{:T(128)}, bf16[1,512,384]{1,2,0:T(8,128)(2,1)S(1)}, bf16[1,512,384]{1,2,0:T(8,128)(2,1)}, f32[1,512,384]{1,2,0:T(8,128)S(1)}, f32[1,512,384]...) while((s32[]{:T(128)}, ...), condition=%wide.region_55.56_spmd.clone, body=%wide.region_54.55_spmd.clone.sunk | while | flops 1024721920 | bytes 76814408 | solution.py:376
  1232.3 5.8 collective-permute-done.14
  1261.7 5.3 collective-permute-done.14
  1427.2 214.2 %while.162 = (s32[]{:T(128)}, bf16[1,512,384]{1,2,0:T(8,128)(2,1)S(1)}, bf16[1,512,384]{1,2,0:T(8,128)(2,1)}, f32[1,512,384]{1,2,0:T(8,128)S(1)}, f32[1,512,384]...) while((s32[]{:T(128)}, ...), condition=%wide.region_49.50_spmd.clone, body=%wide.region_48.49_spmd.clone.sunk | while | flops 1024721920 | bytes 76814408 | solution.py:376
  1658.0 214.5 %while.161 = (s32[]{:T(128)}, bf16[1,512,384]{1,2,0:T(8,128)(2,1)S(1)}, bf16[1,512,384]{1,2,0:T(8,128)(2,1)}, f32[1,512,384]{1,2,0:T(8,128)S(1)}, f32[1,512,384]...) while((s32[]{:T(128)}, ...), condition=%wide.region_43.44_spmd.clone, body=%wide.region_42.43_spmd.clone.sunk | while | flops 1024721920 | bytes 76814408 | solution.py:376
  1874.5 4.9 reduce.57
  1897.8 214.7 %while.160 = (s32[]{:T(128)}, bf16[1,512,384]{1,2,0:T(8,128)(2,1)S(1)}, bf16[1,512,384]{1,2,0:T(8,128)(2,1)}, f32[1,512,384]{1,2,0:T(8,128)S(1)}, f32[1,512,384]...) while((s32[]{:T(128)}, ...), condition=%wide.region_37.38_spmd.clone, body=%wide.region_36.37_spmd.clone.sunk | while | flops 1024721920 | bytes 76814408 | solution.py:376
  2262.2 5.3 fusion.293
  2267.5 5.2 fusion.290
  2272.7 12.7 add_add_fusion.1
  2289.4 5.0 fusion.324
  2294.4 5.0 fusion.325
  2299.4 12.5 add_add_fusion
  2336.6 42.4 %all-reduce.18 = (f32[768]{0:T(1024)}, f32[768]{0:T(1024)}, f32[768]{0:T(1024)}, f32[768]{0:T(1024)}, f32[768]{0:T(1024)}, /*index=5*/f32[3072]{0:T(1024)}, f32[768]{0:T(1024)}, f32[768]{0:T(1024)}, f32[768]{0:T(1024)}) all-reduce(f32[768]{0:T(1024)} %add.1060, ...), channel_id=3, replica_groups=mesh['batch'=2,'blk'=8,'head'=2] {'batch','blk','head'}, use_global_device_ids=true, to_apply=%region_61.62.clone | all-reduce | flops 9216 | bytes 73728
  2399.8 50.8 %reduce-scatter.23.cloned.1.call-done = f32[24,768]{1,0:T(8,128)} async-done(((f32[768,768]{1,0:T(8,128)}), f32[24,768]{1,0:T(8,128)}) %reduce-scatter.23.cloned.1.call-update) | async-done | bytes 73744
  2450.6 141.2 %reduce-scatter.15.cloned.1.call-done = f32[24,3072]{1,0:T(8,128)} async-done(((f32[768,3072]{1,0:T(8,128)}), f32[24,3072]{1,0:T(8,128)}) %reduce-scatter.15.cloned.1.call-update) | async-done | bytes 294928 | tf_op jit(solution)/shard_map/reduce_scatter | solution.py:438
  2591.8 142.0 %reduce-scatter.17.cloned.1.call-done = f32[96,768]{1,0:T(8,128)} async-done(((f32[3072,768]{1,0:T(8,128)}), f32[96,768]{1,0:T(8,128)}) %reduce-scatter.17.cloned.1.call-update) | async-done | bytes 294928 | tf_op jit(solution)/shard_map/reduce_scatter | solution.py:438
  (2460 shorter events, 1966.0 us)
Async XLA Ops:
  7.2 60.6 %all-gather.15.cloned.1.call-start = ((), (), s32[]{:S(2)}) async-start(), calls=%async_computation.38 | async-start | bytes 1216512 | tf_op jit(solution)/shard_map/all_gather | solution.py:220
  7.9 118.8 %all-gather.21.cloned.1.call-start = ((), (), s32[]{:S(2)}) async-start(), calls=%async_computation.41 | async-start | bytes 1216512 | tf_op jit(solution)/shard_map/all_gather | solution.py:221
  8.7 270.8 %all-gather.19.cloned.1.call-start = ((), (), s32[]{:S(2)}) async-start(), calls=%async_computation.40 | async-start | bytes 1216512 | tf_op jit(solution)/shard_map/all_gather | solution.py:218
  9.4 355.1 %all-gather.39.cloned.1.call-start = ((), (), s32[]{:S(2)}) async-start(), calls=%async_computation.50 | async-start | bytes 3538944 | tf_op jit(solution)/shard_map/all_gather | solution.py:282
  85.5 279.0 %all-gather.41.cloned.1.call-start = ((), (), s32[]{:S(2)}) async-start(), calls=%async_computation.51 | async-start | bytes 3538944 | tf_op jit(solution)/shard_map/all_gather | solution.py:283
  148.1 375.1 %all-gather.35.cloned.1.call-start = ((), (), s32[]{:S(2)}) async-start(), calls=%async_computation.48 | async-start | bytes 3538944 | tf_op jit(solution)/shard_map/all_gather | solution.py:282
  169.9 353.4 %all-gather.37.cloned.1.call-start = ((), (), s32[]{:S(2)}) async-start(), calls=%async_computation.49 | async-start | bytes 3538944 | tf_op jit(solution)/shard_map/all_gather | solution.py:283
  192.5 466.1 %all-gather.31.cloned.1.call-start = ((), (), s32[]{:S(2)}) async-start(), calls=%async_computation.46 | async-start | bytes 3538944 | tf_op jit(solution)/shard_map/all_gather | solution.py:282
  214.0 444.7 %all-gather.33.cloned.1.call-start = ((), (), s32[]{:S(2)}) async-start(), calls=%async_computation.47 | async-start | bytes 3538944 | tf_op jit(solution)/shard_map/all_gather | solution.py:283
  237.0 570.0 %all-gather.17.cloned.1.call-start = ((), (), s32[]{:S(2)}) async-start(), calls=%async_computation.39 | async-start | bytes 3538944 | tf_op jit(solution)/shard_map/all_gather | solution.py:282
  258.5 548.5 %all-gather.23.cloned.1.call-start = ((), (), s32[]{:S(2)}) async-start(), calls=%async_computation.42 | async-start | bytes 3538944 | tf_op jit(solution)/shard_map/all_gather | solution.py:283
  272.6 714.6 %all-gather.25.cloned.1.call-start = ((), (), s32[]{:S(2)}) async-start(), calls=%async_computation.43 | async-start | bytes 1216512 | tf_op jit(solution)/shard_map/all_gather | solution.py:223
  273.2 723.4 %all-gather.27.cloned.1.call-start = ((), (), s32[]{:S(2)}) async-start(), calls=%async_computation.44 | async-start | bytes 4866048 | tf_op jit(solution)/shard_map/all_gather | solution.py:227
  273.9 734.5 %all-gather.29.cloned.1.call-start = ((), (), s32[]{:S(2)}) async-start(), calls=%async_computation.45 | async-start | bytes 4866048 | tf_op jit(solution)/shard_map/all_gather | solution.py:229
  519.1 433.1 %all-to-all-start.15 = ((bf16[2,2,49152]{2,1,0:T(2,128)(2,1)}), bf16[2,2,49152]{2,1,0:T(2,128)(2,1)}, u32[]{:S(2)}, u32[]{:S(2)}) async-start(bf16[2,2,49152]{2,1,0:T(2,128)(2,1)} %reshape.1613), calls=%async_computation.15 | async-start | bytes 786432 | tf_op jit(solution)/shard_map/all_to_all | solution.py:293
  1102.4 34.5 %all-to-all-start.28 = ((bf16[2,2,49152]{2,1,0:T(2,128)(2,1)}), bf16[2,2,49152]{2,1,0:T(2,128)(2,1)}, u32[]{:S(2)}, u32[]{:S(2)}) async-start(bf16[2,2,49152]{2,1,0:T(2,128)(2,1)} %reshape.1639), calls=%async_computation.28 | async-start | bytes 786432 | tf_op jit(solution)/shard_map/all_to_all | solution.py:334
  1161.4 1238.4 %reduce-scatter.13.cloned.1.call-start = ((), (), s32[]{:S(2)}) async-start(), calls=%async_computation.52 | async-start | bytes 2433024 | tf_op jit(solution)/shard_map/reduce_scatter | solution.py:438
  1187.1 28.1 %collective-permute-start.12 = (bf16[1,512,384]{1,2,0:T(8,128)(2,1)S(1)}, bf16[1,512,384]{1,2,0:T(8,128)(2,1)S(1)}, u32[]{:S(2)}, u32[]{:S(2)}) collective-permute-start(bf16[1,512,384]{1,2,0:T(8,128)(2,1)S(1)} %copy.602), channel_id=1, source_target_pairs={{14,0},{0,2},{2,4},{4,6},{6,8},{8,10},{10,12},{12,14},{15,1},{1,3}... | collective-permute-start | bytes 1179656 | tf_op jit(solution)/shard_map/while/body/eval_jaxpr/ppermute | solution.py:23
  1215.2 29.4 %collective-permute-start.12 = (bf16[1,512,384]{1,2,0:T(8,128)(2,1)S(1)}, bf16[1,512,384]{1,2,0:T(8,128)(2,1)S(1)}, u32[]{:S(2)}, u32[]{:S(2)}) collective-permute-start(bf16[1,512,384]{1,2,0:T(8,128)(2,1)S(1)} %copy.602), channel_id=1, source_target_pairs={{14,0},{0,2},{2,4},{4,6},{6,8},{8,10},{10,12},{12,14},{15,1},{1,3}... | collective-permute-start | bytes 1179656 | tf_op jit(solution)/shard_map/while/body/eval_jaxpr/ppermute | solution.py:23
  1217.1 27.6 %collective-permute-start.13 = (bf16[1,512,384]{1,2,0:T(8,128)(2,1)}, bf16[1,512,384]{1,2,0:T(8,128)(2,1)}, u32[]{:S(2)}, u32[]{:S(2)}) collective-permute-start(bf16[1,512,384]{1,2,0:T(8,128)(2,1)} %copy.603), channel_id=1, source_target_pairs={{14,0},{0,2},{2,4},{4,6},{6,8},{8,10},{10,12},{12,14},{15,1},{1,3}... | collective-permute-start | bytes 1179656 | tf_op jit(solution)/shard_map/while/body/eval_jaxpr/ppermute | solution.py:23
  1244.8 27.7 %collective-permute-start.12 = (bf16[1,512,384]{1,2,0:T(8,128)(2,1)S(1)}, bf16[1,512,384]{1,2,0:T(8,128)(2,1)S(1)}, u32[]{:S(2)}, u32[]{:S(2)}) collective-permute-start(bf16[1,512,384]{1,2,0:T(8,128)(2,1)S(1)} %copy.602), channel_id=1, source_target_pairs={{14,0},{0,2},{2,4},{4,6},{6,8},{8,10},{10,12},{12,14},{15,1},{1,3}... | collective-permute-start | bytes 1179656 | tf_op jit(solution)/shard_map/while/body/eval_jaxpr/ppermute | solution.py:23
  1417.9 466.4 %all-to-all-start.29 = ((bf16[2,2,49152]{2,1,0:T(2,128)(2,1)}), bf16[2,2,49152]{2,1,0:T(2,128)(2,1)}, u32[]{:S(2)}, u32[]{:S(2)}) async-start(bf16[2,2,49152]{2,1,0:T(2,128)(2,1)} %reshape.1641), calls=%async_computation.29 | async-start | bytes 786432 | tf_op jit(solution)/shard_map/all_to_all | solution.py:390
  1427.3 26.7 collective-permute-start.8
  1454.0 26.7 collective-permute-start.8
  1480.8 26.7 collective-permute-start.8
  1507.6 26.7 collective-permute-start.8
  1534.4 26.7 collective-permute-start.8
  1561.1 26.7 collective-permute-start.8
  1587.9 26.7 collective-permute-start.8
  1614.7 26.7 collective-permute-start.8
  1658.5 26.7 collective-permute-start.4
  1685.2 26.7 collective-permute-start.4
  1712.0 26.7 collective-permute-start.4
  1738.7 26.7 collective-permute-start.4
  1765.5 26.7 collective-permute-start.4
  1792.3 26.7 collective-permute-start.4
  1819.0 26.7 collective-permute-start.4
  1845.8 26.7 collective-permute-start.4
  1893.6 224.1 %all-to-all-start.21 = ((bf16[2,2,49152]{2,1,0:T(2,128)(2,1)}), bf16[2,2,49152]{2,1,0:T(2,128)(2,1)}, u32[]{:S(2)}, u32[]{:S(2)}) async-start(bf16[2,2,49152]{2,1,0:T(2,128)(2,1)} %reshape.1657), calls=%async_computation.21 | async-start | bytes 786432 | tf_op jit(solution)/shard_map/all_to_all | solution.py:390
  1898.0 27.3 collective-permute-start
  1925.4 26.7 collective-permute-start
  1952.2 26.7 collective-permute-start
  2059.1 26.7 collective-permute-start
  2121.8 278.0 %reduce-scatter.19.cloned.1.call-start = ((), (), s32[]{:S(2)}) async-start(), calls=%async_computation.55 | async-start | bytes 2433024
  2183.6 216.1 %reduce-scatter.21.cloned.1.call-start = ((), (), s32[]{:S(2)}) async-start(), calls=%async_computation.56 | async-start | bytes 2433024
  2239.9 210.8 %reduce-scatter.23.cloned.1.call-start = ((), (), s32[]{:S(2)}) async-start(), calls=%async_computation.57 | async-start | bytes 2433024
  2258.6 333.2 %reduce-scatter.15.cloned.1.call-start = ((), (), s32[]{:S(2)}) async-start(), calls=%async_computation.53 | async-start | bytes 9732096 | tf_op jit(solution)/shard_map/reduce_scatter | solution.py:438
  2285.5 448.3 %reduce-scatter.17.cloned.1.call-start = ((), (), s32[]{:S(2)}) async-start(), calls=%async_computation.54 | async-start | bytes 9732096 | tf_op jit(solution)/shard_map/reduce_scatter | solution.py:438
  (571 other events, 5776.5 us)
Sparse Core Ops, SparseCore 0:
  10.9 56.8 all-gather.14
  70.7 53.2 all-gather.20
  126.9 53.0 all-gather.18
  181.5 37.2 all-gather.38
  220.3 37.1 all-gather.40
  258.9 37.1 all-gather.34
  297.8 37.1 all-gather.36
  336.6 37.1 all-gather.30
  375.4 37.1 all-gather.32
  414.1 37.1 all-gather.16
  452.9 37.1 all-gather.22
  492.8 53.2 all-gather.24
  549.1 62.5 all-gather.26
  614.4 62.4 all-gather.28
  1167.7 100.9 reduce-scatter.12
  2142.9 99.2 reduce-scatter.18
  2247.8 98.1 reduce-scatter.20
  2352.6 97.9 reduce-scatter.22
  2457.1 134.6 reduce-scatter.14
  2599.2 134.6 reduce-scatter.16
where the time goes:
time: 2760 us; the launch traced here: 2740 us
  matrix products  837 us (30%)
  waiting for transfers between devices  659 us (24%)
  other arithmetic  492 us (18%)
  local copies, waits for them, and re-layouts  440 us (16%)
  blocking collectives  154 us (6%)
  starting transfers between devices  111 us (4%)
  loops' own time  29.3 us (1%)
    reduce_scatter x3, waiting for transfers between devices, local(): lax.psum_scatter(totals, ('batch', 'blk', 'head'), scatter_dimension=0, t...  283 us
    ppermute x128, waiting for transfers between devices, shifted(): return lax.ppermute(block, axis, route)  234 us
    dot_general x32, matrix products, attend_block(): jnp.einsum('shqk,skhd->sqhd', weights.astype(jnp.bfloat16), split_heads(v...  151 us
    unnamed x621, local copies, waits for them, and re-layouts  145 us
    dot_general x32, matrix products, attend_block(): jnp.einsum('sqhd,skhd->shqk', queries, split_heads(key_block, head_count)...  142 us
    dot_general x32, matrix products, block_grads(): jnp.einsum('sqhd,skhd->shqk', grad_heads, value_heads, preferred_element_...  138 us
    reduce_sum x32, other arithmetic, attend_block(): new_sum = run_sum * rescale + jnp.sum(weights, axis=-1)  121 us
    dot_general x32, matrix products, block_grads(): jnp.einsum('sqhd,skhd->shqk', query_heads, key_heads, preferred_element_t...  117 us
  transfers between devices with their start and end apart: 172, of which 79 were waited for; matrix products, arithmetic and copies ran while one was open for 59% of the time, Pallas kernels for 0%

commit v1 on v0

v1 whole, which is shorter than its diff:
```python
import functools
import math

import jax
import jax.numpy as jnp
from jax import lax
from jax.experimental import pallas as pl
from jax.experimental.pallas import tpu as pltpu
from jax.sharding import PartitionSpec as P

HEADS = 12
HEAD_DIM = 64
CORES = 2
MEMBERS = 4
EXTRA = 16
NEG_BIG = -1e30
EPSILON = 1e-06
F32 = jnp.float32
BF16 = jnp.bfloat16
ALL_AXES = ("batch", "blk", "head")
VMEM_LIMIT = 56 * 2**20


def dot(left_op, right_op, left_dim, right_dim):
    return lax.dot_general(
        left_op, right_op, (((left_dim,), (right_dim,)), ((), ())), preferred_element_type=F32
    )


def shift_planes(array, distance):
    size = lax.axis_size("blk")
    route = [(i, (i + CORES * distance) % size) for i in range(size)]
    return lax.ppermute(array, "blk", route)


def shift_batch(array, distance):
    size = lax.axis_size("batch")
    return lax.ppermute(array, "batch", [(i, (i + distance) % size) for i in range(size)])


def swap_member(array, member):
    size = lax.axis_size("blk")
    if member == 1:
        return lax.ppermute(array, "head", [(0, 1), (1, 0)])
    if member == 2:
        return lax.ppermute(array, "blk", [(i, i ^ 1) for i in range(size)])
    route = [(i * 2 + j, (i ^ 1) * 2 + (j ^ 1)) for i in range(size) for j in range(2)]
    return lax.ppermute(array, ("blk", "head"), route)


def pick(array, index):
    return lax.dynamic_index_in_dim(array, index, 0, keepdims=False)


def reorder_members(stack, core, head_place):
    stack = jnp.where(core == 1, jnp.concatenate([stack[2:], stack[:2]]), stack)
    swapped = jnp.stack([stack[1], stack[0], stack[3], stack[2]])
    return jnp.where(head_place == 1, swapped, stack)


def forward_kernel(block_q, block_k, q_ref, k_ref, v_ref, mask_ref, out_ref, sums_ref, keys, values):
    key_count = k_ref.shape[1]
    query_count = q_ref.shape[1]
    rows = lax.broadcasted_iota(jnp.int32, (EXTRA, key_count), 0)
    joined = jnp.concatenate([k_ref[...], mask_ref[...]], axis=0)
    keys[...] = joined.astype(F32).T.astype(BF16)
    values[:HEAD_DIM, :] = v_ref[...]
    values[HEAD_DIM:, :] = jnp.where(rows == 0, 1.0, 0.0).astype(BF16)
    rows_q = lax.broadcasted_iota(jnp.int32, (EXTRA, block_q), 0)
    ones_row = jnp.where(rows_q == 0, 1.0, 0.0).astype(BF16)
    scale = 1.0 / math.sqrt(HEAD_DIM)

    def query_block(i, unused):
        q_start = pl.multiple_of(i * block_q, block_q)
        scaled = (q_ref[:, pl.ds(q_start, block_q)].astype(F32) * scale).astype(BF16)
        query = jnp.concatenate([scaled, ones_row], axis=0)

        def key_block(j, carry):
            top, acc = carry
            k_start = pl.multiple_of(j * block_k, block_k)
            scores = dot(keys[pl.ds(k_start, block_k), :], query, 1, 0)
            new_top = jnp.maximum(top, jnp.max(scores, axis=0, keepdims=True))
            probs = jnp.exp(scores - new_top)
            acc = acc * jnp.exp(top - new_top) + dot(
                values[:, pl.ds(k_start, block_k)], probs.astype(BF16), 1, 0
            )
            return new_top, acc

        top, acc = lax.fori_loop(
            0,
            key_count // block_k,
            key_block,
            (
                jnp.full((1, block_q), NEG_BIG, F32),
                jnp.zeros((HEAD_DIM + EXTRA, block_q), F32),
            ),
        )
        total = acc[HEAD_DIM : HEAD_DIM + 1, :]
        out_ref[:, pl.ds(q_start, block_q)] = (acc[:HEAD_DIM, :] / total).astype(BF16)
        sums_ref[0, :, pl.ds(q_start, block_q)] = top + jnp.log(total)
        return 0

    lax.fori_loop(0, query_count // block_q, query_block, 0)


def attention_forward(queries, keys, values, mask_rows):
    heads = queries.shape[0] // HEAD_DIM
    query_count = queries.shape[1]
    key_count = keys.shape[1]
    block_q = min(1024, query_count)
    block_k = min(1024, key_count)
    spec_q = pl.BlockSpec((HEAD_DIM, query_count), lambda h: (h, 0))
    spec_k = pl.BlockSpec((HEAD_DIM, key_count), lambda h: (h, 0))
    return pl.pallas_call(
        functools.partial(forward_kernel, block_q, block_k),
        grid=(heads,),
        in_specs=[spec_q, spec_k, spec_k, pl.BlockSpec((EXTRA, key_count), lambda h: (0, 0))],
        out_specs=[spec_q, pl.BlockSpec((1, 1, query_count), lambda h: (h, 0, 0))],
        out_shape=[
            jax.ShapeDtypeStruct((heads * HEAD_DIM, query_count), BF16),
            jax.ShapeDtypeStruct((heads, 1, query_count), F32),
        ],
        scratch_shapes=[
            pltpu.VMEM((key_count, HEAD_DIM + EXTRA), BF16),
            pltpu.VMEM((HEAD_DIM + EXTRA, key_count), BF16),
        ],
        compiler_params=pltpu.CompilerParams(vmem_limit_bytes=VMEM_LIMIT),
        cost_estimate=pl.CostEstimate(
            flops=heads * 16 * HEAD_DIM * query_count * key_count,
            transcendentals=heads * query_count * key_count,
            bytes_accessed=heads * 8 * HEAD_DIM * key_count,
        ),
    )(queries, keys, values, mask_rows)


def split_three(row):
    high = row.astype(BF16)
    rest = row - high.astype(F32)
    middle = rest.astype(BF16)
    low = (rest - middle.astype(F32)).astype(BF16)
    return high.astype(F32), middle.astype(F32), low.astype(F32)


def backward_kernel(
    block_q,
    block_k,
    q_ref,
    k_ref,
    v_ref,
    mask_ref,
    out_ref,
    sums_ref,
    grad_ref,
    dq_ref,
    dk_ref,
    dv_ref,
    query_rows,
    keys,
    grad_rows,
    values,
    scaled_q,
    dq_acc,
):
    key_count = k_ref.shape[1]
    query_count = q_ref.shape[1]
    scale = 1.0 / math.sqrt(HEAD_DIM)
    places_q = lax.broadcasted_iota(jnp.int32, (EXTRA, query_count), 0)
    places_k = lax.broadcasted_iota(jnp.int32, (EXTRA, key_count), 0)

    def extra_rows(row, fourth):
        high, middle, low = split_three(row)
        rows = jnp.where(
            places_q == 0, high, jnp.where(places_q == 1, middle, jnp.where(places_q == 2, low, 0.0))
        )
        return jnp.where(places_q == 3, fourth, rows).astype(BF16)

    query = (q_ref[...].astype(F32) * scale).astype(BF16)
    scaled_q[...] = query
    grads = grad_ref[...]
    deltas = jnp.sum(grads.astype(F32) * out_ref[...].astype(F32), axis=0, keepdims=True)
    joined_q = jnp.concatenate([query, extra_rows(-sums_ref[0], 1.0)], axis=0)
    query_rows[...] = joined_q.astype(F32).T.astype(BF16)
    joined_g = jnp.concatenate([grads, extra_rows(-deltas, 0.0)], axis=0)
    grad_rows[...] = joined_g.astype(F32).T.astype(BF16)
    ones_rows = jnp.where(places_k < 3, 1.0, 0.0)
    mask_row = mask_ref[0:1, :].astype(F32)
    keys[:HEAD_DIM, :] = k_ref[...]
    keys[HEAD_DIM:, :] = jnp.where(places_k == 3, mask_row, ones_rows).astype(BF16)
    values[:HEAD_DIM, :] = v_ref[...]
    values[HEAD_DIM:, :] = ones_rows.astype(BF16)
    dq_acc[...] = jnp.zeros_like(dq_acc)

    def key_block(j, unused):
        k_start = pl.multiple_of(j * block_k, block_k)
        key_part = keys[:, pl.ds(k_start, block_k)]
        value_part = values[:, pl.ds(k_start, block_k)]
        plain_keys = k_ref[:, pl.ds(k_start, block_k)]

        def query_block(i, carry):
            dk, dv = carry
            q_start = pl.multiple_of(i * block_q, block_q)
            probs = jnp.exp(dot(query_rows[pl.ds(q_start, block_q), :], key_part, 1, 0))
            moved = dot(grad_rows[pl.ds(q_start, block_q), :], value_part, 1, 0)
            grad_scores = (probs * moved).astype(BF16)
            dv = dv + dot(grad_ref[:, pl.ds(q_start, block_q)], probs.astype(BF16), 1, 0)
            dk = dk + dot(scaled_q[:, pl.ds(q_start, block_q)], grad_scores, 1, 0)
            dq_acc[:, pl.ds(q_start, block_q)] += dot(plain_keys, grad_scores, 1, 1)
            return dk, dv

        zeros = jnp.zeros((HEAD_DIM, block_k), F32)
        dk, dv = lax.fori_loop(0, query_count // block_q, query_block, (zeros, zeros))
        dk_ref[:, pl.ds(k_start, block_k)] = dk.astype(BF16)
        dv_ref[:, pl.ds(k_start, block_k)] = dv.astype(BF16)
        return 0

    lax.fori_loop(0, key_count // block_k, key_block, 0)
    dq_ref[...] = (dq_acc[...] * scale).astype(BF16)


def attention_backward(queries, keys, values, mask_rows, outs, sums, grads):
    heads = queries.shape[0] // HEAD_DIM
    query_count = queries.shape[1]
    key_count = keys.shape[1]
    block_q = min(1024, query_count)
    block_k = min(1024, key_count)
    spec_q = pl.BlockSpec((HEAD_DIM, query_count), lambda h: (h, 0))
    spec_k = pl.BlockSpec((HEAD_DIM, key_count), lambda h: (h, 0))
    wide = HEAD_DIM + EXTRA
    return pl.pallas_call(
        functools.partial(backward_kernel, block_q, block_k),
        grid=(heads,),
        in_specs=[
            spec_q,
            spec_k,
            spec_k,
            pl.BlockSpec((EXTRA, key_count), lambda h: (0, 0)),
            spec_q,
            pl.BlockSpec((1, 1, query_count), lambda h: (h, 0, 0)),
            spec_q,
        ],
        out_specs=[spec_q, spec_k, spec_k],
        out_shape=[
            jax.ShapeDtypeStruct((heads * HEAD_DIM, query_count), BF16),
            jax.ShapeDtypeStruct((heads * HEAD_DIM, key_count), BF16),
            jax.ShapeDtypeStruct((heads * HEAD_DIM, key_count), BF16),
        ],
        scratch_shapes=[
            pltpu.VMEM((query_count, wide), BF16),
            pltpu.VMEM((wide, key_count), BF16),
            pltpu.VMEM((query_count, wide), BF16),
            pltpu.VMEM((wide, key_count), BF16),
            pltpu.VMEM((HEAD_DIM, query_count), BF16),
            pltpu.VMEM((HEAD_DIM, query_count), F32),
        ],
        compiler_params=pltpu.CompilerParams(vmem_limit_bytes=VMEM_LIMIT),
        cost_estimate=pl.CostEstimate(
            flops=heads * 40 * HEAD_DIM * query_count * key_count,
            transcendentals=heads * query_count * key_count,
            bytes_accessed=heads * 16 * HEAD_DIM * key_count,
        ),
    )(queries, keys, values, mask_rows, outs, sums, grads)


def norm_apply(residue, gain_row, shift_row):
    center = jnp.mean(residue, axis=-1, keepdims=True)
    centred = residue - center
    spread = jnp.mean(centred * centred, axis=-1, keepdims=True)
    return centred * lax.rsqrt(spread + EPSILON) * gain_row + shift_row


def gelu_exact(pre_act):
    return jax.nn.gelu(pre_act, approximate=False)


def pad_rows(array, count):
    return jnp.concatenate([array, jnp.zeros((count,) + array.shape[1:], array.dtype)])


def local(
    layer_input,
    lengths,
    cotangent,
    w_query,
    b_query,
    w_key,
    w_value,
    b_value,
    w_attn_out,
    b_attn_out,
    norm1_gain,
    norm1_bias,
    w_inner,
    b_inner,
    w_outer,
    b_outer,
    norm2_gain,
    norm2_bias,
):
    seqs, part_rows, width = layer_input.shape
    batches = lax.axis_size("batch")
    planes = lax.axis_size("blk") // CORES
    devices = batches * planes * MEMBERS
    spread_planes = planes // seqs
    piece = part_rows // spread_planes
    row_count = planes * piece
    share = width // devices
    wide_share = w_outer.shape[0]
    hidden = wide_share * devices
    folds = hidden // width
    group = width // MEMBERS

    plane = lax.axis_index("blk") // CORES
    core = lax.axis_index("blk") % CORES
    head_place = lax.axis_index("head")
    batch_place = lax.axis_index("batch")
    device = (batch_place * planes + plane) * MEMBERS + core * 2 + head_place
    seq_length = pick(lengths, plane // spread_planes)
    part = plane % spread_planes

    def places(other_plane):
        source = (other_plane - jnp.arange(planes, dtype=jnp.int32)) % planes
        member = jnp.arange(MEMBERS, dtype=jnp.int32)
        cores = core ^ (member // 2)
        heads = head_place ^ (member % 2)
        base = (source[None, :] * CORES + cores[:, None]) * 2 + heads[:, None]
        offset = (other_plane % spread_planes) * piece + jnp.arange(piece, dtype=jnp.int32)
        return (base[:, :, None] * part_rows + offset).reshape(-1)

    def to_planes(array):
        chunks = array.reshape(planes, piece, width)
        pieces = [pick(chunks, plane)]
        for distance in range(1, planes):
            chunk = pick(chunks, (plane + distance) % planes)
            pieces.append(shift_planes(chunk, distance))
        return pieces

    def from_planes(array):
        pieces = array.reshape(planes, piece, width)
        back = [pieces[0]]
        for distance in range(1, planes):
            back.append(shift_planes(pieces[distance], -distance))
        doubled = jnp.concatenate([jnp.stack(back)] * 2)
        ordered = lax.dynamic_slice_in_dim(doubled, planes - plane, planes, 0)
        return ordered.reshape(seqs, part_rows, width)

    small = jnp.concatenate(
        [b_query, b_value, b_attn_out, norm1_gain, norm1_bias, b_outer, norm2_gain, norm2_bias]
        + [b_inner]
    )
    small_row = jnp.pad(small, (0, width - small.shape[0]))[None]
    first_rows = 3 * share
    first_pack = jnp.concatenate([w_query, w_key, w_value, small_row])
    first_pack = pad_rows(first_pack, -first_pack.shape[0] % 16)
    first = lax.all_gather(first_pack, ALL_AXES, axis=0, tiled=False)
    inner_rows = jnp.swapaxes(w_inner.reshape(share, folds, width), 0, 1).reshape(-1, width)
    second_pack = jnp.concatenate([w_attn_out, inner_rows, w_outer])
    second = lax.all_gather(second_pack, ALL_AXES, axis=0, tiled=False)

    small_all = first[:, first_rows]
    vectors = jnp.swapaxes(small_all[:, : 8 * share].reshape(devices, 8, share), 0, 1)
    vectors = vectors.reshape(8, width).astype(F32)
    bias_query, bias_value, bias_out, gain_first = vectors[:4]
    shift_first, bias_outer, gain_second, shift_second = vectors[4:]
    bias_inner = small_all[:, 8 * share : 8 * share + wide_share].reshape(hidden).astype(F32)

    weights_qkv = [
        first[:, i * share : (i + 1) * share].reshape(width, MEMBERS, group) for i in range(3)
    ]
    by_group = jnp.stack([jnp.moveaxis(weight, 1, 0) for weight in weights_qkv], axis=2)
    by_member = reorder_members(by_group, core, head_place).reshape(MEMBERS, width, 3 * group)
    own_weight = by_member[0]
    own_group = core * 2 + head_place
    own_bias = jnp.concatenate(
        [
            pick(bias_query.reshape(MEMBERS, group), own_group),
            jnp.zeros((group,), F32),
            pick(bias_value.reshape(MEMBERS, group), own_group),
        ]
    )

    own_pieces = to_planes(layer_input)
    head_pieces = [swap_member(part_in, 1) for part_in in own_pieces]
    core_pieces = [swap_member(part_in, 2) for part_in in own_pieces]
    both_pieces = [swap_member(part_in, 2) for part_in in head_pieces]
    rows_own = jnp.concatenate(own_pieces)
    rows_all = jnp.concatenate(own_pieces + head_pieces + core_pieces + both_pieces)

    cot_own = jnp.concatenate(to_planes(cotangent))

    valid_own = places(plane) < seq_length
    row_keep = valid_own[:row_count, None]

    def other_plane(distance):
        return (plane // spread_planes) * spread_planes + (part - distance) % spread_planes

    def shift_parts(array, distance):
        size = lax.axis_size("blk")
        route = []
        for i in range(size):
            start = i // CORES // spread_planes * spread_planes
            target = start + (i // CORES - start + distance) % spread_planes
            route.append((i, target * CORES + i % CORES))
        return lax.ppermute(array, "blk", route)

    qkv = dot(own_weight, rows_all, 0, 1) + own_bias[:, None]
    qkv = qkv.astype(BF16)
    queries, keys, values = qkv[:group], qkv[group : 2 * group], qkv[2 * group :]
    valid_keys = [valid_own]
    if spread_planes > 1:
        more = [shift_parts(qkv[group:], distance) for distance in range(1, spread_planes)]
        keys = jnp.concatenate([keys] + [array[:group] for array in more], axis=1)
        values = jnp.concatenate([values] + [array[group:] for array in more], axis=1)
        for distance in range(1, spread_planes):
            valid_keys.append(places(other_plane(distance)) < seq_length)
    valid = jnp.concatenate(valid_keys)
    mask_row = jnp.where(valid, 0.0, NEG_BIG).astype(BF16)[None]
    mask_rows = pad_rows(mask_row, EXTRA - 1)

    outs, sums = attention_forward(queries, keys, values, mask_rows)

    def to_members(array):
        parts = [array[:, :row_count]]
        for member in range(1, MEMBERS):
            sent = array[:, member * row_count : (member + 1) * row_count]
            parts.append(swap_member(sent, member))
        return parts

    attended = jnp.concatenate(to_members(outs))

    weight_out = second[:, :share].reshape(MEMBERS, group, width)
    weight_out = reorder_members(weight_out, core, head_place).reshape(width, width)
    weight_inner = second[:, share : share + share * folds].reshape(devices, folds, share, width)
    weight_inner = jnp.swapaxes(weight_inner, 1, 2).reshape(width, hidden)
    weight_outer = second[:, share + share * folds :].reshape(hidden, width)

    branch = dot(attended, weight_out, 0, 0) + bias_out
    normed1, back_first = jax.vjp(
        norm_apply, rows_own.astype(F32) + branch, gain_first, shift_first
    )
    normed_low = normed1.astype(BF16)
    inner_pre = dot(normed_low, weight_inner, 1, 0) + bias_inner
    active, back_gelu = jax.vjp(gelu_exact, inner_pre)
    active_low = active.astype(BF16)
    outer_out = dot(active_low, weight_outer, 1, 0) + bias_outer
    final_rows, back_second = jax.vjp(
        norm_apply, normed1 + outer_out, gain_second, shift_second
    )
    output = from_planes(final_rows.astype(BF16))

    grad_final = jnp.where(row_keep, cot_own.astype(F32), 0.0)
    grad_resid2, grad_gain2, grad_shift2 = back_second(grad_final)
    grad_outer = grad_resid2.astype(BF16)
    grad_bias_outer = jnp.sum(grad_outer.astype(F32), axis=0)
    grad_weight_outer = dot(active_low, grad_outer, 0, 0)
    (grad_inner_pre,) = back_gelu(dot(grad_outer, weight_outer, 1, 1))
    grad_inner = grad_inner_pre.astype(BF16)
    grad_bias_inner = jnp.sum(grad_inner.astype(F32), axis=0)
    grad_weight_inner = dot(normed_low, grad_inner, 0, 0)
    grad_normed1 = grad_resid2 + dot(grad_inner, weight_inner, 1, 1)
    grad_resid1, grad_gain1, grad_shift1 = back_first(grad_normed1)
    grad_branch = grad_resid1.astype(BF16)
    grad_bias_out = jnp.sum(grad_branch.astype(F32), axis=0)
    grad_weight_out = dot(attended, grad_branch, 1, 0).astype(BF16)
    grad_weight_out = reorder_members(
        grad_weight_out.reshape(MEMBERS, group, width), core, head_place
    )
    grad_attended = dot(weight_out, grad_branch, 1, 1).astype(BF16)

    vector_grads = [
        grad_bias_out,
        grad_gain1,
        grad_shift1,
        grad_bias_outer,
        grad_gain2,
        grad_shift2,
    ]
    vector_pack = jnp.concatenate(
        [vector.reshape(devices, share) for vector in vector_grads]
        + [grad_bias_inner.reshape(devices, wide_share)],
        axis=1,
    )
    vector_pack = jnp.pad(vector_pack, ((0, 0), (0, width - vector_pack.shape[1])))
    inner_pack = jnp.swapaxes(
        grad_weight_inner.astype(BF16).reshape(devices, share, folds, width), 1, 2
    ).reshape(devices, folds * share, width)
    grad_pack = jnp.concatenate(
        [
            grad_weight_out.reshape(devices, share, width),
            inner_pack,
            grad_weight_outer.astype(BF16).reshape(devices, wide_share, width),
            vector_pack.astype(BF16)[:, None],
        ],
        axis=1,
    )
    grad_pack = jnp.pad(grad_pack, ((0, 0), (0, -grad_pack.shape[1] % 16), (0, 0)))
    owned = lax.psum_scatter(grad_pack, ALL_AXES, scatter_dimension=0, tiled=True)[0].astype(F32)
    owned_out = owned[:share]
    owned_inner = owned[share : share + folds * share].reshape(folds, share, width)
    owned_inner = jnp.swapaxes(owned_inner, 0, 1).reshape(share, hidden)
    outer_start = share + folds * share
    owned_outer = owned[outer_start : outer_start + wide_share]
    owned_vectors = owned[outer_start + wide_share]

    grad_parts = [grad_attended[:group]]
    for member in range(1, MEMBERS):
        sent = grad_attended[member * group : (member + 1) * group]
        grad_parts.append(swap_member(sent, member))
    grad_side = jnp.concatenate(grad_parts, axis=1)
    grad_q, grad_k, grad_v = attention_backward(
        queries, keys, values, mask_rows, outs, sums, grad_side
    )
    if spread_planes > 1:
        grad_kv = jnp.concatenate([grad_k, grad_v])
        plane_rows = MEMBERS * row_count
        total = grad_kv[:, :plane_rows].astype(F32)
        for distance in range(1, spread_planes):
            sent = grad_kv[:, distance * plane_rows : (distance + 1) * plane_rows]
            total = total + shift_parts(sent, -distance).astype(F32)
        grad_k, grad_v = total[:group].astype(BF16), total[group:].astype(BF16)
    grad_qkv = jnp.concatenate([grad_q, grad_k, grad_v])

    grad_rows = jnp.concatenate(to_members(grad_qkv))
    weight_rows = jnp.swapaxes(by_member, 0, 1).reshape(width, MEMBERS * 3 * group)
    grad_input = (grad_resid1 + dot(grad_rows, weight_rows, 0, 1)).astype(BF16)
    input_grad = from_planes(grad_input)

    grad_weight = dot(rows_all, grad_qkv, 0, 1).astype(BF16)
    grad_bias = jnp.sum(grad_qkv.astype(F32), axis=1).astype(BF16)
    chunk_rows = width // (batches * planes)
    extra = -chunk_rows % 16 + 16
    bias_block = jnp.pad(grad_bias[None], ((0, extra - 1), (0, 0)))
    chunks = grad_weight.reshape(batches * planes, chunk_rows, 3 * group)
    bias_blocks = jnp.broadcast_to(bias_block, (batches * planes,) + bias_block.shape)
    chunks = jnp.concatenate([chunks, bias_blocks], axis=1)
    chunks = chunks.reshape((batches, planes) + chunks.shape[1:])
    total = pick(chunks, batch_place).astype(F32)
    for distance in range(1, batches):
        sent = pick(chunks, (batch_place + distance) % batches)
        total = total + shift_batch(sent, distance).astype(F32)
    sending = total.astype(BF16)
    total = pick(total, plane)
    for distance in range(1, planes):
        sent = pick(sending, (plane + distance) % planes)
        total = total + shift_planes(sent, distance).astype(F32)
    bias_total = total[chunk_rows]
    member_rows = total[:chunk_rows].reshape(MEMBERS, share, 3 * group)
    member_rows = reorder_members(member_rows, core, head_place)
    tail = jnp.zeros((MEMBERS, -share % 16 + 16, 3 * group), F32).at[:, 0].set(bias_total)
    sending = jnp.concatenate([member_rows, tail], axis=1)
    bias_at = sending.shape[1] - tail.shape[1]
    got = [sending[0]] + [
        swap_member(sending[member], member) for member in range(1, MEMBERS)
    ]
    got = reorder_members(jnp.stack(got), core, head_place)
    got = got.reshape(MEMBERS, got.shape[1], 3, group)
    matrices = [
        jnp.swapaxes(got[:, :share, i], 0, 1).reshape(share, width) for i in range(3)
    ]
    biases = [
        lax.dynamic_slice_in_dim(got[:, bias_at, i].reshape(width), device * share, share)
        for i in (0, 2)
    ]

    def vector(index):
        return owned_vectors[index * share : (index + 1) * share]

    return (
        output,
        input_grad,
        matrices[0],
        biases[0],
        matrices[1],
        matrices[2],
        biases[1],
        owned_out,
        vector(0),
        vector(1),
        vector(2),
        owned_inner,
        owned_vectors[6 * share : 6 * share + wide_share],
        owned_outer,
        vector(3),
        vector(4),
        vector(5),
    )


def solution(mesh):
    rows = P("batch", ("blk", "head"), None)
    matrix = P(ALL_AXES, None)
    vector = P(ALL_AXES)
    parameters = (
        matrix,
        vector,
        matrix,
        matrix,
        vector,
        matrix,
        vector,
        vector,
        vector,
        matrix,
        vector,
        matrix,
        vector,
        vector,
        vector,
    )
    return jax.shard_map(
        local,
        mesh=mesh,
        in_specs=(rows, P("batch"), rows) + parameters,
        out_specs=(rows, rows) + parameters,
        check_vma=False,
    )
```

time: 2760 us -> 809 us (0.29)
  matrix products: 837 us -> 121 us
  waiting for transfers between devices: 659 us -> 127 us
  other arithmetic: 492 us -> 70.4 us
  Pallas kernels: 0 us -> 219 us
  local copies, waits for them, and re-layouts: 440 us -> 221 us
  blocking collectives: 154 us -> 0 us
  starting transfers between devices: 111 us -> 33.5 us
  loops' own time: 29.3 us -> 0 us
    dot_general x296 -> x12, matrix products: 837 us -> 121 us  [dot(): lax.dot_general(left_op, right_op, (((left_dim,), (right_dim,)), ((), ())...]
    reduce_scatter x3 -> x1, waiting for transfers between devices: 283 us -> 0.01 us  [local(): lax.psum_scatter(grad_pack, ALL_AXES, scatter_dimension=0, tiled=True)[0]]
    pallas_call x0 -> x2, Pallas kernels: none -> 219 us  [the longest x1 135 us: attention_backward(): pl.pallas_call(functools.partial(backward_kernel, block_q, block_k), grid...]
    convert_element_type x153 -> x5, other arithmetic: 141 us -> 2.61 us  [the longest x1 1.32 us: local(): mask_row = jnp.where(valid, 0.0, NEG_BIG).astype(BF16)[None]]
    ppermute x128 -> x40, waiting for transfers between devices: 234 us -> 104 us  [the longest x15 64.7 us: shift_planes(): return lax.ppermute(array, 'blk', route)]
    reduce_sum x48 -> x3, other arithmetic: 135 us -> 5.38 us  [the longest x1 3.04 us: local(): grad_bias = jnp.sum(grad_qkv.astype(F32), axis=1).astype(BF16)]
    unnamed x57 -> x4, other arithmetic: 112 us -> 0.01 us
    while x512 -> x0, local copies, waits for them, and re-layouts: 111 us -> none
  transfers between devices with their start and end apart: 172 -> 43, of which waited for: 79 -> 14; matrix products, arithmetic and copies ran while one was open for 59% -> 41% of each run, Pallas kernels for 0% -> 27%
where the time goes in v1:
time: 809 us; the launch traced here: 808 us
  local copies, waits for them, and re-layouts  221 us (27%)
  Pallas kernels  219 us (27%)
  waiting for transfers between devices  127 us (16%)
  matrix products  121 us (15%)
  other arithmetic  70.4 us (9%)
  starting transfers between devices  33.5 us (4%)
  between operations  15.2 us (2%)
    pallas_call x1, Pallas kernels, attention_backward(): pl.pallas_call(functools.partial(backward_kernel, block_q, block_k), grid...  135 us
    dot_general x12, matrix products, dot(): lax.dot_general(left_op, right_op, (((left_dim,), (right_dim,)), ((), ())...  121 us
    pallas_call x1, Pallas kernels, attention_forward(): pl.pallas_call(functools.partial(forward_kernel, block_q, block_k), grid=...  83.7 us
    ppermute x15, waiting for transfers between devices, shift_planes(): return lax.ppermute(array, 'blk', route)  64.7 us
    slice x9, local copies, waits for them, and re-layouts, reorder_members(): swapped = jnp.stack([stack[1], stack[0], stack[3], stack[2]])  41.1 us
    unnamed x154, local copies, waits for them, and re-layouts  37.5 us
    ppermute x8, waiting for transfers between devices, swap_member(): return lax.ppermute(array, 'head', [(0, 1), (1, 0)])  29.5 us
    all_gather x1, waiting for transfers between devices, local(): first = lax.all_gather(first_pack, ALL_AXES, axis=0, tiled=False)  22.9 us
  transfers between devices with their start and end apart: 43, of which 14 were waited for; matrix products, arithmetic and copies ran while one was open for 41% of the time, Pallas kernels for 27%

profile of v1, /device:TPU:0, one launch (start us, length us, event | category | flops | bytes accessed | tf_op | source)
XLA Modules:
  0.0 807.7 jit_solution(5762652849037981248)
XLA Ops:
  7.2 6.1 concatenate.101
  13.4 4.8 concatenate.102
  44.1 7.4 collective-permute-done.2
  52.1 18.1 %collective-permute-done.1 = bf16[256,768]{0,1:T(8,128)(2,1)S(1)} collective-permute-done((bf16[256,768]{0,1:T(8,128)(2,1)}, bf16[256,768]{0,1:T(8,128)(2,1)S(1)}, u32[]{:S(2)}, u32[]{:S(2)}) %collective-permute-start.1) | collective-permute-done | bytes 393248 | tf_op jit(solution)/shard_map/ppermute | solution.py:33
  74.5 6.9 collective-permute-done.5
  92.7 22.9 %all-gather.5.cloned.1.call-done = bf16[2560,768]{1,0:T(8,128)(2,1)} async-done(((bf16[80,768]{1,0:T(8,128)(2,1)}), bf16[2560,768]{1,0:T(8,128)(2,1)}) %all-gather.5.cloned.1.call-update) | async-done | bytes 3932176 | tf_op jit(solution)/shard_map/all_gather | solution.py:354
  119.8 3.6 fusion.61
  125.2 3.9 reshape.468
  129.1 4.8 reshape.467
  133.8 6.9 pad_maximum_fusion
  140.7 8.1 %copy.97 = bf16[4,768,3,192]{1,3,2,0:T(8,128)(2,1)} copy(bf16[4,768,3,192]{3,0,1,2:T(4,128)(2,1)} %pad_maximum_fusion) | data formatting | bytes 7077888 | tf_op jit(solution)/shard_map/stack | solution.py:369
  148.8 9.3 %fusion.60 = (bf16[2,768,3,192]{3,0,1,2:T(2,128)(2,1)S(1)}, bf16[2,768,3,192]{3,0,1,2:T(2,128)(2,1)}) fusion(bf16[4,768,3,192]{3,0,1,2:T(4,128)(2,1)} %pad_maximum_fusion), kind=kLoop, calls=%fused_computation.223 | loop fusion | bytes 7077888 | tf_op jit(solution)/shard_map/slice | solution.py:56
  158.2 4.4 copy.95
  162.5 6.8 copy.96
  169.3 9.5 %maximum_select_fusion = bf16[4,768,3,192]{3,0,1,2:T(4,128)(2,1)S(1)} fusion(bf16[2,768,3,192]{3,0,1,2:T(2,128)(2,1)} %get-tuple-element.134, bf16[2,768,3,192]{3,0,1,2:T(2,128)(2,1)S(1)} %get-tuple-element.133, pred[]{:T(512)S(6)} %eq.31, bf16[4,768,1,192]{3,0,1,2:T(4,128)(2,1)} %bitcast.208, bf16[4,768,1,192]{3,0,1,2:T(4,128)(2,1)} %bitcast.210, ...), kind=kLoop, calls=%fused_computation.31 | loop fusion | flops 19464192 | bytes 10616833 | tf_op jit(solution)/shard_map/jit(_where)/select_n | solution.py:56
  178.8 19.6 %fusion.59 = (bf16[1,768,3,192]{3,0,1,2:T(2,128)(2,1)S(1)}, bf16[1,768,3,192]{3,0,1,2:T(2,128)(2,1)}, bf16[1,768,3,192]{3,0,1,2:T(2,128)(2,1)}, bf16[1,768,3,192]{3,0,1,2:T(2,128)(2,1)}) fusion(bf16[4,768,3,192]{3,0,1,2:T(4,128)(2,1)S(1)} %maximum_select_fusion), kind=kLoop, calls=%fused_computation.222 | loop fusion | bytes 7077888 | tf_op jit(solution)/shard_map/slice | solution.py:57
  199.9 6.4 copy.93
  206.3 6.4 copy.94
  212.7 6.4 copy.92
  219.0 16.1 %broadcast_select_fusion = bf16[1,768,3,192]{3,0,1,2:T(2,128)(2,1)} fusion(bf16[1,768,3,192]{3,0,1,2:T(2,128)(2,1)} %get-tuple-element.132, pred[]{:T(512)S(6)} %eq.30, bf16[1,768,3,192]{3,0,1,2:T(2,128)(2,1)} %get-tuple-element.130, bf16[1,768,3,192]{3,0,1,2:T(2,128)(2,1)} %get-tuple-element.131, bf16[1,768,3,192]{3,0,1,2:T(2,128)(2,1)S(1)} %get-tuple-element.129), kind=kLoop, calls=%fused_computation.40 | loop fusion | flops 3981312 | bytes 4423681 | tf_op jit(solution)/shard_map/jit(_where)/select_n | solution.py:58
  235.2 5.4 copy.83
  240.7 6.8 add_convert_fusion.1
  249.9 83.7 %shard_map.305 = (bf16[192,4096]{1,0:T(8,128)(2,1)}, f32[3,1,4096]{2,1,0:T(1,128)}) custom-call(bf16[192,4096]{1,0:T(8,128)(2,1)} %get-tuple-element.128.q_ref, bf16[192,4096]{1,0:T(8,128)(2,1)} %get-tuple-element.127.k_ref, bf16[192,4096]{1,0:T(8,128)(2,1)} %get-tuple-element.126.v_ref, bf16[16,4096]{1,0:T(8,128)(2,1)} %concatenate.106.mask_ref), custom_call_target="tpu_custom_call" | custom-call | flops 51539607552 | bytes 6291456 | tf_op jit(solution)/shard_map/pallas_call | solution.py:114
  338.5 3.2 maximum_select_fusion.1
  344.4 6.5 fusion.55
  358.0 3.0 fusion.73
  361.5 36.2 %multiply_convert_fusion = (bf16[1024,3072]{1,0:T(8,128)(2,1)}, f32[1024,3072]{1,0:T(8,128)}, f32[1024,3072]{1,0:T(8,128)}) fusion(f32[3072]{0:T(1024)S(1)} %reshape.496, bf16[768,3072]{1,0:T(8,128)(2,1)S(1)} %bitcast.223, f32[1024,768]{0,1:T(8,128)S(1)} %get-tuple-element.204, f32[768]{0:T(1024)S(1)} %add.325, f32[768]{0:T(1024)S(1)} %mul.185, ...), kind=kOutput, calls=%fused_computation.8 | convolution fusion | flops 5043388416 | bytes 39348224 | tf_op jit(solution)/shard_map/dot_general | solution.py:25
  397.8 7.7 fusion.74
  409.4 3.9 fusion.53
  414.3 6.9 convolution_convert_fusion
  421.2 19.1 %fusion.75 = (bf16[3072]{0:T(1024)(128)(2,1)}, bf16[1024,3072]{1,0:T(8,128)(2,1)}) fusion(f32[1024,3072]{1,0:T(8,128)} %get-tuple-element.117, bf16[1024,768]{0,1:T(8,128)(2,1)} %copy-done.17, bf16[3072,768]{1,0:T(8,128)(2,1)} %bitcast.228, f32[1024,3072]{1,0:T(8,128)} %get-tuple-element.205, f32[3072]{0:T(1024)S(1)} %reshape.496), kind=kOutput, calls=%fused_computation.238 | convolution fusion | flops 4882166784 | bytes 37767168 | tf_op jit(solution)/shard_map/dot_general | solution.py:25
  440.3 11.7 %multiply_reduce_fusion.1 = (bf16[768]{0:T(1024)(128)(2,1)}, f32[1024]{0:T(1024)S(1)}, bf16[768]{0:T(1024)(128)(2,1)}, f32[1024,768]{0,1:T(8,128)}) fusion(f32[1024,768]{0,1:T(8,128)S(1)} %get-tuple-element.204, f32[1024]{0:T(1024)S(1)} %fusion.37, f32[1024]{0:T(1024)S(1)} %broadcast_multiply_fusion.1, f32[768]{0:T(1024)S(1)} %mul.185, ...), kind=kOutput, calls=%fused_computation.44 | convolution fusion | flops 4839699456 | bytes 20469760 | tf_op jit(solution)/shard_map/dot_general | solution.py:25
  452.0 7.2 convolution_convert_fusion.1
  463.4 3.7 fusion.52
  467.1 10.2 %reshape.484 = bf16[32,24,4,768]{3,2,1,0:T(4,128)(2,1)} reshape(bf16[768,3072]{1,0:T(8,128)(2,1)} %convolution_convert_fusion.1) | data formatting | bytes 9437184 | tf_op jit(solution)/shard_map/reshape | solution.py:484
  477.3 5.4 copy.103
  490.0 3.2 convolution_convert_fusion.2
  501.8 5.3 fusion.12
  517.0 135.3 %shard_map.306 = (bf16[192,4096]{1,0:T(8,128)(2,1)}, bf16[192,4096]{1,0:T(8,128)(2,1)}, bf16[192,4096]{1,0:T(8,128)(2,1)}) custom-call(bf16[192,4096]{1,0:T(8,128)(2,1)} %get-tuple-element.128.q_ref, bf16[192,4096]{1,0:T(8,128)(2,1)} %get-tuple-element.127.k_ref, bf16[192,4096]{1,0:T(8,128)(2,1)} %get-tuple-element.126.v_ref, ...), custom_call_target="tpu_custom_call" | custom-call | flops 128849018880 | bytes 12582912 | tf_op jit(solution)/shard_map/pallas_call | solution.py:229
  654.8 9.3 %convolution_convert_fusion.4 = bf16[768,576]{0,1:T(8,128)(2,1)} fusion(bf16[4096,768]{0,1:T(8,128)(2,1)} %constant_dynamic-update-slice_fusion, bf16[576,4096]{1,0:T(8,128)(2,1)S(1)} %constant_dynamic-update-slice_fusion.16), kind=kOutput, calls=%fused_computation.71 | convolution fusion | flops 3624321024 | bytes 11894784 | tf_op jit(solution)/shard_map/dot_general | solution.py:25
  666.5 3.0 reduce_sum.160
  678.8 7.3 collective-permute-done.33
  691.4 3.5 collective-permute-done.34
  696.2 6.0 collective-permute-done.35
  707.3 20.6 %collective-permute-done.39 = f32[48,576]{1,0:T(8,128)S(1)} collective-permute-done((f32[48,576]{1,0:T(8,128)S(1)}, f32[48,576]{1,0:T(8,128)S(1)}, u32[]{:S(2)}, u32[]{:S(2)}) %collective-permute-start.39) | collective-permute-done | bytes 110624 | tf_op jit(solution)/shard_map/ppermute | solution.py:44
  727.9 3.1 collective-permute-done.38
  746.8 7.1 add_convert_fusion.2
  767.2 25.6 %collective-permute-done.31 = bf16[256,768]{0,1:T(8,128)(2,1)S(1)} collective-permute-done((bf16[256,768]{0,1:T(8,128)(2,1)S(1)}, bf16[256,768]{0,1:T(8,128)(2,1)S(1)}, u32[]{:S(2)}, u32[]{:S(2)}) %collective-permute-start.31) | collective-permute-done | bytes 393248 | tf_op jit(solution)/shard_map/ppermute | solution.py:33
  (376 shorter events, 164.3 us)
Async XLA Ops:
  7.2 108.4 %all-gather.5.cloned.1.call-start = ((), (), s32[]{:S(2)}) async-start(), calls=%async_computation.2 | async-start | bytes 4055040 | tf_op jit(solution)/shard_map/all_gather | solution.py:354
  18.2 323.5 %all-gather.7.cloned.1.call-start = ((), (), s32[]{:S(2)}) async-start(), calls=%async_computation.3 | async-start | bytes 10948608 | tf_op jit(solution)/shard_map/all_gather | solution.py:357
  20.9 774.8 %reduce-scatter.2.cloned.1.call-start = ((), (), s32[]{:S(2)}) async-start(), calls=%async_computation.1 | async-start | bytes 11354112 | tf_op jit(solution)/shard_map/reduce_scatter | solution.py:496
  23.2 60.3 %collective-permute-start.7 = (bf16[256,768]{0,1:T(8,128)(2,1)S(1)}, bf16[256,768]{0,1:T(8,128)(2,1)}, u32[]{:S(2)}, u32[]{:S(2)}) collective-permute-start(bf16[256,768]{0,1:T(8,128)(2,1)S(1)} %bitcast.245), channel_id=1, source_target_pairs={{0,2},{2,0},{4,6},{6,4},{8,10},{10,8},{12,14},{14,12},{1,3},{3,1},... | collective-permute-start | bytes 1179656 | tf_op jit(solution)/shard_map/ppermute | solution.py:46
  23.8 48.9 %collective-permute-start.3 = (bf16[256,768]{0,1:T(8,128)(2,1)S(1)}, bf16[256,768]{0,1:T(8,128)(2,1)S(1)}, u32[]{:S(2)}, u32[]{:S(2)}) collective-permute-start(bf16[256,768]{0,1:T(8,128)(2,1)S(1)} %bitcast.246), channel_id=1, source_target_pairs={{0,1},{1,0},{2,3},{3,2},{4,5},{5,4},{6,7},{7,6},{8,9},{9,8},{10,11... | collective-permute-start | bytes 1179656 | tf_op jit(solution)/shard_map/ppermute | solution.py:44
  27.2 16.6 %collective-permute-start = (bf16[256,768]{0,1:T(8,128)(2,1)}, bf16[256,768]{0,1:T(8,128)(2,1)S(1)}, u32[]{:S(2)}, u32[]{:S(2)}) collective-permute-start(bf16[256,768]{0,1:T(8,128)(2,1)} %bitcast.261), channel_id=1, source_target_pairs={{0,4},{2,6},{4,8},{6,10},{8,12},{10,14},{12,0},{14,2},{1,5},{3,7},... | collective-permute-start | bytes 1179656 | tf_op jit(solution)/shard_map/ppermute | solution.py:33
  29.7 21.8 %collective-permute-start.2 = (bf16[256,768]{0,1:T(8,128)(2,1)}, bf16[256,768]{0,1:T(8,128)(2,1)S(1)}, u32[]{:S(2)}, u32[]{:S(2)}) collective-permute-start(bf16[256,768]{0,1:T(8,128)(2,1)} %bitcast.260), channel_id=1, source_target_pairs={{0,12},{2,14},{4,0},{6,2},{8,4},{10,6},{12,8},{14,10},{1,13},{3,15... | collective-permute-start | bytes 1179656 | tf_op jit(solution)/shard_map/ppermute | solution.py:33
  32.9 37.3 %collective-permute-start.1 = (bf16[256,768]{0,1:T(8,128)(2,1)}, bf16[256,768]{0,1:T(8,128)(2,1)S(1)}, u32[]{:S(2)}, u32[]{:S(2)}) collective-permute-start(bf16[256,768]{0,1:T(8,128)(2,1)} %bitcast.259), channel_id=1, source_target_pairs={{0,8},{2,10},{4,12},{6,14},{8,0},{10,2},{12,4},{14,6},{1,9},{3,11}... | collective-permute-start | bytes 1179656 | tf_op jit(solution)/shard_map/ppermute | solution.py:33
  43.8 29.7 %collective-permute-start.4 = (bf16[256,768]{0,1:T(8,128)(2,1)S(1)}, bf16[256,768]{0,1:T(8,128)(2,1)S(1)}, u32[]{:S(2)}, u32[]{:S(2)}) collective-permute-start(bf16[256,768]{0,1:T(8,128)(2,1)S(1)} %collective-permute-done), channel_id=1, source_target_pairs={{0,1},{1,0},{2,3},{3,2},{4,5},{5,4},{6,7},{7,6},{8,9},{9,8},{10,11... | collective-permute-start | bytes 1179656 | tf_op jit(solution)/shard_map/ppermute | solution.py:44
  51.6 30.7 %collective-permute-start.6 = (bf16[256,768]{0,1:T(8,128)(2,1)S(1)}, bf16[256,768]{0,1:T(8,128)(2,1)S(1)}, u32[]{:S(2)}, u32[]{:S(2)}) collective-permute-start(bf16[256,768]{0,1:T(8,128)(2,1)S(1)} %collective-permute-done.2), channel_id=1, source_target_pairs={{0,1},{1,0},{2,3},{3,2},{4,5},{5,4},{6,7},{7,6},{8,9},{9,8},{10,11... | collective-permute-start | bytes 1179656 | tf_op jit(solution)/shard_map/ppermute | solution.py:44
  70.2 11.2 %collective-permute-start.5 = (bf16[256,768]{0,1:T(8,128)(2,1)S(1)}, bf16[256,768]{0,1:T(8,128)(2,1)S(1)}, u32[]{:S(2)}, u32[]{:S(2)}) collective-permute-start(bf16[256,768]{0,1:T(8,128)(2,1)S(1)} %collective-permute-done.1), channel_id=1, source_target_pairs={{0,1},{1,0},{2,3},{3,2},{4,5},{5,4},{6,7},{7,6},{8,9},{9,8},{10,11... | collective-permute-start | bytes 1179656 | tf_op jit(solution)/shard_map/ppermute | solution.py:44
  72.7 333.3 %collective-permute-start.22 = (bf16[256,768]{0,1:T(8,128)(2,1)}, bf16[256,768]{0,1:T(8,128)(2,1)}, u32[]{:S(2)}, u32[]{:S(2)}) collective-permute-start(bf16[256,768]{0,1:T(8,128)(2,1)} %bitcast.34), channel_id=1, source_target_pairs={{0,8},{2,10},{4,12},{6,14},{8,0},{10,2},{12,4},{14,6},{1,9},{3,11}... | collective-permute-start | bytes 1179656 | tf_op jit(solution)/shard_map/ppermute | solution.py:33
  73.5 11.9 %collective-permute-start.8 = (bf16[256,768]{0,1:T(8,128)(2,1)S(1)}, bf16[256,768]{0,1:T(8,128)(2,1)S(1)}, u32[]{:S(2)}, u32[]{:S(2)}) collective-permute-start(bf16[256,768]{0,1:T(8,128)(2,1)S(1)} %collective-permute-done), channel_id=1, source_target_pairs={{0,2},{2,0},{4,6},{6,4},{8,10},{10,8},{12,14},{14,12},{1,3},{3,1},... | collective-permute-start | bytes 1179656 | tf_op jit(solution)/shard_map/ppermute | solution.py:46
  81.4 5.4 collective-permute-start.9
  82.2 5.4 collective-permute-start.10
  83.6 5.4 collective-permute-start.11
  85.4 4.8 collective-permute-start.12
  86.8 4.2 collective-permute-start.13
  87.7 4.2 collective-permute-start.14
  89.0 317.0 %collective-permute-start.23 = (bf16[256,768]{0,1:T(8,128)(2,1)}, bf16[256,768]{0,1:T(8,128)(2,1)}, u32[]{:S(2)}, u32[]{:S(2)}) collective-permute-start(bf16[256,768]{0,1:T(8,128)(2,1)} %bitcast.35), channel_id=1, source_target_pairs={{0,12},{2,14},{4,0},{6,2},{8,4},{10,6},{12,8},{14,10},{1,13},{3,15... | collective-permute-start | bytes 1179656 | tf_op jit(solution)/shard_map/ppermute | solution.py:33
  249.9 88.6 %copy-start.1 = (bf16[4,768,3,192]{1,3,2,0:T(8,128)(2,1)S(1)}, bf16[4,768,3,192]{1,3,2,0:T(8,128)(2,1)}, u32[]{:S(2)}) copy-start(bf16[4,768,3,192]{1,3,2,0:T(8,128)(2,1)} %copy.97) | copy-start | bytes 10616836
  249.9 88.6 %copy-start.10 = (bf16[2,768,3,192]{1,3,2,0:T(8,128)(2,1)S(1)}, bf16[2,768,3,192]{1,3,2,0:T(8,128)(2,1)}, u32[]{:S(2)}) copy-start(bf16[2,768,3,192]{1,3,2,0:T(8,128)(2,1)} %copy.96) | copy-start | bytes 5308420
  249.9 88.6 %copy-start.13 = (bf16[1,768,3,192]{1,3,2,0:T(8,128)(2,1)S(1)}, bf16[1,768,3,192]{1,3,2,0:T(8,128)(2,1)}, u32[]{:S(2)}) copy-start(bf16[1,768,3,192]{1,3,2,0:T(8,128)(2,1)} %copy.94) | copy-start | bytes 2654212
  336.4 18.8 %collective-permute-start.17 = (bf16[192,1024]{1,0:T(8,128)(2,1)}, bf16[192,1024]{1,0:T(8,128)(2,1)}, u32[]{:S(2)}, u32[]{:S(2)}) collective-permute-start(bf16[192,1024]{1,0:T(8,128)(2,1)} %get-tuple-element.154), channel_id=1, source_target_pairs={{0,3},{1,2},{2,1},{3,0},{4,7},{5,6},{6,5},{7,4},{8,11},{9,10},{10,... | collective-permute-start | bytes 1179656 | tf_op jit(solution)/shard_map/ppermute | solution.py:48
  337.9 19.5 %collective-permute-start.16 = (bf16[192,1024]{1,0:T(8,128)(2,1)}, bf16[192,1024]{1,0:T(8,128)(2,1)}, u32[]{:S(2)}, u32[]{:S(2)}) collective-permute-start(bf16[192,1024]{1,0:T(8,128)(2,1)} %get-tuple-element.155), channel_id=1, source_target_pairs={{0,2},{2,0},{4,6},{6,4},{8,10},{10,8},{12,14},{14,12},{1,3},{3,1},... | collective-permute-start | bytes 1179656 | tf_op jit(solution)/shard_map/ppermute | solution.py:46
  338.1 19.3 %collective-permute-start.15 = (bf16[192,1024]{1,0:T(8,128)(2,1)}, bf16[192,1024]{1,0:T(8,128)(2,1)}, u32[]{:S(2)}, u32[]{:S(2)}) collective-permute-start(bf16[192,1024]{1,0:T(8,128)(2,1)} %get-tuple-element.156), channel_id=1, source_target_pairs={{0,1},{1,0},{2,3},{3,2},{4,5},{5,4},{6,7},{7,6},{8,9},{9,8},{10,11... | collective-permute-start | bytes 1179656 | tf_op jit(solution)/shard_map/ppermute | solution.py:44
  356.0 50.0 %collective-permute-start.21 = (bf16[256,768]{0,1:T(8,128)(2,1)S(1)}, bf16[256,768]{0,1:T(8,128)(2,1)S(1)}, u32[]{:S(2)}, u32[]{:S(2)}) collective-permute-start(bf16[256,768]{0,1:T(8,128)(2,1)S(1)} %bitcast.258), channel_id=1, source_target_pairs={{0,4},{2,6},{4,8},{6,10},{8,12},{10,14},{12,0},{14,2},{1,5},{3,7},... | collective-permute-start | bytes 1179656 | tf_op jit(solution)/shard_map/ppermute | solution.py:33
  361.1 90.9 %copy-start.6 = (f32[1024,768]{0,1:T(8,128)}, f32[1024,768]{0,1:T(8,128)S(1)}, u32[]{:S(2)}) copy-start(f32[1024,768]{0,1:T(8,128)S(1)} %get-tuple-element.204) | copy-start | bytes 9437188
  361.5 90.5 %copy-start.44 = (f32[1024]{0:T(1024)}, f32[1024]{0:T(1024)S(1)}, u32[]{:S(2)}) copy-start(f32[1024]{0:T(1024)S(1)} %fusion.37) | copy-start | bytes 12292
  461.0 214.5 %collective-permute-start.20 = (bf16[256,768]{0,1:T(8,128)(2,1)}, bf16[256,768]{0,1:T(8,128)(2,1)}, u32[]{:S(2)}, u32[]{:S(2)}) collective-permute-start(bf16[256,768]{0,1:T(8,128)(2,1)} %get-tuple-element.150), channel_id=1, source_target_pairs={{0,4},{2,6},{4,8},{6,10},{8,12},{10,14},{12,0},{14,2},{1,5},{3,7},... | collective-permute-start | bytes 1179656 | tf_op jit(solution)/shard_map/ppermute | solution.py:33
  462.4 211.3 %collective-permute-start.19 = (bf16[256,768]{0,1:T(8,128)(2,1)}, bf16[256,768]{0,1:T(8,128)(2,1)}, u32[]{:S(2)}, u32[]{:S(2)}) collective-permute-start(bf16[256,768]{0,1:T(8,128)(2,1)} %get-tuple-element.151), channel_id=1, source_target_pairs={{0,8},{2,10},{4,12},{6,14},{8,0},{10,2},{12,4},{14,6},{1,9},{3,11}... | collective-permute-start | bytes 1179656 | tf_op jit(solution)/shard_map/ppermute | solution.py:33
  494.3 15.0 %collective-permute-start.26 = (bf16[192,1024]{1,0:T(8,128)(2,1)}, bf16[192,1024]{1,0:T(8,128)(2,1)S(1)}, u32[]{:S(2)}, u32[]{:S(2)}) collective-permute-start(bf16[192,1024]{1,0:T(8,128)(2,1)} %get-tuple-element.143), channel_id=1, source_target_pairs={{0,3},{1,2},{2,1},{3,0},{4,7},{5,6},{6,5},{7,4},{8,11},{9,10},{10,... | collective-permute-start | bytes 1179656 | tf_op jit(solution)/shard_map/ppermute | solution.py:48
  494.7 17.8 %collective-permute-start.25 = (bf16[192,1024]{1,0:T(8,128)(2,1)}, bf16[192,1024]{1,0:T(8,128)(2,1)}, u32[]{:S(2)}, u32[]{:S(2)}) collective-permute-start(bf16[192,1024]{1,0:T(8,128)(2,1)} %get-tuple-element.144), channel_id=1, source_target_pairs={{0,2},{2,0},{4,6},{6,4},{8,10},{10,8},{12,14},{14,12},{1,3},{3,1},... | collective-permute-start | bytes 1179656 | tf_op jit(solution)/shard_map/ppermute | solution.py:46
  496.0 18.5 %collective-permute-start.24 = (bf16[192,1024]{1,0:T(8,128)(2,1)S(1)}, bf16[192,1024]{1,0:T(8,128)(2,1)}, u32[]{:S(2)}, u32[]{:S(2)}) collective-permute-start(bf16[192,1024]{1,0:T(8,128)(2,1)S(1)} %get-tuple-element.145), channel_id=1, source_target_pairs={{0,1},{1,0},{2,3},{3,2},{4,5},{5,4},{6,7},{7,6},{8,9},{9,8},{10,11... | collective-permute-start | bytes 1179656 | tf_op jit(solution)/shard_map/ppermute | solution.py:44
  510.0 162.7 %collective-permute-start.18 = (bf16[256,768]{0,1:T(8,128)(2,1)S(1)}, bf16[256,768]{0,1:T(8,128)(2,1)S(1)}, u32[]{:S(2)}, u32[]{:S(2)}) collective-permute-start(bf16[256,768]{0,1:T(8,128)(2,1)S(1)} %get-tuple-element.152), channel_id=1, source_target_pairs={{0,12},{2,14},{4,0},{6,2},{8,4},{10,6},{12,8},{14,10},{1,13},{3,15... | collective-permute-start | bytes 1179656 | tf_op jit(solution)/shard_map/ppermute | solution.py:33
  671.2 14.9 %collective-permute-start.33 = (bf16[4,112,576]{2,1,0:T(8,128)(2,1)S(1)}, bf16[4,112,576]{2,1,0:T(8,128)(2,1)S(1)}, u32[]{:S(2)}, u32[]{:S(2)}) collective-permute-start(bf16[4,112,576]{2,1,0:T(8,128)(2,1)S(1)} %fusion.28), channel_id=1, source_target_pairs={{0,16},{16,0},{1,17},{17,1},{2,18},{18,2},{3,19},{19,3},{4,20},{20... | collective-permute-start | bytes 1548296 | tf_op jit(solution)/shard_map/ppermute | solution.py:38
  672.4 74.4 %collective-permute-start.29 = (bf16[576,1024]{1,0:T(8,128)(2,1)}, bf16[576,1024]{1,0:T(8,128)(2,1)}, u32[]{:S(2)}, u32[]{:S(2)}) collective-permute-start(bf16[576,1024]{1,0:T(8,128)(2,1)} %get-tuple-element.123), channel_id=1, source_target_pairs={{0,3},{1,2},{2,1},{3,0},{4,7},{5,6},{6,5},{7,4},{8,11},{9,10},{10,... | collective-permute-start | bytes 3538952 | tf_op jit(solution)/shard_map/ppermute | solution.py:48
  672.7 74.1 %collective-permute-start.28 = (bf16[576,1024]{1,0:T(8,128)(2,1)}, bf16[576,1024]{1,0:T(8,128)(2,1)}, u32[]{:S(2)}, u32[]{:S(2)}) collective-permute-start(bf16[576,1024]{1,0:T(8,128)(2,1)} %get-tuple-element.124), channel_id=1, source_target_pairs={{0,2},{2,0},{4,6},{6,4},{8,10},{10,8},{12,14},{14,12},{1,3},{3,1},... | collective-permute-start | bytes 3538952 | tf_op jit(solution)/shard_map/ppermute | solution.py:46
  686.3 8.6 %collective-permute-start.34 = (bf16[112,576]{1,0:T(8,128)(2,1)S(1)}, bf16[112,576]{1,0:T(8,128)(2,1)S(1)}, u32[]{:S(2)}, u32[]{:S(2)}) collective-permute-start(bf16[112,576]{1,0:T(8,128)(2,1)S(1)} %get-tuple-element.184), channel_id=1, source_target_pairs={{0,4},{2,6},{4,8},{6,10},{8,12},{10,14},{12,0},{14,2},{1,5},{3,7},... | collective-permute-start | bytes 387080 | tf_op jit(solution)/shard_map/ppermute | solution.py:33
  688.3 7.8 collective-permute-start.36
  690.3 11.8 %collective-permute-start.35 = (bf16[112,576]{1,0:T(8,128)(2,1)S(1)}, bf16[112,576]{1,0:T(8,128)(2,1)S(1)}, u32[]{:S(2)}, u32[]{:S(2)}) collective-permute-start(bf16[112,576]{1,0:T(8,128)(2,1)S(1)} %get-tuple-element.186), channel_id=1, source_target_pairs={{0,8},{2,10},{4,12},{6,14},{8,0},{10,2},{12,4},{14,6},{1,9},{3,11}... | collective-permute-start | bytes 387080 | tf_op jit(solution)/shard_map/ppermute | solution.py:33
  694.9 51.9 %collective-permute-start.27 = (bf16[576,1024]{1,0:T(8,128)(2,1)}, bf16[576,1024]{1,0:T(8,128)(2,1)}, u32[]{:S(2)}, u32[]{:S(2)}) collective-permute-start(bf16[576,1024]{1,0:T(8,128)(2,1)} %get-tuple-element.125), channel_id=1, source_target_pairs={{0,1},{1,0},{2,3},{3,2},{4,5},{5,4},{6,7},{7,6},{8,9},{9,8},{10,11... | collective-permute-start | bytes 3538952 | tf_op jit(solution)/shard_map/ppermute | solution.py:44
  702.5 2.6 collective-permute-start.37
  703.6 24.3 %collective-permute-start.39 = (f32[48,576]{1,0:T(8,128)S(1)}, f32[48,576]{1,0:T(8,128)S(1)}, u32[]{:S(2)}, u32[]{:S(2)}) collective-permute-start(f32[48,576]{1,0:T(8,128)S(1)} %get-tuple-element.192), channel_id=1, source_target_pairs={{0,1},{1,0},{2,3},{3,2},{4,5},{5,4},{6,7},{7,6},{8,9},{9,8},{10,11... | collective-permute-start | bytes 331784 | tf_op jit(solution)/shard_map/ppermute | solution.py:44
  705.1 25.8 %collective-permute-start.38 = (f32[48,576]{1,0:T(8,128)S(1)}, f32[48,576]{1,0:T(8,128)S(1)}, u32[]{:S(2)}, u32[]{:S(2)}) collective-permute-start(f32[48,576]{1,0:T(8,128)S(1)} %get-tuple-element.194), channel_id=1, source_target_pairs={{0,3},{1,2},{2,1},{3,0},{4,7},{5,6},{6,5},{7,4},{8,11},{9,10},{10,... | collective-permute-start | bytes 331784 | tf_op jit(solution)/shard_map/ppermute | solution.py:48
  755.1 12.0 %collective-permute-start.30 = (bf16[256,768]{0,1:T(8,128)(2,1)S(1)}, bf16[256,768]{0,1:T(8,128)(2,1)S(1)}, u32[]{:S(2)}, u32[]{:S(2)}) collective-permute-start(bf16[256,768]{0,1:T(8,128)(2,1)S(1)} %get-tuple-element.141), channel_id=1, source_target_pairs={{0,12},{2,14},{4,0},{6,2},{8,4},{10,6},{12,8},{14,10},{1,13},{3,15... | collective-permute-start | bytes 1179656 | tf_op jit(solution)/shard_map/ppermute | solution.py:33
  762.3 30.5 %collective-permute-start.32 = (bf16[256,768]{0,1:T(8,128)(2,1)S(1)}, bf16[256,768]{0,1:T(8,128)(2,1)S(1)}, u32[]{:S(2)}, u32[]{:S(2)}) collective-permute-start(bf16[256,768]{0,1:T(8,128)(2,1)S(1)} %get-tuple-element.139), channel_id=1, source_target_pairs={{0,4},{2,6},{4,8},{6,10},{8,12},{10,14},{12,0},{14,2},{1,5},{3,7},... | collective-permute-start | bytes 1179656 | tf_op jit(solution)/shard_map/ppermute | solution.py:33
  762.3 30.5 %collective-permute-start.31 = (bf16[256,768]{0,1:T(8,128)(2,1)S(1)}, bf16[256,768]{0,1:T(8,128)(2,1)S(1)}, u32[]{:S(2)}, u32[]{:S(2)}) collective-permute-start(bf16[256,768]{0,1:T(8,128)(2,1)S(1)} %get-tuple-element.140), channel_id=1, source_target_pairs={{0,8},{2,10},{4,12},{6,14},{8,0},{10,2},{12,4},{14,6},{1,9},{3,11}... | collective-permute-start | bytes 1179656 | tf_op jit(solution)/shard_map/ppermute | solution.py:33
  (53 other events, 530.0 us)
Sparse Core Ops, SparseCore 0:
  18.3 97.2 all-gather.4
  118.5 86.9 all-gather.6
  507.2 144.8 reduce-scatter.1

commit v2 on v1

--- a/solution.py
+++ b/solution.py
@@ -58,6 +58,11 @@
     return jnp.where(head_place == 1, swapped, stack)
 
 
+def in_order(pieces, place):
+    stack = jnp.stack(pieces[::-1] * 2)
+    return lax.dynamic_slice_in_dim(stack, len(pieces) - 1 - place, len(pieces), 0)
+
+
 def forward_kernel(block_q, block_k, q_ref, k_ref, v_ref, mask_ref, out_ref, sums_ref, keys, values):
     key_count = k_ref.shape[1]
     query_count = q_ref.shape[1]
@@ -97,28 +102,32 @@
         )
         total = acc[HEAD_DIM : HEAD_DIM + 1, :]
         out_ref[:, pl.ds(q_start, block_q)] = (acc[:HEAD_DIM, :] / total).astype(BF16)
-        sums_ref[0, :, pl.ds(q_start, block_q)] = top + jnp.log(total)
+        sums_ref[:, pl.ds(q_start, block_q)] = top + jnp.log(total)
         return 0
 
     lax.fori_loop(0, query_count // block_q, query_block, 0)
 
 
-def attention_forward(queries, keys, values, mask_rows):
-    heads = queries.shape[0] // HEAD_DIM
+def attention_forward(queries, keys, values, places, mask_rows):
     query_count = queries.shape[1]
     key_count = keys.shape[1]
     block_q = min(1024, query_count)
     block_k = min(1024, key_count)
-    spec_q = pl.BlockSpec((HEAD_DIM, query_count), lambda h: (h, 0))
-    spec_k = pl.BlockSpec((HEAD_DIM, key_count), lambda h: (h, 0))
+    in_specs = [
+        pl.BlockSpec((HEAD_DIM, array.shape[1]), functools.partial(lambda at, i: (at, 0), place))
+        for array, place in zip((queries, keys, values), places)
+    ]
     return pl.pallas_call(
         functools.partial(forward_kernel, block_q, block_k),
-        grid=(heads,),
-        in_specs=[spec_q, spec_k, spec_k, pl.BlockSpec((EXTRA, key_count), lambda h: (0, 0))],
-        out_specs=[spec_q, pl.BlockSpec((1, 1, query_count), lambda h: (h, 0, 0))],
+        grid=(1,),
+        in_specs=in_specs + [pl.BlockSpec((EXTRA, key_count), lambda i: (0, 0))],
+        out_specs=[
+            pl.BlockSpec((HEAD_DIM, query_count), lambda i: (0, 0)),
+            pl.BlockSpec((1, query_count), lambda i: (0, 0)),
+        ],
         out_shape=[
-            jax.ShapeDtypeStruct((heads * HEAD_DIM, query_count), BF16),
-            jax.ShapeDtypeStruct((heads, 1, query_count), F32),
+            jax.ShapeDtypeStruct((HEAD_DIM, query_count), BF16),
+            jax.ShapeDtypeStruct((1, query_count), F32),
         ],
         scratch_shapes=[
             pltpu.VMEM((key_count, HEAD_DIM + EXTRA), BF16),
@@ -126,9 +135,9 @@
         ],
         compiler_params=pltpu.CompilerParams(vmem_limit_bytes=VMEM_LIMIT),
         cost_estimate=pl.CostEstimate(
-            flops=heads * 16 * HEAD_DIM * query_count * key_count,
-            transcendentals=heads * query_count * key_count,
-            bytes_accessed=heads * 8 * HEAD_DIM * key_count,
+            flops=16 * HEAD_DIM * query_count * key_count,
+            transcendentals=query_count * key_count,
+            bytes_accessed=8 * HEAD_DIM * key_count,
         ),
     )(queries, keys, values, mask_rows)
 
@@ -151,9 +160,7 @@
     out_ref,
     sums_ref,
     grad_ref,
-    dq_ref,
-    dk_ref,
-    dv_ref,
+    grads_out,
     query_rows,
     keys,
     grad_rows,
@@ -178,7 +185,7 @@
     scaled_q[...] = query
     grads = grad_ref[...]
     deltas = jnp.sum(grads.astype(F32) * out_ref[...].astype(F32), axis=0, keepdims=True)
-    joined_q = jnp.concatenate([query, extra_rows(-sums_ref[0], 1.0)], axis=0)
+    joined_q = jnp.concatenate([query, extra_rows(-sums_ref[...], 1.0)], axis=0)
     query_rows[...] = joined_q.astype(F32).T.astype(BF16)
     joined_g = jnp.concatenate([grads, extra_rows(-deltas, 0.0)], axis=0)
     grad_rows[...] = joined_g.astype(F32).T.astype(BF16)
@@ -209,41 +216,37 @@
 
         zeros = jnp.zeros((HEAD_DIM, block_k), F32)
         dk, dv = lax.fori_loop(0, query_count // block_q, query_block, (zeros, zeros))
-        dk_ref[:, pl.ds(k_start, block_k)] = dk.astype(BF16)
-        dv_ref[:, pl.ds(k_start, block_k)] = dv.astype(BF16)
+        grads_out[HEAD_DIM : 2 * HEAD_DIM, pl.ds(k_start, block_k)] = dk.astype(BF16)
+        grads_out[2 * HEAD_DIM :, pl.ds(k_start, block_k)] = dv.astype(BF16)
         return 0
 
     lax.fori_loop(0, key_count // block_k, key_block, 0)
-    dq_ref[...] = (dq_acc[...] * scale).astype(BF16)
-
-
-def attention_backward(queries, keys, values, mask_rows, outs, sums, grads):
-    heads = queries.shape[0] // HEAD_DIM
+    grads_out[:HEAD_DIM, :query_count] = (dq_acc[...] * scale).astype(BF16)
+
+
+def attention_backward(queries, keys, values, places, mask_rows, outs, sums, grads):
     query_count = queries.shape[1]
     key_count = keys.shape[1]
     block_q = min(1024, query_count)
     block_k = min(1024, key_count)
-    spec_q = pl.BlockSpec((HEAD_DIM, query_count), lambda h: (h, 0))
-    spec_k = pl.BlockSpec((HEAD_DIM, key_count), lambda h: (h, 0))
+    in_specs = [
+        pl.BlockSpec((HEAD_DIM, array.shape[1]), functools.partial(lambda at, i: (at, 0), place))
+        for array, place in zip((queries, keys, values), places)
+    ]
+    spec_q = pl.BlockSpec((HEAD_DIM, query_count), lambda i: (0, 0))
     wide = HEAD_DIM + EXTRA
     return pl.pallas_call(
         functools.partial(backward_kernel, block_q, block_k),
-        grid=(heads,),
-        in_specs=[
+        grid=(1,),
+        in_specs=in_specs
+        + [
+            pl.BlockSpec((EXTRA, key_count), lambda i: (0, 0)),
             spec_q,
-            spec_k,
-            spec_k,
-            pl.BlockSpec((EXTRA, key_count), lambda h: (0, 0)),
-            spec_q,
-            pl.BlockSpec((1, 1, query_count), lambda h: (h, 0, 0)),
+            pl.BlockSpec((1, query_count), lambda i: (0, 0)),
             spec_q,
         ],
-        out_specs=[spec_q, spec_k, spec_k],
-        out_shape=[
-            jax.ShapeDtypeStruct((heads * HEAD_DIM, query_count), BF16),
-            jax.ShapeDtypeStruct((heads * HEAD_DIM, key_count), BF16),
-            jax.ShapeDtypeStruct((heads * HEAD_DIM, key_count), BF16),
-        ],
+        out_specs=pl.BlockSpec((3 * HEAD_DIM, key_count), lambda i: (0, 0)),
+        out_shape=jax.ShapeDtypeStruct((3 * HEAD_DIM, key_count), BF16),
         scratch_shapes=[
             pltpu.VMEM((query_count, wide), BF16),
             pltpu.VMEM((wide, key_count), BF16),
@@ -254,9 +257,9 @@
         ],
         compiler_params=pltpu.CompilerParams(vmem_limit_bytes=VMEM_LIMIT),
         cost_estimate=pl.CostEstimate(
-            flops=heads * 40 * HEAD_DIM * query_count * key_count,
-            transcendentals=heads * query_count * key_count,
-            bytes_accessed=heads * 16 * HEAD_DIM * key_count,
+            flops=40 * HEAD_DIM * query_count * key_count,
+            transcendentals=query_count * key_count,
+            bytes_accessed=16 * HEAD_DIM * key_count,
         ),
     )(queries, keys, values, mask_rows, outs, sums, grads)
 
@@ -343,40 +346,39 @@
         ordered = lax.dynamic_slice_in_dim(doubled, planes - plane, planes, 0)
         return ordered.reshape(seqs, part_rows, width)
 
-    small = jnp.concatenate(
-        [b_query, b_value, b_attn_out, norm1_gain, norm1_bias, b_outer, norm2_gain, norm2_bias]
-        + [b_inner]
-    )
-    small_row = jnp.pad(small, (0, width - small.shape[0]))[None]
-    first_rows = 3 * share
-    first_pack = jnp.concatenate([w_query, w_key, w_value, small_row])
-    first_pack = pad_rows(first_pack, -first_pack.shape[0] % 16)
-    first = lax.all_gather(first_pack, ALL_AXES, axis=0, tiled=False)
-    inner_rows = jnp.swapaxes(w_inner.reshape(share, folds, width), 0, 1).reshape(-1, width)
-    second_pack = jnp.concatenate([w_attn_out, inner_rows, w_outer])
-    second = lax.all_gather(second_pack, ALL_AXES, axis=0, tiled=False)
-
-    small_all = first[:, first_rows]
-    vectors = jnp.swapaxes(small_all[:, : 8 * share].reshape(devices, 8, share), 0, 1)
-    vectors = vectors.reshape(8, width).astype(F32)
-    bias_query, bias_value, bias_out, gain_first = vectors[:4]
-    shift_first, bias_outer, gain_second, shift_second = vectors[4:]
-    bias_inner = small_all[:, 8 * share : 8 * share + wide_share].reshape(hidden).astype(F32)
-
-    weights_qkv = [
-        first[:, i * share : (i + 1) * share].reshape(width, MEMBERS, group) for i in range(3)
+    own_group = core * 2 + head_place
+    heads_here = HEADS // MEMBERS
+    piece_rows = (share // 8 + 1) * 8
+    kinds = jnp.stack([w_query, w_key, w_value], axis=1)
+    kinds = kinds.reshape(share, 3, MEMBERS, group)
+    by_group = jnp.moveaxis(kinds, 2, 0).reshape(MEMBERS, share, 3 * group)
+    bias_row = jnp.pad(jnp.concatenate([b_query, b_value]), (0, 3 * group - 2 * share))
+    tail_rows = jnp.pad(bias_row[None], ((0, piece_rows - share - 1), (0, 0)))
+    tail_rows = jnp.broadcast_to(tail_rows, (MEMBERS,) + tail_rows.shape)
+    by_group = jnp.concatenate([by_group, tail_rows], axis=1)
+    by_member = reorder_members(by_group, core, head_place)
+    gathered = [by_member[0]] + [
+        swap_member(by_member[member], member) for member in range(1, MEMBERS)
     ]
-    by_group = jnp.stack([jnp.moveaxis(weight, 1, 0) for weight in weights_qkv], axis=2)
-    by_member = reorder_members(by_group, core, head_place).reshape(MEMBERS, width, 3 * group)
-    own_weight = by_member[0]
-    own_group = core * 2 + head_place
+    gathered = reorder_members(jnp.stack(gathered), core, head_place)
+    gathered = in_order(
+        [gathered] + [shift_planes(gathered, distance) for distance in range(1, planes)], plane
+    )
+    gathered = in_order(
+        [gathered] + [shift_batch(gathered, distance) for distance in range(1, batches)],
+        batch_place,
+    )
+    gathered = gathered.reshape(devices, piece_rows, 3 * group)
+    own_weight = gathered[:, :share].reshape(width, 3 * group)
+    bias_query = gathered[:, share, :share].reshape(MEMBERS, group)
+    bias_value = gathered[:, share, share : 2 * share].reshape(MEMBERS, group)
     own_bias = jnp.concatenate(
         [
-            pick(bias_query.reshape(MEMBERS, group), own_group),
-            jnp.zeros((group,), F32),
-            pick(bias_value.reshape(MEMBERS, group), own_group),
+            pick(bias_query, own_group),
+            jnp.zeros((group,), BF16),
+            pick(bias_value, own_group),
         ]
-    )
+    ).astype(F32)
 
     own_pieces = to_planes(layer_input)
     head_pieces = [swap_member(part_in, 1) for part_in in own_pieces]
@@ -384,8 +386,6 @@
     both_pieces = [swap_member(part_in, 2) for part_in in head_pieces]
     rows_own = jnp.concatenate(own_pieces)
     rows_all = jnp.concatenate(own_pieces + head_pieces + core_pieces + both_pieces)
-
-    cot_own = jnp.concatenate(to_planes(cotangent))
 
     valid_own = places(plane) < seq_length
     row_keep = valid_own[:row_count, None]
@@ -404,19 +404,51 @@
 
     qkv = dot(own_weight, rows_all, 0, 1) + own_bias[:, None]
     qkv = qkv.astype(BF16)
-    queries, keys, values = qkv[:group], qkv[group : 2 * group], qkv[2 * group :]
+    late_cotangent, late_out, late_inner, late_outer, qkv = lax.optimization_barrier(
+        (cotangent, w_attn_out, w_inner, w_outer, qkv)
+    )
+    cot_own = jnp.concatenate(to_planes(late_cotangent))
+
+    small = jnp.concatenate(
+        [b_attn_out, norm1_gain, norm1_bias, b_outer, norm2_gain, norm2_bias, b_inner]
+    )
+    small_row = jnp.pad(small, (0, width - small.shape[0]))[None]
+    inner_rows = jnp.swapaxes(late_inner.reshape(share, folds, width), 0, 1).reshape(-1, width)
+    second_pack = jnp.concatenate([late_outer, inner_rows, late_out, small_row])
+    second_pack = pad_rows(second_pack, -second_pack.shape[0] % 8)
+    second = lax.all_gather(second_pack, ALL_AXES, axis=0, tiled=False)
+    slots = jnp.stack([w_query, w_key, w_value], axis=1)
+    slots = slots.reshape(share, 3, MEMBERS, heads_here, HEAD_DIM)
+    slots = jnp.transpose(slots, (3, 0, 2, 1, 4)).reshape(heads_here * share, width)
+    slots, second = lax.optimization_barrier((slots, second))
+    third = lax.all_gather(slots, ALL_AXES, axis=0, tiled=False)
+
+    inner_start = wide_share
+    out_start = wide_share + share * folds
+    small_all = second[:, out_start + share]
+    vectors = jnp.swapaxes(small_all[:, : 6 * share].reshape(devices, 6, share), 0, 1)
+    vectors = vectors.reshape(6, width).astype(F32)
+    bias_out, gain_first, shift_first, bias_outer, gain_second, shift_second = vectors
+    bias_inner = small_all[:, 6 * share : 6 * share + wide_share].reshape(hidden).astype(F32)
+    weight_out = second[:, out_start : out_start + share].reshape(MEMBERS, group, width)
+    weight_out = reorder_members(weight_out, core, head_place).reshape(width, width)
+    weight_inner = second[:, inner_start:out_start].reshape(devices, folds, share, width)
+    weight_inner = jnp.swapaxes(weight_inner, 1, 2).reshape(width, hidden)
+    weight_outer = second[:, :wide_share].reshape(hidden, width)
+
+    queries = keys = values = qkv
+    starts = (0, heads_here, 2 * heads_here)
     valid_keys = [valid_own]
     if spread_planes > 1:
-        more = [shift_parts(qkv[group:], distance) for distance in range(1, spread_planes)]
-        keys = jnp.concatenate([keys] + [array[:group] for array in more], axis=1)
-        values = jnp.concatenate([values] + [array[group:] for array in more], axis=1)
+        sides = [qkv[group:]]
         for distance in range(1, spread_planes):
+            sides.append(shift_parts(qkv[group:], distance))
             valid_keys.append(places(other_plane(distance)) < seq_length)
+        keys = values = jnp.concatenate(sides, axis=1)
+        starts = (0, 0, heads_here)
     valid = jnp.concatenate(valid_keys)
     mask_row = jnp.where(valid, 0.0, NEG_BIG).astype(BF16)[None]
     mask_rows = pad_rows(mask_row, EXTRA - 1)
-
-    outs, sums = attention_forward(queries, keys, values, mask_rows)
 
     def to_members(array):
         parts = [array[:, :row_count]]
@@ -425,13 +457,16 @@
             parts.append(swap_member(sent, member))
         return parts
 
-    attended = jnp.concatenate(to_members(outs))
-
-    weight_out = second[:, :share].reshape(MEMBERS, group, width)
-    weight_out = reorder_members(weight_out, core, head_place).reshape(width, width)
-    weight_inner = second[:, share : share + share * folds].reshape(devices, folds, share, width)
-    weight_inner = jnp.swapaxes(weight_inner, 1, 2).reshape(width, hidden)
-    weight_outer = second[:, share + share * folds :].reshape(hidden, width)
+    outs, sums, parts = [], [], []
+    for slot in range(heads_here):
+        slot_at = tuple(start + slot for start in starts)
+        out, total = attention_forward(queries, keys, values, slot_at, mask_rows)
+        outs.append(out)
+        sums.append(total)
+        parts.append(to_members(out))
+    attended = jnp.concatenate(
+        [parts[slot][member] for member in range(MEMBERS) for slot in range(heads_here)]
+    )
 
     branch = dot(attended, weight_out, 0, 0) + bias_out
     normed1, back_first = jax.vjp(
@@ -485,79 +520,96 @@
     ).reshape(devices, folds * share, width)
     grad_pack = jnp.concatenate(
         [
+            grad_weight_outer.astype(BF16).reshape(devices, wide_share, width),
+            inner_pack,
             grad_weight_out.reshape(devices, share, width),
-            inner_pack,
-            grad_weight_outer.astype(BF16).reshape(devices, wide_share, width),
             vector_pack.astype(BF16)[:, None],
         ],
         axis=1,
     )
     grad_pack = jnp.pad(grad_pack, ((0, 0), (0, -grad_pack.shape[1] % 16), (0, 0)))
     owned = lax.psum_scatter(grad_pack, ALL_AXES, scatter_dimension=0, tiled=True)[0].astype(F32)
-    owned_out = owned[:share]
-    owned_inner = owned[share : share + folds * share].reshape(folds, share, width)
+    owned_outer = owned[:wide_share]
+    owned_inner = owned[inner_start:out_start].reshape(folds, share, width)
     owned_inner = jnp.swapaxes(owned_inner, 0, 1).reshape(share, hidden)
-    outer_start = share + folds * share
-    owned_outer = owned[outer_start : outer_start + wide_share]
-    owned_vectors = owned[outer_start + wide_share]
-
-    grad_parts = [grad_attended[:group]]
-    for member in range(1, MEMBERS):
-        sent = grad_attended[member * group : (member + 1) * group]
-        grad_parts.append(swap_member(sent, member))
-    grad_side = jnp.concatenate(grad_parts, axis=1)
-    grad_q, grad_k, grad_v = attention_backward(
-        queries, keys, values, mask_rows, outs, sums, grad_side
-    )
-    if spread_planes > 1:
-        grad_kv = jnp.concatenate([grad_k, grad_v])
-        plane_rows = MEMBERS * row_count
-        total = grad_kv[:, :plane_rows].astype(F32)
-        for distance in range(1, spread_planes):
-            sent = grad_kv[:, distance * plane_rows : (distance + 1) * plane_rows]
-            total = total + shift_parts(sent, -distance).astype(F32)
-        grad_k, grad_v = total[:group].astype(BF16), total[group:].astype(BF16)
-    grad_qkv = jnp.concatenate([grad_q, grad_k, grad_v])
-
-    grad_rows = jnp.concatenate(to_members(grad_qkv))
-    weight_rows = jnp.swapaxes(by_member, 0, 1).reshape(width, MEMBERS * 3 * group)
-    grad_input = (grad_resid1 + dot(grad_rows, weight_rows, 0, 1)).astype(BF16)
-    input_grad = from_planes(grad_input)
-
-    grad_weight = dot(rows_all, grad_qkv, 0, 1).astype(BF16)
-    grad_bias = jnp.sum(grad_qkv.astype(F32), axis=1).astype(BF16)
+    owned_out = owned[out_start : out_start + share]
+    owned_vectors = owned[out_start + share]
+
     chunk_rows = width // (batches * planes)
     extra = -chunk_rows % 16 + 16
-    bias_block = jnp.pad(grad_bias[None], ((0, extra - 1), (0, 0)))
-    chunks = grad_weight.reshape(batches * planes, chunk_rows, 3 * group)
-    bias_blocks = jnp.broadcast_to(bias_block, (batches * planes,) + bias_block.shape)
-    chunks = jnp.concatenate([chunks, bias_blocks], axis=1)
-    chunks = chunks.reshape((batches, planes) + chunks.shape[1:])
-    total = pick(chunks, batch_place).astype(F32)
-    for distance in range(1, batches):
-        sent = pick(chunks, (batch_place + distance) % batches)
-        total = total + shift_batch(sent, distance).astype(F32)
-    sending = total.astype(BF16)
-    total = pick(total, plane)
-    for distance in range(1, planes):
-        sent = pick(sending, (plane + distance) % planes)
-        total = total + shift_planes(sent, distance).astype(F32)
-    bias_total = total[chunk_rows]
-    member_rows = total[:chunk_rows].reshape(MEMBERS, share, 3 * group)
-    member_rows = reorder_members(member_rows, core, head_place)
-    tail = jnp.zeros((MEMBERS, -share % 16 + 16, 3 * group), F32).at[:, 0].set(bias_total)
-    sending = jnp.concatenate([member_rows, tail], axis=1)
-    bias_at = sending.shape[1] - tail.shape[1]
-    got = [sending[0]] + [
-        swap_member(sending[member], member) for member in range(1, MEMBERS)
-    ]
-    got = reorder_members(jnp.stack(got), core, head_place)
-    got = got.reshape(MEMBERS, got.shape[1], 3, group)
+
+    def reduce_weights(slot_grads):
+        columns = slot_grads.shape[0]
+        grad_weight = dot(slot_grads, rows_all, 1, 0).T.astype(BF16)
+        grad_bias = jnp.sum(slot_grads.astype(F32), axis=1).astype(BF16)
+        bias_block = jnp.pad(grad_bias[None], ((0, extra - 1), (0, 0)))
+        chunks = grad_weight.reshape(batches * planes, chunk_rows, columns)
+        bias_blocks = jnp.broadcast_to(bias_block, (batches * planes,) + bias_block.shape)
+        chunks = jnp.concatenate([chunks, bias_blocks], axis=1)
+        return chunks.reshape((batches, planes) + chunks.shape[1:])
+
+    def finish_weights(chunks):
+        columns = chunks.shape[-1]
+        total = pick(chunks, batch_place).astype(F32)
+        for distance in range(1, batches):
+            sent = pick(chunks, (batch_place + distance) % batches)
+            total = total + shift_batch(sent, distance).astype(F32)
+        sending = total.astype(BF16)
+        total = pick(total, plane)
+        for distance in range(1, planes):
+            sent = pick(sending, (plane + distance) % planes)
+            total = total + shift_planes(sent, distance).astype(F32)
+        bias_total = total[chunk_rows]
+        member_rows = total[:chunk_rows].reshape(MEMBERS, share, columns)
+        member_rows = reorder_members(member_rows, core, head_place)
+        tail = jnp.broadcast_to(bias_total, (MEMBERS, piece_rows - share, columns))
+        sending = jnp.concatenate([member_rows, tail], axis=1)
+        got = [sending[0]] + [
+            swap_member(sending[member], member) for member in range(1, MEMBERS)
+        ]
+        got = reorder_members(jnp.stack(got), core, head_place)
+        return got.reshape(MEMBERS, piece_rows, columns // (3 * HEAD_DIM), 3, HEAD_DIM)
+
+    plane_rows = MEMBERS * row_count
+    slot_grads = []
+    grad_input = grad_resid1
+    early = None
+    for slot in range(heads_here):
+        grad_parts = []
+        for member in range(MEMBERS):
+            start = member * group + slot * HEAD_DIM
+            sent = grad_attended[start : start + HEAD_DIM]
+            grad_parts.append(swap_member(sent, member) if member else sent)
+        grad_side = jnp.concatenate(grad_parts, axis=1)
+        if slot == heads_here - 1:
+            early = reduce_weights(jnp.concatenate(slot_grads))
+            early, grad_side, grad_input = lax.optimization_barrier(
+                (early, grad_side, grad_input)
+            )
+        slot_at = tuple(start + slot for start in starts)
+        grads = attention_backward(
+            queries, keys, values, slot_at, mask_rows, outs[slot], sums[slot], grad_side
+        )
+        if spread_planes > 1:
+            total = grads[HEAD_DIM:, :plane_rows].astype(F32)
+            for distance in range(1, spread_planes):
+                sent = grads[HEAD_DIM:, distance * plane_rows : (distance + 1) * plane_rows]
+                total = total + shift_parts(sent, -distance).astype(F32)
+            grads = jnp.concatenate([grads[:HEAD_DIM, :plane_rows], total.astype(BF16)])
+        slot_grads.append(grads)
+        arrived = reorder_members(jnp.stack(to_members(grads)), core, head_place)
+        slot_weight = third[:, slot * share : (slot + 1) * share].reshape(width, width)
+        grad_input = grad_input + dot(arrived.reshape(width, row_count), slot_weight, 0, 1)
+    input_grad = from_planes(grad_input.astype(BF16))
+
+    got = jnp.concatenate(
+        [finish_weights(early), finish_weights(reduce_weights(slot_grads[-1]))], axis=2
+    )
     matrices = [
-        jnp.swapaxes(got[:, :share, i], 0, 1).reshape(share, width) for i in range(3)
+        jnp.swapaxes(got[:, :share, :, i], 0, 1).reshape(share, width) for i in range(3)
     ]
     biases = [
-        lax.dynamic_slice_in_dim(got[:, bias_at, i].reshape(width), device * share, share)
+        lax.dynamic_slice_in_dim(got[:, share, :, i].reshape(width), device * share, share)
         for i in (0, 2)
     ]
 

time: 809 us -> 765 us (0.946); the launches traced: 808 us -> 755 us
  local copies, waits for them, and re-layouts: 221 us -> 144 us
  starting transfers between devices: 33.5 us -> 72 us
  other arithmetic: 70.4 us -> 45 us
  Pallas kernels: 219 us -> 228 us
    slice x9 -> x10, local copies, waits for them, and re-layouts: 41.1 us -> 1.45 us  [reorder_members(): swapped = jnp.stack([stack[1], stack[0], stack[3], stack[2]])]
    all_gather x1, waiting for transfers between devices: 22.9 us -> 0.01 us  [local(): third = lax.all_gather(slots, ALL_AXES, axis=0, tiled=False)]
    slice x6, local copies, waits for them, and re-layouts: 21.9 us -> 1.64 us  [reorder_members(): stack = jnp.where(core == 1, jnp.concatenate([stack[2:], stack[:2]]), stack)]
    ppermute x15 -> x21, starting transfers between devices: 18.9 us -> 37 us  [shift_planes(): return lax.ppermute(array, 'blk', route)]
    select_n x6 -> x11, other arithmetic: 22 us -> 6.31 us  [reorder_members(): return jnp.where(head_place == 1, swapped, stack)]
    unnamed x154 -> x213, local copies, waits for them, and re-layouts: 37.5 us -> 49.5 us
    ppermute x8 -> x16, starting transfers between devices: 6.55 us -> 17.5 us  [swap_member(): return lax.ppermute(array, 'head', [(0, 1), (1, 0)])]
    ppermute x4 -> x12, starting transfers between devices: 2.6 us -> 13.1 us  [swap_member(): return lax.ppermute(array, ('blk', 'head'), route)]
  transfers between devices with their start and end apart: 43 -> 75, of which waited for: 14 -> 18; matrix products, arithmetic and copies ran while one was open for 41% -> 29% of each run, Pallas kernels for 27% -> 30%
where the time goes in v2:
time: 765 us; the launch traced here: 755 us
  Pallas kernels  228 us (30%)
  local copies, waits for them, and re-layouts  144 us (19%)
  waiting for transfers between devices  127 us (17%)
  matrix products  122 us (16%)
  starting transfers between devices  72 us (9%)
  other arithmetic  45 us (6%)
  between operations  16.2 us (2%)
    pallas_call x3, Pallas kernels, attention_backward(): pl.pallas_call(functools.partial(backward_kernel, block_q, block_k), grid...  141 us
    dot_general x15, matrix products, dot(): lax.dot_general(left_op, right_op, (((left_dim,), (right_dim,)), ((), ())...  122 us
    pallas_call x3, Pallas kernels, attention_forward(): pl.pallas_call(functools.partial(forward_kernel, block_q, block_k), grid=...  87.8 us
    ppermute x21, waiting for transfers between devices, shift_planes(): return lax.ppermute(array, 'blk', route)  69.3 us
    unnamed x213, local copies, waits for them, and re-layouts  49.5 us
    ppermute x21, starting transfers between devices, shift_planes(): return lax.ppermute(array, 'blk', route)  37 us
    ppermute x16, waiting for transfers between devices, swap_member(): return lax.ppermute(array, 'head', [(0, 1), (1, 0)])  35.3 us
    ppermute x16, starting transfers between devices, swap_member(): return lax.ppermute(array, 'head', [(0, 1), (1, 0)])  17.5 us
  transfers between devices with their start and end apart: 75, of which 18 were waited for; matrix products, arithmetic and copies ran while one was open for 29% of the time, Pallas kernels for 30%

profile of v2, /device:TPU:0, one launch (start us, length us, event | category | flops | bytes accessed | tf_op | source)
XLA Modules:
  0.0 755.5 jit_solution(6430587967059419424)
XLA Ops:
  9.8 3.0 collective-permute-start
  13.0 2.7 collective-permute-start.1
  25.2 19.3 %collective-permute-done.6 = bf16[4,32,576]{2,1,0:T(8,128)(2,1)S(1)} collective-permute-done((bf16[4,32,576]{2,1,0:T(8,128)(2,1)S(1)}, bf16[4,32,576]{2,1,0:T(8,128)(2,1)S(1)}, u32[]{:S(2)}, u32[]{:S(2)}) %collective-permute-start.6) | collective-permute-done | bytes 147488 | tf_op jit(solution)/shard_map/ppermute | solution.py:33
  44.5 8.0 %collective-permute-start.7 = (bf16[4,32,576]{2,1,0:T(8,128)(2,1)S(1)}, bf16[4,32,576]{2,1,0:T(8,128)(2,1)S(1)}, u32[]{:S(2)}, u32[]{:S(2)}) collective-permute-start(bf16[4,32,576]{2,1,0:T(8,128)(2,1)S(1)} %maximum_select_fusion.13), channel_id=1, source_target_pairs={{0,8},{2,10},{4,12},{6,14},{8,0},{10,2},{12,4},{14,6},{1,9},{3,11}... | collective-permute-start | bytes 442376 | tf_op jit(solution)/shard_map/ppermute | solution.py:33
  52.5 7.9 %collective-permute-done.7 = bf16[4,32,576]{2,1,0:T(8,128)(2,1)S(1)} collective-permute-done((bf16[4,32,576]{2,1,0:T(8,128)(2,1)S(1)}, bf16[4,32,576]{2,1,0:T(8,128)(2,1)S(1)}, u32[]{:S(2)}, u32[]{:S(2)}) %collective-permute-start.7) | collective-permute-done | bytes 147488 | tf_op jit(solution)/shard_map/ppermute | solution.py:33
  61.0 7.0 collective-permute-done.8
  76.9 6.9 collective-permute-done.9
  87.9 3.5 collective-permute-done.12
  93.2 6.2 collective-permute-done.13
  110.8 8.8 %add_convert_fusion.1.q_ref.k_ref.v_ref = bf16[576,4096]{1,0:T(8,128)(2,1)} fusion(bf16[768,576]{1,0:T(8,128)(2,1)S(1)} %bitcast.370, bf16[4096,768]{0,1:T(8,128)(2,1)} %constant_dynamic-update-slice_fusion.2, f32[576]{0:T(1024)S(1)} %maximum_convert_fusion), kind=kOutput, calls=%fused_computation.25 | convolution fusion | flops 3628597248 | bytes 11897088 | tf_op jit(solution)/shard_map/dot_general | solution.py:25
  119.7 2.6 concatenate.227
  127.8 29.3 %shard_map.305 = (bf16[64,4096]{1,0:T(8,128)(2,1)}, f32[1,4096]{1,0:T(1,128)}) custom-call(bf16[576,4096]{1,0:T(8,128)(2,1)} %add_convert_fusion.1.q_ref.k_ref.v_ref, bf16[576,4096]{1,0:T(8,128)(2,1)} %add_convert_fusion.1.q_ref.k_ref.v_ref, bf16[576,4096]{1,0:T(8,128)(2,1)} %add_convert_fusion.1.q_ref.k_ref.v_ref, bf16[16,4096]{1,0:T(8,128)(2,1)} %concatenate.224.mask_ref), custom_call_target="tpu_custom_call" | custom-call | flops 17179869184 | bytes 2097152 | tf_op jit(solution)/shard_map/pallas_call | solution.py:120
  160.3 29.2 %shard_map.306 = (bf16[64,4096]{1,0:T(8,128)(2,1)}, f32[1,4096]{1,0:T(1,128)}) custom-call(bf16[576,4096]{1,0:T(8,128)(2,1)} %add_convert_fusion.1.q_ref.k_ref.v_ref, bf16[576,4096]{1,0:T(8,128)(2,1)} %add_convert_fusion.1.q_ref.k_ref.v_ref, bf16[576,4096]{1,0:T(8,128)(2,1)} %add_convert_fusion.1.q_ref.k_ref.v_ref, bf16[16,4096]{1,0:T(8,128)(2,1)} %concatenate.224.mask_ref), custom_call_target="tpu_custom_call" | custom-call | flops 17179869184 | bytes 2097152 | tf_op jit(solution)/shard_map/pallas_call | solution.py:120
  191.9 29.3 %shard_map.307 = (bf16[64,4096]{1,0:T(8,128)(2,1)}, f32[1,4096]{1,0:T(1,128)}) custom-call(bf16[576,4096]{1,0:T(8,128)(2,1)} %add_convert_fusion.1.q_ref.k_ref.v_ref, bf16[576,4096]{1,0:T(8,128)(2,1)} %add_convert_fusion.1.q_ref.k_ref.v_ref, bf16[576,4096]{1,0:T(8,128)(2,1)} %add_convert_fusion.1.q_ref.k_ref.v_ref, bf16[16,4096]{1,0:T(8,128)(2,1)} %concatenate.224.mask_ref), custom_call_target="tpu_custom_call" | custom-call | flops 17179869184 | bytes 2097152 | tf_op jit(solution)/shard_map/pallas_call | solution.py:120
  233.9 2.2 collective-permute-start.35
  244.6 8.0 %fusion.73 = (bf16[32,96,768]{2,1,0:T(8,128)(2,1)}, bf16[32,96,768]{2,1,0:T(8,128)(2,1)}) fusion(bf16[32,224,768]{2,1,0:T(8,128)(2,1)} %bitcast.306), kind=kLoop, calls=%fused_computation.305 | loop fusion | bytes 18874368 | tf_op jit(solution)/shard_map/slice | solution.py:437
  260.3 2.3 copy.116
  262.7 3.2 copy.164
  273.6 37.3 %multiply_convert_fusion = (bf16[1024,3072]{1,0:T(8,128)(2,1)S(1)}, f32[1024,3072]{1,0:T(8,128)}, f32[1024,3072]{1,0:T(8,128)}) fusion(f32[3072]{0:T(1024)} %reshape.853, bf16[768,3072]{1,0:T(8,128)(2,1)} %bitcast.313, f32[1024,768]{0,1:T(8,128)S(1)} %get-tuple-element.279, f32[768]{0:T(1024)} %add.372, f32[768]{0:T(1024)} %mul.185, f32[1024]{0:T(1024)} %fusion.53, ...), kind=kOutput, calls=%fused_computation.8 | convolution fusion | flops 5043388416 | bytes 39348224 | tf_op jit(solution)/shard_map/dot_general | solution.py:25
  310.9 10.0 %fusion.100 = (f32[1024]{0:T(1024)S(1)}, f32[1024,768]{0,1:T(8,128)S(1)}) fusion(f32[768]{0:T(1024)S(1)} %copy-done.64, bf16[1024,3072]{1,0:T(8,128)(2,1)S(1)} %get-tuple-element.122, bf16[3072,768]{1,0:T(8,128)(2,1)} %bitcast.316, f32[768]{0:T(1024)S(1)} %copy-done.61, f32[768]{0:T(1024)S(1)} %copy-done.51, f32[1024]{0:T(1024)S(1)} %copy-done.53, ...), kind=kOutput, calls=%fused_computation.332 | convolution fusion | flops 4837342208 | bytes 17323008 | tf_op jit(solution)/shard_map/dot_general | solution.py:25
  323.7 3.3 multiply_reduce_fusion
  329.1 3.7 fusion.71
  334.5 17.1 %fusion.101 = (bf16[3072]{0:T(1024)(128)(2,1)S(1)}, bf16[1024,3072]{1,0:T(8,128)(2,1)}) fusion(f32[1024,3072]{1,0:T(8,128)} %get-tuple-element.123, bf16[1024,768]{0,1:T(8,128)(2,1)S(1)} %get-tuple-element.111, bf16[3072,768]{1,0:T(8,128)(2,1)} %bitcast.317, f32[1024,3072]{1,0:T(8,128)} %get-tuple-element.280, f32[3072]{0:T(1024)S(1)} %copy-done.55), kind=kOutput, calls=%fused_computation.333 | convolution fusion | flops 4882166784 | bytes 37767168 | tf_op jit(solution)/shard_map/dot_general | solution.py:25
  351.6 9.9 %convolution_convert_fusion = bf16[768,3072]{1,0:T(8,128)(2,1)} fusion(bf16[1024,3072]{1,0:T(8,128)(2,1)} %get-tuple-element.285, f32[1024,768]{0,1:T(8,128)S(1)} %copy-done.1, f32[768]{0:T(1024)S(1)} %copy-done.62, f32[768]{0:T(1024)S(1)} %copy-done.52, f32[1024]{0:T(1024)S(1)} %copy-done.54, f32[1024]{0:T(1024)S(1)} %copy-done.46), kind=kOutput, calls=%fused_computation.26 | convolution fusion | flops 4838129664 | bytes 14170112 | tf_op jit(solution)/shard_map/dot_general | solution.py:25
  361.6 9.4 %multiply_reduce_fusion.1 = (bf16[768]{0:T(1024)(128)(2,1)S(1)}, f32[1024]{0:T(1024)S(1)}, bf16[768]{0:T(1024)(128)(2,1)S(1)}, f32[1024,768]{0,1:T(8,128)}) fusion(f32[1024,768]{0,1:T(8,128)S(1)} %copy-done.1, f32[1024]{0:T(1024)S(1)} %copy-done.54, f32[1024]{0:T(1024)S(1)} %copy-done.46, f32[768]{0:T(1024)S(1)} %copy-done.52, ...), kind=kOutput, calls=%fused_computation.32 | convolution fusion | flops 4839699456 | bytes 20469760 | tf_op jit(solution)/shard_map/dot_general | solution.py:25
  370.9 9.7 %reshape.840 = bf16[32,24,4,768]{3,2,1,0:T(4,128)(2,1)} reshape(bf16[768,3072]{1,0:T(8,128)(2,1)} %convolution_convert_fusion) | data formatting | bytes 9437184 | tf_op jit(solution)/shard_map/reshape | solution.py:519
  380.7 5.6 copy.151
  389.6 3.2 convolution_convert_fusion.2
  403.4 5.6 convolution_convert_fusion.1
  409.1 5.2 fusion.12
  420.1 46.8 %shard_map.309 = bf16[192,4096]{1,0:T(8,128)(2,1)} custom-call(bf16[576,4096]{1,0:T(8,128)(2,1)} %add_convert_fusion.1.q_ref.k_ref.v_ref, bf16[576,4096]{1,0:T(8,128)(2,1)} %add_convert_fusion.1.q_ref.k_ref.v_ref, bf16[576,4096]{1,0:T(8,128)(2,1)} %add_convert_fusion.1.q_ref.k_ref.v_ref, bf16[16,4096]{1,0:T(8,128)(2,1)} %concatenate.224.mask_ref, ...), custom_call_target="tpu_custom_call" | custom-call | flops 42949672960 | bytes 4194304 | tf_op jit(solution)/shard_map/pallas_call | solution.py:238
  471.5 47.1 %shard_map.308 = bf16[192,4096]{1,0:T(8,128)(2,1)} custom-call(bf16[576,4096]{1,0:T(8,128)(2,1)} %add_convert_fusion.1.q_ref.k_ref.v_ref, bf16[576,4096]{1,0:T(8,128)(2,1)} %add_convert_fusion.1.q_ref.k_ref.v_ref, bf16[576,4096]{1,0:T(8,128)(2,1)} %add_convert_fusion.1.q_ref.k_ref.v_ref, bf16[16,4096]{1,0:T(8,128)(2,1)} %concatenate.224.mask_ref, ...), custom_call_target="tpu_custom_call" | custom-call | flops 42949672960 | bytes 4194304 | tf_op jit(solution)/shard_map/pallas_call | solution.py:238
  518.6 6.7 fusion.18
  526.3 2.2 collective-permute-start.33
  535.6 12.8 %collective-permute-done.33 = bf16[256,768]{0,1:T(8,128)(2,1)S(1)} collective-permute-done((bf16[256,768]{0,1:T(8,128)(2,1)S(1)}, bf16[256,768]{0,1:T(8,128)(2,1)S(1)}, u32[]{:S(2)}, u32[]{:S(2)}) %collective-permute-start.33) | collective-permute-done | bytes 393248 | tf_op jit(solution)/shard_map/ppermute | solution.py:33
  553.9 7.3 collective-permute-done.51
  561.8 6.8 collective-permute-done.47
  568.6 12.7 %collective-permute-done.48 = bf16[192,1024]{1,0:T(8,128)(2,1)S(1)} collective-permute-done((bf16[192,1024]{1,0:T(8,128)(2,1)S(1)}, bf16[192,1024]{1,0:T(8,128)(2,1)S(1)}, u32[]{:S(2)}, u32[]{:S(2)}) %collective-permute-start.48) | collective-permute-done | bytes 393248 | tf_op jit(solution)/shard_map/ppermute | solution.py:44
  584.8 3.5 fusion.75
  589.7 3.0 add_add_fusion.2
  592.7 46.8 %shard_map.310 = bf16[192,4096]{1,0:T(8,128)(2,1)} custom-call(bf16[576,4096]{1,0:T(8,128)(2,1)} %add_convert_fusion.1.q_ref.k_ref.v_ref, bf16[576,4096]{1,0:T(8,128)(2,1)} %add_convert_fusion.1.q_ref.k_ref.v_ref, bf16[576,4096]{1,0:T(8,128)(2,1)} %add_convert_fusion.1.q_ref.k_ref.v_ref, bf16[16,4096]{1,0:T(8,128)(2,1)} %concatenate.224.mask_ref, ...), custom_call_target="tpu_custom_call" | custom-call | flops 42949672960 | bytes 4194304 | tf_op jit(solution)/shard_map/pallas_call | solution.py:238
  641.2 5.4 convolution_convert_fusion.4
  656.3 3.2 collective-permute-start.68
  662.8 2.6 collective-permute-start.70
  670.2 6.5 collective-permute-done.58
  682.3 4.6 collective-permute-done.54
  695.7 3.3 collective-permute-start.55
  712.7 20.7 %collective-permute-done.56 = bf16[256,768]{0,1:T(8,128)(2,1)S(1)} collective-permute-done((bf16[256,768]{0,1:T(8,128)(2,1)}, bf16[256,768]{0,1:T(8,128)(2,1)S(1)}, u32[]{:S(2)}, u32[]{:S(2)}) %collective-permute-start.56) | collective-permute-done | bytes 393248 | tf_op jit(solution)/shard_map/ppermute | solution.py:33
  (577 shorter events, 198.0 us)
Async XLA Ops:
  7.2 233.6 %all-gather.5.cloned.1.call-start = ((), (), s32[]{:S(2)}) async-start(), calls=%async_computation.2 | async-start | bytes 11354112 | tf_op jit(solution)/shard_map/all_gather | solution.py:419
  9.8 60.3 %collective-permute-start = (bf16[256,768]{0,1:T(8,128)(2,1)}, bf16[256,768]{0,1:T(8,128)(2,1)S(1)}, u32[]{:S(2)}, u32[]{:S(2)}) collective-permute-start(bf16[256,768]{0,1:T(8,128)(2,1)} %bitcast.1), channel_id=1, source_target_pairs={{0,4},{2,6},{4,8},{6,10},{8,12},{10,14},{12,0},{14,2},{1,5},{3,7},... | collective-permute-start | bytes 1179656 | tf_op jit(solution)/shard_map/ppermute | solution.py:33
  13.0 57.9 %collective-permute-start.1 = (bf16[256,768]{0,1:T(8,128)(2,1)S(1)}, bf16[256,768]{0,1:T(8,128)(2,1)S(1)}, u32[]{:S(2)}, u32[]{:S(2)}) collective-permute-start(bf16[256,768]{0,1:T(8,128)(2,1)S(1)} %bitcast.378), channel_id=1, source_target_pairs={{0,8},{2,10},{4,12},{6,14},{8,0},{10,2},{12,4},{14,6},{1,9},{3,11}... | collective-permute-start | bytes 1179656 | tf_op jit(solution)/shard_map/ppermute | solution.py:33
  21.2 52.0 %collective-permute-start.2 = (bf16[256,768]{0,1:T(8,128)(2,1)S(1)}, bf16[256,768]{0,1:T(8,128)(2,1)S(1)}, u32[]{:S(2)}, u32[]{:S(2)}) collective-permute-start(bf16[256,768]{0,1:T(8,128)(2,1)S(1)} %bitcast.379), channel_id=1, source_target_pairs={{0,12},{2,14},{4,0},{6,2},{8,4},{10,6},{12,8},{14,10},{1,13},{3,15... | collective-permute-start | bytes 1179656 | tf_op jit(solution)/shard_map/ppermute | solution.py:33
  22.6 52.0 %collective-permute-start.10 = (bf16[256,768]{0,1:T(8,128)(2,1)S(1)}, bf16[256,768]{0,1:T(8,128)(2,1)S(1)}, u32[]{:S(2)}, u32[]{:S(2)}) collective-permute-start(bf16[256,768]{0,1:T(8,128)(2,1)S(1)} %bitcast.331), channel_id=1, source_target_pairs={{0,1},{1,0},{2,3},{3,2},{4,5},{5,4},{6,7},{7,6},{8,9},{9,8},{10,11... | collective-permute-start | bytes 1179656 | tf_op jit(solution)/shard_map/ppermute | solution.py:44
  24.7 19.9 %collective-permute-start.6 = (bf16[4,32,576]{2,1,0:T(8,128)(2,1)S(1)}, bf16[4,32,576]{2,1,0:T(8,128)(2,1)S(1)}, u32[]{:S(2)}, u32[]{:S(2)}) collective-permute-start(bf16[4,32,576]{2,1,0:T(8,128)(2,1)S(1)} %maximum_select_fusion.13), channel_id=1, source_target_pairs={{0,12},{2,14},{4,0},{6,2},{8,4},{10,6},{12,8},{14,10},{1,13},{3,15... | collective-permute-start | bytes 442376 | tf_op jit(solution)/shard_map/ppermute | solution.py:33
  44.5 15.9 %collective-permute-start.7 = (bf16[4,32,576]{2,1,0:T(8,128)(2,1)S(1)}, bf16[4,32,576]{2,1,0:T(8,128)(2,1)S(1)}, u32[]{:S(2)}, u32[]{:S(2)}) collective-permute-start(bf16[4,32,576]{2,1,0:T(8,128)(2,1)S(1)} %maximum_select_fusion.13), channel_id=1, source_target_pairs={{0,8},{2,10},{4,12},{6,14},{8,0},{10,2},{12,4},{14,6},{1,9},{3,11}... | collective-permute-start | bytes 442376 | tf_op jit(solution)/shard_map/ppermute | solution.py:33
  68.4 15.5 %collective-permute-start.9 = (bf16[4,4,32,576]{3,2,1,0:T(8,128)(2,1)S(1)}, bf16[4,4,32,576]{3,2,1,0:T(8,128)(2,1)S(1)}, u32[]{:S(2)}, u32[]{:S(2)}) collective-permute-start(bf16[4,4,32,576]{3,2,1,0:T(8,128)(2,1)S(1)} %constant_dynamic-slice_fusion.8), channel_id=1, source_target_pairs={{0,16},{16,0},{1,17},{17,1},{2,18},{18,2},{3,19},{19,3},{4,20},{20... | collective-permute-start | bytes 1769480 | tf_op jit(solution)/shard_map/ppermute | solution.py:38
  70.1 31.2 %collective-permute-start.14 = (bf16[256,768]{0,1:T(8,128)(2,1)S(1)}, bf16[256,768]{0,1:T(8,128)(2,1)}, u32[]{:S(2)}, u32[]{:S(2)}) collective-permute-start(bf16[256,768]{0,1:T(8,128)(2,1)S(1)} %bitcast.332), channel_id=1, source_target_pairs={{0,2},{2,0},{4,6},{6,4},{8,10},{10,8},{12,14},{14,12},{1,3},{3,1},... | collective-permute-start | bytes 1179656 | tf_op jit(solution)/shard_map/ppermute | solution.py:46
  71.0 14.5 %collective-permute-start.11 = (bf16[256,768]{0,1:T(8,128)(2,1)S(1)}, bf16[256,768]{0,1:T(8,128)(2,1)}, u32[]{:S(2)}, u32[]{:S(2)}) collective-permute-start(bf16[256,768]{0,1:T(8,128)(2,1)S(1)} %collective-permute-done), channel_id=1, source_target_pairs={{0,1},{1,0},{2,3},{3,2},{4,5},{5,4},{6,7},{7,6},{8,9},{9,8},{10,11... | collective-permute-start | bytes 1179656 | tf_op jit(solution)/shard_map/ppermute | solution.py:44
  73.3 18.2 %collective-permute-start.12 = (bf16[256,768]{0,1:T(8,128)(2,1)S(1)}, bf16[256,768]{0,1:T(8,128)(2,1)}, u32[]{:S(2)}, u32[]{:S(2)}) collective-permute-start(bf16[256,768]{0,1:T(8,128)(2,1)S(1)} %collective-permute-done.1), channel_id=1, source_target_pairs={{0,1},{1,0},{2,3},{3,2},{4,5},{5,4},{6,7},{7,6},{8,9},{9,8},{10,11... | collective-permute-start | bytes 1179656 | tf_op jit(solution)/shard_map/ppermute | solution.py:44
  74.6 24.8 %collective-permute-start.13 = (bf16[256,768]{0,1:T(8,128)(2,1)S(1)}, bf16[256,768]{0,1:T(8,128)(2,1)}, u32[]{:S(2)}, u32[]{:S(2)}) collective-permute-start(bf16[256,768]{0,1:T(8,128)(2,1)S(1)} %collective-permute-done.2), channel_id=1, source_target_pairs={{0,1},{1,0},{2,3},{3,2},{4,5},{5,4},{6,7},{7,6},{8,9},{9,8},{10,11... | collective-permute-start | bytes 1179656 | tf_op jit(solution)/shard_map/ppermute | solution.py:44
  83.9 19.7 %collective-permute-start.15 = (bf16[256,768]{0,1:T(8,128)(2,1)S(1)}, bf16[256,768]{0,1:T(8,128)(2,1)}, u32[]{:S(2)}, u32[]{:S(2)}) collective-permute-start(bf16[256,768]{0,1:T(8,128)(2,1)S(1)} %collective-permute-done), channel_id=1, source_target_pairs={{0,2},{2,0},{4,6},{6,4},{8,10},{10,8},{12,14},{14,12},{1,3},{3,1},... | collective-permute-start | bytes 1179656 | tf_op jit(solution)/shard_map/ppermute | solution.py:46
  85.5 19.9 %collective-permute-start.16 = (bf16[256,768]{0,1:T(8,128)(2,1)S(1)}, bf16[256,768]{0,1:T(8,128)(2,1)S(1)}, u32[]{:S(2)}, u32[]{:S(2)}) collective-permute-start(bf16[256,768]{0,1:T(8,128)(2,1)S(1)} %collective-permute-done.1), channel_id=1, source_target_pairs={{0,2},{2,0},{4,6},{6,4},{8,10},{10,8},{12,14},{14,12},{1,3},{3,1},... | collective-permute-start | bytes 1179656 | tf_op jit(solution)/shard_map/ppermute | solution.py:46
  91.4 15.3 %collective-permute-start.17 = (bf16[256,768]{0,1:T(8,128)(2,1)S(1)}, bf16[256,768]{0,1:T(8,128)(2,1)S(1)}, u32[]{:S(2)}, u32[]{:S(2)}) collective-permute-start(bf16[256,768]{0,1:T(8,128)(2,1)S(1)} %collective-permute-done.2), channel_id=1, source_target_pairs={{0,2},{2,0},{4,6},{6,4},{8,10},{10,8},{12,14},{14,12},{1,3},{3,1},... | collective-permute-start | bytes 1179656 | tf_op jit(solution)/shard_map/ppermute | solution.py:46
  122.3 462.5 %all-gather.7.cloned.1.call-start = ((), (), s32[]{:S(2)}) async-start(), calls=%async_computation.3 | async-start | bytes 3649536 | tf_op jit(solution)/shard_map/all_gather | solution.py:424
  158.8 69.3 %collective-permute-start.22 = (bf16[64,1024]{1,0:T(8,128)(2,1)S(1)}, bf16[64,1024]{1,0:T(8,128)(2,1)S(1)}, u32[]{:S(2)}, u32[]{:S(2)}) collective-permute-start(bf16[64,1024]{1,0:T(8,128)(2,1)S(1)} %get-tuple-element.215), channel_id=1, source_target_pairs={{0,1},{1,0},{2,3},{3,2},{4,5},{5,4},{6,7},{7,6},{8,9},{9,8},{10,11... | collective-permute-start | bytes 393224 | tf_op jit(solution)/shard_map/ppermute | solution.py:44
  191.4 37.5 %collective-permute-start.23 = (bf16[64,1024]{1,0:T(8,128)(2,1)}, bf16[64,1024]{1,0:T(8,128)(2,1)S(1)}, u32[]{:S(2)}, u32[]{:S(2)}) collective-permute-start(bf16[64,1024]{1,0:T(8,128)(2,1)} %get-tuple-element.211), channel_id=1, source_target_pairs={{0,1},{1,0},{2,3},{3,2},{4,5},{5,4},{6,7},{7,6},{8,9},{9,8},{10,11... | collective-permute-start | bytes 393224 | tf_op jit(solution)/shard_map/ppermute | solution.py:44
  233.3 90.2 %collective-permute-start.34 = (bf16[256,768]{0,1:T(8,128)(2,1)}, bf16[256,768]{0,1:T(8,128)(2,1)}, u32[]{:S(2)}, u32[]{:S(2)}) collective-permute-start(bf16[256,768]{0,1:T(8,128)(2,1)} %bitcast.50), channel_id=1, source_target_pairs={{0,4},{2,6},{4,8},{6,10},{8,12},{10,14},{12,0},{14,2},{1,5},{3,7},... | collective-permute-start | bytes 1179656 | tf_op jit(solution)/shard_map/ppermute | solution.py:33
  233.9 89.6 %collective-permute-start.35 = (bf16[256,768]{0,1:T(8,128)(2,1)}, bf16[256,768]{0,1:T(8,128)(2,1)}, u32[]{:S(2)}, u32[]{:S(2)}) collective-permute-start(bf16[256,768]{0,1:T(8,128)(2,1)} %bitcast.51), channel_id=1, source_target_pairs={{0,8},{2,10},{4,12},{6,14},{8,0},{10,2},{12,4},{14,6},{1,9},{3,11}... | collective-permute-start | bytes 1179656 | tf_op jit(solution)/shard_map/ppermute | solution.py:33
  236.8 86.7 %collective-permute-start.36 = (bf16[256,768]{0,1:T(8,128)(2,1)}, bf16[256,768]{0,1:T(8,128)(2,1)}, u32[]{:S(2)}, u32[]{:S(2)}) collective-permute-start(bf16[256,768]{0,1:T(8,128)(2,1)} %bitcast.52), channel_id=1, source_target_pairs={{0,12},{2,14},{4,0},{6,2},{8,4},{10,6},{12,8},{14,10},{1,13},{3,15... | collective-permute-start | bytes 1179656 | tf_op jit(solution)/shard_map/ppermute | solution.py:33
  389.5 353.7 %reduce-scatter.2.cloned.1.call-start = ((), (), s32[]{:S(2)}) async-start(), calls=%async_computation.1 | async-start | bytes 11354112 | tf_op jit(solution)/shard_map/reduce_scatter | solution.py:531
  393.8 22.3 %collective-permute-start.40 = (bf16[64,1024]{1,0:T(8,128)(2,1)}, bf16[64,1024]{1,0:T(8,128)(2,1)}, u32[]{:S(2)}, u32[]{:S(2)}) collective-permute-start(bf16[64,1024]{1,0:T(8,128)(2,1)} %get-tuple-element.165), channel_id=1, source_target_pairs={{0,1},{1,0},{2,3},{3,2},{4,5},{5,4},{6,7},{7,6},{8,9},{9,8},{10,11... | collective-permute-start | bytes 393224 | tf_op jit(solution)/shard_map/ppermute | solution.py:44
  395.3 21.5 %collective-permute-start.41 = (bf16[64,1024]{1,0:T(8,128)(2,1)}, bf16[64,1024]{1,0:T(8,128)(2,1)}, u32[]{:S(2)}, u32[]{:S(2)}) collective-permute-start(bf16[64,1024]{1,0:T(8,128)(2,1)} %get-tuple-element.164), channel_id=1, source_target_pairs={{0,2},{2,0},{4,6},{6,4},{8,10},{10,8},{12,14},{14,12},{1,3},{3,1},... | collective-permute-start | bytes 393224 | tf_op jit(solution)/shard_map/ppermute | solution.py:46
  395.3 22.9 %collective-permute-start.42 = (bf16[64,1024]{1,0:T(8,128)(2,1)}, bf16[64,1024]{1,0:T(8,128)(2,1)}, u32[]{:S(2)}, u32[]{:S(2)}) collective-permute-start(bf16[64,1024]{1,0:T(8,128)(2,1)} %get-tuple-element.163), channel_id=1, source_target_pairs={{0,3},{1,2},{2,1},{3,0},{4,7},{5,6},{6,5},{7,4},{8,11},{9,10},{10,... | collective-permute-start | bytes 393224 | tf_op jit(solution)/shard_map/ppermute | solution.py:48
  396.0 70.9 %collective-permute-start.37 = (bf16[64,1024]{1,0:T(8,128)(2,1)}, bf16[64,1024]{1,0:T(8,128)(2,1)}, u32[]{:S(2)}, u32[]{:S(2)}) collective-permute-start(bf16[64,1024]{1,0:T(8,128)(2,1)} %get-tuple-element.169), channel_id=1, source_target_pairs={{0,1},{1,0},{2,3},{3,2},{4,5},{5,4},{6,7},{7,6},{8,9},{9,8},{10,11... | collective-permute-start | bytes 393224 | tf_op jit(solution)/shard_map/ppermute | solution.py:44
  397.4 70.2 %collective-permute-start.38 = (bf16[64,1024]{1,0:T(8,128)(2,1)}, bf16[64,1024]{1,0:T(8,128)(2,1)}, u32[]{:S(2)}, u32[]{:S(2)}) collective-permute-start(bf16[64,1024]{1,0:T(8,128)(2,1)} %get-tuple-element.168), channel_id=1, source_target_pairs={{0,2},{2,0},{4,6},{6,4},{8,10},{10,8},{12,14},{14,12},{1,3},{3,1},... | collective-permute-start | bytes 393224 | tf_op jit(solution)/shard_map/ppermute | solution.py:46
  416.1 52.7 %collective-permute-start.39 = (bf16[64,1024]{1,0:T(8,128)(2,1)S(1)}, bf16[64,1024]{1,0:T(8,128)(2,1)S(1)}, u32[]{:S(2)}, u32[]{:S(2)}) collective-permute-start(bf16[64,1024]{1,0:T(8,128)(2,1)S(1)} %get-tuple-element.167), channel_id=1, source_target_pairs={{0,3},{1,2},{2,1},{3,0},{4,7},{5,6},{6,5},{7,4},{8,11},{9,10},{10,... | collective-permute-start | bytes 393224 | tf_op jit(solution)/shard_map/ppermute | solution.py:48
  416.8 108.7 %collective-permute-start.43 = (bf16[64,1024]{1,0:T(8,128)(2,1)}, bf16[64,1024]{1,0:T(8,128)(2,1)S(1)}, u32[]{:S(2)}, u32[]{:S(2)}) collective-permute-start(bf16[64,1024]{1,0:T(8,128)(2,1)} %get-tuple-element.162), channel_id=1, source_target_pairs={{0,1},{1,0},{2,3},{3,2},{4,5},{5,4},{6,7},{7,6},{8,9},{9,8},{10,11... | collective-permute-start | bytes 393224 | tf_op jit(solution)/shard_map/ppermute | solution.py:44
  418.2 110.2 %collective-permute-start.44 = (bf16[64,1024]{1,0:T(8,128)(2,1)}, bf16[64,1024]{1,0:T(8,128)(2,1)S(1)}, u32[]{:S(2)}, u32[]{:S(2)}) collective-permute-start(bf16[64,1024]{1,0:T(8,128)(2,1)} %get-tuple-element.161), channel_id=1, source_target_pairs={{0,2},{2,0},{4,6},{6,4},{8,10},{10,8},{12,14},{14,12},{1,3},{3,1},... | collective-permute-start | bytes 393224 | tf_op jit(solution)/shard_map/ppermute | solution.py:46
  466.9 61.6 %collective-permute-start.45 = (bf16[64,1024]{1,0:T(8,128)(2,1)}, bf16[64,1024]{1,0:T(8,128)(2,1)}, u32[]{:S(2)}, u32[]{:S(2)}) collective-permute-start(bf16[64,1024]{1,0:T(8,128)(2,1)} %get-tuple-element.160), channel_id=1, source_target_pairs={{0,3},{1,2},{2,1},{3,0},{4,7},{5,6},{6,5},{7,4},{8,11},{9,10},{10,... | collective-permute-start | bytes 393224 | tf_op jit(solution)/shard_map/ppermute | solution.py:48
  467.6 65.8 %collective-permute-start.31 = (bf16[256,768]{0,1:T(8,128)(2,1)}, bf16[256,768]{0,1:T(8,128)(2,1)S(1)}, u32[]{:S(2)}, u32[]{:S(2)}) collective-permute-start(bf16[256,768]{0,1:T(8,128)(2,1)} %get-tuple-element.177), channel_id=1, source_target_pairs={{0,12},{2,14},{4,0},{6,2},{8,4},{10,6},{12,8},{14,10},{1,13},{3,15... | collective-permute-start | bytes 1179656 | tf_op jit(solution)/shard_map/ppermute | solution.py:33
  468.8 66.0 %collective-permute-start.32 = (bf16[256,768]{0,1:T(8,128)(2,1)}, bf16[256,768]{0,1:T(8,128)(2,1)S(1)}, u32[]{:S(2)}, u32[]{:S(2)}) collective-permute-start(bf16[256,768]{0,1:T(8,128)(2,1)} %get-tuple-element.176), channel_id=1, source_target_pairs={{0,8},{2,10},{4,12},{6,14},{8,0},{10,2},{12,4},{14,6},{1,9},{3,11}... | collective-permute-start | bytes 1179656 | tf_op jit(solution)/shard_map/ppermute | solution.py:33
  526.3 22.1 %collective-permute-start.33 = (bf16[256,768]{0,1:T(8,128)(2,1)S(1)}, bf16[256,768]{0,1:T(8,128)(2,1)S(1)}, u32[]{:S(2)}, u32[]{:S(2)}) collective-permute-start(bf16[256,768]{0,1:T(8,128)(2,1)S(1)} %copy-done.27), channel_id=1, source_target_pairs={{0,4},{2,6},{4,8},{6,10},{8,12},{10,14},{12,0},{14,2},{1,5},{3,7},... | collective-permute-start | bytes 1179656 | tf_op jit(solution)/shard_map/ppermute | solution.py:33
  528.4 24.1 %collective-permute-start.49 = (bf16[192,1024]{1,0:T(8,128)(2,1)S(1)}, bf16[192,1024]{1,0:T(8,128)(2,1)S(1)}, u32[]{:S(2)}, u32[]{:S(2)}) collective-permute-start(bf16[192,1024]{1,0:T(8,128)(2,1)S(1)} %get-tuple-element.147), channel_id=1, source_target_pairs={{0,2},{2,0},{4,6},{6,4},{8,10},{10,8},{12,14},{14,12},{1,3},{3,1},... | collective-permute-start | bytes 1179656 | tf_op jit(solution)/shard_map/ppermute | solution.py:46
  530.8 23.1 %collective-permute-start.50 = (bf16[192,1024]{1,0:T(8,128)(2,1)S(1)}, bf16[192,1024]{1,0:T(8,128)(2,1)S(1)}, u32[]{:S(2)}, u32[]{:S(2)}) collective-permute-start(bf16[192,1024]{1,0:T(8,128)(2,1)S(1)} %get-tuple-element.150), channel_id=1, source_target_pairs={{0,3},{1,2},{2,1},{3,0},{4,7},{5,6},{6,5},{7,4},{8,11},{9,10},{10,... | collective-permute-start | bytes 1179656 | tf_op jit(solution)/shard_map/ppermute | solution.py:48
  533.4 27.8 %collective-permute-start.51 = (bf16[192,1024]{1,0:T(8,128)(2,1)S(1)}, bf16[192,1024]{1,0:T(8,128)(2,1)S(1)}, u32[]{:S(2)}, u32[]{:S(2)}) collective-permute-start(bf16[192,1024]{1,0:T(8,128)(2,1)S(1)} %get-tuple-element.148), channel_id=1, source_target_pairs={{0,1},{1,0},{2,3},{3,2},{4,5},{5,4},{6,7},{7,6},{8,9},{9,8},{10,11... | collective-permute-start | bytes 1179656 | tf_op jit(solution)/shard_map/ppermute | solution.py:44
  534.8 27.0 %collective-permute-start.46 = (bf16[192,1024]{1,0:T(8,128)(2,1)S(1)}, bf16[192,1024]{1,0:T(8,128)(2,1)S(1)}, u32[]{:S(2)}, u32[]{:S(2)}) collective-permute-start(bf16[192,1024]{1,0:T(8,128)(2,1)S(1)} %get-tuple-element.155), channel_id=1, source_target_pairs={{0,2},{2,0},{4,6},{6,4},{8,10},{10,8},{12,14},{14,12},{1,3},{3,1},... | collective-permute-start | bytes 1179656 | tf_op jit(solution)/shard_map/ppermute | solution.py:46
  548.4 20.2 %collective-permute-start.47 = (bf16[192,1024]{1,0:T(8,128)(2,1)S(1)}, bf16[192,1024]{1,0:T(8,128)(2,1)S(1)}, u32[]{:S(2)}, u32[]{:S(2)}) collective-permute-start(bf16[192,1024]{1,0:T(8,128)(2,1)S(1)} %get-tuple-element.158), channel_id=1, source_target_pairs={{0,3},{1,2},{2,1},{3,0},{4,7},{5,6},{6,5},{7,4},{8,11},{9,10},{10,... | collective-permute-start | bytes 1179656 | tf_op jit(solution)/shard_map/ppermute | solution.py:48
  552.5 28.7 %collective-permute-start.48 = (bf16[192,1024]{1,0:T(8,128)(2,1)S(1)}, bf16[192,1024]{1,0:T(8,128)(2,1)S(1)}, u32[]{:S(2)}, u32[]{:S(2)}) collective-permute-start(bf16[192,1024]{1,0:T(8,128)(2,1)S(1)} %get-tuple-element.156), channel_id=1, source_target_pairs={{0,1},{1,0},{2,3},{3,2},{4,5},{5,4},{6,7},{7,6},{8,9},{9,8},{10,11... | collective-permute-start | bytes 1179656 | tf_op jit(solution)/shard_map/ppermute | solution.py:44
  666.3 15.4 %collective-permute-start.52 = (bf16[192,1024]{1,0:T(8,128)(2,1)}, bf16[192,1024]{1,0:T(8,128)(2,1)S(1)}, u32[]{:S(2)}, u32[]{:S(2)}) collective-permute-start(bf16[192,1024]{1,0:T(8,128)(2,1)} %get-tuple-element.139), channel_id=1, source_target_pairs={{0,2},{2,0},{4,6},{6,4},{8,10},{10,8},{12,14},{14,12},{1,3},{3,1},... | collective-permute-start | bytes 1179656 | tf_op jit(solution)/shard_map/ppermute | solution.py:46
  666.5 15.8 %collective-permute-start.53 = (bf16[192,1024]{1,0:T(8,128)(2,1)}, bf16[192,1024]{1,0:T(8,128)(2,1)S(1)}, u32[]{:S(2)}, u32[]{:S(2)}) collective-permute-start(bf16[192,1024]{1,0:T(8,128)(2,1)} %get-tuple-element.142), channel_id=1, source_target_pairs={{0,3},{1,2},{2,1},{3,0},{4,7},{5,6},{6,5},{7,4},{8,11},{9,10},{10,... | collective-permute-start | bytes 1179656 | tf_op jit(solution)/shard_map/ppermute | solution.py:48
  668.5 18.3 %collective-permute-start.54 = (bf16[192,1024]{1,0:T(8,128)(2,1)S(1)}, bf16[192,1024]{1,0:T(8,128)(2,1)S(1)}, u32[]{:S(2)}, u32[]{:S(2)}) collective-permute-start(bf16[192,1024]{1,0:T(8,128)(2,1)S(1)} %get-tuple-element.140), channel_id=1, source_target_pairs={{0,1},{1,0},{2,3},{3,2},{4,5},{5,4},{6,7},{7,6},{8,9},{9,8},{10,11... | collective-permute-start | bytes 1179656 | tf_op jit(solution)/shard_map/ppermute | solution.py:44
  677.8 14.7 %collective-permute-start.59 = (bf16[112,384]{1,0:T(8,128)(2,1)S(1)}, bf16[112,384]{1,0:T(8,128)(2,1)S(1)}, u32[]{:S(2)}, u32[]{:S(2)}) collective-permute-start(bf16[112,384]{1,0:T(8,128)(2,1)S(1)} %get-tuple-element.219), channel_id=1, source_target_pairs={{0,4},{2,6},{4,8},{6,10},{8,12},{10,14},{12,0},{14,2},{1,5},{3,7},... | collective-permute-start | bytes 258056 | tf_op jit(solution)/shard_map/ppermute | solution.py:33
  679.8 12.6 %collective-permute-start.60 = (bf16[112,384]{1,0:T(8,128)(2,1)S(1)}, bf16[112,384]{1,0:T(8,128)(2,1)S(1)}, u32[]{:S(2)}, u32[]{:S(2)}) collective-permute-start(bf16[112,384]{1,0:T(8,128)(2,1)S(1)} %get-tuple-element.221), channel_id=1, source_target_pairs={{0,8},{2,10},{4,12},{6,14},{8,0},{10,2},{12,4},{14,6},{1,9},{3,11}... | collective-permute-start | bytes 258056 | tf_op jit(solution)/shard_map/ppermute | solution.py:33
  695.7 16.3 %collective-permute-start.55 = (bf16[256,768]{0,1:T(8,128)(2,1)}, bf16[256,768]{0,1:T(8,128)(2,1)S(1)}, u32[]{:S(2)}, u32[]{:S(2)}) collective-permute-start(bf16[256,768]{0,1:T(8,128)(2,1)} %get-tuple-element.134), channel_id=1, source_target_pairs={{0,12},{2,14},{4,0},{6,2},{8,4},{10,6},{12,8},{14,10},{1,13},{3,15... | collective-permute-start | bytes 1179656 | tf_op jit(solution)/shard_map/ppermute | solution.py:33
  698.9 34.5 %collective-permute-start.56 = (bf16[256,768]{0,1:T(8,128)(2,1)}, bf16[256,768]{0,1:T(8,128)(2,1)S(1)}, u32[]{:S(2)}, u32[]{:S(2)}) collective-permute-start(bf16[256,768]{0,1:T(8,128)(2,1)} %get-tuple-element.133), channel_id=1, source_target_pairs={{0,8},{2,10},{4,12},{6,14},{8,0},{10,2},{12,4},{14,6},{1,9},{3,11}... | collective-permute-start | bytes 1179656 | tf_op jit(solution)/shard_map/ppermute | solution.py:33
  699.3 34.9 %collective-permute-start.57 = (bf16[256,768]{0,1:T(8,128)(2,1)}, bf16[256,768]{0,1:T(8,128)(2,1)}, u32[]{:S(2)}, u32[]{:S(2)}) collective-permute-start(bf16[256,768]{0,1:T(8,128)(2,1)} %get-tuple-element.132), channel_id=1, source_target_pairs={{0,4},{2,6},{4,8},{6,10},{8,12},{10,14},{12,0},{14,2},{1,5},{3,7},... | collective-permute-start | bytes 1179656 | tf_op jit(solution)/shard_map/ppermute | solution.py:33
  (110 other events, 1047.5 us)
Sparse Core Ops, SparseCore 0:
  122.4 91.7 all-gather.4
  389.7 61.0 all-gather.6
  456.7 156.8 reduce-scatter.1

commit v3 on v2

--- a/solution.py
+++ b/solution.py
@@ -19,6 +19,7 @@
 BF16 = jnp.bfloat16
 ALL_AXES = ("batch", "blk", "head")
 VMEM_LIMIT = 56 * 2**20
+LAYER_VMEM = 60 * 2**20
 
 
 def dot(left_op, right_op, left_dim, right_dim):
@@ -63,9 +64,10 @@
     return lax.dynamic_slice_in_dim(stack, len(pieces) - 1 - place, len(pieces), 0)
 
 
-def forward_kernel(block_q, block_k, q_ref, k_ref, v_ref, mask_ref, out_ref, sums_ref, keys, values):
+def forward_kernel(block_k, q_ref, k_ref, v_ref, mask_ref, *rest):
+    out_refs, (sums_ref, keys, values) = rest[:MEMBERS], rest[MEMBERS:]
     key_count = k_ref.shape[1]
-    query_count = q_ref.shape[1]
+    block_q = q_ref.shape[1] // MEMBERS
     rows = lax.broadcasted_iota(jnp.int32, (EXTRA, key_count), 0)
     joined = jnp.concatenate([k_ref[...], mask_ref[...]], axis=0)
     keys[...] = joined.astype(F32).T.astype(BF16)
@@ -75,9 +77,9 @@
     ones_row = jnp.where(rows_q == 0, 1.0, 0.0).astype(BF16)
     scale = 1.0 / math.sqrt(HEAD_DIM)
 
-    def query_block(i, unused):
-        q_start = pl.multiple_of(i * block_q, block_q)
-        scaled = (q_ref[:, pl.ds(q_start, block_q)].astype(F32) * scale).astype(BF16)
+    for member in range(MEMBERS):
+        q_places = pl.ds(member * block_q, block_q)
+        scaled = (q_ref[:, q_places].astype(F32) * scale).astype(BF16)
         query = jnp.concatenate([scaled, ones_row], axis=0)
 
         def key_block(j, carry):
@@ -101,34 +103,32 @@
             ),
         )
         total = acc[HEAD_DIM : HEAD_DIM + 1, :]
-        out_ref[:, pl.ds(q_start, block_q)] = (acc[:HEAD_DIM, :] / total).astype(BF16)
-        sums_ref[:, pl.ds(q_start, block_q)] = top + jnp.log(total)
-        return 0
-
-    lax.fori_loop(0, query_count // block_q, query_block, 0)
+        out_refs[member][...] = (acc[:HEAD_DIM, :] / total).astype(BF16)
+        sums_ref[:, q_places] = top + jnp.log(total)
+
+
+def head_specs(arrays, places):
+    return [
+        pl.BlockSpec((HEAD_DIM, array.shape[1]), functools.partial(lambda at, i: (at, 0), place))
+        for array, place in zip(arrays, places)
+    ]
+
+
+def whole(shape):
+    return pl.BlockSpec(shape, lambda *unused: (0,) * len(shape))
 
 
 def attention_forward(queries, keys, values, places, mask_rows):
     query_count = queries.shape[1]
     key_count = keys.shape[1]
-    block_q = min(1024, query_count)
-    block_k = min(1024, key_count)
-    in_specs = [
-        pl.BlockSpec((HEAD_DIM, array.shape[1]), functools.partial(lambda at, i: (at, 0), place))
-        for array, place in zip((queries, keys, values), places)
-    ]
-    return pl.pallas_call(
-        functools.partial(forward_kernel, block_q, block_k),
+    part = (HEAD_DIM, query_count // MEMBERS)
+    result = pl.pallas_call(
+        functools.partial(forward_kernel, min(1024, key_count)),
         grid=(1,),
-        in_specs=in_specs + [pl.BlockSpec((EXTRA, key_count), lambda i: (0, 0))],
-        out_specs=[
-            pl.BlockSpec((HEAD_DIM, query_count), lambda i: (0, 0)),
-            pl.BlockSpec((1, query_count), lambda i: (0, 0)),
-        ],
-        out_shape=[
-            jax.ShapeDtypeStruct((HEAD_DIM, query_count), BF16),
-            jax.ShapeDtypeStruct((1, query_count), F32),
-        ],
+        in_specs=head_specs((queries, keys, values), places) + [whole((EXTRA, key_count))],
+        out_specs=[whole(part)] * MEMBERS + [whole((1, query_count))],
+        out_shape=[jax.ShapeDtypeStruct(part, BF16)] * MEMBERS
+        + [jax.ShapeDtypeStruct((1, query_count), F32)],
         scratch_shapes=[
             pltpu.VMEM((key_count, HEAD_DIM + EXTRA), BF16),
             pltpu.VMEM((HEAD_DIM + EXTRA, key_count), BF16),
@@ -140,6 +140,7 @@
             bytes_accessed=8 * HEAD_DIM * key_count,
         ),
     )(queries, keys, values, mask_rows)
+    return result[:MEMBERS], result[MEMBERS]
 
 
 def split_three(row):
@@ -150,26 +151,14 @@
     return high.astype(F32), middle.astype(F32), low.astype(F32)
 
 
-def backward_kernel(
-    block_q,
-    block_k,
-    q_ref,
-    k_ref,
-    v_ref,
-    mask_ref,
-    out_ref,
-    sums_ref,
-    grad_ref,
-    grads_out,
-    query_rows,
-    keys,
-    grad_rows,
-    values,
-    scaled_q,
-    dq_acc,
-):
+def backward_kernel(block_q, block_k, pieces, q_ref, k_ref, v_ref, mask_ref, sums_ref, *rest):
+    out_refs, rest = rest[:MEMBERS], rest[MEMBERS:]
+    grad_refs, rest = rest[:MEMBERS], rest[MEMBERS:]
+    result_refs, rest = rest[:pieces], rest[pieces:]
+    query_rows, keys, grad_rows, values, scaled_q, grads, dq_acc, dkv = rest
     key_count = k_ref.shape[1]
     query_count = q_ref.shape[1]
+    part = query_count // MEMBERS
     scale = 1.0 / math.sqrt(HEAD_DIM)
     places_q = lax.broadcasted_iota(jnp.int32, (EXTRA, query_count), 0)
     places_k = lax.broadcasted_iota(jnp.int32, (EXTRA, key_count), 0)
@@ -183,11 +172,16 @@
 
     query = (q_ref[...].astype(F32) * scale).astype(BF16)
     scaled_q[...] = query
-    grads = grad_ref[...]
-    deltas = jnp.sum(grads.astype(F32) * out_ref[...].astype(F32), axis=0, keepdims=True)
+    deltas = []
+    for member in range(MEMBERS):
+        grad = grad_refs[member][...]
+        grads[:, member * part : (member + 1) * part] = grad
+        product = grad.astype(F32) * out_refs[member][...].astype(F32)
+        deltas.append(jnp.sum(product, axis=0, keepdims=True))
+    deltas = jnp.concatenate(deltas, axis=1)
     joined_q = jnp.concatenate([query, extra_rows(-sums_ref[...], 1.0)], axis=0)
     query_rows[...] = joined_q.astype(F32).T.astype(BF16)
-    joined_g = jnp.concatenate([grads, extra_rows(-deltas, 0.0)], axis=0)
+    joined_g = jnp.concatenate([grads[...], extra_rows(-deltas, 0.0)], axis=0)
     grad_rows[...] = joined_g.astype(F32).T.astype(BF16)
     ones_rows = jnp.where(places_k < 3, 1.0, 0.0)
     mask_row = mask_ref[0:1, :].astype(F32)
@@ -209,51 +203,52 @@
             probs = jnp.exp(dot(query_rows[pl.ds(q_start, block_q), :], key_part, 1, 0))
             moved = dot(grad_rows[pl.ds(q_start, block_q), :], value_part, 1, 0)
             grad_scores = (probs * moved).astype(BF16)
-            dv = dv + dot(grad_ref[:, pl.ds(q_start, block_q)], probs.astype(BF16), 1, 0)
+            dv = dv + dot(grads[:, pl.ds(q_start, block_q)], probs.astype(BF16), 1, 0)
             dk = dk + dot(scaled_q[:, pl.ds(q_start, block_q)], grad_scores, 1, 0)
             dq_acc[:, pl.ds(q_start, block_q)] += dot(plain_keys, grad_scores, 1, 1)
             return dk, dv
 
         zeros = jnp.zeros((HEAD_DIM, block_k), F32)
         dk, dv = lax.fori_loop(0, query_count // block_q, query_block, (zeros, zeros))
-        grads_out[HEAD_DIM : 2 * HEAD_DIM, pl.ds(k_start, block_k)] = dk.astype(BF16)
-        grads_out[2 * HEAD_DIM :, pl.ds(k_start, block_k)] = dv.astype(BF16)
+        dkv[:HEAD_DIM, pl.ds(k_start, block_k)] = dk.astype(BF16)
+        dkv[HEAD_DIM:, pl.ds(k_start, block_k)] = dv.astype(BF16)
         return 0
 
     lax.fori_loop(0, key_count // block_k, key_block, 0)
-    grads_out[:HEAD_DIM, :query_count] = (dq_acc[...] * scale).astype(BF16)
-
-
-def attention_backward(queries, keys, values, places, mask_rows, outs, sums, grads):
+    for index, result_ref in enumerate(result_refs):
+        lanes = slice(index * part, (index + 1) * part)
+        if index < MEMBERS:
+            result_ref[:HEAD_DIM, :] = (dq_acc[:, lanes] * scale).astype(BF16)
+        else:
+            result_ref[:HEAD_DIM, :] = jnp.zeros((HEAD_DIM, part), BF16)
+        result_ref[HEAD_DIM:, :] = dkv[:, lanes]
+
+
+def attention_backward(queries, keys, values, places, mask_rows, sums, outs, grads):
     query_count = queries.shape[1]
     key_count = keys.shape[1]
-    block_q = min(1024, query_count)
-    block_k = min(1024, key_count)
-    in_specs = [
-        pl.BlockSpec((HEAD_DIM, array.shape[1]), functools.partial(lambda at, i: (at, 0), place))
-        for array, place in zip((queries, keys, values), places)
-    ]
-    spec_q = pl.BlockSpec((HEAD_DIM, query_count), lambda i: (0, 0))
+    part = query_count // MEMBERS
+    pieces = key_count // part
     wide = HEAD_DIM + EXTRA
     return pl.pallas_call(
-        functools.partial(backward_kernel, block_q, block_k),
+        functools.partial(
+            backward_kernel, min(1024, query_count), min(1024, key_count), pieces
+        ),
         grid=(1,),
-        in_specs=in_specs
-        + [
-            pl.BlockSpec((EXTRA, key_count), lambda i: (0, 0)),
-            spec_q,
-            pl.BlockSpec((1, query_count), lambda i: (0, 0)),
-            spec_q,
-        ],
-        out_specs=pl.BlockSpec((3 * HEAD_DIM, key_count), lambda i: (0, 0)),
-        out_shape=jax.ShapeDtypeStruct((3 * HEAD_DIM, key_count), BF16),
+        in_specs=head_specs((queries, keys, values), places)
+        + [whole((EXTRA, key_count)), whole((1, query_count))]
+        + [whole((HEAD_DIM, part))] * (2 * MEMBERS),
+        out_specs=[whole((3 * HEAD_DIM, part))] * pieces,
+        out_shape=[jax.ShapeDtypeStruct((3 * HEAD_DIM, part), BF16)] * pieces,
         scratch_shapes=[
             pltpu.VMEM((query_count, wide), BF16),
             pltpu.VMEM((wide, key_count), BF16),
             pltpu.VMEM((query_count, wide), BF16),
             pltpu.VMEM((wide, key_count), BF16),
             pltpu.VMEM((HEAD_DIM, query_count), BF16),
+            pltpu.VMEM((HEAD_DIM, query_count), BF16),
             pltpu.VMEM((HEAD_DIM, query_count), F32),
+            pltpu.VMEM((2 * HEAD_DIM, key_count), BF16),
         ],
         compiler_params=pltpu.CompilerParams(vmem_limit_bytes=VMEM_LIMIT),
         cost_estimate=pl.CostEstimate(
@@ -261,18 +256,346 @@
             transcendentals=query_count * key_count,
             bytes_accessed=16 * HEAD_DIM * key_count,
         ),
-    )(queries, keys, values, mask_rows, outs, sums, grads)
-
-
-def norm_apply(residue, gain_row, shift_row):
-    center = jnp.mean(residue, axis=-1, keepdims=True)
-    centred = residue - center
-    spread = jnp.mean(centred * centred, axis=-1, keepdims=True)
-    return centred * lax.rsqrt(spread + EPSILON) * gain_row + shift_row
-
-
-def gelu_exact(pre_act):
-    return jax.nn.gelu(pre_act, approximate=False)
+    )(queries, keys, values, mask_rows, sums, *outs, *grads)
+
+
+def project_kernel(count, weight_ref, bias_ref, *rest):
+    piece_refs, (all_ref, out_ref) = rest[:count], rest[count:]
+    rows = piece_refs[0].shape[0]
+    for index, piece_ref in enumerate(piece_refs):
+        all_ref[index * rows : (index + 1) * rows, :] = piece_ref[...]
+    weight = weight_ref[...].astype(F32).T.astype(BF16)
+    step = all_ref.shape[0] // MEMBERS
+    for member in range(MEMBERS):
+        lanes = slice(member * step, (member + 1) * step)
+        out_ref[:, lanes] = (dot(weight, all_ref[lanes, :], 1, 1) + bias_ref[...]).astype(BF16)
+
+
+def project(weight, bias_column, pieces):
+    count, (rows, width) = len(pieces), pieces[0].shape
+    columns = weight.shape[1]
+    return pl.pallas_call(
+        functools.partial(project_kernel, count),
+        grid=(1,),
+        in_specs=[whole(weight.shape), whole(bias_column.shape)] + [whole((rows, width))] * count,
+        out_specs=[whole((count * rows, width)), whole((columns, count * rows))],
+        out_shape=[
+            jax.ShapeDtypeStruct((count * rows, width), BF16),
+            jax.ShapeDtypeStruct((columns, count * rows), BF16),
+        ],
+        compiler_params=pltpu.CompilerParams(vmem_limit_bytes=VMEM_LIMIT),
+        cost_estimate=pl.CostEstimate(
+            flops=2 * count * rows * width * columns,
+            transcendentals=0,
+            bytes_accessed=6 * count * rows * width,
+        ),
+    )(weight, bias_column, *pieces)
+
+
+def weight_grad_kernel(slots, chunks, chunk_rows, rows_ref, *rest):
+    grad_refs, out_ref = rest[:-1], rest[-1]
+    part = grad_refs[0].shape[1]
+    columns = grad_refs[0].shape[0]
+    ones = jnp.ones((8, part), BF16)
+    for slot in range(slots):
+        lanes = slice(slot * columns, (slot + 1) * columns)
+        total, bias = 0.0, 0.0
+        for member in range(MEMBERS):
+            grad = grad_refs[slot * MEMBERS + member][...]
+            total = total + dot(grad, rows_ref[member * part : (member + 1) * part, :], 1, 0)
+            bias = bias + dot(ones, grad, 1, 1)
+        turned = total.T.astype(BF16)
+        bias = jnp.broadcast_to(bias[0:1].astype(BF16), (out_ref.shape[1] - chunk_rows, columns))
+        for chunk in range(chunks):
+            out_ref[chunk, :chunk_rows, lanes] = turned[chunk * chunk_rows : (chunk + 1) * chunk_rows]
+            out_ref[chunk, chunk_rows:, lanes] = bias
+
+
+def weight_grad(rows_all, slot_pieces, chunks, chunk_rows, block_rows):
+    slots = len(slot_pieces)
+    columns, part = slot_pieces[0][0].shape
+    shape = (chunks, block_rows, slots * columns)
+    return pl.pallas_call(
+        functools.partial(weight_grad_kernel, slots, chunks, chunk_rows),
+        grid=(1,),
+        in_specs=[whole(rows_all.shape)] + [whole((columns, part))] * (slots * MEMBERS),
+        out_specs=whole(shape),
+        out_shape=jax.ShapeDtypeStruct(shape, BF16),
+        compiler_params=pltpu.CompilerParams(vmem_limit_bytes=VMEM_LIMIT),
+        cost_estimate=pl.CostEstimate(
+            flops=2 * slots * columns * rows_all.size,
+            transcendentals=0,
+            bytes_accessed=2 * rows_all.size,
+        ),
+    )(rows_all, *[piece for pieces in slot_pieces for piece in pieces])
+
+
+def input_grad_kernel(last, info_ref, acc_ref, weight_ref, *rest):
+    piece_refs, out_refs, joined = rest[:MEMBERS], rest[MEMBERS:-1], rest[-1]
+    columns = piece_refs[0].shape[0]
+    for member in range(MEMBERS):
+        start = pl.multiple_of(info_ref[member], HEAD_DIM)
+        joined[pl.ds(start, columns), :] = piece_refs[member][...]
+    rows = acc_ref.shape[0] // len(out_refs)
+    total = acc_ref[...] + dot(joined[...], weight_ref[...], 0, 1)
+    for index, out_ref in enumerate(out_refs):
+        out_ref[...] = total[index * rows : (index + 1) * rows].astype(out_ref.dtype)
+
+
+def input_grad_step(info, acc, weight, pieces, out_count, dtype):
+    columns, part = pieces[0].shape
+    rows, width = acc.shape
+    out = (rows // out_count, width)
+    return pl.pallas_call(
+        functools.partial(input_grad_kernel, out_count),
+        grid_spec=pltpu.PrefetchScalarGridSpec(
+            num_scalar_prefetch=1,
+            grid=(1,),
+            in_specs=[whole(acc.shape), whole(weight.shape)] + [whole((columns, part))] * MEMBERS,
+            out_specs=[whole(out)] * out_count,
+            scratch_shapes=[pltpu.VMEM((MEMBERS * columns, part), BF16)],
+        ),
+        out_shape=[jax.ShapeDtypeStruct(out, dtype)] * out_count,
+        compiler_params=pltpu.CompilerParams(vmem_limit_bytes=VMEM_LIMIT),
+        cost_estimate=pl.CostEstimate(
+            flops=2 * rows * width * MEMBERS * columns,
+            transcendentals=0,
+            bytes_accessed=8 * rows * width,
+        ),
+    )(info, acc, weight, *pieces)
+
+
+def collect_kernel(count, place_ref, *rest):
+    piece_refs, out_ref = rest[:count], rest[count]
+    for index, piece_ref in enumerate(piece_refs):
+        out_ref[lax.rem(place_ref[0] + index, count)] = piece_ref[...]
+
+
+def collect(pieces, place):
+    count, shape = len(pieces), pieces[0].shape
+    return pl.pallas_call(
+        functools.partial(collect_kernel, count),
+        grid_spec=pltpu.PrefetchScalarGridSpec(
+            num_scalar_prefetch=1,
+            grid=(1,),
+            in_specs=[whole(shape)] * count,
+            out_specs=whole((count,) + shape),
+        ),
+        out_shape=jax.ShapeDtypeStruct((count,) + shape, pieces[0].dtype),
+        compiler_params=pltpu.CompilerParams(vmem_limit_bytes=VMEM_LIMIT),
+    )(place[None], *pieces)
+
+
+def gelu_parts(value):
+    size = jnp.abs(value) * math.sqrt(0.5)
+    t = 1.0 / (1.0 + 0.3275911 * size)
+    bell = jnp.exp(-0.5 * value * value)
+    poly = 1.061405429 * t - 1.453152027
+    poly = poly * t + 1.421413741
+    poly = poly * t - 0.284496736
+    poly = poly * t + 0.254829592
+    tail = 0.5 * poly * t * bell
+    share = jnp.where(value < 0, tail, 1.0 - tail)
+    return value * share, share + value * bell * (1.0 / math.sqrt(2.0 * math.pi))
+
+
+def row_mean(array):
+    return jnp.mean(array, axis=-1, keepdims=True)
+
+
+def column_sum(array):
+    return jnp.sum(array, axis=0, keepdims=True)
+
+
+def layer_kernel(blocks, planes, parts, info_ref, rows_ref, vectors_ref, inner_bias_ref, *rest):
+    weight_out, weight_inner, weight_outer = rest[:3]
+    att_refs, rest = rest[3 : 3 + parts], rest[3 + parts :]
+    cot_refs, rest = rest[:planes], rest[planes:]
+    final_refs, rest = rest[:planes], rest[planes:]
+    grad_att_refs, rest = rest[:parts], rest[parts:]
+    resid_ref, grad_outer_w, grad_inner_w, grad_out_w, grad_vectors, grad_inner_bias = rest[:6]
+    attended, hat1, scale1, low, acc, active, slope, grad_low, grad_hidden = rest[6:]
+    step = pl.program_id(0)
+    row_count, width = rows_ref.shape
+    piece = row_count // planes
+    group = width // MEMBERS
+    block = jnp.where(step < blocks, step, step - blocks)
+    pieces = [slice(k * piece, (k + 1) * piece) for k in range(planes)]
+
+    def group_rows(member):
+        return pl.ds(pl.multiple_of(info_ref[member], HEAD_DIM), group)
+
+    def vector(index):
+        return vectors_ref[index : index + 1, :]
+
+    @pl.when(step == 0)
+    def _():
+        for index, att_ref in enumerate(att_refs):
+            attended[index * HEAD_DIM : (index + 1) * HEAD_DIM, :] = att_ref[...]
+        weight = jnp.concatenate([weight_out[group_rows(m), :] for m in range(MEMBERS)])
+        for k in range(planes):
+            branch = dot(attended[:, pieces[k]], weight, 0, 0) + vector(0)
+            value = rows_ref[pieces[k], :].astype(F32) + branch
+            centred = value - row_mean(value)
+            scale = lax.rsqrt(row_mean(centred * centred) + EPSILON)
+            hat = centred * scale
+            normed = hat * vector(1) + vector(2)
+            hat1[pieces[k], :] = hat
+            scale1[pieces[k], :] = scale
+            low[pieces[k], :] = normed.astype(BF16)
+            acc[pieces[k], :] = normed + vector(3)
+        grad_vectors[...] = jnp.zeros_like(grad_vectors)
+        grad_inner_bias[...] = jnp.zeros_like(grad_inner_bias)
+
+    @pl.when(step < blocks)
+    def _():
+        bias = inner_bias_ref[pl.ds(block, 1), :]
+        for k in range(planes):
+            inner = dot(low[pieces[k], :], weight_inner[...], 1, 0) + bias
+            value, derivative = gelu_parts(inner)
+            value = value.astype(BF16)
+            active[block, pieces[k], :] = value
+            slope[block, pieces[k], :] = derivative
+            acc[pieces[k], :] += dot(value, weight_outer[...], 1, 0)
+
+    @pl.when(step == blocks)
+    def _():
+        gain_sum, shift_sum, bias_sum = 0.0, 0.0, 0.0
+        for k in range(planes):
+            value = acc[pieces[k], :]
+            centred = value - row_mean(value)
+            scale = lax.rsqrt(row_mean(centred * centred) + EPSILON)
+            hat = centred * scale
+            final_refs[k][...] = (hat * vector(4) + vector(5)).astype(BF16)
+            places = lax.broadcasted_iota(jnp.int32, (piece, width), 0)
+            grad = jnp.where(
+                places < info_ref[MEMBERS + k], cot_refs[k][...].astype(F32), 0.0
+            )
+            gain_sum += column_sum(grad * hat)
+            shift_sum += column_sum(grad)
+            grad = grad * vector(4)
+            grad = scale * (grad - row_mean(grad) - hat * row_mean(grad * hat))
+            rounded = grad.astype(BF16)
+            bias_sum += column_sum(rounded.astype(F32))
+            grad_low[pieces[k], :] = rounded
+            acc[pieces[k], :] = grad
+        grad_vectors[3:4, :] = bias_sum
+        grad_vectors[4:5, :] = gain_sum
+        grad_vectors[5:6, :] = shift_sum
+
+    @pl.when(step >= blocks)
+    def _():
+        bias_sum = 0.0
+        for k in range(planes):
+            moved = dot(grad_low[pieces[k], :], weight_outer[...], 1, 1)
+            grad = (moved * slope[block, pieces[k], :]).astype(BF16)
+            grad_hidden[pieces[k], :] = grad
+            bias_sum += column_sum(grad.astype(F32))
+            acc[pieces[k], :] += dot(grad, weight_inner[...], 1, 1)
+        grad_inner_bias[pl.ds(block, 1), :] = bias_sum
+        for m in range(MEMBERS // 2):
+            lanes = slice(m * 2 * group, (m + 1) * 2 * group)
+            grad_outer_w[lanes, :] = dot(active[block, :, lanes], grad_low[...], 0, 0).astype(BF16)
+            grad_inner_w[lanes, :] = dot(low[:, lanes], grad_hidden[...], 0, 0).astype(BF16)
+
+    @pl.when(step == 2 * blocks - 1)
+    def _():
+        gain_sum, shift_sum, bias_sum = 0.0, 0.0, 0.0
+        for k in range(planes):
+            grad, hat = acc[pieces[k], :], hat1[pieces[k], :]
+            gain_sum += column_sum(grad * hat)
+            shift_sum += column_sum(grad)
+            grad = grad * vector(1)
+            grad = scale1[pieces[k], :] * (grad - row_mean(grad) - hat * row_mean(grad * hat))
+            resid_ref[pieces[k], :] = grad
+            rounded = grad.astype(BF16)
+            bias_sum += column_sum(rounded.astype(F32))
+            grad_low[pieces[k], :] = rounded
+        grad_vectors[0:1, :] = bias_sum
+        grad_vectors[1:2, :] = gain_sum
+        grad_vectors[2:3, :] = shift_sum
+        heads = group // HEAD_DIM
+        for m in range(MEMBERS):
+            rows = slice(m * group, (m + 1) * group)
+            grad_out_w[group_rows(m), :] = dot(attended[rows, :], grad_low[...], 1, 0).astype(BF16)
+            moved = dot(weight_out[group_rows(m), :], grad_low[...], 1, 1).astype(BF16)
+            for j in range(heads):
+                grad_att_refs[m * heads + j][...] = moved[j * HEAD_DIM : (j + 1) * HEAD_DIM, :]
+
+
+def layer_rows(info, rows_all, vectors, inner_bias, weights, att_parts, cot_pieces):
+    weight_out, weight_inner, weight_outer = weights
+    hidden, width = weight_outer.shape
+    blocks, planes, parts = hidden // width, len(cot_pieces), len(att_parts)
+    row_count = att_parts[0].shape[1]
+    piece = row_count // planes
+    once = pl.Buffered(1)
+
+    def fixed(shape):
+        return pl.BlockSpec(shape, lambda *unused: (0,) * len(shape), pipeline_mode=once)
+
+    square = (width, width)
+    weight_spec = pl.BlockSpec(square, lambda i, info: (lax.rem(i, blocks), 0))
+    grad_spec = pl.BlockSpec(square, lambda i, info: (jnp.maximum(i - blocks, 0), 0))
+    small = [fixed((8, width)), fixed((8, width))]
+
+    def shape(dims, dtype):
+        return jax.ShapeDtypeStruct(dims, dtype)
+
+    result = pl.pallas_call(
+        functools.partial(layer_kernel, blocks, planes, parts),
+        grid_spec=pltpu.PrefetchScalarGridSpec(
+            num_scalar_prefetch=1,
+            grid=(2 * blocks,),
+            in_specs=[fixed((row_count, width))]
+            + small
+            + [fixed(square), weight_spec, weight_spec]
+            + [fixed((HEAD_DIM, row_count))] * parts
+            + [fixed((piece, width))] * planes,
+            out_specs=[fixed((piece, width))] * planes
+            + [fixed((HEAD_DIM, row_count))] * parts
+            + [fixed((row_count, width)), grad_spec, grad_spec, fixed(square)]
+            + small,
+            scratch_shapes=[
+                pltpu.VMEM((width, row_count), BF16),
+                pltpu.VMEM((row_count, width), F32),
+                pltpu.VMEM((row_count, 1), F32),
+                pltpu.VMEM((row_count, width), BF16),
+                pltpu.VMEM((row_count, width), F32),
+                pltpu.VMEM((blocks, row_count, width), BF16),
+                pltpu.VMEM((blocks, row_count, width), F32),
+                pltpu.VMEM((row_count, width), BF16),
+                pltpu.VMEM((row_count, width), BF16),
+            ],
+        ),
+        out_shape=[shape((piece, width), BF16)] * planes
+        + [shape((HEAD_DIM, row_count), BF16)] * parts
+        + [
+            shape((row_count, width), F32),
+            shape((hidden, width), BF16),
+            shape((hidden, width), BF16),
+            shape(square, BF16),
+            shape((8, width), F32),
+            shape((8, width), F32),
+        ],
+        compiler_params=pltpu.CompilerParams(vmem_limit_bytes=LAYER_VMEM),
+        cost_estimate=pl.CostEstimate(
+            flops=12 * row_count * width * hidden,
+            transcendentals=row_count * hidden,
+            bytes_accessed=8 * width * hidden,
+        ),
+    )(
+        info,
+        rows_all,
+        vectors,
+        inner_bias,
+        weight_out,
+        weight_inner,
+        weight_outer,
+        *att_parts,
+        *cot_pieces,
+    )
+    return result[:planes], result[planes : planes + parts], result[planes + parts :]
 
 
 def pad_rows(array, count):
@@ -337,14 +660,11 @@
             pieces.append(shift_planes(chunk, distance))
         return pieces
 
-    def from_planes(array):
-        pieces = array.reshape(planes, piece, width)
+    def from_planes(pieces):
         back = [pieces[0]]
         for distance in range(1, planes):
             back.append(shift_planes(pieces[distance], -distance))
-        doubled = jnp.concatenate([jnp.stack(back)] * 2)
-        ordered = lax.dynamic_slice_in_dim(doubled, planes - plane, planes, 0)
-        return ordered.reshape(seqs, part_rows, width)
+        return collect(back, plane).reshape(seqs, part_rows, width)
 
     own_group = core * 2 + head_place
     heads_here = HEADS // MEMBERS
@@ -384,11 +704,11 @@
     head_pieces = [swap_member(part_in, 1) for part_in in own_pieces]
     core_pieces = [swap_member(part_in, 2) for part_in in own_pieces]
     both_pieces = [swap_member(part_in, 2) for part_in in head_pieces]
-    rows_own = jnp.concatenate(own_pieces)
-    rows_all = jnp.concatenate(own_pieces + head_pieces + core_pieces + both_pieces)
-
+    all_pieces = own_pieces + head_pieces + core_pieces + both_pieces
     valid_own = places(plane) < seq_length
-    row_keep = valid_own[:row_count, None]
+    row_starts = (own_group ^ jnp.arange(MEMBERS, dtype=jnp.int32)) * group
+    kept_rows = seq_length - places(plane)[:row_count:piece]
+    info = jnp.concatenate([row_starts, kept_rows])
 
     def other_plane(distance):
         return (plane // spread_planes) * spread_planes + (part - distance) % spread_planes
@@ -402,12 +722,11 @@
             route.append((i, target * CORES + i % CORES))
         return lax.ppermute(array, "blk", route)
 
-    qkv = dot(own_weight, rows_all, 0, 1) + own_bias[:, None]
-    qkv = qkv.astype(BF16)
+    rows_all, qkv = project(own_weight, own_bias[:, None], all_pieces)
     late_cotangent, late_out, late_inner, late_outer, qkv = lax.optimization_barrier(
         (cotangent, w_attn_out, w_inner, w_outer, qkv)
     )
-    cot_own = jnp.concatenate(to_planes(late_cotangent))
+    cot_pieces = to_planes(late_cotangent)
 
     small = jnp.concatenate(
         [b_attn_out, norm1_gain, norm1_bias, b_outer, norm2_gain, norm2_bias, b_inner]
@@ -427,13 +746,12 @@
     out_start = wide_share + share * folds
     small_all = second[:, out_start + share]
     vectors = jnp.swapaxes(small_all[:, : 6 * share].reshape(devices, 6, share), 0, 1)
-    vectors = vectors.reshape(6, width).astype(F32)
-    bias_out, gain_first, shift_first, bias_outer, gain_second, shift_second = vectors
-    bias_inner = small_all[:, 6 * share : 6 * share + wide_share].reshape(hidden).astype(F32)
-    weight_out = second[:, out_start : out_start + share].reshape(MEMBERS, group, width)
-    weight_out = reorder_members(weight_out, core, head_place).reshape(width, width)
+    vectors = pad_rows(vectors.reshape(6, width).astype(F32), 2)
+    bias_inner = small_all[:, 6 * share : 6 * share + wide_share].astype(F32)
+    bias_inner = pad_rows(bias_inner.reshape(folds, width), 8 - folds)
+    weight_out = second[:, out_start : out_start + share].reshape(width, width)
     weight_inner = second[:, inner_start:out_start].reshape(devices, folds, share, width)
-    weight_inner = jnp.swapaxes(weight_inner, 1, 2).reshape(width, hidden)
+    weight_inner = jnp.swapaxes(weight_inner, 0, 1).reshape(hidden, width)
     weight_outer = second[:, :wide_share].reshape(hidden, width)
 
     queries = keys = values = qkv
@@ -450,12 +768,10 @@
     mask_row = jnp.where(valid, 0.0, NEG_BIG).astype(BF16)[None]
     mask_rows = pad_rows(mask_row, EXTRA - 1)
 
-    def to_members(array):
-        parts = [array[:, :row_count]]
-        for member in range(1, MEMBERS):
-            sent = array[:, member * row_count : (member + 1) * row_count]
-            parts.append(swap_member(sent, member))
-        return parts
+    def to_members(pieces):
+        return [pieces[0]] + [
+            swap_member(pieces[member], member) for member in range(1, MEMBERS)
+        ]
 
     outs, sums, parts = [], [], []
     for slot in range(heads_here):
@@ -464,70 +780,40 @@
         outs.append(out)
         sums.append(total)
         parts.append(to_members(out))
-    attended = jnp.concatenate(
-        [parts[slot][member] for member in range(MEMBERS) for slot in range(heads_here)]
-    )
-
-    branch = dot(attended, weight_out, 0, 0) + bias_out
-    normed1, back_first = jax.vjp(
-        norm_apply, rows_own.astype(F32) + branch, gain_first, shift_first
-    )
-    normed_low = normed1.astype(BF16)
-    inner_pre = dot(normed_low, weight_inner, 1, 0) + bias_inner
-    active, back_gelu = jax.vjp(gelu_exact, inner_pre)
-    active_low = active.astype(BF16)
-    outer_out = dot(active_low, weight_outer, 1, 0) + bias_outer
-    final_rows, back_second = jax.vjp(
-        norm_apply, normed1 + outer_out, gain_second, shift_second
-    )
-    output = from_planes(final_rows.astype(BF16))
-
-    grad_final = jnp.where(row_keep, cot_own.astype(F32), 0.0)
-    grad_resid2, grad_gain2, grad_shift2 = back_second(grad_final)
-    grad_outer = grad_resid2.astype(BF16)
-    grad_bias_outer = jnp.sum(grad_outer.astype(F32), axis=0)
-    grad_weight_outer = dot(active_low, grad_outer, 0, 0)
-    (grad_inner_pre,) = back_gelu(dot(grad_outer, weight_outer, 1, 1))
-    grad_inner = grad_inner_pre.astype(BF16)
-    grad_bias_inner = jnp.sum(grad_inner.astype(F32), axis=0)
-    grad_weight_inner = dot(normed_low, grad_inner, 0, 0)
-    grad_normed1 = grad_resid2 + dot(grad_inner, weight_inner, 1, 1)
-    grad_resid1, grad_gain1, grad_shift1 = back_first(grad_normed1)
-    grad_branch = grad_resid1.astype(BF16)
-    grad_bias_out = jnp.sum(grad_branch.astype(F32), axis=0)
-    grad_weight_out = dot(attended, grad_branch, 1, 0).astype(BF16)
-    grad_weight_out = reorder_members(
-        grad_weight_out.reshape(MEMBERS, group, width), core, head_place
-    )
-    grad_attended = dot(weight_out, grad_branch, 1, 1).astype(BF16)
-
-    vector_grads = [
-        grad_bias_out,
-        grad_gain1,
-        grad_shift1,
-        grad_bias_outer,
-        grad_gain2,
-        grad_shift2,
-    ]
+    att_parts = [parts[slot][member] for member in range(MEMBERS) for slot in range(heads_here)]
+    final_pieces, grad_att, more = layer_rows(
+        info,
+        rows_all,
+        vectors,
+        bias_inner,
+        (weight_out, weight_inner, weight_outer),
+        att_parts,
+        cot_pieces,
+    )
+    output = from_planes(final_pieces)
+    grad_input, grad_outer_w, grad_inner_w, grad_out_w, grad_vectors, grad_inner_bias = more
+
+    vector_pack = jnp.swapaxes(grad_vectors[:6].reshape(6, devices, share), 0, 1)
     vector_pack = jnp.concatenate(
-        [vector.reshape(devices, share) for vector in vector_grads]
-        + [grad_bias_inner.reshape(devices, wide_share)],
+        [
+            vector_pack.reshape(devices, 6 * share),
+            grad_inner_bias[:folds].reshape(devices, wide_share),
+        ],
         axis=1,
-    )
+    ).astype(BF16)
     vector_pack = jnp.pad(vector_pack, ((0, 0), (0, width - vector_pack.shape[1])))
-    inner_pack = jnp.swapaxes(
-        grad_weight_inner.astype(BF16).reshape(devices, share, folds, width), 1, 2
-    ).reshape(devices, folds * share, width)
+    pack_rows = out_start + share
     grad_pack = jnp.concatenate(
         [
-            grad_weight_outer.astype(BF16).reshape(devices, wide_share, width),
-            inner_pack,
-            grad_weight_out.reshape(devices, share, width),
-            vector_pack.astype(BF16)[:, None],
+            grad_outer_w.reshape(devices, wide_share, width),
+            jnp.swapaxes(grad_inner_w.reshape(folds, devices, share, width), 0, 1).reshape(
+                devices, folds * share, width
+            ),
+            grad_out_w.reshape(devices, share, width),
+            jnp.pad(vector_pack[:, None], ((0, 0), (0, 7 - pack_rows % 8), (0, 0))),
         ],
         axis=1,
     )
-    grad_pack = jnp.pad(grad_pack, ((0, 0), (0, -grad_pack.shape[1] % 16), (0, 0)))
     owned = lax.psum_scatter(grad_pack, ALL_AXES, scatter_dimension=0, tiled=True)[0].astype(F32)
     owned_outer = owned[:wide_share]
     owned_inner = owned[inner_start:out_start].reshape(folds, share, width)
@@ -536,16 +822,10 @@
     owned_vectors = owned[out_start + share]
 
     chunk_rows = width // (batches * planes)
-    extra = -chunk_rows % 16 + 16
-
-    def reduce_weights(slot_grads):
-        columns = slot_grads.shape[0]
-        grad_weight = dot(slot_grads, rows_all, 1, 0).T.astype(BF16)
-        grad_bias = jnp.sum(slot_grads.astype(F32), axis=1).astype(BF16)
-        bias_block = jnp.pad(grad_bias[None], ((0, extra - 1), (0, 0)))
-        chunks = grad_weight.reshape(batches * planes, chunk_rows, columns)
-        bias_blocks = jnp.broadcast_to(bias_block, (batches * planes,) + bias_block.shape)
-        chunks = jnp.concatenate([chunks, bias_blocks], axis=1)
+    block_rows = chunk_rows + -chunk_rows % 16 + 16
+
+    def reduce_weights(slot_pieces):
+        chunks = weight_grad(rows_all, slot_pieces, batches * planes, chunk_rows, block_rows)
         return chunks.reshape((batches, planes) + chunks.shape[1:])
 
     def finish_weights(chunks):
@@ -570,40 +850,39 @@
         got = reorder_members(jnp.stack(got), core, head_place)
         return got.reshape(MEMBERS, piece_rows, columns // (3 * HEAD_DIM), 3, HEAD_DIM)
 
-    plane_rows = MEMBERS * row_count
     slot_grads = []
-    grad_input = grad_resid1
     early = None
     for slot in range(heads_here):
-        grad_parts = []
-        for member in range(MEMBERS):
-            start = member * group + slot * HEAD_DIM
-            sent = grad_attended[start : start + HEAD_DIM]
-            grad_parts.append(swap_member(sent, member) if member else sent)
-        grad_side = jnp.concatenate(grad_parts, axis=1)
-        if slot == heads_here - 1:
-            early = reduce_weights(jnp.concatenate(slot_grads))
-            early, grad_side, grad_input = lax.optimization_barrier(
-                (early, grad_side, grad_input)
-            )
+        last = slot == heads_here - 1
+        sent = [grad_att[member * heads_here + slot] for member in range(MEMBERS)]
+        grad_side = to_members(sent)
+        if last:
+            early = reduce_weights(slot_grads)
+            early, grad_side = lax.optimization_barrier((early, grad_side))
         slot_at = tuple(start + slot for start in starts)
         grads = attention_backward(
-            queries, keys, values, slot_at, mask_rows, outs[slot], sums[slot], grad_side
+            queries, keys, values, slot_at, mask_rows, sums[slot], outs[slot], grad_side
         )
-        if spread_planes > 1:
-            total = grads[HEAD_DIM:, :plane_rows].astype(F32)
-            for distance in range(1, spread_planes):
-                sent = grads[HEAD_DIM:, distance * plane_rows : (distance + 1) * plane_rows]
-                total = total + shift_parts(sent, -distance).astype(F32)
-            grads = jnp.concatenate([grads[:HEAD_DIM, :plane_rows], total.astype(BF16)])
-        slot_grads.append(grads)
-        arrived = reorder_members(jnp.stack(to_members(grads)), core, head_place)
+        own = list(grads[:MEMBERS])
+        for distance in range(1, spread_planes):
+            for member in range(MEMBERS):
+                moved = shift_parts(grads[distance * MEMBERS + member], -distance)
+                own[member] = (own[member].astype(F32) + moved.astype(F32)).astype(BF16)
+        slot_grads.append(own)
         slot_weight = third[:, slot * share : (slot + 1) * share].reshape(width, width)
-        grad_input = grad_input + dot(arrived.reshape(width, row_count), slot_weight, 0, 1)
-    input_grad = from_planes(grad_input.astype(BF16))
+        stepped = input_grad_step(
+            row_starts,
+            grad_input,
+            slot_weight,
+            to_members(own),
+            planes if last else 1,
+            BF16 if last else F32,
+        )
+        grad_input = stepped[0]
+    input_grad = from_planes(stepped)
 
     got = jnp.concatenate(
-        [finish_weights(early), finish_weights(reduce_weights(slot_grads[-1]))], axis=2
+        [finish_weights(early), finish_weights(reduce_weights(slot_grads[-1:]))], axis=2
     )
     matrices = [
         jnp.swapaxes(got[:, :share, :, i], 0, 1).reshape(share, width) for i in range(3)

time: 765 us -> 709 us (0.927)
  matrix products: 122 us -> 0 us
  Pallas kernels: 228 us -> 337 us
  local copies, waits for them, and re-layouts: 144 us -> 56.5 us
  waiting for transfers between devices: 127 us -> 184 us
  other arithmetic: 45 us -> 14.8 us
  starting transfers between devices: 72 us -> 93.6 us
    dot_general x15 -> x0, matrix products: 122 us -> none  [dot(): lax.dot_general(left_op, right_op, (((left_dim,), (right_dim,)), ((), ())...]
    pallas_call x6 -> x15, Pallas kernels: 228 us -> 337 us  [the longest x3 141 us: attention_backward(): pl.pallas_call(functools.partial(backward_kernel, min(1024, query_count),...]
    unnamed x213 -> x159, local copies, waits for them, and re-layouts: 49.5 us -> 6.9 us
    all_gather x1, waiting for transfers between devices: 0.01 us -> 31 us  [local(): second = lax.all_gather(second_pack, ALL_AXES, axis=0, tiled=False)]
    ppermute x12, waiting for transfers between devices: 6.81 us -> 35.6 us  [swap_member(): return lax.ppermute(array, ('blk', 'head'), route)]
    ppermute x21, waiting for transfers between devices: 69.3 us -> 92.2 us  [shift_planes(): return lax.ppermute(array, 'blk', route)]
    ppermute x21, starting transfers between devices: 37 us -> 58.7 us  [shift_planes(): return lax.ppermute(array, 'blk', route)]
    ppermute x3, waiting for transfers between devices: 15.5 us -> 0.01 us  [shift_batch(): lax.ppermute(array, 'batch', [(i, (i + distance) % size) for i in range(s...]
  transfers between devices with their start and end apart: 75 -> 75, of which waited for: 18 -> 22; matrix products, arithmetic and copies ran while one was open for 29% -> 8% of each run, Pallas kernels for 30% -> 47%
where the time goes in v3:
time: 709 us; the launch traced here: 701 us
  Pallas kernels  337 us (48%)
  waiting for transfers between devices  184 us (26%)
  starting transfers between devices  93.6 us (13%)
  local copies, waits for them, and re-layouts  56.5 us (8%)
  between operations  15.4 us (2%)
  other arithmetic  14.8 us (2%)
    pallas_call x3, Pallas kernels, attention_backward(): pl.pallas_call(functools.partial(backward_kernel, min(1024, query_count),...  141 us
    ppermute x21, waiting for transfers between devices, shift_planes(): return lax.ppermute(array, 'blk', route)  92.2 us
    pallas_call x3, Pallas kernels, attention_forward(): pl.pallas_call(functools.partial(forward_kernel, min(1024, key_count)), g...  88 us
    pallas_call x1, Pallas kernels, layer_rows(): pl.pallas_call(functools.partial(layer_kernel, blocks, planes, parts), gr...  59 us
    ppermute x21, starting transfers between devices, shift_planes(): return lax.ppermute(array, 'blk', route)  58.7 us
    ppermute x12, waiting for transfers between devices, swap_member(): return lax.ppermute(array, ('blk', 'head'), route)  35.6 us
    all_gather x1, waiting for transfers between devices, local(): second = lax.all_gather(second_pack, ALL_AXES, axis=0, tiled=False)  31 us
    ppermute x16, waiting for transfers between devices, swap_member(): return lax.ppermute(array, 'head', [(0, 1), (1, 0)])  24.9 us
  transfers between devices with their start and end apart: 75, of which 22 were waited for; matrix products, arithmetic and copies ran while one was open for 8% of the time, Pallas kernels for 47%

profile of v3, /device:TPU:0, one launch (start us, length us, event | category | flops | bytes accessed | tf_op | source)
XLA Modules:
  0.0 701.1 jit_solution(5498233012406464224)
XLA Ops:
  12.2 2.6 collective-permute-start.1
  15.0 2.1 collective-permute-start.7
  19.0 3.7 collective-permute-start.3
  23.7 8.0 %collective-permute-done.3 = bf16[4,32,576]{2,1,0:T(8,128)(2,1)S(1)} collective-permute-done((bf16[4,32,576]{2,1,0:T(8,128)(2,1)S(1)}, bf16[4,32,576]{2,1,0:T(8,128)(2,1)S(1)}, u32[]{:S(2)}, u32[]{:S(2)}) %collective-permute-start.3) | collective-permute-done | bytes 147488 | tf_op jit(solution)/shard_map/ppermute | solution.py:34
  31.7 10.5 %collective-permute-done.4 = bf16[4,32,576]{2,1,0:T(8,128)(2,1)S(1)} collective-permute-done((bf16[4,32,576]{2,1,0:T(8,128)(2,1)S(1)}, bf16[4,32,576]{2,1,0:T(8,128)(2,1)S(1)}, u32[]{:S(2)}, u32[]{:S(2)}) %collective-permute-start.4) | collective-permute-done | bytes 147488 | tf_op jit(solution)/shard_map/ppermute | solution.py:34
  47.0 14.8 %collective-permute-done.8.rest_2_ = bf16[256,768]{1,0:T(8,128)(2,1)} collective-permute-done((bf16[256,768]{1,0:T(8,128)(2,1)S(1)}, bf16[256,768]{1,0:T(8,128)(2,1)}, u32[]{:S(2)}, u32[]{:S(2)}) %collective-permute-start.8) | collective-permute-done | bytes 393248 | tf_op jit(solution)/shard_map/ppermute | solution.py:34
  66.2 2.1 concatenate.167
  68.4 5.5 collective-permute-done.11.rest_5_
  74.0 8.4 %collective-permute-done.12.rest_6_ = bf16[256,768]{1,0:T(8,128)(2,1)S(1)} collective-permute-done((bf16[256,768]{1,0:T(8,128)(2,1)}, bf16[256,768]{1,0:T(8,128)(2,1)S(1)}, u32[]{:S(2)}, u32[]{:S(2)}) %collective-permute-start.12) | collective-permute-done | bytes 393248 | tf_op jit(solution)/shard_map/ppermute | solution.py:45
  82.4 7.5 %collective-permute-done.13.rest_7_ = bf16[256,768]{1,0:T(8,128)(2,1)} collective-permute-done((bf16[256,768]{1,0:T(8,128)(2,1)}, bf16[256,768]{1,0:T(8,128)(2,1)}, u32[]{:S(2)}, u32[]{:S(2)}) %collective-permute-start.13) | collective-permute-done | bytes 393248 | tf_op jit(solution)/shard_map/ppermute | solution.py:45
  94.9 10.7 %shard_map.305 = (bf16[4096,768]{1,0:T(8,128)(2,1)}, bf16[576,4096]{1,0:T(8,128)(2,1)}) custom-call(bf16[768,576]{1,0:T(8,128)(2,1)} %bitcast.253, f32[576,1]{1,0:T(8,128)} %copy.144.bias_ref, bf16[256,768]{1,0:T(8,128)(2,1)} %copy-done.14, bf16[256,768]{1,0:T(8,128)(2,1)} %collective-permute-done.7.rest_1_, ...), custom_call_target="tpu_custom_call" | custom-call | flops 3623878656 | bytes 18874368 | tf_op jit(solution)/shard_map/pallas_call | solution.py:277
  105.6 2.6 concatenate.168
  113.7 29.3 %shard_map.306 = (bf16[64,1024]{1,0:T(8,128)(2,1)}, bf16[64,1024]{1,0:T(8,128)(2,1)}, bf16[64,1024]{1,0:T(8,128)(2,1)}, bf16[64,1024]{1,0:T(8,128)(2,1)}, f32[1,4096]{1,0:T(1,128)}) custom-call(bf16[576,4096]{1,0:T(8,128)(2,1)} %get-tuple-element.90.q_ref.k_ref.v_ref, bf16[576,4096]{1,0:T(8,128)(2,1)} %get-tuple-element.90.q_ref.k_ref.v_ref, ...), custom_call_target="tpu_custom_call" | custom-call | flops 17179869184 | bytes 2097152 | tf_op jit(solution)/shard_map/pallas_call | solution.py:125
  144.4 29.6 %shard_map.307 = (bf16[64,1024]{1,0:T(8,128)(2,1)}, bf16[64,1024]{1,0:T(8,128)(2,1)}, bf16[64,1024]{1,0:T(8,128)(2,1)}, bf16[64,1024]{1,0:T(8,128)(2,1)}, f32[1,4096]{1,0:T(1,128)}) custom-call(bf16[576,4096]{1,0:T(8,128)(2,1)} %get-tuple-element.90.q_ref.k_ref.v_ref, bf16[576,4096]{1,0:T(8,128)(2,1)} %get-tuple-element.90.q_ref.k_ref.v_ref, ...), custom_call_target="tpu_custom_call" | custom-call | flops 17179869184 | bytes 2097152 | tf_op jit(solution)/shard_map/pallas_call | solution.py:125
  174.5 31.0 %all-gather.5.cloned.1.call-done = bf16[7168,768]{1,0:T(8,128)(2,1)} async-done(((bf16[224,768]{1,0:T(8,128)(2,1)}), bf16[7168,768]{1,0:T(8,128)(2,1)}) %all-gather.5.cloned.1.call-update) | async-done | bytes 11010064 | tf_op jit(solution)/shard_map/all_gather | solution.py:738
  205.7 29.2 %shard_map.308 = (bf16[64,1024]{1,0:T(8,128)(2,1)}, bf16[64,1024]{1,0:T(8,128)(2,1)}, bf16[64,1024]{1,0:T(8,128)(2,1)}, bf16[64,1024]{1,0:T(8,128)(2,1)}, f32[1,4096]{1,0:T(1,128)}) custom-call(bf16[576,4096]{1,0:T(8,128)(2,1)} %get-tuple-element.90.q_ref.k_ref.v_ref, bf16[576,4096]{1,0:T(8,128)(2,1)} %get-tuple-element.90.q_ref.k_ref.v_ref, ...), custom_call_target="tpu_custom_call" | custom-call | flops 17179869184 | bytes 2097152 | tf_op jit(solution)/shard_map/pallas_call | solution.py:125
  240.8 2.9 collective-permute-start.33
  245.0 8.0 %fusion.44 = (bf16[32,96,768]{2,1,0:T(8,128)(2,1)}, bf16[32,96,768]{2,1,0:T(8,128)(2,1)}) fusion(bf16[32,224,768]{2,1,0:T(8,128)(2,1)} %bitcast.216), kind=kLoop, calls=%fused_computation.170 | loop fusion | bytes 18874368 | tf_op jit(solution)/shard_map/slice | solution.py:755
  257.0 2.4 slice.315
  259.4 4.8 copy.149
  264.9 5.2 collective-permute-done.32.rest_17_
  271.1 59.0 %shard_map.309 = (bf16[256,768]{1,0:T(8,128)(2,1)}, bf16[256,768]{1,0:T(8,128)(2,1)}, bf16[256,768]{1,0:T(8,128)(2,1)}, bf16[256,768]{1,0:T(8,128)(2,1)}, bf16[6...) custom-call(s32[8]{0:T(128)} %pad_add_fusion.info_ref, ...), custom_call_target="tpu_custom_call" | custom-call | flops 28991029248 | bytes 18874368 | tf_op jit(solution)/shard_map/pallas_call | solution.py:545
  332.2 3.1 copy.168
  338.6 5.2 fusion.1
  347.6 46.8 %shard_map.313 = (bf16[192,1024]{1,0:T(8,128)(2,1)}, bf16[192,1024]{1,0:T(8,128)(2,1)}, bf16[192,1024]{1,0:T(8,128)(2,1)}, bf16[192,1024]{1,0:T(8,128)(2,1)}) custom-call(bf16[576,4096]{1,0:T(8,128)(2,1)} %get-tuple-element.90.q_ref.k_ref.v_ref, bf16[576,4096]{1,0:T(8,128)(2,1)} %get-tuple-element.90.q_ref.k_ref.v_ref, ...), custom_call_target="tpu_custom_call" | custom-call | flops 42949672960 | bytes 4194304 | tf_op jit(solution)/shard_map/pallas_call | solution.py:233
  395.7 47.0 %shard_map.311 = (bf16[192,1024]{1,0:T(8,128)(2,1)}, bf16[192,1024]{1,0:T(8,128)(2,1)}, bf16[192,1024]{1,0:T(8,128)(2,1)}, bf16[192,1024]{1,0:T(8,128)(2,1)}) custom-call(bf16[576,4096]{1,0:T(8,128)(2,1)} %get-tuple-element.90.q_ref.k_ref.v_ref, bf16[576,4096]{1,0:T(8,128)(2,1)} %get-tuple-element.90.q_ref.k_ref.v_ref, ...), custom_call_target="tpu_custom_call" | custom-call | flops 42949672960 | bytes 4194304 | tf_op jit(solution)/shard_map/pallas_call | solution.py:233
  442.7 8.3 %shard_map.315 = bf16[8,112,384]{2,1,0:T(8,128)(2,1)} custom-call(bf16[4096,768]{1,0:T(8,128)(2,1)} %get-tuple-element.84.rows_ref, bf16[192,1024]{1,0:T(8,128)(2,1)} %get-tuple-element.115.rest_0_, bf16[192,1024]{1,0:T(8,128)(2,1)} %get-tuple-element.116.rest_1_, bf16[192,1024]{1,0:T(8,128)(2,1)} %get-tuple-element.117.rest_2_, ...), custom_call_target="tpu_custom_call" | custom-call | flops 2415919104 | bytes 6291456 | tf_op jit(solution)/shard_map/pallas_call | solution.py:318
  451.7 47.1 %shard_map.316 = (bf16[192,1024]{1,0:T(8,128)(2,1)}, bf16[192,1024]{1,0:T(8,128)(2,1)}, bf16[192,1024]{1,0:T(8,128)(2,1)}, bf16[192,1024]{1,0:T(8,128)(2,1)}) custom-call(bf16[576,4096]{1,0:T(8,128)(2,1)} %get-tuple-element.90.q_ref.k_ref.v_ref, bf16[576,4096]{1,0:T(8,128)(2,1)} %get-tuple-element.90.q_ref.k_ref.v_ref, ...), custom_call_target="tpu_custom_call" | custom-call | flops 42949672960 | bytes 4194304 | tf_op jit(solution)/shard_map/pallas_call | solution.py:233
  498.8 5.8 shard_map.319
  507.0 16.6 %collective-permute-start.34 = (bf16[256,768]{1,0:T(8,128)(2,1)}, bf16[256,768]{1,0:T(8,128)(2,1)S(1)}, u32[]{:S(2)}, u32[]{:S(2)}) collective-permute-start(bf16[256,768]{1,0:T(8,128)(2,1)} %get-tuple-element.105), channel_id=1, source_target_pairs={{0,12},{2,14},{4,0},{6,2},{8,4},{10,6},{12,8},{14,10},{1,13},{3,15... | collective-permute-start | bytes 1179656 | tf_op jit(solution)/shard_map/ppermute | solution.py:34
  523.6 2.2 collective-permute-start.35
  526.9 4.9 collective-permute-start.66
  534.2 9.3 %collective-permute-done.66 = bf16[112,192]{1,0:T(8,128)(2,1)S(1)} collective-permute-done((bf16[112,192]{1,0:T(8,128)(2,1)S(1)}, bf16[112,192]{1,0:T(8,128)(2,1)S(1)}, u32[]{:S(2)}, u32[]{:S(2)}) %collective-permute-start.66) | collective-permute-done | bytes 43040 | tf_op jit(solution)/shard_map/ppermute | solution.py:34
  544.1 12.1 %collective-permute-done.67 = bf16[112,192]{1,0:T(8,128)(2,1)S(1)} collective-permute-done((bf16[112,192]{1,0:T(8,128)(2,1)S(1)}, bf16[112,192]{1,0:T(8,128)(2,1)S(1)}, u32[]{:S(2)}, u32[]{:S(2)}) %collective-permute-start.67) | collective-permute-done | bytes 43040 | tf_op jit(solution)/shard_map/ppermute | solution.py:34
  556.4 7.3 %collective-permute-start.59 = (bf16[112,384]{1,0:T(8,128)(2,1)S(1)}, bf16[112,384]{1,0:T(8,128)(2,1)S(1)}, u32[]{:S(2)}, u32[]{:S(2)}) collective-permute-start(bf16[112,384]{1,0:T(8,128)(2,1)S(1)} %get-tuple-element.183), channel_id=1, source_target_pairs={{0,4},{2,6},{4,8},{6,10},{8,12},{10,14},{12,0},{14,2},{1,5},{3,7},... | collective-permute-start | bytes 258056 | tf_op jit(solution)/shard_map/ppermute | solution.py:34
  565.7 2.8 collective-permute-start.61
  577.4 3.0 collective-permute-done.36.rest_3_
  582.7 19.6 %collective-permute-done.63 = f32[32,384]{1,0:T(8,128)S(1)} collective-permute-done((f32[32,384]{1,0:T(8,128)S(1)}, f32[32,384]{1,0:T(8,128)S(1)}, u32[]{:S(2)}, u32[]{:S(2)}) %collective-permute-start.63) | collective-permute-done | bytes 49184 | tf_op jit(solution)/shard_map/ppermute | solution.py:49
  603.9 2.7 shard_map.310
  610.6 3.9 fusion.45
  614.5 6.6 shard_map.312.acc_ref
  621.1 14.1 %collective-permute-done.48.rest_3_ = bf16[192,1024]{1,0:T(8,128)(2,1)} collective-permute-done((bf16[192,1024]{1,0:T(8,128)(2,1)S(1)}, bf16[192,1024]{1,0:T(8,128)(2,1)}, u32[]{:S(2)}, u32[]{:S(2)}) %collective-permute-start.48) | collective-permute-done | bytes 393248 | tf_op jit(solution)/shard_map/ppermute | solution.py:49
  635.1 6.5 shard_map.314.acc_ref
  641.7 5.9 shard_map.317
  647.5 5.0 collective-permute-start.55
  658.5 3.9 collective-permute-done.55.rest_1_
  662.4 24.0 %collective-permute-done.56.rest_2_ = bf16[256,768]{1,0:T(8,128)(2,1)S(1)} collective-permute-done((bf16[256,768]{1,0:T(8,128)(2,1)}, bf16[256,768]{1,0:T(8,128)(2,1)S(1)}, u32[]{:S(2)}, u32[]{:S(2)}) %collective-permute-start.56) | collective-permute-done | bytes 393248 | tf_op jit(solution)/shard_map/ppermute | solution.py:34
  687.4 2.6 shard_map.318
  (432 shorter events, 90.0 us)
Async XLA Ops:
  7.2 198.4 %all-gather.5.cloned.1.call-start = ((), (), s32[]{:S(2)}) async-start(), calls=%async_computation.2 | async-start | bytes 11354112 | tf_op jit(solution)/shard_map/all_gather | solution.py:738
  15.0 32.0 %collective-permute-start.7 = (bf16[256,768]{1,0:T(8,128)(2,1)S(1)}, bf16[256,768]{1,0:T(8,128)(2,1)}, u32[]{:S(2)}, u32[]{:S(2)}) collective-permute-start(bf16[256,768]{1,0:T(8,128)(2,1)S(1)} %get-tuple-element.169), channel_id=1, source_target_pairs={{0,4},{2,6},{4,8},{6,10},{8,12},{10,14},{12,0},{14,2},{1,5},{3,7},... | collective-permute-start | bytes 1179656 | tf_op jit(solution)/shard_map/ppermute | solution.py:34
  19.0 12.7 %collective-permute-start.3 = (bf16[4,32,576]{2,1,0:T(8,128)(2,1)S(1)}, bf16[4,32,576]{2,1,0:T(8,128)(2,1)S(1)}, u32[]{:S(2)}, u32[]{:S(2)}) collective-permute-start(bf16[4,32,576]{2,1,0:T(8,128)(2,1)S(1)} %maximum_select_fusion.7), channel_id=1, source_target_pairs={{0,12},{2,14},{4,0},{6,2},{8,4},{10,6},{12,8},{14,10},{1,13},{3,15... | collective-permute-start | bytes 442376 | tf_op jit(solution)/shard_map/ppermute | solution.py:34
  22.7 19.6 %collective-permute-start.4 = (bf16[4,32,576]{2,1,0:T(8,128)(2,1)S(1)}, bf16[4,32,576]{2,1,0:T(8,128)(2,1)S(1)}, u32[]{:S(2)}, u32[]{:S(2)}) collective-permute-start(bf16[4,32,576]{2,1,0:T(8,128)(2,1)S(1)} %maximum_select_fusion.7), channel_id=1, source_target_pairs={{0,8},{2,10},{4,12},{6,14},{8,0},{10,2},{12,4},{14,6},{1,9},{3,11}... | collective-permute-start | bytes 442376 | tf_op jit(solution)/shard_map/ppermute | solution.py:34
  22.7 19.6 %collective-permute-start.5 = (bf16[4,32,576]{2,1,0:T(8,128)(2,1)S(1)}, bf16[4,32,576]{2,1,0:T(8,128)(2,1)S(1)}, u32[]{:S(2)}, u32[]{:S(2)}) collective-permute-start(bf16[4,32,576]{2,1,0:T(8,128)(2,1)S(1)} %maximum_select_fusion.7), channel_id=1, source_target_pairs={{0,4},{2,6},{4,8},{6,10},{8,12},{10,14},{12,0},{14,2},{1,5},{3,7},... | collective-permute-start | bytes 442376 | tf_op jit(solution)/shard_map/ppermute | solution.py:34
  42.7 22.9 %collective-permute-start.6 = (bf16[4,4,32,576]{3,2,1,0:T(8,128)(2,1)S(1)}, bf16[4,4,32,576]{3,2,1,0:T(8,128)(2,1)S(1)}, u32[]{:S(2)}, u32[]{:S(2)}) collective-permute-start(bf16[4,4,32,576]{3,2,1,0:T(8,128)(2,1)S(1)} %constant_dynamic-slice_fusion.2), channel_id=1, source_target_pairs={{0,16},{16,0},{1,17},{17,1},{2,18},{18,2},{3,19},{19,3},{4,20},{20... | collective-permute-start | bytes 1769480 | tf_op jit(solution)/shard_map/ppermute | solution.py:39
  44.3 17.5 %collective-permute-start.8 = (bf16[256,768]{1,0:T(8,128)(2,1)S(1)}, bf16[256,768]{1,0:T(8,128)(2,1)}, u32[]{:S(2)}, u32[]{:S(2)}) collective-permute-start(bf16[256,768]{1,0:T(8,128)(2,1)S(1)} %get-tuple-element.171), channel_id=1, source_target_pairs={{0,8},{2,10},{4,12},{6,14},{8,0},{10,2},{12,4},{14,6},{1,9},{3,11}... | collective-permute-start | bytes 1179656 | tf_op jit(solution)/shard_map/ppermute | solution.py:34
  45.0 18.6 %collective-permute-start.9 = (bf16[256,768]{1,0:T(8,128)(2,1)S(1)}, bf16[256,768]{1,0:T(8,128)(2,1)}, u32[]{:S(2)}, u32[]{:S(2)}) collective-permute-start(bf16[256,768]{1,0:T(8,128)(2,1)S(1)} %get-tuple-element.168), channel_id=1, source_target_pairs={{0,12},{2,14},{4,0},{6,2},{8,4},{10,6},{12,8},{14,10},{1,13},{3,15... | collective-permute-start | bytes 1179656 | tf_op jit(solution)/shard_map/ppermute | solution.py:34
  45.5 19.6 %collective-permute-start.10 = (bf16[256,768]{1,0:T(8,128)(2,1)S(1)}, bf16[256,768]{1,0:T(8,128)(2,1)S(1)}, u32[]{:S(2)}, u32[]{:S(2)}) collective-permute-start(bf16[256,768]{1,0:T(8,128)(2,1)S(1)} %get-tuple-element.170.rest_0_), channel_id=1, source_target_pairs={{0,1},{1,0},{2,3},{3,2},{4,5},{5,4},{6,7},{7,6},{8,9},{9,8},{10,11... | collective-permute-start | bytes 1179656 | tf_op jit(solution)/shard_map/ppermute | solution.py:45
  47.0 18.7 %collective-permute-start.14 = (bf16[256,768]{1,0:T(8,128)(2,1)S(1)}, bf16[256,768]{1,0:T(8,128)(2,1)S(1)}, u32[]{:S(2)}, u32[]{:S(2)}) collective-permute-start(bf16[256,768]{1,0:T(8,128)(2,1)S(1)} %get-tuple-element.170.rest_0_), channel_id=1, source_target_pairs={{0,2},{2,0},{4,6},{6,4},{8,10},{10,8},{12,14},{14,12},{1,3},{3,1},... | collective-permute-start | bytes 1179656 | tf_op jit(solution)/shard_map/ppermute | solution.py:47
  63.6 18.8 %collective-permute-start.12 = (bf16[256,768]{1,0:T(8,128)(2,1)}, bf16[256,768]{1,0:T(8,128)(2,1)S(1)}, u32[]{:S(2)}, u32[]{:S(2)}) collective-permute-start(bf16[256,768]{1,0:T(8,128)(2,1)} %collective-permute-done.8.rest_2_), channel_id=1, source_target_pairs={{0,1},{1,0},{2,3},{3,2},{4,5},{5,4},{6,7},{7,6},{8,9},{9,8},{10,11... | collective-permute-start | bytes 1179656 | tf_op jit(solution)/shard_map/ppermute | solution.py:45
  65.1 24.8 %collective-permute-start.13 = (bf16[256,768]{1,0:T(8,128)(2,1)}, bf16[256,768]{1,0:T(8,128)(2,1)}, u32[]{:S(2)}, u32[]{:S(2)}) collective-permute-start(bf16[256,768]{1,0:T(8,128)(2,1)} %collective-permute-done.9.rest_3_), channel_id=1, source_target_pairs={{0,1},{1,0},{2,3},{3,2},{4,5},{5,4},{6,7},{7,6},{8,9},{9,8},{10,11... | collective-permute-start | bytes 1179656 | tf_op jit(solution)/shard_map/ppermute | solution.py:45
  65.6 24.3 %collective-permute-start.15 = (bf16[256,768]{1,0:T(8,128)(2,1)}, bf16[256,768]{1,0:T(8,128)(2,1)}, u32[]{:S(2)}, u32[]{:S(2)}) collective-permute-start(bf16[256,768]{1,0:T(8,128)(2,1)} %collective-permute-done.7.rest_1_), channel_id=1, source_target_pairs={{0,2},{2,0},{4,6},{6,4},{8,10},{10,8},{12,14},{14,12},{1,3},{3,1},... | collective-permute-start | bytes 1179656 | tf_op jit(solution)/shard_map/ppermute | solution.py:47
  65.8 24.6 %collective-permute-start.16 = (bf16[256,768]{1,0:T(8,128)(2,1)}, bf16[256,768]{1,0:T(8,128)(2,1)}, u32[]{:S(2)}, u32[]{:S(2)}) collective-permute-start(bf16[256,768]{1,0:T(8,128)(2,1)} %collective-permute-done.8.rest_2_), channel_id=1, source_target_pairs={{0,2},{2,0},{4,6},{6,4},{8,10},{10,8},{12,14},{14,12},{1,3},{3,1},... | collective-permute-start | bytes 1179656 | tf_op jit(solution)/shard_map/ppermute | solution.py:47
  74.0 19.9 %collective-permute-start.17 = (bf16[256,768]{1,0:T(8,128)(2,1)}, bf16[256,768]{1,0:T(8,128)(2,1)S(1)}, u32[]{:S(2)}, u32[]{:S(2)}) collective-permute-start(bf16[256,768]{1,0:T(8,128)(2,1)} %collective-permute-done.9.rest_3_), channel_id=1, source_target_pairs={{0,2},{2,0},{4,6},{6,4},{8,10},{10,8},{12,14},{14,12},{1,3},{3,1},... | collective-permute-start | bytes 1179656 | tf_op jit(solution)/shard_map/ppermute | solution.py:47
  108.3 502.4 %all-gather.7.cloned.1.call-start = ((), (), s32[]{:S(2)}) async-start(), calls=%async_computation.3 | async-start | bytes 3649536 | tf_op jit(solution)/shard_map/all_gather | solution.py:743
  142.9 93.9 %collective-permute-start.22 = (bf16[64,1024]{1,0:T(8,128)(2,1)}, bf16[64,1024]{1,0:T(8,128)(2,1)S(1)}, u32[]{:S(2)}, u32[]{:S(2)}) collective-permute-start(bf16[64,1024]{1,0:T(8,128)(2,1)} %get-tuple-element.94.rest_1_), channel_id=1, source_target_pairs={{0,1},{1,0},{2,3},{3,2},{4,5},{5,4},{6,7},{7,6},{8,9},{9,8},{10,11... | collective-permute-start | bytes 393224 | tf_op jit(solution)/shard_map/ppermute | solution.py:45
  174.0 64.0 %collective-permute-start.23 = (bf16[64,1024]{1,0:T(8,128)(2,1)}, bf16[64,1024]{1,0:T(8,128)(2,1)S(1)}, u32[]{:S(2)}, u32[]{:S(2)}) collective-permute-start(bf16[64,1024]{1,0:T(8,128)(2,1)} %get-tuple-element.95.rest_1_), channel_id=1, source_target_pairs={{0,1},{1,0},{2,3},{3,2},{4,5},{5,4},{6,7},{7,6},{8,9},{9,8},{10,11... | collective-permute-start | bytes 393224 | tf_op jit(solution)/shard_map/ppermute | solution.py:45
  205.6 484.3 %reduce-scatter.2.cloned.1.call-start = ((), (), s32[]{:S(2)}) async-start(), calls=%async_computation.1 | async-start | bytes 11354112 | tf_op jit(solution)/shard_map/reduce_scatter | solution.py:817
  236.8 28.1 %collective-permute-start.31 = (bf16[256,768]{1,0:T(8,128)(2,1)S(1)}, bf16[256,768]{1,0:T(8,128)(2,1)S(1)}, u32[]{:S(2)}, u32[]{:S(2)}) collective-permute-start(bf16[256,768]{1,0:T(8,128)(2,1)S(1)} %get-tuple-element.166), channel_id=1, source_target_pairs={{0,4},{2,6},{4,8},{6,10},{8,12},{10,14},{12,0},{14,2},{1,5},{3,7},... | collective-permute-start | bytes 1179656 | tf_op jit(solution)/shard_map/ppermute | solution.py:34
  238.0 32.1 %collective-permute-start.32 = (bf16[256,768]{1,0:T(8,128)(2,1)S(1)}, bf16[256,768]{1,0:T(8,128)(2,1)S(1)}, u32[]{:S(2)}, u32[]{:S(2)}) collective-permute-start(bf16[256,768]{1,0:T(8,128)(2,1)S(1)} %get-tuple-element.165), channel_id=1, source_target_pairs={{0,8},{2,10},{4,12},{6,14},{8,0},{10,2},{12,4},{14,6},{1,9},{3,11}... | collective-permute-start | bytes 1179656 | tf_op jit(solution)/shard_map/ppermute | solution.py:34
  240.8 29.4 %collective-permute-start.33 = (bf16[256,768]{1,0:T(8,128)(2,1)S(1)}, bf16[256,768]{1,0:T(8,128)(2,1)S(1)}, u32[]{:S(2)}, u32[]{:S(2)}) collective-permute-start(bf16[256,768]{1,0:T(8,128)(2,1)S(1)} %get-tuple-element.164), channel_id=1, source_target_pairs={{0,12},{2,14},{4,0},{6,2},{8,4},{10,6},{12,8},{14,10},{1,13},{3,15... | collective-permute-start | bytes 1179656 | tf_op jit(solution)/shard_map/ppermute | solution.py:34
  337.6 56.8 %collective-permute-start.37 = (bf16[64,1024]{1,0:T(8,128)(2,1)S(1)}, bf16[64,1024]{1,0:T(8,128)(2,1)S(1)}, u32[]{:S(2)}, u32[]{:S(2)}) collective-permute-start(bf16[64,1024]{1,0:T(8,128)(2,1)S(1)} %copy-done.56), channel_id=1, source_target_pairs={{0,1},{1,0},{2,3},{3,2},{4,5},{5,4},{6,7},{7,6},{8,9},{9,8},{10,11... | collective-permute-start | bytes 393224 | tf_op jit(solution)/shard_map/ppermute | solution.py:45
  338.6 56.4 %collective-permute-start.38 = (bf16[64,1024]{1,0:T(8,128)(2,1)S(1)}, bf16[64,1024]{1,0:T(8,128)(2,1)S(1)}, u32[]{:S(2)}, u32[]{:S(2)}) collective-permute-start(bf16[64,1024]{1,0:T(8,128)(2,1)S(1)} %copy-done.54), channel_id=1, source_target_pairs={{0,2},{2,0},{4,6},{6,4},{8,10},{10,8},{12,14},{14,12},{1,3},{3,1},... | collective-permute-start | bytes 393224 | tf_op jit(solution)/shard_map/ppermute | solution.py:47
  344.7 50.3 %collective-permute-start.39 = (bf16[64,1024]{1,0:T(8,128)(2,1)S(1)}, bf16[64,1024]{1,0:T(8,128)(2,1)S(1)}, u32[]{:S(2)}, u32[]{:S(2)}) collective-permute-start(bf16[64,1024]{1,0:T(8,128)(2,1)S(1)} %copy-done.52), channel_id=1, source_target_pairs={{0,3},{1,2},{2,1},{3,0},{4,7},{5,6},{6,5},{7,4},{8,11},{9,10},{10,... | collective-permute-start | bytes 393224 | tf_op jit(solution)/shard_map/ppermute | solution.py:49
  345.8 105.1 %collective-permute-start.49 = (bf16[64,1024]{1,0:T(8,128)(2,1)S(1)}, bf16[64,1024]{1,0:T(8,128)(2,1)S(1)}, u32[]{:S(2)}, u32[]{:S(2)}) collective-permute-start(bf16[64,1024]{1,0:T(8,128)(2,1)S(1)} %copy-done.50), channel_id=1, source_target_pairs={{0,1},{1,0},{2,3},{3,2},{4,5},{5,4},{6,7},{7,6},{8,9},{9,8},{10,11... | collective-permute-start | bytes 393224 | tf_op jit(solution)/shard_map/ppermute | solution.py:45
  346.9 104.0 %collective-permute-start.50 = (bf16[64,1024]{1,0:T(8,128)(2,1)S(1)}, bf16[64,1024]{1,0:T(8,128)(2,1)S(1)}, u32[]{:S(2)}, u32[]{:S(2)}) collective-permute-start(bf16[64,1024]{1,0:T(8,128)(2,1)S(1)} %copy-done.48), channel_id=1, source_target_pairs={{0,2},{2,0},{4,6},{6,4},{8,10},{10,8},{12,14},{14,12},{1,3},{3,1},... | collective-permute-start | bytes 393224 | tf_op jit(solution)/shard_map/ppermute | solution.py:47
  394.4 56.6 %collective-permute-start.51 = (bf16[64,1024]{1,0:T(8,128)(2,1)S(1)}, bf16[64,1024]{1,0:T(8,128)(2,1)S(1)}, u32[]{:S(2)}, u32[]{:S(2)}) collective-permute-start(bf16[64,1024]{1,0:T(8,128)(2,1)S(1)} %copy-done.47), channel_id=1, source_target_pairs={{0,3},{1,2},{2,1},{3,0},{4,7},{5,6},{6,5},{7,4},{8,11},{9,10},{10,... | collective-permute-start | bytes 393224 | tf_op jit(solution)/shard_map/ppermute | solution.py:49
  505.6 20.3 %collective-permute-start.65 = (bf16[4,112,192]{2,1,0:T(8,128)(2,1)S(1)}, bf16[4,112,192]{2,1,0:T(8,128)(2,1)S(1)}, u32[]{:S(2)}, u32[]{:S(2)}) collective-permute-start(bf16[4,112,192]{2,1,0:T(8,128)(2,1)S(1)} %dynamic-slice_bitcast_fusion.9), channel_id=1, source_target_pairs={{0,16},{16,0},{1,17},{17,1},{2,18},{18,2},{3,19},{19,3},{4,20},{20... | collective-permute-start | bytes 516104 | tf_op jit(solution)/shard_map/ppermute | solution.py:39
  507.0 69.1 %collective-permute-start.34 = (bf16[256,768]{1,0:T(8,128)(2,1)}, bf16[256,768]{1,0:T(8,128)(2,1)S(1)}, u32[]{:S(2)}, u32[]{:S(2)}) collective-permute-start(bf16[256,768]{1,0:T(8,128)(2,1)} %get-tuple-element.105), channel_id=1, source_target_pairs={{0,12},{2,14},{4,0},{6,2},{8,4},{10,6},{12,8},{14,10},{1,13},{3,15... | collective-permute-start | bytes 1179656 | tf_op jit(solution)/shard_map/ppermute | solution.py:34
  523.6 53.8 %collective-permute-start.35 = (bf16[256,768]{1,0:T(8,128)(2,1)}, bf16[256,768]{1,0:T(8,128)(2,1)S(1)}, u32[]{:S(2)}, u32[]{:S(2)}) collective-permute-start(bf16[256,768]{1,0:T(8,128)(2,1)} %get-tuple-element.106), channel_id=1, source_target_pairs={{0,8},{2,10},{4,12},{6,14},{8,0},{10,2},{12,4},{14,6},{1,9},{3,11}... | collective-permute-start | bytes 1179656 | tf_op jit(solution)/shard_map/ppermute | solution.py:34
  526.9 16.7 %collective-permute-start.66 = (bf16[112,192]{1,0:T(8,128)(2,1)S(1)}, bf16[112,192]{1,0:T(8,128)(2,1)S(1)}, u32[]{:S(2)}, u32[]{:S(2)}) collective-permute-start(bf16[112,192]{1,0:T(8,128)(2,1)S(1)} %get-tuple-element.186), channel_id=1, source_target_pairs={{0,4},{2,6},{4,8},{6,10},{8,12},{10,14},{12,0},{14,2},{1,5},{3,7},... | collective-permute-start | bytes 129032 | tf_op jit(solution)/shard_map/ppermute | solution.py:34
  531.7 24.4 %collective-permute-start.67 = (bf16[112,192]{1,0:T(8,128)(2,1)S(1)}, bf16[112,192]{1,0:T(8,128)(2,1)S(1)}, u32[]{:S(2)}, u32[]{:S(2)}) collective-permute-start(bf16[112,192]{1,0:T(8,128)(2,1)S(1)} %get-tuple-element.188), channel_id=1, source_target_pairs={{0,8},{2,10},{4,12},{6,14},{8,0},{10,2},{12,4},{14,6},{1,9},{3,11}... | collective-permute-start | bytes 129032 | tf_op jit(solution)/shard_map/ppermute | solution.py:34
  532.1 24.0 %collective-permute-start.68 = (bf16[112,192]{1,0:T(8,128)(2,1)S(1)}, bf16[112,192]{1,0:T(8,128)(2,1)S(1)}, u32[]{:S(2)}, u32[]{:S(2)}) collective-permute-start(bf16[112,192]{1,0:T(8,128)(2,1)S(1)} %get-tuple-element.187), channel_id=1, source_target_pairs={{0,12},{2,14},{4,0},{6,2},{8,4},{10,6},{12,8},{14,10},{1,13},{3,15... | collective-permute-start | bytes 129032 | tf_op jit(solution)/shard_map/ppermute | solution.py:34
  543.5 12.7 %collective-permute-start.58 = (bf16[4,112,384]{2,1,0:T(8,128)(2,1)S(1)}, bf16[4,112,384]{2,1,0:T(8,128)(2,1)S(1)}, u32[]{:S(2)}, u32[]{:S(2)}) collective-permute-start(bf16[4,112,384]{2,1,0:T(8,128)(2,1)S(1)} %dynamic-slice_bitcast_fusion.8), channel_id=1, source_target_pairs={{0,16},{16,0},{1,17},{17,1},{2,18},{18,2},{3,19},{19,3},{4,20},{20... | collective-permute-start | bytes 1032200 | tf_op jit(solution)/shard_map/ppermute | solution.py:39
  556.4 12.2 %collective-permute-start.59 = (bf16[112,384]{1,0:T(8,128)(2,1)S(1)}, bf16[112,384]{1,0:T(8,128)(2,1)S(1)}, u32[]{:S(2)}, u32[]{:S(2)}) collective-permute-start(bf16[112,384]{1,0:T(8,128)(2,1)S(1)} %get-tuple-element.183), channel_id=1, source_target_pairs={{0,4},{2,6},{4,8},{6,10},{8,12},{10,14},{12,0},{14,2},{1,5},{3,7},... | collective-permute-start | bytes 258056 | tf_op jit(solution)/shard_map/ppermute | solution.py:34
  574.9 33.4 %collective-permute-start.46 = (bf16[192,1024]{1,0:T(8,128)(2,1)S(1)}, bf16[192,1024]{1,0:T(8,128)(2,1)}, u32[]{:S(2)}, u32[]{:S(2)}) collective-permute-start(bf16[192,1024]{1,0:T(8,128)(2,1)S(1)} %copy-done.10), channel_id=1, source_target_pairs={{0,1},{1,0},{2,3},{3,2},{4,5},{5,4},{6,7},{7,6},{8,9},{9,8},{10,11... | collective-permute-start | bytes 1179656 | tf_op jit(solution)/shard_map/ppermute | solution.py:45
  576.2 32.2 %collective-permute-start.40 = (bf16[192,1024]{1,0:T(8,128)(2,1)}, bf16[192,1024]{1,0:T(8,128)(2,1)}, u32[]{:S(2)}, u32[]{:S(2)}) collective-permute-start(bf16[192,1024]{1,0:T(8,128)(2,1)} %get-tuple-element.116.rest_1_), channel_id=1, source_target_pairs={{0,1},{1,0},{2,3},{3,2},{4,5},{5,4},{6,7},{7,6},{8,9},{9,8},{10,11... | collective-permute-start | bytes 1179656 | tf_op jit(solution)/shard_map/ppermute | solution.py:45
  577.4 31.7 %collective-permute-start.41 = (bf16[192,1024]{1,0:T(8,128)(2,1)}, bf16[192,1024]{1,0:T(8,128)(2,1)}, u32[]{:S(2)}, u32[]{:S(2)}) collective-permute-start(bf16[192,1024]{1,0:T(8,128)(2,1)} %get-tuple-element.117.rest_2_), channel_id=1, source_target_pairs={{0,2},{2,0},{4,6},{6,4},{8,10},{10,8},{12,14},{14,12},{1,3},{3,1},... | collective-permute-start | bytes 1179656 | tf_op jit(solution)/shard_map/ppermute | solution.py:47
  580.4 29.1 %collective-permute-start.42 = (bf16[192,1024]{1,0:T(8,128)(2,1)}, bf16[192,1024]{1,0:T(8,128)(2,1)}, u32[]{:S(2)}, u32[]{:S(2)}) collective-permute-start(bf16[192,1024]{1,0:T(8,128)(2,1)} %get-tuple-element.118.rest_3_), channel_id=1, source_target_pairs={{0,3},{1,2},{2,1},{3,0},{4,7},{5,6},{6,5},{7,4},{8,11},{9,10},{10,... | collective-permute-start | bytes 1179656 | tf_op jit(solution)/shard_map/ppermute | solution.py:49
  580.4 21.9 %collective-permute-start.63 = (f32[32,384]{1,0:T(8,128)S(1)}, f32[32,384]{1,0:T(8,128)S(1)}, u32[]{:S(2)}, u32[]{:S(2)}) collective-permute-start(f32[32,384]{1,0:T(8,128)S(1)} %get-tuple-element.194), channel_id=1, source_target_pairs={{0,3},{1,2},{2,1},{3,0},{4,7},{5,6},{6,5},{7,4},{8,11},{9,10},{10,... | collective-permute-start | bytes 147464 | tf_op jit(solution)/shard_map/ppermute | solution.py:49
  606.8 34.8 %collective-permute-start.52 = (bf16[192,1024]{1,0:T(8,128)(2,1)S(1)}, bf16[192,1024]{1,0:T(8,128)(2,1)}, u32[]{:S(2)}, u32[]{:S(2)}) collective-permute-start(bf16[192,1024]{1,0:T(8,128)(2,1)S(1)} %copy-done.9), channel_id=1, source_target_pairs={{0,1},{1,0},{2,3},{3,2},{4,5},{5,4},{6,7},{7,6},{8,9},{9,8},{10,11... | collective-permute-start | bytes 1179656 | tf_op jit(solution)/shard_map/ppermute | solution.py:45
  608.3 33.4 %collective-permute-start.53 = (bf16[192,1024]{1,0:T(8,128)(2,1)S(1)}, bf16[192,1024]{1,0:T(8,128)(2,1)}, u32[]{:S(2)}, u32[]{:S(2)}) collective-permute-start(bf16[192,1024]{1,0:T(8,128)(2,1)S(1)} %copy-done.8), channel_id=1, source_target_pairs={{0,2},{2,0},{4,6},{6,4},{8,10},{10,8},{12,14},{14,12},{1,3},{3,1},... | collective-permute-start | bytes 1179656 | tf_op jit(solution)/shard_map/ppermute | solution.py:47
  608.4 33.3 %collective-permute-start.54 = (bf16[192,1024]{1,0:T(8,128)(2,1)S(1)}, bf16[192,1024]{1,0:T(8,128)(2,1)}, u32[]{:S(2)}, u32[]{:S(2)}) collective-permute-start(bf16[192,1024]{1,0:T(8,128)(2,1)S(1)} %copy-done.7), channel_id=1, source_target_pairs={{0,3},{1,2},{2,1},{3,0},{4,7},{5,6},{6,5},{7,4},{8,11},{9,10},{10,... | collective-permute-start | bytes 1179656 | tf_op jit(solution)/shard_map/ppermute | solution.py:49
  609.4 25.7 %collective-permute-start.48 = (bf16[192,1024]{1,0:T(8,128)(2,1)S(1)}, bf16[192,1024]{1,0:T(8,128)(2,1)}, u32[]{:S(2)}, u32[]{:S(2)}) collective-permute-start(bf16[192,1024]{1,0:T(8,128)(2,1)S(1)} %copy-done.5), channel_id=1, source_target_pairs={{0,3},{1,2},{2,1},{3,0},{4,7},{5,6},{6,5},{7,4},{8,11},{9,10},{10,... | collective-permute-start | bytes 1179656 | tf_op jit(solution)/shard_map/ppermute | solution.py:49
  647.5 14.9 %collective-permute-start.55 = (bf16[256,768]{1,0:T(8,128)(2,1)}, bf16[256,768]{1,0:T(8,128)(2,1)S(1)}, u32[]{:S(2)}, u32[]{:S(2)}) collective-permute-start(bf16[256,768]{1,0:T(8,128)(2,1)} %get-tuple-element.142), channel_id=1, source_target_pairs={{0,12},{2,14},{4,0},{6,2},{8,4},{10,6},{12,8},{14,10},{1,13},{3,15... | collective-permute-start | bytes 1179656 | tf_op jit(solution)/shard_map/ppermute | solution.py:34
  652.5 34.0 %collective-permute-start.56 = (bf16[256,768]{1,0:T(8,128)(2,1)}, bf16[256,768]{1,0:T(8,128)(2,1)S(1)}, u32[]{:S(2)}, u32[]{:S(2)}) collective-permute-start(bf16[256,768]{1,0:T(8,128)(2,1)} %get-tuple-element.143), channel_id=1, source_target_pairs={{0,8},{2,10},{4,12},{6,14},{8,0},{10,2},{12,4},{14,6},{1,9},{3,11}... | collective-permute-start | bytes 1179656 | tf_op jit(solution)/shard_map/ppermute | solution.py:34
  652.5 34.0 %collective-permute-start.57 = (bf16[256,768]{1,0:T(8,128)(2,1)}, bf16[256,768]{1,0:T(8,128)(2,1)S(1)}, u32[]{:S(2)}, u32[]{:S(2)}) collective-permute-start(bf16[256,768]{1,0:T(8,128)(2,1)} %get-tuple-element.144), channel_id=1, source_target_pairs={{0,4},{2,6},{4,8},{6,10},{8,12},{10,14},{12,0},{14,2},{1,5},{3,7},... | collective-permute-start | bytes 1179656 | tf_op jit(solution)/shard_map/ppermute | solution.py:34
  (102 other events, 927.4 us)
Sparse Core Ops, SparseCore 0:
  108.4 97.1 all-gather.4
  208.5 75.2 all-gather.6
  344.0 157.8 reduce-scatter.1

commit v4 on v3

--- a/solution.py
+++ b/solution.py
@@ -64,8 +64,9 @@
     return lax.dynamic_slice_in_dim(stack, len(pieces) - 1 - place, len(pieces), 0)
 
 
-def forward_kernel(block_k, q_ref, k_ref, v_ref, mask_ref, *rest):
-    out_refs, (sums_ref, keys, values) = rest[:MEMBERS], rest[MEMBERS:]
+def forward_kernel(block_k, members, q_ref, k_ref, v_ref, mask_ref, *rest):
+    count = len(members)
+    out_refs, sum_refs, (keys, values) = rest[:count], rest[count : 2 * count], rest[2 * count :]
     key_count = k_ref.shape[1]
     block_q = q_ref.shape[1] // MEMBERS
     rows = lax.broadcasted_iota(jnp.int32, (EXTRA, key_count), 0)
@@ -77,7 +78,7 @@
     ones_row = jnp.where(rows_q == 0, 1.0, 0.0).astype(BF16)
     scale = 1.0 / math.sqrt(HEAD_DIM)
 
-    for member in range(MEMBERS):
+    for index, member in enumerate(members):
         q_places = pl.ds(member * block_q, block_q)
         scaled = (q_ref[:, q_places].astype(F32) * scale).astype(BF16)
         query = jnp.concatenate([scaled, ones_row], axis=0)
@@ -103,8 +104,8 @@
             ),
         )
         total = acc[HEAD_DIM : HEAD_DIM + 1, :]
-        out_refs[member][...] = (acc[:HEAD_DIM, :] / total).astype(BF16)
-        sums_ref[:, q_places] = top + jnp.log(total)
+        out_refs[index][...] = (acc[:HEAD_DIM, :] / total).astype(BF16)
+        sum_refs[index][...] = top + jnp.log(total)
 
 
 def head_specs(arrays, places):
@@ -118,29 +119,29 @@
     return pl.BlockSpec(shape, lambda *unused: (0,) * len(shape))
 
 
-def attention_forward(queries, keys, values, places, mask_rows):
-    query_count = queries.shape[1]
+def attention_forward(queries, keys, values, places, mask_rows, members):
+    part_count = queries.shape[1] // MEMBERS
     key_count = keys.shape[1]
-    part = (HEAD_DIM, query_count // MEMBERS)
+    count = len(members)
     result = pl.pallas_call(
-        functools.partial(forward_kernel, min(1024, key_count)),
+        functools.partial(forward_kernel, min(1024, key_count), members),
         grid=(1,),
         in_specs=head_specs((queries, keys, values), places) + [whole((EXTRA, key_count))],
-        out_specs=[whole(part)] * MEMBERS + [whole((1, query_count))],
-        out_shape=[jax.ShapeDtypeStruct(part, BF16)] * MEMBERS
-        + [jax.ShapeDtypeStruct((1, query_count), F32)],
+        out_specs=[whole((HEAD_DIM, part_count))] * count + [whole((1, part_count))] * count,
+        out_shape=[jax.ShapeDtypeStruct((HEAD_DIM, part_count), BF16)] * count
+        + [jax.ShapeDtypeStruct((1, part_count), F32)] * count,
         scratch_shapes=[
             pltpu.VMEM((key_count, HEAD_DIM + EXTRA), BF16),
             pltpu.VMEM((HEAD_DIM + EXTRA, key_count), BF16),
         ],
         compiler_params=pltpu.CompilerParams(vmem_limit_bytes=VMEM_LIMIT),
         cost_estimate=pl.CostEstimate(
-            flops=16 * HEAD_DIM * query_count * key_count,
-            transcendentals=query_count * key_count,
+            flops=16 * HEAD_DIM * count * part_count * key_count,
+            transcendentals=count * part_count * key_count,
             bytes_accessed=8 * HEAD_DIM * key_count,
         ),
     )(queries, keys, values, mask_rows)
-    return result[:MEMBERS], result[MEMBERS]
+    return dict(zip(members, result[:count])), dict(zip(members, result[count:]))
 
 
 def split_three(row):
@@ -151,10 +152,17 @@
     return high.astype(F32), middle.astype(F32), low.astype(F32)
 
 
-def backward_kernel(block_q, block_k, pieces, q_ref, k_ref, v_ref, mask_ref, sums_ref, *rest):
+def backward_kernel(block_q, chosen, first, last, q_ref, k_ref, v_ref, mask_ref, *rest):
+    sum_refs, rest = rest[:MEMBERS], rest[MEMBERS:]
     out_refs, rest = rest[:MEMBERS], rest[MEMBERS:]
     grad_refs, rest = rest[:MEMBERS], rest[MEMBERS:]
-    result_refs, rest = rest[:pieces], rest[pieces:]
+    if not first:
+        start_ref, rest = rest[0], rest[1:]
+    result_refs, rest = rest[: len(chosen)], rest[len(chosen) :]
+    if not last:
+        partial_ref, rest = rest[0], rest[1:]
+    elif not first:
+        dq_refs, rest = rest[:MEMBERS], rest[MEMBERS:]
     query_rows, keys, grad_rows, values, scaled_q, grads, dq_acc, dkv = rest
     key_count = k_ref.shape[1]
     query_count = q_ref.shape[1]
@@ -179,7 +187,8 @@
         product = grad.astype(F32) * out_refs[member][...].astype(F32)
         deltas.append(jnp.sum(product, axis=0, keepdims=True))
     deltas = jnp.concatenate(deltas, axis=1)
-    joined_q = jnp.concatenate([query, extra_rows(-sums_ref[...], 1.0)], axis=0)
+    sums = jnp.concatenate([sum_ref[...] for sum_ref in sum_refs], axis=1)
+    joined_q = jnp.concatenate([query, extra_rows(-sums, 1.0)], axis=0)
     query_rows[...] = joined_q.astype(F32).T.astype(BF16)
     joined_g = jnp.concatenate([grads[...], extra_rows(-deltas, 0.0)], axis=0)
     grad_rows[...] = joined_g.astype(F32).T.astype(BF16)
@@ -189,13 +198,13 @@
     keys[HEAD_DIM:, :] = jnp.where(places_k == 3, mask_row, ones_rows).astype(BF16)
     values[:HEAD_DIM, :] = v_ref[...]
     values[HEAD_DIM:, :] = ones_rows.astype(BF16)
-    dq_acc[...] = jnp.zeros_like(dq_acc)
+    dq_acc[...] = jnp.zeros_like(dq_acc) if first else start_ref[...]
 
     def key_block(j, unused):
-        k_start = pl.multiple_of(j * block_k, block_k)
-        key_part = keys[:, pl.ds(k_start, block_k)]
-        value_part = values[:, pl.ds(k_start, block_k)]
-        plain_keys = k_ref[:, pl.ds(k_start, block_k)]
+        k_start = pl.multiple_of((chosen.start + j * chosen.step) * part, part)
+        key_part = keys[:, pl.ds(k_start, part)]
+        value_part = values[:, pl.ds(k_start, part)]
+        plain_keys = k_ref[:, pl.ds(k_start, part)]
 
         def query_block(i, carry):
             dk, dv = carry
@@ -208,38 +217,62 @@
             dq_acc[:, pl.ds(q_start, block_q)] += dot(plain_keys, grad_scores, 1, 1)
             return dk, dv
 
-        zeros = jnp.zeros((HEAD_DIM, block_k), F32)
+        zeros = jnp.zeros((HEAD_DIM, part), F32)
         dk, dv = lax.fori_loop(0, query_count // block_q, query_block, (zeros, zeros))
-        dkv[:HEAD_DIM, pl.ds(k_start, block_k)] = dk.astype(BF16)
-        dkv[HEAD_DIM:, pl.ds(k_start, block_k)] = dv.astype(BF16)
+        place = pl.multiple_of(j * part, part)
+        dkv[:HEAD_DIM, pl.ds(place, part)] = dk.astype(BF16)
+        dkv[HEAD_DIM:, pl.ds(place, part)] = dv.astype(BF16)
         return 0
 
-    lax.fori_loop(0, key_count // block_k, key_block, 0)
+    lax.fori_loop(0, len(chosen), key_block, 0)
+
+    def query_grads(member):
+        return (dq_acc[:, member * part : (member + 1) * part] * scale).astype(BF16)
+
+    together = first and last
     for index, result_ref in enumerate(result_refs):
-        lanes = slice(index * part, (index + 1) * part)
-        if index < MEMBERS:
-            result_ref[:HEAD_DIM, :] = (dq_acc[:, lanes] * scale).astype(BF16)
+        found = dkv[:, index * part : (index + 1) * part]
+        if together:
+            if chosen[index] < MEMBERS:
+                result_ref[:HEAD_DIM, :] = query_grads(chosen[index])
+            else:
+                result_ref[:HEAD_DIM, :] = jnp.zeros((HEAD_DIM, part), BF16)
+            result_ref[HEAD_DIM:, :] = found
         else:
-            result_ref[:HEAD_DIM, :] = jnp.zeros((HEAD_DIM, part), BF16)
-        result_ref[HEAD_DIM:, :] = dkv[:, lanes]
-
-
-def attention_backward(queries, keys, values, places, mask_rows, sums, outs, grads):
+            result_ref[...] = found
+    if not last:
+        partial_ref[...] = dq_acc[...]
+    elif not first:
+        for member in range(MEMBERS):
+            dq_refs[member][...] = query_grads(member)
+
+
+def attention_backward(
+    queries, keys, values, places, mask_rows, sums, outs, grads, chosen, start=None, last=True
+):
     query_count = queries.shape[1]
     key_count = keys.shape[1]
     part = query_count // MEMBERS
-    pieces = key_count // part
     wide = HEAD_DIM + EXTRA
-    return pl.pallas_call(
-        functools.partial(
-            backward_kernel, min(1024, query_count), min(1024, key_count), pieces
-        ),
+    first = start is None
+    height = (3 if first and last else 2) * HEAD_DIM
+    count = len(chosen)
+    results = [((height, part), BF16)] * count
+    if not last:
+        results.append(((HEAD_DIM, query_count), F32))
+    elif not first:
+        results += [((HEAD_DIM, part), BF16)] * MEMBERS
+    extra = [] if first else [start]
+    found = pl.pallas_call(
+        functools.partial(backward_kernel, min(1024, query_count), chosen, first, last),
         grid=(1,),
         in_specs=head_specs((queries, keys, values), places)
-        + [whole((EXTRA, key_count)), whole((1, query_count))]
-        + [whole((HEAD_DIM, part))] * (2 * MEMBERS),
-        out_specs=[whole((3 * HEAD_DIM, part))] * pieces,
-        out_shape=[jax.ShapeDtypeStruct((3 * HEAD_DIM, part), BF16)] * pieces,
+        + [whole((EXTRA, key_count))]
+        + [whole((1, part))] * MEMBERS
+        + [whole((HEAD_DIM, part))] * (2 * MEMBERS)
+        + [whole(array.shape) for array in extra],
+        out_specs=[whole(dims) for dims, dtype in results],
+        out_shape=[jax.ShapeDtypeStruct(dims, dtype) for dims, dtype in results],
         scratch_shapes=[
             pltpu.VMEM((query_count, wide), BF16),
             pltpu.VMEM((wide, key_count), BF16),
@@ -248,121 +281,156 @@
             pltpu.VMEM((HEAD_DIM, query_count), BF16),
             pltpu.VMEM((HEAD_DIM, query_count), BF16),
             pltpu.VMEM((HEAD_DIM, query_count), F32),
-            pltpu.VMEM((2 * HEAD_DIM, key_count), BF16),
+            pltpu.VMEM((2 * HEAD_DIM, count * part), BF16),
         ],
         compiler_params=pltpu.CompilerParams(vmem_limit_bytes=VMEM_LIMIT),
         cost_estimate=pl.CostEstimate(
-            flops=40 * HEAD_DIM * query_count * key_count,
-            transcendentals=query_count * key_count,
+            flops=40 * HEAD_DIM * query_count * count * part,
+            transcendentals=query_count * count * part,
             bytes_accessed=16 * HEAD_DIM * key_count,
         ),
-    )(queries, keys, values, mask_rows, sums, *outs, *grads)
-
-
-def project_kernel(count, weight_ref, bias_ref, *rest):
-    piece_refs, (all_ref, out_ref) = rest[:count], rest[count:]
-    rows = piece_refs[0].shape[0]
-    for index, piece_ref in enumerate(piece_refs):
-        all_ref[index * rows : (index + 1) * rows, :] = piece_ref[...]
+    )(queries, keys, values, mask_rows, *sums, *outs, *grads, *extra)
+    return list(found[:count]), list(found[count:])
+
+
+def joined_rows(refs, member):
+    count = len(refs) // MEMBERS
+    return jnp.concatenate([ref[...] for ref in refs[member * count : (member + 1) * count]])
+
+
+def project_kernel(weight_ref, bias_ref, *rest):
+    piece_refs, out_ref = rest[:-1], rest[-1]
     weight = weight_ref[...].astype(F32).T.astype(BF16)
-    step = all_ref.shape[0] // MEMBERS
+    step = out_ref.shape[1] // MEMBERS
     for member in range(MEMBERS):
         lanes = slice(member * step, (member + 1) * step)
-        out_ref[:, lanes] = (dot(weight, all_ref[lanes, :], 1, 1) + bias_ref[...]).astype(BF16)
+        rows = joined_rows(piece_refs, member)
+        out_ref[:, lanes] = (dot(weight, rows, 1, 1) + bias_ref[...]).astype(BF16)
 
 
 def project(weight, bias_column, pieces):
     count, (rows, width) = len(pieces), pieces[0].shape
     columns = weight.shape[1]
     return pl.pallas_call(
-        functools.partial(project_kernel, count),
+        project_kernel,
         grid=(1,),
         in_specs=[whole(weight.shape), whole(bias_column.shape)] + [whole((rows, width))] * count,
-        out_specs=[whole((count * rows, width)), whole((columns, count * rows))],
-        out_shape=[
-            jax.ShapeDtypeStruct((count * rows, width), BF16),
-            jax.ShapeDtypeStruct((columns, count * rows), BF16),
-        ],
+        out_specs=whole((columns, count * rows)),
+        out_shape=jax.ShapeDtypeStruct((columns, count * rows), BF16),
         compiler_params=pltpu.CompilerParams(vmem_limit_bytes=VMEM_LIMIT),
         cost_estimate=pl.CostEstimate(
             flops=2 * count * rows * width * columns,
             transcendentals=0,
-            bytes_accessed=6 * count * rows * width,
+            bytes_accessed=4 * count * rows * width,
         ),
     )(weight, bias_column, *pieces)
 
 
-def weight_grad_kernel(slots, chunks, chunk_rows, rows_ref, *rest):
-    grad_refs, out_ref = rest[:-1], rest[-1]
-    part = grad_refs[0].shape[1]
-    columns = grad_refs[0].shape[0]
+def stacked(refs):
+    parts = [ref[...] for ref in refs]
+    return parts[0] if len(parts) == 1 else jnp.concatenate(parts)
+
+
+def flatten(nested):
+    return [array for slot in nested for member in slot for array in member]
+
+
+def regroup(refs, counts):
+    refs = list(refs)
+    return [[[refs.pop(0) for _ in range(n)] for n in slot] for slot in counts]
+
+
+def counts_of(nested):
+    return [[len(member) for member in slot] for slot in nested]
+
+
+def weight_grad_kernel(counts, pieces, chunk_rows, *rest):
+    row_refs, grad_refs, out_ref = rest[:pieces], rest[pieces:-1], rest[-1]
+    slots = regroup(grad_refs, counts)
+    chunks = out_ref.shape[0]
+    columns = out_ref.shape[2] // len(slots)
+    part = slots[0][0][0].shape[1]
     ones = jnp.ones((8, part), BF16)
-    for slot in range(slots):
+    totals, biases = [0.0] * len(slots), [0.0] * len(slots)
+    for member in range(MEMBERS):
+        rows = joined_rows(row_refs, member)
+        for slot, members in enumerate(slots):
+            grad = stacked(members[member])
+            totals[slot] = totals[slot] + dot(grad, rows, 1, 0)
+            biases[slot] = biases[slot] + dot(ones, grad, 1, 1)
+    for slot in range(len(slots)):
         lanes = slice(slot * columns, (slot + 1) * columns)
-        total, bias = 0.0, 0.0
-        for member in range(MEMBERS):
-            grad = grad_refs[slot * MEMBERS + member][...]
-            total = total + dot(grad, rows_ref[member * part : (member + 1) * part, :], 1, 0)
-            bias = bias + dot(ones, grad, 1, 1)
-        turned = total.T.astype(BF16)
-        bias = jnp.broadcast_to(bias[0:1].astype(BF16), (out_ref.shape[1] - chunk_rows, columns))
+        turned = totals[slot].T.astype(BF16)
+        bias = biases[slot][0:1].astype(BF16)
+        bias = jnp.broadcast_to(bias, (out_ref.shape[1] - chunk_rows, columns))
         for chunk in range(chunks):
             out_ref[chunk, :chunk_rows, lanes] = turned[chunk * chunk_rows : (chunk + 1) * chunk_rows]
             out_ref[chunk, chunk_rows:, lanes] = bias
 
 
-def weight_grad(rows_all, slot_pieces, chunks, chunk_rows, block_rows):
-    slots = len(slot_pieces)
-    columns, part = slot_pieces[0][0].shape
-    shape = (chunks, block_rows, slots * columns)
+def weight_grad(row_pieces, slots, chunks, chunk_rows, block_rows):
+    arrays = flatten(slots)
+    shape = (chunks, block_rows, len(slots) * 3 * HEAD_DIM)
     return pl.pallas_call(
-        functools.partial(weight_grad_kernel, slots, chunks, chunk_rows),
+        functools.partial(weight_grad_kernel, counts_of(slots), len(row_pieces), chunk_rows),
         grid=(1,),
-        in_specs=[whole(rows_all.shape)] + [whole((columns, part))] * (slots * MEMBERS),
+        in_specs=[whole(array.shape) for array in list(row_pieces) + arrays],
         out_specs=whole(shape),
         out_shape=jax.ShapeDtypeStruct(shape, BF16),
         compiler_params=pltpu.CompilerParams(vmem_limit_bytes=VMEM_LIMIT),
         cost_estimate=pl.CostEstimate(
-            flops=2 * slots * columns * rows_all.size,
+            flops=2 * shape[2] * len(row_pieces) * row_pieces[0].size,
             transcendentals=0,
-            bytes_accessed=2 * rows_all.size,
+            bytes_accessed=2 * len(row_pieces) * row_pieces[0].size,
         ),
-    )(rows_all, *[piece for pieces in slot_pieces for piece in pieces])
-
-
-def input_grad_kernel(last, info_ref, acc_ref, weight_ref, *rest):
-    piece_refs, out_refs, joined = rest[:MEMBERS], rest[MEMBERS:-1], rest[-1]
-    columns = piece_refs[0].shape[0]
-    for member in range(MEMBERS):
-        start = pl.multiple_of(info_ref[member], HEAD_DIM)
-        joined[pl.ds(start, columns), :] = piece_refs[member][...]
+    )(*row_pieces, *arrays)
+
+
+def input_grad_kernel(counts, info_ref, acc_ref, *rest):
+    slots = len(counts)
+    weight_refs, rest = rest[:slots], rest[slots:]
+    grads = regroup(rest[: sum(map(sum, counts))], counts)
+    out_refs, joined = rest[sum(map(sum, counts)) : -1], rest[-1]
+    total = acc_ref[...]
+    width = total.shape[1]
+    for slot, members in enumerate(grads):
+        for member, refs in enumerate(members):
+            start = info_ref[member]
+            for ref in refs:
+                height = ref.shape[0]
+                joined[slot, pl.ds(pl.multiple_of(start, HEAD_DIM), height), :] = ref[...]
+                start = start + height
+        weight = weight_refs[slot][...].reshape(width, width)
+        total = total + dot(joined[slot], weight, 0, 1)
     rows = acc_ref.shape[0] // len(out_refs)
-    total = acc_ref[...] + dot(joined[...], weight_ref[...], 0, 1)
     for index, out_ref in enumerate(out_refs):
         out_ref[...] = total[index * rows : (index + 1) * rows].astype(out_ref.dtype)
 
 
-def input_grad_step(info, acc, weight, pieces, out_count, dtype):
-    columns, part = pieces[0].shape
+def input_grad_step(info, acc, weights, slots, out_count, dtype):
+    arrays = flatten(slots)
     rows, width = acc.shape
     out = (rows // out_count, width)
     return pl.pallas_call(
-        functools.partial(input_grad_kernel, out_count),
+        functools.partial(input_grad_kernel, counts_of(slots)),
         grid_spec=pltpu.PrefetchScalarGridSpec(
             num_scalar_prefetch=1,
             grid=(1,),
-            in_specs=[whole(acc.shape), whole(weight.shape)] + [whole((columns, part))] * MEMBERS,
+            in_specs=[whole(acc.shape)]
+            + [pl.BlockSpec(dims, functools.partial(lambda at, i, info: at, place))
+               for array, dims, place in weights]
+            + [whole(array.shape) for array in arrays],
             out_specs=[whole(out)] * out_count,
-            scratch_shapes=[pltpu.VMEM((MEMBERS * columns, part), BF16)],
+            scratch_shapes=[pltpu.VMEM((len(slots), width, rows), BF16)],
         ),
         out_shape=[jax.ShapeDtypeStruct(out, dtype)] * out_count,
         compiler_params=pltpu.CompilerParams(vmem_limit_bytes=VMEM_LIMIT),
         cost_estimate=pl.CostEstimate(
-            flops=2 * rows * width * MEMBERS * columns,
+            flops=2 * rows * width * width * len(slots),
             transcendentals=0,
             bytes_accessed=8 * rows * width,
         ),
-    )(info, acc, weight, *pieces)
+    )(info, acc, *[array for array, dims, place in weights], *arrays)
 
 
 def collect_kernel(count, place_ref, *rest):
@@ -407,16 +475,17 @@
     return jnp.sum(array, axis=0, keepdims=True)
 
 
-def layer_kernel(blocks, planes, parts, info_ref, rows_ref, vectors_ref, inner_bias_ref, *rest):
-    weight_out, weight_inner, weight_outer = rest[:3]
+def layer_kernel(blocks, planes, parts, info_ref, vectors_ref, inner_bias_ref, *rest):
+    row_refs, rest = rest[:planes], rest[planes:]
+    packed_out, packed_inner, packed_outer = rest[:3]
     att_refs, rest = rest[3 : 3 + parts], rest[3 + parts :]
     cot_refs, rest = rest[:planes], rest[planes:]
     final_refs, rest = rest[:planes], rest[planes:]
     grad_att_refs, rest = rest[:parts], rest[parts:]
     resid_ref, grad_outer_w, grad_inner_w, grad_out_w, grad_vectors, grad_inner_bias = rest[:6]
-    attended, hat1, scale1, low, acc, active, slope, grad_low, grad_hidden = rest[6:]
+    attended, hat1, scale1, low, acc, active, slope, grad_low, grad_hidden, weight_out = rest[6:]
     step = pl.program_id(0)
-    row_count, width = rows_ref.shape
+    row_count, width = acc.shape
     piece = row_count // planes
     group = width // MEMBERS
     block = jnp.where(step < blocks, step, step - blocks)
@@ -432,10 +501,11 @@
     def _():
         for index, att_ref in enumerate(att_refs):
             attended[index * HEAD_DIM : (index + 1) * HEAD_DIM, :] = att_ref[...]
+        weight_out[...] = packed_out[...].reshape(width, width)
         weight = jnp.concatenate([weight_out[group_rows(m), :] for m in range(MEMBERS)])
         for k in range(planes):
             branch = dot(attended[:, pieces[k]], weight, 0, 0) + vector(0)
-            value = rows_ref[pieces[k], :].astype(F32) + branch
+            value = row_refs[k][...].astype(F32) + branch
             centred = value - row_mean(value)
             scale = lax.rsqrt(row_mean(centred * centred) + EPSILON)
             hat = centred * scale
@@ -450,13 +520,15 @@
     @pl.when(step < blocks)
     def _():
         bias = inner_bias_ref[pl.ds(block, 1), :]
+        weight_inner = packed_inner[...].reshape(width, width)
+        weight_outer = packed_outer[...].reshape(width, width)
         for k in range(planes):
-            inner = dot(low[pieces[k], :], weight_inner[...], 1, 0) + bias
+            inner = dot(low[pieces[k], :], weight_inner, 1, 0) + bias
             value, derivative = gelu_parts(inner)
             value = value.astype(BF16)
             active[block, pieces[k], :] = value
             slope[block, pieces[k], :] = derivative
-            acc[pieces[k], :] += dot(value, weight_outer[...], 1, 0)
+            acc[pieces[k], :] += dot(value, weight_outer, 1, 0)
 
     @pl.when(step == blocks)
     def _():
@@ -486,12 +558,14 @@
     @pl.when(step >= blocks)
     def _():
         bias_sum = 0.0
+        weight_inner = packed_inner[...].reshape(width, width)
+        weight_outer = packed_outer[...].reshape(width, width)
         for k in range(planes):
-            moved = dot(grad_low[pieces[k], :], weight_outer[...], 1, 1)
+            moved = dot(grad_low[pieces[k], :], weight_outer, 1, 1)
             grad = (moved * slope[block, pieces[k], :]).astype(BF16)
             grad_hidden[pieces[k], :] = grad
             bias_sum += column_sum(grad.astype(F32))
-            acc[pieces[k], :] += dot(grad, weight_inner[...], 1, 1)
+            acc[pieces[k], :] += dot(grad, weight_inner, 1, 1)
         grad_inner_bias[pl.ds(block, 1), :] = bias_sum
         for m in range(MEMBERS // 2):
             lanes = slice(m * 2 * group, (m + 1) * 2 * group)
@@ -523,10 +597,10 @@
                 grad_att_refs[m * heads + j][...] = moved[j * HEAD_DIM : (j + 1) * HEAD_DIM, :]
 
 
-def layer_rows(info, rows_all, vectors, inner_bias, weights, att_parts, cot_pieces):
-    weight_out, weight_inner, weight_outer = weights
-    hidden, width = weight_outer.shape
-    blocks, planes, parts = hidden // width, len(cot_pieces), len(att_parts)
+def layer_rows(info, row_pieces, vectors, inner_bias, weights, att_parts, cot_pieces):
+    width = row_pieces[0].shape[1]
+    blocks, planes, parts = weights[0], len(cot_pieces), len(att_parts)
+    hidden = blocks * width
     row_count = att_parts[0].shape[1]
     piece = row_count // planes
     once = pl.Buffered(1)
@@ -535,7 +609,14 @@
         return pl.BlockSpec(shape, lambda *unused: (0,) * len(shape), pipeline_mode=once)
 
     square = (width, width)
-    weight_spec = pl.BlockSpec(square, lambda i, info: (lax.rem(i, blocks), 0))
+    weight_specs = [
+        pl.BlockSpec(
+            dims,
+            functools.partial(lambda at, i, info: at(lax.rem(i, blocks)), place),
+            pipeline_mode=pl.Buffered(1 if index == 0 else 2),
+        )
+        for index, (array, dims, place) in enumerate(weights[1:])
+    ]
     grad_spec = pl.BlockSpec(square, lambda i, info: (jnp.maximum(i - blocks, 0), 0))
     small = [fixed((8, width)), fixed((8, width))]
 
@@ -547,9 +628,9 @@
         grid_spec=pltpu.PrefetchScalarGridSpec(
             num_scalar_prefetch=1,
             grid=(2 * blocks,),
-            in_specs=[fixed((row_count, width))]
-            + small
-            + [fixed(square), weight_spec, weight_spec]
+            in_specs=small
+            + [fixed((piece, width))] * planes
+            + weight_specs
             + [fixed((HEAD_DIM, row_count))] * parts
             + [fixed((piece, width))] * planes,
             out_specs=[fixed((piece, width))] * planes
@@ -566,6 +647,7 @@
                 pltpu.VMEM((blocks, row_count, width), F32),
                 pltpu.VMEM((row_count, width), BF16),
                 pltpu.VMEM((row_count, width), BF16),
+                pltpu.VMEM(square, BF16),
             ],
         ),
         out_shape=[shape((piece, width), BF16)] * planes
@@ -586,12 +668,10 @@
         ),
     )(
         info,
-        rows_all,
         vectors,
         inner_bias,
-        weight_out,
-        weight_inner,
-        weight_outer,
+        *row_pieces,
+        *[array for array, dims, place in weights[1:]],
         *att_parts,
         *cot_pieces,
     )
@@ -660,12 +740,7 @@
             pieces.append(shift_planes(chunk, distance))
         return pieces
 
-    def from_planes(pieces):
-        back = [pieces[0]]
-        for distance in range(1, planes):
-            back.append(shift_planes(pieces[distance], -distance))
-        return collect(back, plane).reshape(seqs, part_rows, width)
-
+    own_pieces = to_planes(layer_input)
     own_group = core * 2 + head_place
     heads_here = HEADS // MEMBERS
     piece_rows = (share // 8 + 1) * 8
@@ -676,6 +751,7 @@
     tail_rows = jnp.pad(bias_row[None], ((0, piece_rows - share - 1), (0, 0)))
     tail_rows = jnp.broadcast_to(tail_rows, (MEMBERS,) + tail_rows.shape)
     by_group = jnp.concatenate([by_group, tail_rows], axis=1)
+    by_group, own_pieces[1] = lax.optimization_barrier((by_group, own_pieces[1]))
     by_member = reorder_members(by_group, core, head_place)
     gathered = [by_member[0]] + [
         swap_member(by_member[member], member) for member in range(1, MEMBERS)
@@ -700,7 +776,6 @@
         ]
     ).astype(F32)
 
-    own_pieces = to_planes(layer_input)
     head_pieces = [swap_member(part_in, 1) for part_in in own_pieces]
     core_pieces = [swap_member(part_in, 2) for part_in in own_pieces]
     both_pieces = [swap_member(part_in, 2) for part_in in head_pieces]
@@ -722,24 +797,23 @@
             route.append((i, target * CORES + i % CORES))
         return lax.ppermute(array, "blk", route)
 
-    rows_all, qkv = project(own_weight, own_bias[:, None], all_pieces)
-    late_cotangent, late_out, late_inner, late_outer, qkv = lax.optimization_barrier(
-        (cotangent, w_attn_out, w_inner, w_outer, qkv)
-    )
+    qkv = project(own_weight, own_bias[:, None], all_pieces)
+    late_cotangent, qkv = lax.optimization_barrier((cotangent, qkv))
     cot_pieces = to_planes(late_cotangent)
 
     small = jnp.concatenate(
         [b_attn_out, norm1_gain, norm1_bias, b_outer, norm2_gain, norm2_bias, b_inner]
     )
     small_row = jnp.pad(small, (0, width - small.shape[0]))[None]
-    inner_rows = jnp.swapaxes(late_inner.reshape(share, folds, width), 0, 1).reshape(-1, width)
-    second_pack = jnp.concatenate([late_outer, inner_rows, late_out, small_row])
+    inner_rows = jnp.swapaxes(w_inner.reshape(share, folds, width), 0, 1).reshape(-1, width)
+    second_pack = jnp.concatenate([w_outer, inner_rows, w_attn_out, small_row])
     second_pack = pad_rows(second_pack, -second_pack.shape[0] % 8)
+    second_pack, gate = lax.optimization_barrier((second_pack, head_pieces[-1]))
     second = lax.all_gather(second_pack, ALL_AXES, axis=0, tiled=False)
     slots = jnp.stack([w_query, w_key, w_value], axis=1)
     slots = slots.reshape(share, 3, MEMBERS, heads_here, HEAD_DIM)
     slots = jnp.transpose(slots, (3, 0, 2, 1, 4)).reshape(heads_here * share, width)
-    slots, second = lax.optimization_barrier((slots, second))
+    slots, gate = lax.optimization_barrier((slots, qkv[0, 0]))
     third = lax.all_gather(slots, ALL_AXES, axis=0, tiled=False)
 
     inner_start = wide_share
@@ -749,10 +823,30 @@
     vectors = pad_rows(vectors.reshape(6, width).astype(F32), 2)
     bias_inner = small_all[:, 6 * share : 6 * share + wide_share].astype(F32)
     bias_inner = pad_rows(bias_inner.reshape(folds, width), 8 - folds)
-    weight_out = second[:, out_start : out_start + share].reshape(width, width)
-    weight_inner = second[:, inner_start:out_start].reshape(devices, folds, share, width)
-    weight_inner = jnp.swapaxes(weight_inner, 0, 1).reshape(hidden, width)
-    weight_outer = second[:, :wide_share].reshape(hidden, width)
+    square = (width, width)
+    if share % 8 == 0:
+        narrow = (devices, share, width)
+        layer_weights = (
+            folds,
+            (second, narrow, lambda j: (0, out_start // share, 0)),
+            (second, narrow, lambda j: (0, inner_start // share + j, 0)),
+            (second, (devices // folds, wide_share, width), lambda j: (j, 0, 0)),
+        )
+        slot_weights = [(third, narrow, (0, slot, 0)) for slot in range(heads_here)]
+    else:
+        inner = second[:, inner_start:out_start].reshape(devices, folds, share, width)
+        inner = jnp.swapaxes(inner, 0, 1).reshape((folds,) + square)
+        outer = second[:, :wide_share].reshape((folds,) + square)
+        layer_weights = (
+            folds,
+            (second[:, out_start : out_start + share].reshape(square), square, lambda j: (0, 0)),
+            (inner, (1,) + square, lambda j: (j, 0, 0)),
+            (outer, (1,) + square, lambda j: (j, 0, 0)),
+        )
+        slot_weights = [
+            (third[:, slot * share : (slot + 1) * share].reshape(square), square, (0, 0))
+            for slot in range(heads_here)
+        ]
 
     queries = keys = values = qkv
     starts = (0, heads_here, 2 * heads_here)
@@ -773,24 +867,29 @@
             swap_member(pieces[member], member) for member in range(1, MEMBERS)
         ]
 
+    far, near = range(1, MEMBERS, 2), range(0, MEMBERS, 2)
     outs, sums, parts = [], [], []
     for slot in range(heads_here):
         slot_at = tuple(start + slot for start in starts)
-        out, total = attention_forward(queries, keys, values, slot_at, mask_rows)
-        outs.append(out)
-        sums.append(total)
-        parts.append(to_members(out))
+        chosen = [range(MEMBERS)] if slot < heads_here - 1 else [far, near]
+        out, total, moved = {}, {}, {}
+        for members in chosen:
+            found = attention_forward(queries, keys, values, slot_at, mask_rows, members)
+            out.update(found[0])
+            total.update(found[1])
+            for member in members:
+                piece_out = found[0][member]
+                moved[member] = swap_member(piece_out, member) if member else piece_out
+        outs.append([out[member] for member in range(MEMBERS)])
+        sums.append([total[member] for member in range(MEMBERS)])
+        parts.append(moved)
     att_parts = [parts[slot][member] for member in range(MEMBERS) for slot in range(heads_here)]
     final_pieces, grad_att, more = layer_rows(
-        info,
-        rows_all,
-        vectors,
-        bias_inner,
-        (weight_out, weight_inner, weight_outer),
-        att_parts,
-        cot_pieces,
+        info, own_pieces, vectors, bias_inner, layer_weights, att_parts, cot_pieces
     )
-    output = from_planes(final_pieces)
+    output_pieces = [final_pieces[0]] + [
+        shift_planes(final_pieces[distance], -distance) for distance in range(1, planes)
+    ]
     grad_input, grad_outer_w, grad_inner_w, grad_out_w, grad_vectors, grad_inner_bias = more
 
     vector_pack = jnp.swapaxes(grad_vectors[:6].reshape(6, devices, share), 0, 1)
@@ -824,10 +923,6 @@
     chunk_rows = width // (batches * planes)
     block_rows = chunk_rows + -chunk_rows % 16 + 16
 
-    def reduce_weights(slot_pieces):
-        chunks = weight_grad(rows_all, slot_pieces, batches * planes, chunk_rows, block_rows)
-        return chunks.reshape((batches, planes) + chunks.shape[1:])
-
     def finish_weights(chunks):
         columns = chunks.shape[-1]
         total = pick(chunks, batch_place).astype(F32)
@@ -850,40 +945,63 @@
         got = reorder_members(jnp.stack(got), core, head_place)
         return got.reshape(MEMBERS, piece_rows, columns // (3 * HEAD_DIM), 3, HEAD_DIM)
 
-    slot_grads = []
-    early = None
+    def own_places(found):
+        own = {index: array for index, array in found.items() if index < MEMBERS}
+        for index, array in found.items():
+            if index >= MEMBERS:
+                moved = shift_parts(array, -(index // MEMBERS)).astype(F32)
+                kept = own[index % MEMBERS]
+                own[index % MEMBERS] = (kept.astype(F32) + moved).astype(BF16)
+        return own
+
+    def send(member, array):
+        return swap_member(array, member) if member else array
+
+    pieces_here = MEMBERS * spread_planes
+    kept_slots, sent_slots = [], []
     for slot in range(heads_here):
-        last = slot == heads_here - 1
-        sent = [grad_att[member * heads_here + slot] for member in range(MEMBERS)]
-        grad_side = to_members(sent)
-        if last:
-            early = reduce_weights(slot_grads)
-            early, grad_side = lax.optimization_barrier((early, grad_side))
+        grad_side = [
+            send(member, grad_att[member * heads_here + slot]) for member in range(MEMBERS)
+        ]
         slot_at = tuple(start + slot for start in starts)
-        grads = attention_backward(
-            queries, keys, values, slot_at, mask_rows, sums[slot], outs[slot], grad_side
-        )
-        own = list(grads[:MEMBERS])
-        for distance in range(1, spread_planes):
-            for member in range(MEMBERS):
-                moved = shift_parts(grads[distance * MEMBERS + member], -distance)
-                own[member] = (own[member].astype(F32) + moved.astype(F32)).astype(BF16)
-        slot_grads.append(own)
-        slot_weight = third[:, slot * share : (slot + 1) * share].reshape(width, width)
-        stepped = input_grad_step(
-            row_starts,
-            grad_input,
-            slot_weight,
-            to_members(own),
-            planes if last else 1,
-            BF16 if last else F32,
-        )
-        grad_input = stepped[0]
-    input_grad = from_planes(stepped)
-
-    got = jnp.concatenate(
-        [finish_weights(early), finish_weights(reduce_weights(slot_grads[-1:]))], axis=2
+        given = (queries, keys, values, slot_at, mask_rows, sums[slot], outs[slot])
+        if slot == 1:
+            output_pieces, grad_side = lax.optimization_barrier((output_pieces, grad_side))
+        if slot < heads_here - 1:
+            chosen = range(pieces_here)
+            found, unused = attention_backward(*given, grad_side, chosen)
+            own = own_places(dict(zip(chosen, found)))
+            kept_slots.append([[own[member]] for member in range(MEMBERS)])
+            sent_slots.append([[send(member, own[member])] for member in range(MEMBERS)])
+            continue
+        sent_slots[:-1], grad_side = lax.optimization_barrier((sent_slots[:-1], grad_side))
+        chosen = range(1, pieces_here, 2)
+        found, (partial,) = attention_backward(*given, grad_side, chosen, last=False)
+        own = own_places(dict(zip(chosen, found)))
+        sent = {member: send(member, own[member]) for member in far}
+        grad_input = input_grad_step(
+            row_starts, grad_input, slot_weights[:-1], sent_slots, 1, F32
+        )[0]
+        partial, grad_input = lax.optimization_barrier((partial, grad_input))
+        chosen = range(0, pieces_here, 2)
+        found, query_grads = attention_backward(*given, grad_side, chosen, start=partial)
+        own.update(own_places(dict(zip(chosen, found))))
+        sent.update({member: send(member, own[member]) for member in near})
+        kept_slots.append([[query_grads[member], own[member]] for member in range(MEMBERS)])
+        last_sent = [
+            [send(member, query_grads[member]), sent[member]] for member in range(MEMBERS)
+        ]
+    input_pieces = input_grad_step(
+        row_starts, grad_input, slot_weights[-1:], [last_sent], planes, BF16
     )
+    input_pieces = [input_pieces[0]] + [
+        shift_planes(input_pieces[distance], -distance) for distance in range(1, planes)
+    ]
+    input_grad = collect(input_pieces, plane).reshape(seqs, part_rows, width)
+    output = collect(output_pieces, plane).reshape(seqs, part_rows, width)
+
+    chunks = weight_grad(all_pieces, kept_slots, batches * planes, chunk_rows, block_rows)
+    got = finish_weights(chunks.reshape((batches, planes) + chunks.shape[1:]))
     matrices = [
         jnp.swapaxes(got[:, :share, :, i], 0, 1).reshape(share, width) for i in range(3)
     ]

time: 709 us -> 617 us (0.87)
  waiting for transfers between devices: 184 us -> 117 us
  local copies, waits for them, and re-layouts: 56.5 us -> 34.5 us
    ppermute x12, waiting for transfers between devices: 35.6 us -> 1.21 us  [swap_member(): return lax.ppermute(array, ('blk', 'head'), route)]
    all_gather x1, waiting for transfers between devices: 31 us -> 0.01 us  [local(): second = lax.all_gather(second_pack, ALL_AXES, axis=0, tiled=False)]
    ppermute x21 -> x18, waiting for transfers between devices: 92.2 us -> 68.6 us  [shift_planes(): return lax.ppermute(array, 'blk', route)]
    slice x3 -> x1, local copies, waits for them, and re-layouts: 14.2 us -> 0.05 us  [local(): got[:, share, :, i].reshape(width)]
    ppermute x3 -> x2, waiting for transfers between devices: 0.01 us -> 11.3 us  [shift_batch(): lax.ppermute(array, 'batch', [(i, (i + distance) % size) for i in range(s...]
    ppermute x16, waiting for transfers between devices: 24.9 us -> 35.2 us  [swap_member(): return lax.ppermute(array, 'head', [(0, 1), (1, 0)])]
    pallas_call x9 -> x8, Pallas kernels: 132 us -> 124 us  [the longest x4 90.2 us: attention_forward(): pl.pallas_call(functools.partial(forward_kernel, min(1024, key_count), me...]
    pallas_call x3 -> x4, Pallas kernels: 141 us -> 145 us  [attention_backward(): pl.pallas_call(functools.partial(backward_kernel, min(1024, query_count),...]
  transfers between devices with their start and end apart: 75 -> 71, of which waited for: 22 -> 12; matrix products, arithmetic and copies ran while one was open for 8% -> 6% of each run, Pallas kernels for 47% -> 55%
where the time goes in v4:
time: 617 us; the launch traced here: 608 us
  Pallas kernels  334 us (54%)
  waiting for transfers between devices  117 us (19%)
  starting transfers between devices  95.6 us (15%)
  local copies, waits for them, and re-layouts  34.5 us (6%)
  between operations  15.7 us (3%)
  other arithmetic  12.3 us (2%)
    pallas_call x4, Pallas kernels, attention_backward(): pl.pallas_call(functools.partial(backward_kernel, min(1024, query_count),...  145 us
    pallas_call x4, Pallas kernels, attention_forward(): pl.pallas_call(functools.partial(forward_kernel, min(1024, key_count), me...  90.2 us
    ppermute x18, waiting for transfers between devices, shift_planes(): return lax.ppermute(array, 'blk', route)  68.6 us
    ppermute x18, starting transfers between devices, shift_planes(): return lax.ppermute(array, 'blk', route)  60.4 us
    pallas_call x1, Pallas kernels, layer_rows(): pl.pallas_call(functools.partial(layer_kernel, blocks, planes, parts), gr...  59.4 us
    ppermute x16, waiting for transfers between devices, swap_member(): return lax.ppermute(array, 'head', [(0, 1), (1, 0)])  35.2 us
    ppermute x16, starting transfers between devices, swap_member(): return lax.ppermute(array, 'head', [(0, 1), (1, 0)])  17.7 us
    pallas_call x2, Pallas kernels, input_grad_step(): pl.pallas_call(functools.partial(input_grad_kernel, counts_of(slots)), gr...  14.4 us
  transfers between devices with their start and end apart: 71, of which 12 were waited for; matrix products, arithmetic and copies ran while one was open for 6% of the time, Pallas kernels for 55%

profile of v4, /device:TPU:0, one launch (start us, length us, event | category | flops | bytes accessed | tf_op | source)
XLA Modules:
  0.0 608.5 jit_solution(3334968405611605858)
XLA Ops:
  7.4 1.6 dynamic-slice_bitcast_fusion.5
  9.1 5.1 collective-permute-start
  14.2 8.4 %collective-permute-done.rest_3_ = bf16[256,768]{1,0:T(8,128)(2,1)S(1)} collective-permute-done((bf16[256,768]{1,0:T(8,128)(2,1)S(1)}, bf16[256,768]{1,0:T(8,128)(2,1)S(1)}, u32[]{:S(2)}, u32[]{:S(2)}) %collective-permute-start) | collective-permute-done | bytes 393248 | tf_op jit(solution)/shard_map/ppermute | solution.py:34
  22.6 1.5 collective-permute-start.1
  24.3 2.6 concatenate.109
  26.9 5.6 collective-permute-done.1.rest_7_
  32.6 1.6 collective-permute-start.11
  38.0 10.6 %collective-permute-done.2.rest_1_ = bf16[256,768]{1,0:T(8,128)(2,1)} collective-permute-done((bf16[256,768]{1,0:T(8,128)(2,1)S(1)}, bf16[256,768]{1,0:T(8,128)(2,1)}, u32[]{:S(2)}, u32[]{:S(2)}) %collective-permute-start.2) | collective-permute-done | bytes 393248 | tf_op jit(solution)/shard_map/ppermute | solution.py:34
  49.4 1.7 collective-permute-start.6
  51.7 2.1 collective-permute-start.3
  54.0 4.2 collective-permute-start.7
  58.4 8.9 %collective-permute-done.7 = bf16[4,32,576]{2,1,0:T(8,128)(2,1)S(1)} collective-permute-done((bf16[4,32,576]{2,1,0:T(8,128)(2,1)S(1)}, bf16[4,32,576]{2,1,0:T(8,128)(2,1)S(1)}, u32[]{:S(2)}, u32[]{:S(2)}) %collective-permute-start.7) | collective-permute-done | bytes 147488 | tf_op jit(solution)/shard_map/ppermute | solution.py:34
  67.3 25.0 %collective-permute-start.9 = (bf16[4,32,576]{2,1,0:T(8,128)(2,1)S(1)}, bf16[4,32,576]{2,1,0:T(8,128)(2,1)S(1)}, u32[]{:S(2)}, u32[]{:S(2)}) collective-permute-start(bf16[4,32,576]{2,1,0:T(8,128)(2,1)S(1)} %maximum_select_fusion.8), channel_id=1, source_target_pairs={{0,4},{2,6},{4,8},{6,10},{8,12},{10,14},{12,0},{14,2},{1,5},{3,7},... | collective-permute-start | bytes 442376 | tf_op jit(solution)/shard_map/ppermute | solution.py:34
  92.4 9.2 %collective-permute-done.8 = bf16[4,32,576]{2,1,0:T(8,128)(2,1)S(1)} collective-permute-done((bf16[4,32,576]{2,1,0:T(8,128)(2,1)S(1)}, bf16[4,32,576]{2,1,0:T(8,128)(2,1)S(1)}, u32[]{:S(2)}, u32[]{:S(2)}) %collective-permute-start.8) | collective-permute-done | bytes 147488 | tf_op jit(solution)/shard_map/ppermute | solution.py:34
  101.9 1.7 collective-permute-start.10
  104.5 2.0 collective-permute-start.13
  108.3 15.0 %collective-permute-done.12.rest_5_ = bf16[256,768]{1,0:T(8,128)(2,1)} collective-permute-done((bf16[256,768]{1,0:T(8,128)(2,1)}, bf16[256,768]{1,0:T(8,128)(2,1)}, u32[]{:S(2)}, u32[]{:S(2)}) %collective-permute-start.12) | collective-permute-done | bytes 393248 | tf_op jit(solution)/shard_map/ppermute | solution.py:45
  123.8 14.5 %collective-permute-done.13.rest_6_ = bf16[256,768]{1,0:T(8,128)(2,1)} collective-permute-done((bf16[256,768]{1,0:T(8,128)(2,1)}, bf16[256,768]{1,0:T(8,128)(2,1)}, u32[]{:S(2)}, u32[]{:S(2)}) %collective-permute-start.13) | collective-permute-done | bytes 393248 | tf_op jit(solution)/shard_map/ppermute | solution.py:45
  143.4 9.4 %shard_map.305.q_ref.k_ref.v_ref = bf16[576,4096]{1,0:T(8,128)(2,1)} custom-call(bf16[768,576]{1,0:T(8,128)(2,1)} %bitcast.194, f32[576,1]{1,0:T(8,128)} %copy.106.bias_ref, bf16[256,768]{1,0:T(8,128)(2,1)} %copy-done.4, bf16[256,768]{1,0:T(8,128)(2,1)} %collective-permute-done.2.rest_1_, bf16[256,768]{1,0:T(8,128)(2,1)} %collective-permute-done.3.rest_2_, ...), custom_call_target="tpu_custom_call" | custom-call | flops 3623878656 | bytes 12582912 | tf_op jit(solution)/shard_map/pallas_call | solution.py:314
  152.9 29.3 %shard_map.307 = (bf16[64,1024]{1,0:T(8,128)(2,1)}, bf16[64,1024]{1,0:T(8,128)(2,1)}, bf16[64,1024]{1,0:T(8,128)(2,1)}, bf16[64,1024]{1,0:T(8,128)(2,1)}, f32[1,...) custom-call(bf16[576,4096]{1,0:T(8,128)(2,1)} %shard_map.305.q_ref.k_ref.v_ref, ...), custom_call_target="tpu_custom_call" | custom-call | flops 17179869184 | bytes 2097152 | tf_op jit(solution)/shard_map/pallas_call | solution.py:126
  182.2 29.5 %shard_map.306 = (bf16[64,1024]{1,0:T(8,128)(2,1)}, bf16[64,1024]{1,0:T(8,128)(2,1)}, bf16[64,1024]{1,0:T(8,128)(2,1)}, bf16[64,1024]{1,0:T(8,128)(2,1)}, f32[1,...) custom-call(bf16[576,4096]{1,0:T(8,128)(2,1)} %shard_map.305.q_ref.k_ref.v_ref, ...), custom_call_target="tpu_custom_call" | custom-call | flops 17179869184 | bytes 2097152 | tf_op jit(solution)/shard_map/pallas_call | solution.py:126
  212.2 1.7 collective-permute-start.29
  214.1 15.7 %shard_map.309 = (bf16[64,1024]{1,0:T(8,128)(2,1)}, bf16[64,1024]{1,0:T(8,128)(2,1)}, f32[1,1024]{1,0:T(1,128)}, f32[1,1024]{1,0:T(1,128)}) custom-call(bf16[576,4096]{1,0:T(8,128)(2,1)} %shard_map.305.q_ref.k_ref.v_ref, bf16[576,4096]{1,0:T(8,128)(2,1)} %shard_map.305.q_ref.k_ref.v_ref, bf16[576,4096]{1,0:T(8,128)(2,1)} %shard_map.305.q_ref.k_ref.v_ref, ...), custom_call_target="tpu_custom_call" | custom-call | flops 8589934592 | bytes 2097152 | tf_op jit(solution)/shard_map/pallas_call | solution.py:126
  230.7 3.8 collective-permute-start.32
  237.7 15.6 %shard_map.308 = (bf16[64,1024]{1,0:T(8,128)(2,1)}, bf16[64,1024]{1,0:T(8,128)(2,1)}, f32[1,1024]{1,0:T(1,128)}, f32[1,1024]{1,0:T(1,128)}) custom-call(bf16[576,4096]{1,0:T(8,128)(2,1)} %shard_map.305.q_ref.k_ref.v_ref, bf16[576,4096]{1,0:T(8,128)(2,1)} %shard_map.305.q_ref.k_ref.v_ref, bf16[576,4096]{1,0:T(8,128)(2,1)} %shard_map.305.q_ref.k_ref.v_ref, ...), custom_call_target="tpu_custom_call" | custom-call | flops 8589934592 | bytes 2097152 | tf_op jit(solution)/shard_map/pallas_call | solution.py:126
  259.0 2.0 collective-permute-done.32.rest_21_
  261.9 59.4 %shard_map.310 = (bf16[256,768]{1,0:T(8,128)(2,1)}, bf16[256,768]{1,0:T(8,128)(2,1)}, bf16[256,768]{1,0:T(8,128)(2,1)}, bf16[256,768]{1,0:T(8,128)(2,1)}, bf16[6...) custom-call(s32[8]{0:T(128)} %pad_add_fusion.info_ref, ...), custom_call_target="tpu_custom_call" | custom-call | flops 28991029248 | bytes 18874368 | tf_op jit(solution)/shard_map/pallas_call | solution.py:626
  323.4 3.1 copy.114
  326.6 1.8 collective-permute-start.37
  329.0 1.6 collective-permute-start.42
  330.6 5.3 fusion.1
  336.9 9.4 %collective-permute-start.34 = (bf16[256,768]{1,0:T(8,128)(2,1)S(1)}, bf16[256,768]{1,0:T(8,128)(2,1)S(1)}, u32[]{:S(2)}, u32[]{:S(2)}) collective-permute-start(bf16[256,768]{1,0:T(8,128)(2,1)S(1)} %copy-done.49), channel_id=1, source_target_pairs={{0,12},{2,14},{4,0},{6,2},{8,4},{10,6},{12,8},{14,10},{1,13},{3,15... | collective-permute-start | bytes 1179656 | tf_op jit(solution)/shard_map/ppermute | solution.py:34
  348.7 47.0 %shard_map.312 = (bf16[192,1024]{1,0:T(8,128)(2,1)}, bf16[192,1024]{1,0:T(8,128)(2,1)}, bf16[192,1024]{1,0:T(8,128)(2,1)}, bf16[192,1024]{1,0:T(8,128)(2,1)}) custom-call(bf16[576,4096]{1,0:T(8,128)(2,1)} %shard_map.305.q_ref.k_ref.v_ref, bf16[576,4096]{1,0:T(8,128)(2,1)} %shard_map.305.q_ref.k_ref.v_ref, bf16[576,4096]{1,0:T(8,128)(2,1)} %shard_map.305.q_ref.k_ref.v_ref, ...), custom_call_target="tpu_custom_call" | custom-call | flops 42949672960 | bytes 4194304 | tf_op jit(solution)/shard_map/pallas_call | solution.py:266
  399.1 46.8 %shard_map.314 = (bf16[192,1024]{1,0:T(8,128)(2,1)}, bf16[192,1024]{1,0:T(8,128)(2,1)}, bf16[192,1024]{1,0:T(8,128)(2,1)}, bf16[192,1024]{1,0:T(8,128)(2,1)}) custom-call(bf16[576,4096]{1,0:T(8,128)(2,1)} %shard_map.305.q_ref.k_ref.v_ref, bf16[576,4096]{1,0:T(8,128)(2,1)} %shard_map.305.q_ref.k_ref.v_ref, bf16[576,4096]{1,0:T(8,128)(2,1)} %shard_map.305.q_ref.k_ref.v_ref, ...), custom_call_target="tpu_custom_call" | custom-call | flops 42949672960 | bytes 4194304 | tf_op jit(solution)/shard_map/pallas_call | solution.py:266
  448.3 25.7 %shard_map.313 = (bf16[128,1024]{1,0:T(8,128)(2,1)}, bf16[128,1024]{1,0:T(8,128)(2,1)}, f32[64,4096]{1,0:T(8,128)}) custom-call(bf16[576,4096]{1,0:T(8,128)(2,1)} %shard_map.305.q_ref.k_ref.v_ref, bf16[576,4096]{1,0:T(8,128)(2,1)} %shard_map.305.q_ref.k_ref.v_ref, bf16[576,4096]{1,0:T(8,128)(2,1)} %shard_map.305.q_ref.k_ref.v_ref, ...), custom_call_target="tpu_custom_call" | custom-call | flops 21474836480 | bytes 4194304 | tf_op jit(solution)/shard_map/pallas_call | solution.py:266
  475.0 8.6 %shard_map.315.acc_ref = f32[1024,768]{1,0:T(8,128)} custom-call(s32[4]{0:T(128)} %copy-done.29, f32[1024,768]{1,0:T(8,128)} %get-tuple-element.161.acc_ref, bf16[32,72,768]{2,1,0:T(8,128)(2,1)} %bitcast.165, bf16[32,72,768]{2,1,0:T(8,128)(2,1)} %bitcast.166, bf16[192,1024]{1,0:T(8,128)(2,1)} %get-tuple-element.162.rest_2_.rest_16_, ...), custom_call_target="tpu_custom_call" | custom-call | flops 2415919104 | bytes 6291456 | tf_op jit(solution)/shard_map/pallas_call | solution.py:414
  483.6 25.5 %shard_map.316 = (bf16[128,1024]{1,0:T(8,128)(2,1)}, bf16[128,1024]{1,0:T(8,128)(2,1)}, bf16[64,1024]{1,0:T(8,128)(2,1)}, bf16[64,1024]{1,0:T(8,128)(2,1)}, bf16...) custom-call(bf16[576,4096]{1,0:T(8,128)(2,1)} %shard_map.305.q_ref.k_ref.v_ref, ...), custom_call_target="tpu_custom_call" | custom-call | flops 21474836480 | bytes 4194304 | tf_op jit(solution)/shard_map/pallas_call | solution.py:266
  509.2 10.3 %shard_map.319 = bf16[8,112,576]{2,1,0:T(8,128)(2,1)} custom-call(bf16[256,768]{1,0:T(8,128)(2,1)} %copy-done.4, bf16[256,768]{1,0:T(8,128)(2,1)} %collective-permute-done.2.rest_1_, bf16[256,768]{1,0:T(8,128)(2,1)} %collective-permute-done.3.rest_2_, bf16[256,768]{1,0:T(8,128)(2,1)} %copy-done.39, bf16[256,768]{1,0:T(8,128)(2,1)} %collective-permute-done.11.rest_4_, ...), custom_call_target="tpu_custom_call" | custom-call | flops 3623878656 | bytes 6291456 | tf_op jit(solution)/shard_map/pallas_call | solution.py:374
  524.4 11.3 %collective-permute-done.61 = bf16[4,112,576]{2,1,0:T(8,128)(2,1)S(1)} collective-permute-done((bf16[4,112,576]{2,1,0:T(8,128)(2,1)S(1)}, bf16[4,112,576]{2,1,0:T(8,128)(2,1)S(1)}, u32[]{:S(2)}, u32[]{:S(2)}) %collective-permute-start.61) | collective-permute-done | bytes 516128 | tf_op jit(solution)/shard_map/ppermute | solution.py:39
  535.9 1.6 collective-permute-start.56
  537.6 2.4 collective-permute-start.62
  540.0 1.8 collective-permute-start.63
  544.4 5.8 shard_map.317
  550.2 1.8 collective-permute-start.58
  554.6 7.4 %collective-permute-done.58.rest_1_ = bf16[256,768]{1,0:T(8,128)(2,1)S(1)} collective-permute-done((bf16[256,768]{1,0:T(8,128)(2,1)}, bf16[256,768]{1,0:T(8,128)(2,1)S(1)}, u32[]{:S(2)}, u32[]{:S(2)}) %collective-permute-start.58) | collective-permute-done | bytes 393248 | tf_op jit(solution)/shard_map/ppermute | solution.py:34
  563.2 2.6 shard_map.311
  565.9 22.1 %collective-permute-done.59.rest_2_ = bf16[256,768]{1,0:T(8,128)(2,1)S(1)} collective-permute-done((bf16[256,768]{1,0:T(8,128)(2,1)}, bf16[256,768]{1,0:T(8,128)(2,1)S(1)}, u32[]{:S(2)}, u32[]{:S(2)}) %collective-permute-start.59) | collective-permute-done | bytes 393248 | tf_op jit(solution)/shard_map/ppermute | solution.py:34
  589.0 2.6 shard_map.318
  (433 shorter events, 60.2 us)
Async XLA Ops:
  7.2 248.4 %all-gather.5.cloned.1.call-start = ((), (), s32[]{:S(2)}) async-start(), calls=%async_computation.2 | async-start | bytes 11354112 | tf_op jit(solution)/shard_map/all_gather | solution.py:812
  32.6 441.4 %all-gather.7.cloned.1.call-start = ((), (), s32[]{:S(2)}) async-start(), calls=%async_computation.3 | async-start | bytes 3649536 | tf_op jit(solution)/shard_map/all_gather | solution.py:817
  32.6 71.9 %collective-permute-start.11 = (bf16[256,768]{1,0:T(8,128)(2,1)S(1)}, bf16[256,768]{1,0:T(8,128)(2,1)}, u32[]{:S(2)}, u32[]{:S(2)}) collective-permute-start(bf16[256,768]{1,0:T(8,128)(2,1)S(1)} %get-tuple-element.208.rest_0_), channel_id=1, source_target_pairs={{0,1},{1,0},{2,3},{3,2},{4,5},{5,4},{6,7},{7,6},{8,9},{9,8},{10,11... | collective-permute-start | bytes 1179656 | tf_op jit(solution)/shard_map/ppermute | solution.py:45
  34.2 72.3 %collective-permute-start.14 = (bf16[256,768]{1,0:T(8,128)(2,1)S(1)}, bf16[256,768]{1,0:T(8,128)(2,1)}, u32[]{:S(2)}, u32[]{:S(2)}) collective-permute-start(bf16[256,768]{1,0:T(8,128)(2,1)S(1)} %get-tuple-element.208.rest_0_), channel_id=1, source_target_pairs={{0,2},{2,0},{4,6},{6,4},{8,10},{10,8},{12,14},{14,12},{1,3},{3,1},... | collective-permute-start | bytes 1179656 | tf_op jit(solution)/shard_map/ppermute | solution.py:47
  36.5 560.8 %reduce-scatter.2.cloned.1.call-start = ((), (), s32[]{:S(2)}) async-start(), calls=%async_computation.1 | async-start | bytes 11354112 | tf_op jit(solution)/shard_map/reduce_scatter | solution.py:916
  51.7 52.7 %collective-permute-start.3 = (bf16[256,768]{1,0:T(8,128)(2,1)S(1)}, bf16[256,768]{1,0:T(8,128)(2,1)}, u32[]{:S(2)}, u32[]{:S(2)}) collective-permute-start(bf16[256,768]{1,0:T(8,128)(2,1)S(1)} %get-tuple-element.207), channel_id=1, source_target_pairs={{0,8},{2,10},{4,12},{6,14},{8,0},{10,2},{12,4},{14,6},{1,9},{3,11}... | collective-permute-start | bytes 1179656 | tf_op jit(solution)/shard_map/ppermute | solution.py:34
  58.3 43.2 %collective-permute-start.8 = (bf16[4,32,576]{2,1,0:T(8,128)(2,1)S(1)}, bf16[4,32,576]{2,1,0:T(8,128)(2,1)S(1)}, u32[]{:S(2)}, u32[]{:S(2)}) collective-permute-start(bf16[4,32,576]{2,1,0:T(8,128)(2,1)S(1)} %maximum_select_fusion.8), channel_id=1, source_target_pairs={{0,8},{2,10},{4,12},{6,14},{8,0},{10,2},{12,4},{14,6},{1,9},{3,11}... | collective-permute-start | bytes 442376 | tf_op jit(solution)/shard_map/ppermute | solution.py:34
  67.3 34.2 %collective-permute-start.9 = (bf16[4,32,576]{2,1,0:T(8,128)(2,1)S(1)}, bf16[4,32,576]{2,1,0:T(8,128)(2,1)S(1)}, u32[]{:S(2)}, u32[]{:S(2)}) collective-permute-start(bf16[4,32,576]{2,1,0:T(8,128)(2,1)S(1)} %maximum_select_fusion.8), channel_id=1, source_target_pairs={{0,4},{2,6},{4,8},{6,10},{8,12},{10,14},{12,0},{14,2},{1,5},{3,7},... | collective-permute-start | bytes 442376 | tf_op jit(solution)/shard_map/ppermute | solution.py:34
  101.9 36.9 %collective-permute-start.10 = (bf16[4,4,32,576]{3,2,1,0:T(8,128)(2,1)S(1)}, bf16[4,4,32,576]{3,2,1,0:T(8,128)(2,1)S(1)}, u32[]{:S(2)}, u32[]{:S(2)}) collective-permute-start(bf16[4,4,32,576]{3,2,1,0:T(8,128)(2,1)S(1)} %constant_dynamic-slice_fusion.2), channel_id=1, source_target_pairs={{0,16},{16,0},{1,17},{17,1},{2,18},{18,2},{3,19},{19,3},{4,20},{20... | collective-permute-start | bytes 1769480 | tf_op jit(solution)/shard_map/ppermute | solution.py:39
  104.4 18.9 %collective-permute-start.12 = (bf16[256,768]{1,0:T(8,128)(2,1)}, bf16[256,768]{1,0:T(8,128)(2,1)}, u32[]{:S(2)}, u32[]{:S(2)}) collective-permute-start(bf16[256,768]{1,0:T(8,128)(2,1)} %collective-permute-done.2.rest_1_), channel_id=1, source_target_pairs={{0,1},{1,0},{2,3},{3,2},{4,5},{5,4},{6,7},{7,6},{8,9},{9,8},{10,11... | collective-permute-start | bytes 1179656 | tf_op jit(solution)/shard_map/ppermute | solution.py:45
  104.4 18.9 %collective-permute-start.15 = (bf16[256,768]{1,0:T(8,128)(2,1)}, bf16[256,768]{1,0:T(8,128)(2,1)}, u32[]{:S(2)}, u32[]{:S(2)}) collective-permute-start(bf16[256,768]{1,0:T(8,128)(2,1)} %collective-permute-done.2.rest_1_), channel_id=1, source_target_pairs={{0,2},{2,0},{4,6},{6,4},{8,10},{10,8},{12,14},{14,12},{1,3},{3,1},... | collective-permute-start | bytes 1179656 | tf_op jit(solution)/shard_map/ppermute | solution.py:47
  104.5 33.8 %collective-permute-start.13 = (bf16[256,768]{1,0:T(8,128)(2,1)}, bf16[256,768]{1,0:T(8,128)(2,1)}, u32[]{:S(2)}, u32[]{:S(2)}) collective-permute-start(bf16[256,768]{1,0:T(8,128)(2,1)} %collective-permute-done.3.rest_2_), channel_id=1, source_target_pairs={{0,1},{1,0},{2,3},{3,2},{4,5},{5,4},{6,7},{7,6},{8,9},{9,8},{10,11... | collective-permute-start | bytes 1179656 | tf_op jit(solution)/shard_map/ppermute | solution.py:45
  106.5 31.8 %collective-permute-start.16 = (bf16[256,768]{1,0:T(8,128)(2,1)}, bf16[256,768]{1,0:T(8,128)(2,1)}, u32[]{:S(2)}, u32[]{:S(2)}) collective-permute-start(bf16[256,768]{1,0:T(8,128)(2,1)} %collective-permute-done.3.rest_2_), channel_id=1, source_target_pairs={{0,2},{2,0},{4,6},{6,4},{8,10},{10,8},{12,14},{14,12},{1,3},{3,1},... | collective-permute-start | bytes 1179656 | tf_op jit(solution)/shard_map/ppermute | solution.py:47
  123.3 19.0 %collective-permute-start.17 = (bf16[256,768]{1,0:T(8,128)(2,1)}, bf16[256,768]{1,0:T(8,128)(2,1)S(1)}, u32[]{:S(2)}, u32[]{:S(2)}) collective-permute-start(bf16[256,768]{1,0:T(8,128)(2,1)} %copy-done.39), channel_id=1, source_target_pairs={{0,2},{2,0},{4,6},{6,4},{8,10},{10,8},{12,14},{14,12},{1,3},{3,1},... | collective-permute-start | bytes 1179656 | tf_op jit(solution)/shard_map/ppermute | solution.py:47
  123.3 19.0 %collective-permute-start.18 = (bf16[256,768]{1,0:T(8,128)(2,1)}, bf16[256,768]{1,0:T(8,128)(2,1)S(1)}, u32[]{:S(2)}, u32[]{:S(2)}) collective-permute-start(bf16[256,768]{1,0:T(8,128)(2,1)} %collective-permute-done.11.rest_4_), channel_id=1, source_target_pairs={{0,2},{2,0},{4,6},{6,4},{8,10},{10,8},{12,14},{14,12},{1,3},{3,1},... | collective-permute-start | bytes 1179656 | tf_op jit(solution)/shard_map/ppermute | solution.py:47
  211.7 19.0 %collective-permute-start.23 = (bf16[64,1024]{1,0:T(8,128)(2,1)S(1)}, bf16[64,1024]{1,0:T(8,128)(2,1)S(1)}, u32[]{:S(2)}, u32[]{:S(2)}) collective-permute-start(bf16[64,1024]{1,0:T(8,128)(2,1)S(1)} %copy-done.56), channel_id=1, source_target_pairs={{0,1},{1,0},{2,3},{3,2},{4,5},{5,4},{6,7},{7,6},{8,9},{9,8},{10,11... | collective-permute-start | bytes 393224 | tf_op jit(solution)/shard_map/ppermute | solution.py:45
  211.8 18.9 %collective-permute-start.26 = (bf16[64,1024]{1,0:T(8,128)(2,1)S(1)}, bf16[64,1024]{1,0:T(8,128)(2,1)S(1)}, u32[]{:S(2)}, u32[]{:S(2)}) collective-permute-start(bf16[64,1024]{1,0:T(8,128)(2,1)S(1)} %copy-done.57), channel_id=1, source_target_pairs={{0,2},{2,0},{4,6},{6,4},{8,10},{10,8},{12,14},{14,12},{1,3},{3,1},... | collective-permute-start | bytes 393224 | tf_op jit(solution)/shard_map/ppermute | solution.py:47
  212.2 22.4 %collective-permute-start.29 = (bf16[64,1024]{1,0:T(8,128)(2,1)S(1)}, bf16[64,1024]{1,0:T(8,128)(2,1)S(1)}, u32[]{:S(2)}, u32[]{:S(2)}) collective-permute-start(bf16[64,1024]{1,0:T(8,128)(2,1)S(1)} %copy-done.58), channel_id=1, source_target_pairs={{0,3},{1,2},{2,1},{3,0},{4,7},{5,6},{6,5},{7,4},{8,11},{9,10},{10,... | collective-permute-start | bytes 393224 | tf_op jit(solution)/shard_map/ppermute | solution.py:49
  213.9 21.8 %collective-permute-start.22 = (bf16[64,1024]{1,0:T(8,128)(2,1)}, bf16[64,1024]{1,0:T(8,128)(2,1)S(1)}, u32[]{:S(2)}, u32[]{:S(2)}) collective-permute-start(bf16[64,1024]{1,0:T(8,128)(2,1)} %get-tuple-element.114.rest_5_), channel_id=1, source_target_pairs={{0,1},{1,0},{2,3},{3,2},{4,5},{5,4},{6,7},{7,6},{8,9},{9,8},{10,11... | collective-permute-start | bytes 393224 | tf_op jit(solution)/shard_map/ppermute | solution.py:45
  214.0 22.7 %collective-permute-start.25 = (bf16[64,1024]{1,0:T(8,128)(2,1)}, bf16[64,1024]{1,0:T(8,128)(2,1)S(1)}, u32[]{:S(2)}, u32[]{:S(2)}) collective-permute-start(bf16[64,1024]{1,0:T(8,128)(2,1)} %get-tuple-element.117.rest_6_), channel_id=1, source_target_pairs={{0,2},{2,0},{4,6},{6,4},{8,10},{10,8},{12,14},{14,12},{1,3},{3,1},... | collective-permute-start | bytes 393224 | tf_op jit(solution)/shard_map/ppermute | solution.py:47
  230.7 28.3 %collective-permute-start.31 = (bf16[256,768]{1,0:T(8,128)(2,1)S(1)}, bf16[256,768]{1,0:T(8,128)(2,1)S(1)}, u32[]{:S(2)}, u32[]{:S(2)}) collective-permute-start(bf16[256,768]{1,0:T(8,128)(2,1)S(1)} %get-tuple-element.205), channel_id=1, source_target_pairs={{0,4},{2,6},{4,8},{6,10},{8,12},{10,14},{12,0},{14,2},{1,5},{3,7},... | collective-permute-start | bytes 1179656 | tf_op jit(solution)/shard_map/ppermute | solution.py:34
  230.7 30.3 %collective-permute-start.32 = (bf16[256,768]{1,0:T(8,128)(2,1)S(1)}, bf16[256,768]{1,0:T(8,128)(2,1)S(1)}, u32[]{:S(2)}, u32[]{:S(2)}) collective-permute-start(bf16[256,768]{1,0:T(8,128)(2,1)S(1)} %get-tuple-element.204), channel_id=1, source_target_pairs={{0,8},{2,10},{4,12},{6,14},{8,0},{10,2},{12,4},{14,6},{1,9},{3,11}... | collective-permute-start | bytes 1179656 | tf_op jit(solution)/shard_map/ppermute | solution.py:34
  234.6 26.4 %collective-permute-start.33 = (bf16[256,768]{1,0:T(8,128)(2,1)S(1)}, bf16[256,768]{1,0:T(8,128)(2,1)S(1)}, u32[]{:S(2)}, u32[]{:S(2)}) collective-permute-start(bf16[256,768]{1,0:T(8,128)(2,1)S(1)} %get-tuple-element.203), channel_id=1, source_target_pairs={{0,12},{2,14},{4,0},{6,2},{8,4},{10,6},{12,8},{14,10},{1,13},{3,15... | collective-permute-start | bytes 1179656 | tf_op jit(solution)/shard_map/ppermute | solution.py:34
  235.7 17.7 %collective-permute-start.28 = (bf16[64,1024]{1,0:T(8,128)(2,1)S(1)}, bf16[64,1024]{1,0:T(8,128)(2,1)S(1)}, u32[]{:S(2)}, u32[]{:S(2)}) collective-permute-start(bf16[64,1024]{1,0:T(8,128)(2,1)S(1)} %copy-done.59), channel_id=1, source_target_pairs={{0,3},{1,2},{2,1},{3,0},{4,7},{5,6},{6,5},{7,4},{8,11},{9,10},{10,... | collective-permute-start | bytes 393224 | tf_op jit(solution)/shard_map/ppermute | solution.py:49
  328.4 17.9 %collective-permute-start.38 = (bf16[64,1024]{1,0:T(8,128)(2,1)S(1)}, bf16[64,1024]{1,0:T(8,128)(2,1)S(1)}, u32[]{:S(2)}, u32[]{:S(2)}) collective-permute-start(bf16[64,1024]{1,0:T(8,128)(2,1)S(1)} %copy-done.84), channel_id=1, source_target_pairs={{0,2},{2,0},{4,6},{6,4},{8,10},{10,8},{12,14},{14,12},{1,3},{3,1},... | collective-permute-start | bytes 393224 | tf_op jit(solution)/shard_map/ppermute | solution.py:47
  328.4 18.8 %collective-permute-start.40 = (bf16[64,1024]{1,0:T(8,128)(2,1)S(1)}, bf16[64,1024]{1,0:T(8,128)(2,1)S(1)}, u32[]{:S(2)}, u32[]{:S(2)}) collective-permute-start(bf16[64,1024]{1,0:T(8,128)(2,1)S(1)} %copy-done.83), channel_id=1, source_target_pairs={{0,1},{1,0},{2,3},{3,2},{4,5},{5,4},{6,7},{7,6},{8,9},{9,8},{10,11... | collective-permute-start | bytes 393224 | tf_op jit(solution)/shard_map/ppermute | solution.py:45
  328.7 18.6 %collective-permute-start.41 = (bf16[64,1024]{1,0:T(8,128)(2,1)S(1)}, bf16[64,1024]{1,0:T(8,128)(2,1)S(1)}, u32[]{:S(2)}, u32[]{:S(2)}) collective-permute-start(bf16[64,1024]{1,0:T(8,128)(2,1)S(1)} %copy-done.82), channel_id=1, source_target_pairs={{0,2},{2,0},{4,6},{6,4},{8,10},{10,8},{12,14},{14,12},{1,3},{3,1},... | collective-permute-start | bytes 393224 | tf_op jit(solution)/shard_map/ppermute | solution.py:47
  329.0 18.4 %collective-permute-start.42 = (bf16[64,1024]{1,0:T(8,128)(2,1)S(1)}, bf16[64,1024]{1,0:T(8,128)(2,1)S(1)}, u32[]{:S(2)}, u32[]{:S(2)}) collective-permute-start(bf16[64,1024]{1,0:T(8,128)(2,1)S(1)} %copy-done.79), channel_id=1, source_target_pairs={{0,3},{1,2},{2,1},{3,0},{4,7},{5,6},{6,5},{7,4},{8,11},{9,10},{10,... | collective-permute-start | bytes 393224 | tf_op jit(solution)/shard_map/ppermute | solution.py:49
  336.9 59.5 %collective-permute-start.34 = (bf16[256,768]{1,0:T(8,128)(2,1)S(1)}, bf16[256,768]{1,0:T(8,128)(2,1)S(1)}, u32[]{:S(2)}, u32[]{:S(2)}) collective-permute-start(bf16[256,768]{1,0:T(8,128)(2,1)S(1)} %copy-done.49), channel_id=1, source_target_pairs={{0,12},{2,14},{4,0},{6,2},{8,4},{10,6},{12,8},{14,10},{1,13},{3,15... | collective-permute-start | bytes 1179656 | tf_op jit(solution)/shard_map/ppermute | solution.py:34
  346.3 50.7 %collective-permute-start.35 = (bf16[256,768]{1,0:T(8,128)(2,1)S(1)}, bf16[256,768]{1,0:T(8,128)(2,1)S(1)}, u32[]{:S(2)}, u32[]{:S(2)}) collective-permute-start(bf16[256,768]{1,0:T(8,128)(2,1)S(1)} %copy-done.47), channel_id=1, source_target_pairs={{0,8},{2,10},{4,12},{6,14},{8,0},{10,2},{12,4},{14,6},{1,9},{3,11}... | collective-permute-start | bytes 1179656 | tf_op jit(solution)/shard_map/ppermute | solution.py:34
  347.2 50.9 %collective-permute-start.36 = (bf16[256,768]{1,0:T(8,128)(2,1)S(1)}, bf16[256,768]{1,0:T(8,128)(2,1)S(1)}, u32[]{:S(2)}, u32[]{:S(2)}) collective-permute-start(bf16[256,768]{1,0:T(8,128)(2,1)S(1)} %copy-done.45), channel_id=1, source_target_pairs={{0,4},{2,6},{4,8},{6,10},{8,12},{10,14},{12,0},{14,2},{1,5},{3,7},... | collective-permute-start | bytes 1179656 | tf_op jit(solution)/shard_map/ppermute | solution.py:34
  347.3 48.4 %collective-permute-start.39 = (bf16[64,1024]{1,0:T(8,128)(2,1)S(1)}, bf16[64,1024]{1,0:T(8,128)(2,1)S(1)}, u32[]{:S(2)}, u32[]{:S(2)}) collective-permute-start(bf16[64,1024]{1,0:T(8,128)(2,1)S(1)} %copy-done.71), channel_id=1, source_target_pairs={{0,3},{1,2},{2,1},{3,0},{4,7},{5,6},{6,5},{7,4},{8,11},{9,10},{10,... | collective-permute-start | bytes 393224 | tf_op jit(solution)/shard_map/ppermute | solution.py:49
  347.4 50.9 %collective-permute-start.46 = (bf16[64,1024]{1,0:T(8,128)(2,1)S(1)}, bf16[64,1024]{1,0:T(8,128)(2,1)S(1)}, u32[]{:S(2)}, u32[]{:S(2)}) collective-permute-start(bf16[64,1024]{1,0:T(8,128)(2,1)S(1)} %copy-done.67), channel_id=1, source_target_pairs={{0,1},{1,0},{2,3},{3,2},{4,5},{5,4},{6,7},{7,6},{8,9},{9,8},{10,11... | collective-permute-start | bytes 393224 | tf_op jit(solution)/shard_map/ppermute | solution.py:45
  395.7 50.2 %collective-permute-start.47 = (bf16[64,1024]{1,0:T(8,128)(2,1)S(1)}, bf16[64,1024]{1,0:T(8,128)(2,1)S(1)}, u32[]{:S(2)}, u32[]{:S(2)}) collective-permute-start(bf16[64,1024]{1,0:T(8,128)(2,1)S(1)} %copy-done.61), channel_id=1, source_target_pairs={{0,2},{2,0},{4,6},{6,4},{8,10},{10,8},{12,14},{14,12},{1,3},{3,1},... | collective-permute-start | bytes 393224 | tf_op jit(solution)/shard_map/ppermute | solution.py:47
  396.4 50.8 %collective-permute-start.48 = (bf16[64,1024]{1,0:T(8,128)(2,1)S(1)}, bf16[64,1024]{1,0:T(8,128)(2,1)S(1)}, u32[]{:S(2)}, u32[]{:S(2)}) collective-permute-start(bf16[64,1024]{1,0:T(8,128)(2,1)S(1)} %copy-done.60), channel_id=1, source_target_pairs={{0,3},{1,2},{2,1},{3,0},{4,7},{5,6},{6,5},{7,4},{8,11},{9,10},{10,... | collective-permute-start | bytes 393224 | tf_op jit(solution)/shard_map/ppermute | solution.py:49
  397.0 50.2 %collective-permute-start.43 = (bf16[192,1024]{1,0:T(8,128)(2,1)}, bf16[192,1024]{1,0:T(8,128)(2,1)S(1)}, u32[]{:S(2)}, u32[]{:S(2)}) collective-permute-start(bf16[192,1024]{1,0:T(8,128)(2,1)} %get-tuple-element.149.rest_17_), channel_id=1, source_target_pairs={{0,1},{1,0},{2,3},{3,2},{4,5},{5,4},{6,7},{7,6},{8,9},{9,8},{10,11... | collective-permute-start | bytes 1179656 | tf_op jit(solution)/shard_map/ppermute | solution.py:45
  398.1 50.1 %collective-permute-start.44 = (bf16[192,1024]{1,0:T(8,128)(2,1)}, bf16[192,1024]{1,0:T(8,128)(2,1)S(1)}, u32[]{:S(2)}, u32[]{:S(2)}) collective-permute-start(bf16[192,1024]{1,0:T(8,128)(2,1)} %get-tuple-element.150.rest_18_), channel_id=1, source_target_pairs={{0,2},{2,0},{4,6},{6,4},{8,10},{10,8},{12,14},{14,12},{1,3},{3,1},... | collective-permute-start | bytes 1179656 | tf_op jit(solution)/shard_map/ppermute | solution.py:47
  398.3 49.9 %collective-permute-start.45 = (bf16[192,1024]{1,0:T(8,128)(2,1)}, bf16[192,1024]{1,0:T(8,128)(2,1)S(1)}, u32[]{:S(2)}, u32[]{:S(2)}) collective-permute-start(bf16[192,1024]{1,0:T(8,128)(2,1)} %get-tuple-element.151.rest_19_), channel_id=1, source_target_pairs={{0,3},{1,2},{2,1},{3,0},{4,7},{5,6},{6,5},{7,4},{8,11},{9,10},{10,... | collective-permute-start | bytes 1179656 | tf_op jit(solution)/shard_map/ppermute | solution.py:49
  446.0 28.0 %collective-permute-start.49 = (bf16[192,1024]{1,0:T(8,128)(2,1)}, bf16[192,1024]{1,0:T(8,128)(2,1)S(1)}, u32[]{:S(2)}, u32[]{:S(2)}) collective-permute-start(bf16[192,1024]{1,0:T(8,128)(2,1)} %get-tuple-element.175.rest_21_), channel_id=1, source_target_pairs={{0,1},{1,0},{2,3},{3,2},{4,5},{5,4},{6,7},{7,6},{8,9},{9,8},{10,11... | collective-permute-start | bytes 1179656 | tf_op jit(solution)/shard_map/ppermute | solution.py:45
  447.2 26.8 %collective-permute-start.50 = (bf16[192,1024]{1,0:T(8,128)(2,1)}, bf16[192,1024]{1,0:T(8,128)(2,1)S(1)}, u32[]{:S(2)}, u32[]{:S(2)}) collective-permute-start(bf16[192,1024]{1,0:T(8,128)(2,1)} %get-tuple-element.176.rest_22_), channel_id=1, source_target_pairs={{0,2},{2,0},{4,6},{6,4},{8,10},{10,8},{12,14},{14,12},{1,3},{3,1},... | collective-permute-start | bytes 1179656 | tf_op jit(solution)/shard_map/ppermute | solution.py:47
  447.2 26.8 %collective-permute-start.51 = (bf16[192,1024]{1,0:T(8,128)(2,1)}, bf16[192,1024]{1,0:T(8,128)(2,1)S(1)}, u32[]{:S(2)}, u32[]{:S(2)}) collective-permute-start(bf16[192,1024]{1,0:T(8,128)(2,1)} %get-tuple-element.177.rest_23_), channel_id=1, source_target_pairs={{0,3},{1,2},{2,1},{3,0},{4,7},{5,6},{6,5},{7,4},{8,11},{9,10},{10,... | collective-permute-start | bytes 1179656 | tf_op jit(solution)/shard_map/ppermute | solution.py:49
  522.3 20.8 %collective-permute-start.55 = (bf16[128,1024]{1,0:T(8,128)(2,1)S(1)}, bf16[128,1024]{1,0:T(8,128)(2,1)S(1)}, u32[]{:S(2)}, u32[]{:S(2)}) collective-permute-start(bf16[128,1024]{1,0:T(8,128)(2,1)S(1)} %copy-done.51), channel_id=1, source_target_pairs={{0,2},{2,0},{4,6},{6,4},{8,10},{10,8},{12,14},{14,12},{1,3},{3,1},... | collective-permute-start | bytes 786440 | tf_op jit(solution)/shard_map/ppermute | solution.py:47
  523.0 16.9 %collective-permute-start.52 = (bf16[64,1024]{1,0:T(8,128)(2,1)S(1)}, bf16[64,1024]{1,0:T(8,128)(2,1)S(1)}, u32[]{:S(2)}, u32[]{:S(2)}) collective-permute-start(bf16[64,1024]{1,0:T(8,128)(2,1)S(1)} %copy-done.80), channel_id=1, source_target_pairs={{0,1},{1,0},{2,3},{3,2},{4,5},{5,4},{6,7},{7,6},{8,9},{9,8},{10,11... | collective-permute-start | bytes 393224 | tf_op jit(solution)/shard_map/ppermute | solution.py:45
  552.1 36.0 %collective-permute-start.59 = (bf16[256,768]{1,0:T(8,128)(2,1)}, bf16[256,768]{1,0:T(8,128)(2,1)S(1)}, u32[]{:S(2)}, u32[]{:S(2)}) collective-permute-start(bf16[256,768]{1,0:T(8,128)(2,1)} %get-tuple-element.190), channel_id=1, source_target_pairs={{0,8},{2,10},{4,12},{6,14},{8,0},{10,2},{12,4},{14,6},{1,9},{3,11}... | collective-permute-start | bytes 1179656 | tf_op jit(solution)/shard_map/ppermute | solution.py:34
  552.6 35.5 %collective-permute-start.60 = (bf16[256,768]{1,0:T(8,128)(2,1)}, bf16[256,768]{1,0:T(8,128)(2,1)S(1)}, u32[]{:S(2)}, u32[]{:S(2)}) collective-permute-start(bf16[256,768]{1,0:T(8,128)(2,1)} %get-tuple-element.191), channel_id=1, source_target_pairs={{0,4},{2,6},{4,8},{6,10},{8,12},{10,14},{12,0},{14,2},{1,5},{3,7},... | collective-permute-start | bytes 1179656 | tf_op jit(solution)/shard_map/ppermute | solution.py:34
  553.2 38.4 %collective-permute-start.65 = (f32[32,576]{1,0:T(8,128)S(1)}, f32[32,576]{1,0:T(8,128)S(1)}, u32[]{:S(2)}, u32[]{:S(2)}) collective-permute-start(f32[32,576]{1,0:T(8,128)S(1)} %get-tuple-element.229), channel_id=1, source_target_pairs={{0,2},{2,0},{4,6},{6,4},{8,10},{10,8},{12,14},{14,12},{1,3},{3,1},... | collective-permute-start | bytes 221192 | tf_op jit(solution)/shard_map/ppermute | solution.py:47
  553.3 38.3 %collective-permute-start.66 = (f32[32,576]{1,0:T(8,128)S(1)}, f32[32,576]{1,0:T(8,128)S(1)}, u32[]{:S(2)}, u32[]{:S(2)}) collective-permute-start(f32[32,576]{1,0:T(8,128)S(1)} %get-tuple-element.230), channel_id=1, source_target_pairs={{0,3},{1,2},{2,1},{3,0},{4,7},{5,6},{6,5},{7,4},{8,11},{9,10},{10,... | collective-permute-start | bytes 221192 | tf_op jit(solution)/shard_map/ppermute | solution.py:49
  562.0 29.6 %collective-permute-start.67 = (f32[32,576]{1,0:T(8,128)S(1)}, f32[32,576]{1,0:T(8,128)S(1)}, u32[]{:S(2)}, u32[]{:S(2)}) collective-permute-start(f32[32,576]{1,0:T(8,128)S(1)} %get-tuple-element.231), channel_id=1, source_target_pairs={{0,1},{1,0},{2,3},{3,2},{4,5},{5,4},{6,7},{7,6},{8,9},{9,8},{10,11... | collective-permute-start | bytes 221192 | tf_op jit(solution)/shard_map/ppermute | solution.py:45
  (116 other events, 1651.4 us)
Sparse Core Ops, SparseCore 0:
  32.7 125.6 all-gather.4
  161.3 57.9 all-gather.6
  336.0 153.6 reduce-scatter.1

commit v5 on v4

--- a/solution.py
+++ b/solution.py
@@ -64,48 +64,56 @@
     return lax.dynamic_slice_in_dim(stack, len(pieces) - 1 - place, len(pieces), 0)
 
 
+def split_three(row):
+    high = row.astype(BF16)
+    rest = row - high.astype(F32)
+    middle = rest.astype(BF16)
+    low = (rest - middle.astype(F32)).astype(BF16)
+    return high, middle, low
+
+
 def forward_kernel(block_k, members, q_ref, k_ref, v_ref, mask_ref, *rest):
     count = len(members)
     out_refs, sum_refs, (keys, values) = rest[:count], rest[count : 2 * count], rest[2 * count :]
     key_count = k_ref.shape[1]
     block_q = q_ref.shape[1] // MEMBERS
     rows = lax.broadcasted_iota(jnp.int32, (EXTRA, key_count), 0)
-    joined = jnp.concatenate([k_ref[...], mask_ref[...]], axis=0)
+    joined = jnp.concatenate([k_ref[...]] * 3 + [mask_ref[...]], axis=0)
     keys[...] = joined.astype(F32).T.astype(BF16)
     values[:HEAD_DIM, :] = v_ref[...]
     values[HEAD_DIM:, :] = jnp.where(rows == 0, 1.0, 0.0).astype(BF16)
     rows_q = lax.broadcasted_iota(jnp.int32, (EXTRA, block_q), 0)
     ones_row = jnp.where(rows_q == 0, 1.0, 0.0).astype(BF16)
-    scale = 1.0 / math.sqrt(HEAD_DIM)
-
-    for index, member in enumerate(members):
-        q_places = pl.ds(member * block_q, block_q)
-        scaled = (q_ref[:, q_places].astype(F32) * scale).astype(BF16)
-        query = jnp.concatenate([scaled, ones_row], axis=0)
-
-        def key_block(j, carry):
-            top, acc = carry
+    scale = math.log2(math.e) / math.sqrt(HEAD_DIM)
+
+    def prepared(member):
+        scaled = q_ref[:, pl.ds(member * block_q, block_q)].astype(F32) * scale
+        return jnp.concatenate(list(split_three(scaled)) + [ones_row], axis=0)
+
+    def advance(state, scores, value_part):
+        top, acc = state
+        new_top = jnp.maximum(top, jnp.max(scores, axis=0, keepdims=True))
+        probs = jnp.exp2(scores - new_top).astype(BF16)
+        return new_top, acc * jnp.exp2(top - new_top) + dot(value_part, probs, 1, 0)
+
+    for start in range(0, count, 2):
+        queries = [prepared(member) for member in members[start : start + 2]]
+
+        def key_block(j, states):
             k_start = pl.multiple_of(j * block_k, block_k)
-            scores = dot(keys[pl.ds(k_start, block_k), :], query, 1, 0)
-            new_top = jnp.maximum(top, jnp.max(scores, axis=0, keepdims=True))
-            probs = jnp.exp(scores - new_top)
-            acc = acc * jnp.exp(top - new_top) + dot(
-                values[:, pl.ds(k_start, block_k)], probs.astype(BF16), 1, 0
+            key_part = keys[pl.ds(k_start, block_k), :]
+            value_part = values[:, pl.ds(k_start, block_k)]
+            scores = [dot(key_part, query, 1, 0) for query in queries]
+            return tuple(
+                advance(state, score, value_part) for state, score in zip(states, scores)
             )
-            return new_top, acc
-
-        top, acc = lax.fori_loop(
-            0,
-            key_count // block_k,
-            key_block,
-            (
-                jnp.full((1, block_q), NEG_BIG, F32),
-                jnp.zeros((HEAD_DIM + EXTRA, block_q), F32),
-            ),
-        )
-        total = acc[HEAD_DIM : HEAD_DIM + 1, :]
-        out_refs[index][...] = (acc[:HEAD_DIM, :] / total).astype(BF16)
-        sum_refs[index][...] = top + jnp.log(total)
+
+        begin = (jnp.full((1, block_q), NEG_BIG, F32), jnp.zeros((HEAD_DIM + EXTRA, block_q), F32))
+        states = lax.fori_loop(0, key_count // block_k, key_block, (begin,) * len(queries))
+        for index, (top, acc) in enumerate(states):
+            total = acc[HEAD_DIM : HEAD_DIM + 1, :]
+            out_refs[start + index][...] = (acc[:HEAD_DIM, :] / total).astype(BF16)
+            sum_refs[start + index][...] = top * math.log(2.0) + jnp.log(total)
 
 
 def head_specs(arrays, places):
@@ -124,14 +132,14 @@
     key_count = keys.shape[1]
     count = len(members)
     result = pl.pallas_call(
-        functools.partial(forward_kernel, min(1024, key_count), members),
+        functools.partial(forward_kernel, min(512, key_count), members),
         grid=(1,),
         in_specs=head_specs((queries, keys, values), places) + [whole((EXTRA, key_count))],
         out_specs=[whole((HEAD_DIM, part_count))] * count + [whole((1, part_count))] * count,
         out_shape=[jax.ShapeDtypeStruct((HEAD_DIM, part_count), BF16)] * count
         + [jax.ShapeDtypeStruct((1, part_count), F32)] * count,
         scratch_shapes=[
-            pltpu.VMEM((key_count, HEAD_DIM + EXTRA), BF16),
+            pltpu.VMEM((key_count, 3 * HEAD_DIM + EXTRA), BF16),
             pltpu.VMEM((HEAD_DIM + EXTRA, key_count), BF16),
         ],
         compiler_params=pltpu.CompilerParams(vmem_limit_bytes=VMEM_LIMIT),
@@ -142,14 +150,6 @@
         ),
     )(queries, keys, values, mask_rows)
     return dict(zip(members, result[:count])), dict(zip(members, result[count:]))
-
-
-def split_three(row):
-    high = row.astype(BF16)
-    rest = row - high.astype(F32)
-    middle = rest.astype(BF16)
-    low = (rest - middle.astype(F32)).astype(BF16)
-    return high.astype(F32), middle.astype(F32), low.astype(F32)
 
 
 def backward_kernel(block_q, chosen, first, last, q_ref, k_ref, v_ref, mask_ref, *rest):
@@ -172,7 +172,7 @@
     places_k = lax.broadcasted_iota(jnp.int32, (EXTRA, key_count), 0)
 
     def extra_rows(row, fourth):
-        high, middle, low = split_three(row)
+        high, middle, low = [piece.astype(F32) for piece in split_three(row)]
         rows = jnp.where(
             places_q == 0, high, jnp.where(places_q == 1, middle, jnp.where(places_q == 2, low, 0.0))
         )
@@ -269,7 +269,8 @@
         in_specs=head_specs((queries, keys, values), places)
         + [whole((EXTRA, key_count))]
         + [whole((1, part))] * MEMBERS
-        + [whole((HEAD_DIM, part))] * (2 * MEMBERS)
+        + [whole((HEAD_DIM, part))] * MEMBERS
+        + head_specs([grad for grad, place in grads], [place for grad, place in grads])
         + [whole(array.shape) for array in extra],
         out_specs=[whole(dims) for dims, dtype in results],
         out_shape=[jax.ShapeDtypeStruct(dims, dtype) for dims, dtype in results],
@@ -289,7 +290,7 @@
             transcendentals=query_count * count * part,
             bytes_accessed=16 * HEAD_DIM * key_count,
         ),
-    )(queries, keys, values, mask_rows, *sums, *outs, *grads, *extra)
+    )(queries, keys, values, mask_rows, *sums, *outs, *[grad for grad, place in grads], *extra)
     return list(found[:count]), list(found[count:])
 
 
@@ -481,7 +482,7 @@
     att_refs, rest = rest[3 : 3 + parts], rest[3 + parts :]
     cot_refs, rest = rest[:planes], rest[planes:]
     final_refs, rest = rest[:planes], rest[planes:]
-    grad_att_refs, rest = rest[:parts], rest[parts:]
+    grad_att_refs, rest = rest[: 2 * MEMBERS], rest[2 * MEMBERS :]
     resid_ref, grad_outer_w, grad_inner_w, grad_out_w, grad_vectors, grad_inner_bias = rest[:6]
     attended, hat1, scale1, low, acc, active, slope, grad_low, grad_hidden, weight_out = rest[6:]
     step = pl.program_id(0)
@@ -588,13 +589,12 @@
         grad_vectors[0:1, :] = bias_sum
         grad_vectors[1:2, :] = gain_sum
         grad_vectors[2:3, :] = shift_sum
-        heads = group // HEAD_DIM
         for m in range(MEMBERS):
             rows = slice(m * group, (m + 1) * group)
             grad_out_w[group_rows(m), :] = dot(attended[rows, :], grad_low[...], 1, 0).astype(BF16)
             moved = dot(weight_out[group_rows(m), :], grad_low[...], 1, 1).astype(BF16)
-            for j in range(heads):
-                grad_att_refs[m * heads + j][...] = moved[j * HEAD_DIM : (j + 1) * HEAD_DIM, :]
+            grad_att_refs[2 * m][...] = moved[:HEAD_DIM, :]
+            grad_att_refs[2 * m + 1][...] = moved[HEAD_DIM:, :]
 
 
 def layer_rows(info, row_pieces, vectors, inner_bias, weights, att_parts, cot_pieces):
@@ -603,6 +603,7 @@
     hidden = blocks * width
     row_count = att_parts[0].shape[1]
     piece = row_count // planes
+    group = width // MEMBERS
     once = pl.Buffered(1)
 
     def fixed(shape):
@@ -634,7 +635,7 @@
             + [fixed((HEAD_DIM, row_count))] * parts
             + [fixed((piece, width))] * planes,
             out_specs=[fixed((piece, width))] * planes
-            + [fixed((HEAD_DIM, row_count))] * parts
+            + [fixed((HEAD_DIM, row_count)), fixed((group - HEAD_DIM, row_count))] * MEMBERS
             + [fixed((row_count, width)), grad_spec, grad_spec, fixed(square)]
             + small,
             scratch_shapes=[
@@ -651,7 +652,7 @@
             ],
         ),
         out_shape=[shape((piece, width), BF16)] * planes
-        + [shape((HEAD_DIM, row_count), BF16)] * parts
+        + [shape((HEAD_DIM, row_count), BF16), shape((group - HEAD_DIM, row_count), BF16)] * MEMBERS
         + [
             shape((row_count, width), F32),
             shape((hidden, width), BF16),
@@ -675,7 +676,7 @@
         *att_parts,
         *cot_pieces,
     )
-    return result[:planes], result[planes : planes + parts], result[planes + parts :]
+    return result[:planes], result[planes : planes + 2 * MEMBERS], result[planes + 2 * MEMBERS :]
 
 
 def pad_rows(array, count):
@@ -732,15 +733,16 @@
         offset = (other_plane % spread_planes) * piece + jnp.arange(piece, dtype=jnp.int32)
         return (base[:, :, None] * part_rows + offset).reshape(-1)
 
+    def chunks_for_planes(array):
+        chunks = array.reshape(planes, piece, width)
+        return [pick(chunks, (plane + distance) % planes) for distance in range(planes)]
+
     def to_planes(array):
-        chunks = array.reshape(planes, piece, width)
-        pieces = [pick(chunks, plane)]
-        for distance in range(1, planes):
-            chunk = pick(chunks, (plane + distance) % planes)
-            pieces.append(shift_planes(chunk, distance))
-        return pieces
-
-    own_pieces = to_planes(layer_input)
+        chunks = chunks_for_planes(array)
+        return [chunks[0]] + [shift_planes(chunks[k], k) for k in range(1, planes)]
+
+    stage = lax.optimization_barrier
+
     own_group = core * 2 + head_place
     heads_here = HEADS // MEMBERS
     piece_rows = (share // 8 + 1) * 8
@@ -751,19 +753,34 @@
     tail_rows = jnp.pad(bias_row[None], ((0, piece_rows - share - 1), (0, 0)))
     tail_rows = jnp.broadcast_to(tail_rows, (MEMBERS,) + tail_rows.shape)
     by_group = jnp.concatenate([by_group, tail_rows], axis=1)
-    by_group, own_pieces[1] = lax.optimization_barrier((by_group, own_pieces[1]))
     by_member = reorder_members(by_group, core, head_place)
+
+    chunks = chunks_for_planes(layer_input)
+    own_pieces = chunks[:1] + [shift_planes(chunks[k], k) for k in range(1, planes - 1)]
+    head_pieces = [swap_member(own_pieces[0], 1)]
     gathered = [by_member[0]] + [
         swap_member(by_member[member], member) for member in range(1, MEMBERS)
     ]
+    own_pieces, head_pieces, gathered, chunks = stage((own_pieces, head_pieces, gathered, chunks))
+    own_pieces = own_pieces + [shift_planes(chunks[-1], planes - 1)]
+    head_pieces = head_pieces + [swap_member(own_pieces[k], 1) for k in range(1, planes - 1)]
+    core_pieces = [swap_member(own_pieces[0], 2)]
+    both_pieces = [swap_member(head_pieces[0], 2)]
     gathered = reorder_members(jnp.stack(gathered), core, head_place)
-    gathered = in_order(
-        [gathered] + [shift_planes(gathered, distance) for distance in range(1, planes)], plane
+    gathered = [gathered] + [shift_planes(gathered, distance) for distance in range(1, planes)]
+    own_pieces, head_pieces, core_pieces, both_pieces, gathered = stage(
+        (own_pieces, head_pieces, core_pieces, both_pieces, gathered)
     )
-    gathered = in_order(
-        [gathered] + [shift_batch(gathered, distance) for distance in range(1, batches)],
-        batch_place,
+    core_pieces = core_pieces + [swap_member(own_pieces[k], 2) for k in range(1, planes)]
+    both_pieces = both_pieces + [swap_member(head_pieces[k], 2) for k in range(1, planes - 1)]
+    head_pieces = head_pieces + [swap_member(own_pieces[-1], 1)]
+    gathered = in_order(gathered, plane)
+    gathered = [gathered] + [shift_batch(gathered, distance) for distance in range(1, batches)]
+    core_pieces, both_pieces, head_pieces, gathered = stage(
+        (core_pieces, both_pieces, head_pieces, gathered)
     )
+    both_pieces = both_pieces + [swap_member(head_pieces[-1], 2)]
+    gathered = in_order(gathered, batch_place)
     gathered = gathered.reshape(devices, piece_rows, 3 * group)
     own_weight = gathered[:, :share].reshape(width, 3 * group)
     bias_query = gathered[:, share, :share].reshape(MEMBERS, group)
@@ -776,9 +793,6 @@
         ]
     ).astype(F32)
 
-    head_pieces = [swap_member(part_in, 1) for part_in in own_pieces]
-    core_pieces = [swap_member(part_in, 2) for part_in in own_pieces]
-    both_pieces = [swap_member(part_in, 2) for part_in in head_pieces]
     all_pieces = own_pieces + head_pieces + core_pieces + both_pieces
     valid_own = places(plane) < seq_length
     row_starts = (own_group ^ jnp.arange(MEMBERS, dtype=jnp.int32)) * group
@@ -923,28 +937,6 @@
     chunk_rows = width // (batches * planes)
     block_rows = chunk_rows + -chunk_rows % 16 + 16
 
-    def finish_weights(chunks):
-        columns = chunks.shape[-1]
-        total = pick(chunks, batch_place).astype(F32)
-        for distance in range(1, batches):
-            sent = pick(chunks, (batch_place + distance) % batches)
-            total = total + shift_batch(sent, distance).astype(F32)
-        sending = total.astype(BF16)
-        total = pick(total, plane)
-        for distance in range(1, planes):
-            sent = pick(sending, (plane + distance) % planes)
-            total = total + shift_planes(sent, distance).astype(F32)
-        bias_total = total[chunk_rows]
-        member_rows = total[:chunk_rows].reshape(MEMBERS, share, columns)
-        member_rows = reorder_members(member_rows, core, head_place)
-        tail = jnp.broadcast_to(bias_total, (MEMBERS, piece_rows - share, columns))
-        sending = jnp.concatenate([member_rows, tail], axis=1)
-        got = [sending[0]] + [
-            swap_member(sending[member], member) for member in range(1, MEMBERS)
-        ]
-        got = reorder_members(jnp.stack(got), core, head_place)
-        return got.reshape(MEMBERS, piece_rows, columns // (3 * HEAD_DIM), 3, HEAD_DIM)
-
     def own_places(found):
         own = {index: array for index, array in found.items() if index < MEMBERS}
         for index, array in found.items():
@@ -960,21 +952,23 @@
     pieces_here = MEMBERS * spread_planes
     kept_slots, sent_slots = [], []
     for slot in range(heads_here):
-        grad_side = [
-            send(member, grad_att[member * heads_here + slot]) for member in range(MEMBERS)
-        ]
+        if slot < 2:
+            grad_sent = [send(member, grad_att[2 * member + slot]) for member in range(MEMBERS)]
         slot_at = tuple(start + slot for start in starts)
         given = (queries, keys, values, slot_at, mask_rows, sums[slot], outs[slot])
+        place = max(slot - 1, 0)
         if slot == 1:
-            output_pieces, grad_side = lax.optimization_barrier((output_pieces, grad_side))
+            output_pieces, grad_sent = lax.optimization_barrier((output_pieces, grad_sent))
         if slot < heads_here - 1:
             chosen = range(pieces_here)
+            grad_side = [(array, place) for array in grad_sent]
             found, unused = attention_backward(*given, grad_side, chosen)
             own = own_places(dict(zip(chosen, found)))
             kept_slots.append([[own[member]] for member in range(MEMBERS)])
             sent_slots.append([[send(member, own[member])] for member in range(MEMBERS)])
             continue
-        sent_slots[:-1], grad_side = lax.optimization_barrier((sent_slots[:-1], grad_side))
+        sent_slots[:-1], grad_sent = lax.optimization_barrier((sent_slots[:-1], grad_sent))
+        grad_side = [(array, place) for array in grad_sent]
         chosen = range(1, pieces_here, 2)
         found, (partial,) = attention_backward(*given, grad_side, chosen, last=False)
         own = own_places(dict(zip(chosen, found)))
@@ -994,14 +988,37 @@
     input_pieces = input_grad_step(
         row_starts, grad_input, slot_weights[-1:], [last_sent], planes, BF16
     )
-    input_pieces = [input_pieces[0]] + [
-        shift_planes(input_pieces[distance], -distance) for distance in range(1, planes)
+    chunks = weight_grad(all_pieces, kept_slots, batches * planes, chunk_rows, block_rows)
+    chunks = chunks.reshape((batches, planes) + chunks.shape[1:])
+    parts = [pick(chunks, (batch_place + distance) % batches) for distance in range(batches)]
+
+    def move(first, last):
+        return [shift_planes(input_pieces[k], -k) for k in range(first, last)]
+
+    parts, input_pieces = stage((parts, input_pieces))
+    arrived = move(1, 2)
+    moved = [shift_batch(parts[distance], distance) for distance in range(1, batches)]
+    arrived, moved = stage((arrived, moved))
+    total = sum([part_in.astype(F32) for part_in in [parts[0]] + moved])
+    sending = total.astype(BF16)
+    sending = [pick(sending, (plane + distance) % planes) for distance in range(1, planes)]
+    arrived = arrived + move(2, planes - 1)
+    moved = [shift_planes(sending[k - 1], k) for k in range(1, planes)]
+    arrived, moved, total = stage((arrived, moved, total))
+    total = pick(total, plane) + sum([part_in.astype(F32) for part_in in moved])
+    columns = total.shape[-1]
+    member_rows = total[:chunk_rows].reshape(MEMBERS, share, columns)
+    member_rows = reorder_members(member_rows, core, head_place)
+    tail = jnp.broadcast_to(total[chunk_rows], (MEMBERS, piece_rows - share, columns))
+    sending = jnp.concatenate([member_rows, tail], axis=1)
+    arrived = arrived + move(planes - 1, planes)
+    got = [sending[0]] + [
+        swap_member(sending[member], member) for member in range(1, MEMBERS)
     ]
-    input_grad = collect(input_pieces, plane).reshape(seqs, part_rows, width)
+    got = reorder_members(jnp.stack(got), core, head_place)
+    got = got.reshape(MEMBERS, piece_rows, heads_here, 3, HEAD_DIM)
+    input_grad = collect([input_pieces[0]] + arrived, plane).reshape(seqs, part_rows, width)
     output = collect(output_pieces, plane).reshape(seqs, part_rows, width)
-
-    chunks = weight_grad(all_pieces, kept_slots, batches * planes, chunk_rows, block_rows)
-    got = finish_weights(chunks.reshape((batches, planes) + chunks.shape[1:]))
     matrices = [
         jnp.swapaxes(got[:, :share, :, i], 0, 1).reshape(share, width) for i in range(3)
     ]

time: 617 us -> 575 us (0.932); the launches traced: 608 us -> 573 us
  waiting for transfers between devices: 117 us -> 89.1 us
  starting transfers between devices: 95.6 us -> 85.2 us
    ppermute x16 -> x15, waiting for transfers between devices: 35.2 us -> 19.5 us  [swap_member(): return lax.ppermute(array, 'head', [(0, 1), (1, 0)])]
    pallas_call x1, Pallas kernels: 59.4 us -> 72.1 us  [layer_rows(): pl.pallas_call(functools.partial(layer_kernel, blocks, planes, parts), gr...]
    ppermute x18, waiting for transfers between devices: 68.6 us -> 57.8 us  [shift_planes(): return lax.ppermute(array, 'blk', route)]
    pallas_call x4, Pallas kernels: 90.2 us -> 80.2 us  [attention_forward(): pl.pallas_call(functools.partial(forward_kernel, min(512, key_count), mem...]
    ppermute x2, waiting for transfers between devices: 11.3 us -> 3.1 us  [shift_batch(): lax.ppermute(array, 'batch', [(i, (i + distance) % size) for i in range(s...]
    ppermute x12 -> x11, waiting for transfers between devices: 1.21 us -> 8.66 us  [swap_member(): return lax.ppermute(array, ('blk', 'head'), route)]
    ppermute x18, starting transfers between devices: 60.4 us -> 53.5 us  [shift_planes(): return lax.ppermute(array, 'blk', route)]
    ppermute x16 -> x15, starting transfers between devices: 17.7 us -> 14.5 us  [swap_member(): return lax.ppermute(array, 'head', [(0, 1), (1, 0)])]
  transfers between devices with their start and end apart: 71 -> 68, of which waited for: 12 -> 17; matrix products, arithmetic and copies ran while one was open for 6% -> 6% of each run, Pallas kernels for 55% -> 59%
where the time goes in v5:
time: 575 us; the launch traced here: 573 us
  Pallas kernels  337 us (59%)
  waiting for transfers between devices  89.1 us (15%)
  starting transfers between devices  85.2 us (15%)
  local copies, waits for them, and re-layouts  34.4 us (6%)
  between operations  15.6 us (3%)
  other arithmetic  12.1 us (2%)
    pallas_call x4, Pallas kernels, attention_backward(): pl.pallas_call(functools.partial(backward_kernel, min(1024, query_count),...  145 us
    pallas_call x4, Pallas kernels, attention_forward(): pl.pallas_call(functools.partial(forward_kernel, min(512, key_count), mem...  80.2 us
    pallas_call x1, Pallas kernels, layer_rows(): pl.pallas_call(functools.partial(layer_kernel, blocks, planes, parts), gr...  72.1 us
    ppermute x18, waiting for transfers between devices, shift_planes(): return lax.ppermute(array, 'blk', route)  57.8 us
    ppermute x18, starting transfers between devices, shift_planes(): return lax.ppermute(array, 'blk', route)  53.5 us
    ppermute x15, waiting for transfers between devices, swap_member(): return lax.ppermute(array, 'head', [(0, 1), (1, 0)])  19.5 us
    pallas_call x2, Pallas kernels, input_grad_step(): pl.pallas_call(functools.partial(input_grad_kernel, counts_of(slots)), gr...  14.6 us
    ppermute x15, starting transfers between devices, swap_member(): return lax.ppermute(array, 'head', [(0, 1), (1, 0)])  14.5 us
  transfers between devices with their start and end apart: 68, of which 17 were waited for; matrix products, arithmetic and copies ran while one was open for 6% of the time, Pallas kernels for 59%

profile of v5, /device:TPU:0, one launch (start us, length us, event | category | flops | bytes accessed | tf_op | source)
XLA Modules:
  0.0 573.0 jit_solution(5880831636425331329)
XLA Ops:
  8.9 3.1 collective-permute-start
  12.0 2.6 collective-permute-start.1
  18.1 7.6 %collective-permute-done.3 = bf16[32,576]{1,0:T(8,128)(2,1)S(1)} collective-permute-done((bf16[32,576]{1,0:T(8,128)(2,1)S(1)}, bf16[32,576]{1,0:T(8,128)(2,1)S(1)}, u32[]{:S(2)}, u32[]{:S(2)}) %collective-permute-start.3) | collective-permute-done | bytes 36896 | tf_op jit(solution)/shard_map/ppermute | solution.py:45
  25.7 3.8 collective-permute-done.5
  29.5 10.4 %collective-permute-done.1.rest_2_ = bf16[256,768]{1,0:T(8,128)(2,1)S(1)} collective-permute-done((bf16[256,768]{1,0:T(8,128)(2,1)S(1)}, bf16[256,768]{1,0:T(8,128)(2,1)S(1)}, u32[]{:S(2)}, u32[]{:S(2)}) %collective-permute-start.1) | collective-permute-done | bytes 393248 | tf_op jit(solution)/shard_map/ppermute | solution.py:34
  40.2 2.2 collective-permute-start.12
  42.4 1.6 collective-permute-start.13
  44.7 4.5 collective-permute-done.11
  50.7 4.6 collective-permute-done.12
  56.8 6.0 %collective-permute-done.6.rest_3_ = bf16[256,768]{1,0:T(8,128)(2,1)} collective-permute-done((bf16[256,768]{1,0:T(8,128)(2,1)S(1)}, bf16[256,768]{1,0:T(8,128)(2,1)}, u32[]{:S(2)}, u32[]{:S(2)}) %collective-permute-start.6) | collective-permute-done | bytes 393248 | tf_op jit(solution)/shard_map/ppermute | solution.py:34
  62.8 4.0 collective-permute-done.8.rest_6_
  67.9 1.6 collective-permute-start.20
  71.8 2.6 concatenate.82
  74.5 7.3 %collective-permute-done.19.rest_7_ = bf16[256,768]{1,0:T(8,128)(2,1)S(1)} collective-permute-done((bf16[256,768]{1,0:T(8,128)(2,1)}, bf16[256,768]{1,0:T(8,128)(2,1)S(1)}, u32[]{:S(2)}, u32[]{:S(2)}) %collective-permute-start.19) | collective-permute-done | bytes 393248 | tf_op jit(solution)/shard_map/ppermute | solution.py:45
  81.8 2.9 collective-permute-done.20
  93.9 9.1 %shard_map.305.q_ref.k_ref.v_ref = bf16[576,4096]{1,0:T(8,128)(2,1)} custom-call(bf16[768,576]{1,0:T(8,128)(2,1)} %bitcast.161, f32[576,1]{1,0:T(8,128)} %copy.106.bias_ref, bf16[256,768]{1,0:T(8,128)(2,1)} %copy-done.3, bf16[256,768]{1,0:T(8,128)(2,1)} %copy-done.38, bf16[256,768]{1,0:T(8,128)(2,1)} %copy-done.39, ...), custom_call_target="tpu_custom_call" | custom-call | flops 3623878656 | bytes 12582912 | tf_op jit(solution)/shard_map/pallas_call | solution.py:315
  103.0 25.9 %shard_map.307 = (bf16[64,1024]{1,0:T(8,128)(2,1)}, bf16[64,1024]{1,0:T(8,128)(2,1)}, bf16[64,1024]{1,0:T(8,128)(2,1)}, bf16[64,1024]{1,0:T(8,128)(2,1)}, f32[1,...) custom-call(bf16[576,4096]{1,0:T(8,128)(2,1)} %shard_map.305.q_ref.k_ref.v_ref, ...), custom_call_target="tpu_custom_call" | custom-call | flops 17179869184 | bytes 2097152 | tf_op jit(solution)/shard_map/pallas_call | solution.py:134
  128.9 25.7 %shard_map.306 = (bf16[64,1024]{1,0:T(8,128)(2,1)}, bf16[64,1024]{1,0:T(8,128)(2,1)}, bf16[64,1024]{1,0:T(8,128)(2,1)}, bf16[64,1024]{1,0:T(8,128)(2,1)}, f32[1,...) custom-call(bf16[576,4096]{1,0:T(8,128)(2,1)} %shard_map.305.q_ref.k_ref.v_ref, ...), custom_call_target="tpu_custom_call" | custom-call | flops 17179869184 | bytes 2097152 | tf_op jit(solution)/shard_map/pallas_call | solution.py:134
  158.3 14.4 %shard_map.309 = (bf16[64,1024]{1,0:T(8,128)(2,1)}, bf16[64,1024]{1,0:T(8,128)(2,1)}, f32[1,1024]{1,0:T(1,128)}, f32[1,1024]{1,0:T(1,128)}) custom-call(bf16[576,4096]{1,0:T(8,128)(2,1)} %shard_map.305.q_ref.k_ref.v_ref, bf16[576,4096]{1,0:T(8,128)(2,1)} %shard_map.305.q_ref.k_ref.v_ref, bf16[576,4096]{1,0:T(8,128)(2,1)} %shard_map.305.q_ref.k_ref.v_ref, ...), custom_call_target="tpu_custom_call" | custom-call | flops 8589934592 | bytes 2097152 | tf_op jit(solution)/shard_map/pallas_call | solution.py:134
  173.5 7.2 %collective-permute-start.31 = (bf16[256,768]{1,0:T(8,128)(2,1)S(1)}, bf16[256,768]{1,0:T(8,128)(2,1)S(1)}, u32[]{:S(2)}, u32[]{:S(2)}) collective-permute-start(bf16[256,768]{1,0:T(8,128)(2,1)S(1)} %get-tuple-element.289), channel_id=1, source_target_pairs={{0,4},{2,6},{4,8},{6,10},{8,12},{10,14},{12,0},{14,2},{1,5},{3,7},... | collective-permute-start | bytes 1179656 | tf_op jit(solution)/shard_map/ppermute | solution.py:34
  180.7 3.3 collective-permute-start.32
  185.6 14.2 %shard_map.308 = (bf16[64,1024]{1,0:T(8,128)(2,1)}, bf16[64,1024]{1,0:T(8,128)(2,1)}, f32[1,1024]{1,0:T(1,128)}, f32[1,1024]{1,0:T(1,128)}) custom-call(bf16[576,4096]{1,0:T(8,128)(2,1)} %shard_map.305.q_ref.k_ref.v_ref, bf16[576,4096]{1,0:T(8,128)(2,1)} %shard_map.305.q_ref.k_ref.v_ref, bf16[576,4096]{1,0:T(8,128)(2,1)} %shard_map.305.q_ref.k_ref.v_ref, ...), custom_call_target="tpu_custom_call" | custom-call | flops 8589934592 | bytes 2097152 | tf_op jit(solution)/shard_map/pallas_call | solution.py:134
  203.6 2.6 collective-permute-done.30.rest_18_
  206.3 5.3 collective-permute-done.32.rest_21_
  212.5 72.1 %shard_map.310 = (bf16[256,768]{1,0:T(8,128)(2,1)}, bf16[256,768]{1,0:T(8,128)(2,1)}, bf16[256,768]{1,0:T(8,128)(2,1)}, bf16[256,768]{1,0:T(8,128)(2,1)}, bf16[6...) custom-call(s32[8]{0:T(128)} %pad_add_fusion.info_ref, ...), custom_call_target="tpu_custom_call" | custom-call | flops 28991029248 | bytes 18874368 | tf_op jit(solution)/shard_map/pallas_call | solution.py:627
  286.7 3.1 copy.114
  290.4 1.7 collective-permute-start.42
  292.0 10.7 %collective-permute-start.34 = (bf16[256,768]{1,0:T(8,128)(2,1)S(1)}, bf16[256,768]{1,0:T(8,128)(2,1)S(1)}, u32[]{:S(2)}, u32[]{:S(2)}) collective-permute-start(bf16[256,768]{1,0:T(8,128)(2,1)S(1)} %copy-done.53), channel_id=1, source_target_pairs={{0,12},{2,14},{4,0},{6,2},{8,4},{10,6},{12,8},{14,10},{1,13},{3,15... | collective-permute-start | bytes 1179656 | tf_op jit(solution)/shard_map/ppermute | solution.py:34
  302.8 5.3 fusion.1
  312.0 46.9 %shard_map.312 = (bf16[192,1024]{1,0:T(8,128)(2,1)}, bf16[192,1024]{1,0:T(8,128)(2,1)}, bf16[192,1024]{1,0:T(8,128)(2,1)}, bf16[192,1024]{1,0:T(8,128)(2,1)}) custom-call(bf16[576,4096]{1,0:T(8,128)(2,1)} %shard_map.305.q_ref.k_ref.v_ref, bf16[576,4096]{1,0:T(8,128)(2,1)} %shard_map.305.q_ref.k_ref.v_ref, bf16[576,4096]{1,0:T(8,128)(2,1)} %shard_map.305.q_ref.k_ref.v_ref, ...), custom_call_target="tpu_custom_call" | custom-call | flops 42949672960 | bytes 4194304 | tf_op jit(solution)/shard_map/pallas_call | solution.py:266
  361.2 47.1 %shard_map.313 = (bf16[192,1024]{1,0:T(8,128)(2,1)}, bf16[192,1024]{1,0:T(8,128)(2,1)}, bf16[192,1024]{1,0:T(8,128)(2,1)}, bf16[192,1024]{1,0:T(8,128)(2,1)}) custom-call(bf16[576,4096]{1,0:T(8,128)(2,1)} %shard_map.305.q_ref.k_ref.v_ref, bf16[576,4096]{1,0:T(8,128)(2,1)} %shard_map.305.q_ref.k_ref.v_ref, bf16[576,4096]{1,0:T(8,128)(2,1)} %shard_map.305.q_ref.k_ref.v_ref, ...), custom_call_target="tpu_custom_call" | custom-call | flops 42949672960 | bytes 4194304 | tf_op jit(solution)/shard_map/pallas_call | solution.py:266
  408.9 1.6 collective-permute-start.48
  410.5 25.7 %shard_map.314 = (bf16[128,1024]{1,0:T(8,128)(2,1)}, bf16[128,1024]{1,0:T(8,128)(2,1)}, f32[64,4096]{1,0:T(8,128)}) custom-call(bf16[576,4096]{1,0:T(8,128)(2,1)} %shard_map.305.q_ref.k_ref.v_ref, bf16[576,4096]{1,0:T(8,128)(2,1)} %shard_map.305.q_ref.k_ref.v_ref, bf16[576,4096]{1,0:T(8,128)(2,1)} %shard_map.305.q_ref.k_ref.v_ref, ...), custom_call_target="tpu_custom_call" | custom-call | flops 21474836480 | bytes 4194304 | tf_op jit(solution)/shard_map/pallas_call | solution.py:266
  438.8 8.8 %shard_map.315.acc_ref = f32[1024,768]{1,0:T(8,128)} custom-call(s32[4]{0:T(128)} %copy-done.28, f32[1024,768]{1,0:T(8,128)} %get-tuple-element.245.acc_ref, bf16[32,72,768]{2,1,0:T(8,128)(2,1)} %bitcast.147, bf16[32,72,768]{2,1,0:T(8,128)(2,1)} %bitcast.148, bf16[192,1024]{1,0:T(8,128)(2,1)} %get-tuple-element.246.rest_2_.rest_16_, ...), custom_call_target="tpu_custom_call" | custom-call | flops 2415919104 | bytes 6291456 | tf_op jit(solution)/shard_map/pallas_call | solution.py:415
  447.6 25.5 %shard_map.316 = (bf16[128,1024]{1,0:T(8,128)(2,1)}, bf16[128,1024]{1,0:T(8,128)(2,1)}, bf16[64,1024]{1,0:T(8,128)(2,1)}, bf16[64,1024]{1,0:T(8,128)(2,1)}, bf16...) custom-call(bf16[576,4096]{1,0:T(8,128)(2,1)} %shard_map.305.q_ref.k_ref.v_ref, ...), custom_call_target="tpu_custom_call" | custom-call | flops 21474836480 | bytes 4194304 | tf_op jit(solution)/shard_map/pallas_call | solution.py:266
  474.4 10.2 %shard_map.317 = bf16[8,112,576]{2,1,0:T(8,128)(2,1)} custom-call(bf16[256,768]{1,0:T(8,128)(2,1)} %copy-done.3, bf16[256,768]{1,0:T(8,128)(2,1)} %copy-done.38, bf16[256,768]{1,0:T(8,128)(2,1)} %copy-done.39, bf16[256,768]{1,0:T(8,128)(2,1)} %collective-permute-done.6.rest_3_, bf16[256,768]{1,0:T(8,128)(2,1)} %copy-done.40, ...), custom_call_target="tpu_custom_call" | custom-call | flops 3623878656 | bytes 6291456 | tf_op jit(solution)/shard_map/pallas_call | solution.py:375
  484.6 1.6 collective-permute-start.53
  487.6 2.2 collective-permute-done.53.rest_7_
  491.2 5.8 %shard_map.318 = (bf16[256,768]{1,0:T(8,128)(2,1)}, bf16[256,768]{1,0:T(8,128)(2,1)}, bf16[256,768]{1,0:T(8,128)(2,1)}, bf16[256,768]{1,0:T(8,128)(2,1)}) custom-call(s32[4]{0:T(128)} %copy-done.28, f32[1024,768]{1,0:T(8,128)} %shard_map.315.acc_ref, bf16[32,72,768]{2,1,0:T(8,128)(2,1)} %bitcast.149, bf16[64,1024]{1,0:T(8,128)(2,1)} %get-tuple-element.251.rest_24_.rest_1_, ...), custom_call_target="tpu_custom_call" | custom-call | flops 1207959552 | bytes 6291456 | tf_op jit(solution)/shard_map/pallas_call | solution.py:415
  498.4 3.9 collective-permute-start.55
  502.8 9.4 %collective-permute-done.55.rest_1_ = bf16[256,768]{1,0:T(8,128)(2,1)S(1)} collective-permute-done((bf16[256,768]{1,0:T(8,128)(2,1)}, bf16[256,768]{1,0:T(8,128)(2,1)S(1)}, u32[]{:S(2)}, u32[]{:S(2)}) %collective-permute-start.55) | collective-permute-done | bytes 393248 | tf_op jit(solution)/shard_map/ppermute | solution.py:34
  513.0 14.4 %collective-permute-start.58 = (bf16[112,576]{1,0:T(8,128)(2,1)S(1)}, bf16[112,576]{1,0:T(8,128)(2,1)S(1)}, u32[]{:S(2)}, u32[]{:S(2)}) collective-permute-start(bf16[112,576]{1,0:T(8,128)(2,1)S(1)} %get-tuple-element.310), channel_id=1, source_target_pairs={{0,4},{2,6},{4,8},{6,10},{8,12},{10,14},{12,0},{14,2},{1,5},{3,7},... | collective-permute-start | bytes 387080 | tf_op jit(solution)/shard_map/ppermute | solution.py:34
  527.4 2.4 collective-permute-start.60
  529.9 14.5 %collective-permute-done.57.rest_2_ = bf16[256,768]{1,0:T(8,128)(2,1)S(1)} collective-permute-done((bf16[256,768]{1,0:T(8,128)(2,1)}, bf16[256,768]{1,0:T(8,128)(2,1)S(1)}, u32[]{:S(2)}, u32[]{:S(2)}) %collective-permute-start.57) | collective-permute-done | bytes 393248 | tf_op jit(solution)/shard_map/ppermute | solution.py:34
  544.4 3.1 collective-permute-done.59
  547.8 1.6 collective-permute-start.63
  550.0 2.6 shard_map.311
  553.5 2.6 shard_map.319
  (407 shorter events, 62.0 us)
Async XLA Ops:
  7.2 194.2 %all-gather.5.cloned.1.call-start = ((), (), s32[]{:S(2)}) async-start(), calls=%async_computation.2 | async-start | bytes 11354112 | tf_op jit(solution)/shard_map/all_gather | solution.py:826
  8.9 20.7 %collective-permute-start = (bf16[256,768]{1,0:T(8,128)(2,1)S(1)}, bf16[256,768]{1,0:T(8,128)(2,1)S(1)}, u32[]{:S(2)}, u32[]{:S(2)}) collective-permute-start(bf16[256,768]{1,0:T(8,128)(2,1)S(1)} %get-tuple-element.292), channel_id=1, source_target_pairs={{0,4},{2,6},{4,8},{6,10},{8,12},{10,14},{12,0},{14,2},{1,5},{3,7},... | collective-permute-start | bytes 1179656 | tf_op jit(solution)/shard_map/ppermute | solution.py:34
  12.0 28.0 %collective-permute-start.1 = (bf16[256,768]{1,0:T(8,128)(2,1)S(1)}, bf16[256,768]{1,0:T(8,128)(2,1)S(1)}, u32[]{:S(2)}, u32[]{:S(2)}) collective-permute-start(bf16[256,768]{1,0:T(8,128)(2,1)S(1)} %get-tuple-element.294), channel_id=1, source_target_pairs={{0,8},{2,10},{4,12},{6,14},{8,0},{10,2},{12,4},{14,6},{1,9},{3,11}... | collective-permute-start | bytes 1179656 | tf_op jit(solution)/shard_map/ppermute | solution.py:34
  14.5 25.4 %collective-permute-start.2 = (bf16[256,768]{1,0:T(8,128)(2,1)S(1)}, bf16[256,768]{1,0:T(8,128)(2,1)S(1)}, u32[]{:S(2)}, u32[]{:S(2)}) collective-permute-start(bf16[256,768]{1,0:T(8,128)(2,1)S(1)} %get-tuple-element.173.rest_0_), channel_id=1, source_target_pairs={{0,1},{1,0},{2,3},{3,2},{4,5},{5,4},{6,7},{7,6},{8,9},{9,8},{10,11... | collective-permute-start | bytes 1179656 | tf_op jit(solution)/shard_map/ppermute | solution.py:45
  40.2 15.1 %collective-permute-start.12 = (bf16[4,32,576]{2,1,0:T(8,128)(2,1)S(1)}, bf16[4,32,576]{2,1,0:T(8,128)(2,1)S(1)}, u32[]{:S(2)}, u32[]{:S(2)}) collective-permute-start(bf16[4,32,576]{2,1,0:T(8,128)(2,1)S(1)} %maximum_select_fusion.7), channel_id=1, source_target_pairs={{0,8},{2,10},{4,12},{6,14},{8,0},{10,2},{12,4},{14,6},{1,9},{3,11}... | collective-permute-start | bytes 442376 | tf_op jit(solution)/shard_map/ppermute | solution.py:34
  42.4 14.4 %collective-permute-start.13 = (bf16[4,32,576]{2,1,0:T(8,128)(2,1)S(1)}, bf16[4,32,576]{2,1,0:T(8,128)(2,1)S(1)}, u32[]{:S(2)}, u32[]{:S(2)}) collective-permute-start(bf16[4,32,576]{2,1,0:T(8,128)(2,1)S(1)} %maximum_select_fusion.7), channel_id=1, source_target_pairs={{0,12},{2,14},{4,0},{6,2},{8,4},{10,6},{12,8},{14,10},{1,13},{3,15... | collective-permute-start | bytes 442376 | tf_op jit(solution)/shard_map/ppermute | solution.py:34
  44.0 12.8 %collective-permute-start.10 = (bf16[256,768]{1,0:T(8,128)(2,1)S(1)}, bf16[256,768]{1,0:T(8,128)(2,1)S(1)}, u32[]{:S(2)}, u32[]{:S(2)}) collective-permute-start(bf16[256,768]{1,0:T(8,128)(2,1)S(1)} %collective-permute-done.2.rest_4_), channel_id=1, source_target_pairs={{0,2},{2,0},{4,6},{6,4},{8,10},{10,8},{12,14},{14,12},{1,3},{3,1},... | collective-permute-start | bytes 1179656 | tf_op jit(solution)/shard_map/ppermute | solution.py:47
  44.0 18.8 %collective-permute-start.6 = (bf16[256,768]{1,0:T(8,128)(2,1)S(1)}, bf16[256,768]{1,0:T(8,128)(2,1)}, u32[]{:S(2)}, u32[]{:S(2)}) collective-permute-start(bf16[256,768]{1,0:T(8,128)(2,1)S(1)} %get-tuple-element.153), channel_id=1, source_target_pairs={{0,12},{2,14},{4,0},{6,2},{8,4},{10,6},{12,8},{14,10},{1,13},{3,15... | collective-permute-start | bytes 1179656 | tf_op jit(solution)/shard_map/ppermute | solution.py:34
  49.2 13.7 %collective-permute-start.7 = (bf16[256,768]{1,0:T(8,128)(2,1)S(1)}, bf16[256,768]{1,0:T(8,128)(2,1)}, u32[]{:S(2)}, u32[]{:S(2)}) collective-permute-start(bf16[256,768]{1,0:T(8,128)(2,1)S(1)} %collective-permute-done.rest_1_), channel_id=1, source_target_pairs={{0,1},{1,0},{2,3},{3,2},{4,5},{5,4},{6,7},{7,6},{8,9},{9,8},{10,11... | collective-permute-start | bytes 1179656 | tf_op jit(solution)/shard_map/ppermute | solution.py:45
  67.9 16.8 %collective-permute-start.20 = (bf16[4,4,32,576]{3,2,1,0:T(8,128)(2,1)S(1)}, bf16[4,4,32,576]{3,2,1,0:T(8,128)(2,1)S(1)}, u32[]{:S(2)}, u32[]{:S(2)}) collective-permute-start(bf16[4,4,32,576]{3,2,1,0:T(8,128)(2,1)S(1)} %constant_dynamic-slice_fusion.2), channel_id=1, source_target_pairs={{0,16},{16,0},{1,17},{17,1},{2,18},{18,2},{3,19},{19,3},{4,20},{20... | collective-permute-start | bytes 1769480 | tf_op jit(solution)/shard_map/ppermute | solution.py:39
  84.7 353.0 %all-gather.7.cloned.1.call-start = ((), (), s32[]{:S(2)}) async-start(), calls=%async_computation.3 | async-start | bytes 3649536 | tf_op jit(solution)/shard_map/all_gather | solution.py:831
  86.6 475.2 %reduce-scatter.2.cloned.1.call-start = ((), (), s32[]{:S(2)}) async-start(), calls=%async_computation.1 | async-start | bytes 11354112 | tf_op jit(solution)/shard_map/reduce_scatter | solution.py:930
  154.6 18.9 %collective-permute-start.23 = (bf16[64,1024]{1,0:T(8,128)(2,1)S(1)}, bf16[64,1024]{1,0:T(8,128)(2,1)S(1)}, u32[]{:S(2)}, u32[]{:S(2)}) collective-permute-start(bf16[64,1024]{1,0:T(8,128)(2,1)S(1)} %copy-done.62), channel_id=1, source_target_pairs={{0,1},{1,0},{2,3},{3,2},{4,5},{5,4},{6,7},{7,6},{8,9},{9,8},{10,11... | collective-permute-start | bytes 393224 | tf_op jit(solution)/shard_map/ppermute | solution.py:45
  156.1 24.6 %collective-permute-start.26 = (bf16[64,1024]{1,0:T(8,128)(2,1)S(1)}, bf16[64,1024]{1,0:T(8,128)(2,1)S(1)}, u32[]{:S(2)}, u32[]{:S(2)}) collective-permute-start(bf16[64,1024]{1,0:T(8,128)(2,1)S(1)} %copy-done.63), channel_id=1, source_target_pairs={{0,2},{2,0},{4,6},{6,4},{8,10},{10,8},{12,14},{14,12},{1,3},{3,1},... | collective-permute-start | bytes 393224 | tf_op jit(solution)/shard_map/ppermute | solution.py:47
  156.4 27.7 %collective-permute-start.29 = (bf16[64,1024]{1,0:T(8,128)(2,1)S(1)}, bf16[64,1024]{1,0:T(8,128)(2,1)S(1)}, u32[]{:S(2)}, u32[]{:S(2)}) collective-permute-start(bf16[64,1024]{1,0:T(8,128)(2,1)S(1)} %copy-done.64), channel_id=1, source_target_pairs={{0,3},{1,2},{2,1},{3,0},{4,7},{5,6},{6,5},{7,4},{8,11},{9,10},{10,... | collective-permute-start | bytes 393224 | tf_op jit(solution)/shard_map/ppermute | solution.py:49
  156.8 27.2 %collective-permute-start.22 = (bf16[64,1024]{1,0:T(8,128)(2,1)}, bf16[64,1024]{1,0:T(8,128)(2,1)S(1)}, u32[]{:S(2)}, u32[]{:S(2)}) collective-permute-start(bf16[64,1024]{1,0:T(8,128)(2,1)} %get-tuple-element.190.rest_5_), channel_id=1, source_target_pairs={{0,1},{1,0},{2,3},{3,2},{4,5},{5,4},{6,7},{7,6},{8,9},{9,8},{10,11... | collective-permute-start | bytes 393224 | tf_op jit(solution)/shard_map/ppermute | solution.py:45
  158.3 25.9 %collective-permute-start.25 = (bf16[64,1024]{1,0:T(8,128)(2,1)}, bf16[64,1024]{1,0:T(8,128)(2,1)S(1)}, u32[]{:S(2)}, u32[]{:S(2)}) collective-permute-start(bf16[64,1024]{1,0:T(8,128)(2,1)} %get-tuple-element.193.rest_6_), channel_id=1, source_target_pairs={{0,2},{2,0},{4,6},{6,4},{8,10},{10,8},{12,14},{14,12},{1,3},{3,1},... | collective-permute-start | bytes 393224 | tf_op jit(solution)/shard_map/ppermute | solution.py:47
  173.5 32.7 %collective-permute-start.31 = (bf16[256,768]{1,0:T(8,128)(2,1)S(1)}, bf16[256,768]{1,0:T(8,128)(2,1)S(1)}, u32[]{:S(2)}, u32[]{:S(2)}) collective-permute-start(bf16[256,768]{1,0:T(8,128)(2,1)S(1)} %get-tuple-element.289), channel_id=1, source_target_pairs={{0,4},{2,6},{4,8},{6,10},{8,12},{10,14},{12,0},{14,2},{1,5},{3,7},... | collective-permute-start | bytes 1179656 | tf_op jit(solution)/shard_map/ppermute | solution.py:34
  180.7 30.8 %collective-permute-start.32 = (bf16[256,768]{1,0:T(8,128)(2,1)S(1)}, bf16[256,768]{1,0:T(8,128)(2,1)S(1)}, u32[]{:S(2)}, u32[]{:S(2)}) collective-permute-start(bf16[256,768]{1,0:T(8,128)(2,1)S(1)} %get-tuple-element.288), channel_id=1, source_target_pairs={{0,8},{2,10},{4,12},{6,14},{8,0},{10,2},{12,4},{14,6},{1,9},{3,11}... | collective-permute-start | bytes 1179656 | tf_op jit(solution)/shard_map/ppermute | solution.py:34
  184.0 27.6 %collective-permute-start.33 = (bf16[256,768]{1,0:T(8,128)(2,1)S(1)}, bf16[256,768]{1,0:T(8,128)(2,1)S(1)}, u32[]{:S(2)}, u32[]{:S(2)}) collective-permute-start(bf16[256,768]{1,0:T(8,128)(2,1)S(1)} %get-tuple-element.287), channel_id=1, source_target_pairs={{0,12},{2,14},{4,0},{6,2},{8,4},{10,6},{12,8},{14,10},{1,13},{3,15... | collective-permute-start | bytes 1179656 | tf_op jit(solution)/shard_map/ppermute | solution.py:34
  184.1 15.9 %collective-permute-start.28 = (bf16[64,1024]{1,0:T(8,128)(2,1)S(1)}, bf16[64,1024]{1,0:T(8,128)(2,1)S(1)}, u32[]{:S(2)}, u32[]{:S(2)}) collective-permute-start(bf16[64,1024]{1,0:T(8,128)(2,1)S(1)} %copy-done.65), channel_id=1, source_target_pairs={{0,3},{1,2},{2,1},{3,0},{4,7},{5,6},{6,5},{7,4},{8,11},{9,10},{10,... | collective-permute-start | bytes 393224 | tf_op jit(solution)/shard_map/ppermute | solution.py:49
  184.2 16.3 %collective-permute-start.24 = (bf16[64,1024]{1,0:T(8,128)(2,1)S(1)}, bf16[64,1024]{1,0:T(8,128)(2,1)S(1)}, u32[]{:S(2)}, u32[]{:S(2)}) collective-permute-start(bf16[64,1024]{1,0:T(8,128)(2,1)S(1)} %copy-done.60), channel_id=1, source_target_pairs={{0,1},{1,0},{2,3},{3,2},{4,5},{5,4},{6,7},{7,6},{8,9},{9,8},{10,11... | collective-permute-start | bytes 393224 | tf_op jit(solution)/shard_map/ppermute | solution.py:45
  289.8 18.3 %collective-permute-start.40 = (bf16[64,1024]{1,0:T(8,128)(2,1)S(1)}, bf16[64,1024]{1,0:T(8,128)(2,1)S(1)}, u32[]{:S(2)}, u32[]{:S(2)}) collective-permute-start(bf16[64,1024]{1,0:T(8,128)(2,1)S(1)} %copy-done.77), channel_id=1, source_target_pairs={{0,1},{1,0},{2,3},{3,2},{4,5},{5,4},{6,7},{7,6},{8,9},{9,8},{10,11... | collective-permute-start | bytes 393224 | tf_op jit(solution)/shard_map/ppermute | solution.py:45
  290.4 19.7 %collective-permute-start.41 = (bf16[64,1024]{1,0:T(8,128)(2,1)S(1)}, bf16[64,1024]{1,0:T(8,128)(2,1)S(1)}, u32[]{:S(2)}, u32[]{:S(2)}) collective-permute-start(bf16[64,1024]{1,0:T(8,128)(2,1)S(1)} %copy-done.76), channel_id=1, source_target_pairs={{0,2},{2,0},{4,6},{6,4},{8,10},{10,8},{12,14},{14,12},{1,3},{3,1},... | collective-permute-start | bytes 393224 | tf_op jit(solution)/shard_map/ppermute | solution.py:47
  290.4 19.7 %collective-permute-start.42 = (bf16[64,1024]{1,0:T(8,128)(2,1)S(1)}, bf16[64,1024]{1,0:T(8,128)(2,1)S(1)}, u32[]{:S(2)}, u32[]{:S(2)}) collective-permute-start(bf16[64,1024]{1,0:T(8,128)(2,1)S(1)} %copy-done.75), channel_id=1, source_target_pairs={{0,3},{1,2},{2,1},{3,0},{4,7},{5,6},{6,5},{7,4},{8,11},{9,10},{10,... | collective-permute-start | bytes 393224 | tf_op jit(solution)/shard_map/ppermute | solution.py:49
  292.0 67.7 %collective-permute-start.34 = (bf16[256,768]{1,0:T(8,128)(2,1)S(1)}, bf16[256,768]{1,0:T(8,128)(2,1)S(1)}, u32[]{:S(2)}, u32[]{:S(2)}) collective-permute-start(bf16[256,768]{1,0:T(8,128)(2,1)S(1)} %copy-done.53), channel_id=1, source_target_pairs={{0,12},{2,14},{4,0},{6,2},{8,4},{10,6},{12,8},{14,10},{1,13},{3,15... | collective-permute-start | bytes 1179656 | tf_op jit(solution)/shard_map/ppermute | solution.py:34
  309.1 52.0 %collective-permute-start.35 = (bf16[256,768]{1,0:T(8,128)(2,1)S(1)}, bf16[256,768]{1,0:T(8,128)(2,1)S(1)}, u32[]{:S(2)}, u32[]{:S(2)}) collective-permute-start(bf16[256,768]{1,0:T(8,128)(2,1)S(1)} %copy-done.52), channel_id=1, source_target_pairs={{0,8},{2,10},{4,12},{6,14},{8,0},{10,2},{12,4},{14,6},{1,9},{3,11}... | collective-permute-start | bytes 1179656 | tf_op jit(solution)/shard_map/ppermute | solution.py:34
  310.0 51.1 %collective-permute-start.36 = (bf16[256,768]{1,0:T(8,128)(2,1)S(1)}, bf16[256,768]{1,0:T(8,128)(2,1)S(1)}, u32[]{:S(2)}, u32[]{:S(2)}) collective-permute-start(bf16[256,768]{1,0:T(8,128)(2,1)S(1)} %copy-done.51), channel_id=1, source_target_pairs={{0,4},{2,6},{4,8},{6,10},{8,12},{10,14},{12,0},{14,2},{1,5},{3,7},... | collective-permute-start | bytes 1179656 | tf_op jit(solution)/shard_map/ppermute | solution.py:34
  310.1 48.8 %collective-permute-start.38 = (bf16[128,1024]{1,0:T(8,128)(2,1)S(1)}, bf16[128,1024]{1,0:T(8,128)(2,1)S(1)}, u32[]{:S(2)}, u32[]{:S(2)}) collective-permute-start(bf16[128,1024]{1,0:T(8,128)(2,1)S(1)} %copy-done.58), channel_id=1, source_target_pairs={{0,2},{2,0},{4,6},{6,4},{8,10},{10,8},{12,14},{14,12},{1,3},{3,1},... | collective-permute-start | bytes 786440 | tf_op jit(solution)/shard_map/ppermute | solution.py:47
  310.7 48.7 %collective-permute-start.39 = (bf16[128,1024]{1,0:T(8,128)(2,1)S(1)}, bf16[128,1024]{1,0:T(8,128)(2,1)S(1)}, u32[]{:S(2)}, u32[]{:S(2)}) collective-permute-start(bf16[128,1024]{1,0:T(8,128)(2,1)S(1)} %copy-done.57), channel_id=1, source_target_pairs={{0,3},{1,2},{2,1},{3,0},{4,7},{5,6},{6,5},{7,4},{8,11},{9,10},{10,... | collective-permute-start | bytes 786440 | tf_op jit(solution)/shard_map/ppermute | solution.py:49
  358.9 50.0 %collective-permute-start.43 = (bf16[192,1024]{1,0:T(8,128)(2,1)}, bf16[192,1024]{1,0:T(8,128)(2,1)S(1)}, u32[]{:S(2)}, u32[]{:S(2)}) collective-permute-start(bf16[192,1024]{1,0:T(8,128)(2,1)} %get-tuple-element.221.rest_17_), channel_id=1, source_target_pairs={{0,1},{1,0},{2,3},{3,2},{4,5},{5,4},{6,7},{7,6},{8,9},{9,8},{10,11... | collective-permute-start | bytes 1179656 | tf_op jit(solution)/shard_map/ppermute | solution.py:45
  359.4 51.1 %collective-permute-start.44 = (bf16[192,1024]{1,0:T(8,128)(2,1)}, bf16[192,1024]{1,0:T(8,128)(2,1)S(1)}, u32[]{:S(2)}, u32[]{:S(2)}) collective-permute-start(bf16[192,1024]{1,0:T(8,128)(2,1)} %get-tuple-element.222.rest_18_), channel_id=1, source_target_pairs={{0,2},{2,0},{4,6},{6,4},{8,10},{10,8},{12,14},{14,12},{1,3},{3,1},... | collective-permute-start | bytes 1179656 | tf_op jit(solution)/shard_map/ppermute | solution.py:47
  359.7 50.8 %collective-permute-start.45 = (bf16[192,1024]{1,0:T(8,128)(2,1)}, bf16[192,1024]{1,0:T(8,128)(2,1)S(1)}, u32[]{:S(2)}, u32[]{:S(2)}) collective-permute-start(bf16[192,1024]{1,0:T(8,128)(2,1)} %get-tuple-element.223.rest_19_), channel_id=1, source_target_pairs={{0,3},{1,2},{2,1},{3,0},{4,7},{5,6},{6,5},{7,4},{8,11},{9,10},{10,... | collective-permute-start | bytes 1179656 | tf_op jit(solution)/shard_map/ppermute | solution.py:49
  408.3 29.5 %collective-permute-start.46 = (bf16[192,1024]{1,0:T(8,128)(2,1)}, bf16[192,1024]{1,0:T(8,128)(2,1)S(1)}, u32[]{:S(2)}, u32[]{:S(2)}) collective-permute-start(bf16[192,1024]{1,0:T(8,128)(2,1)} %get-tuple-element.233.rest_21_), channel_id=1, source_target_pairs={{0,1},{1,0},{2,3},{3,2},{4,5},{5,4},{6,7},{7,6},{8,9},{9,8},{10,11... | collective-permute-start | bytes 1179656 | tf_op jit(solution)/shard_map/ppermute | solution.py:45
  408.9 28.9 %collective-permute-start.47 = (bf16[192,1024]{1,0:T(8,128)(2,1)}, bf16[192,1024]{1,0:T(8,128)(2,1)S(1)}, u32[]{:S(2)}, u32[]{:S(2)}) collective-permute-start(bf16[192,1024]{1,0:T(8,128)(2,1)} %get-tuple-element.234.rest_22_), channel_id=1, source_target_pairs={{0,2},{2,0},{4,6},{6,4},{8,10},{10,8},{12,14},{14,12},{1,3},{3,1},... | collective-permute-start | bytes 1179656 | tf_op jit(solution)/shard_map/ppermute | solution.py:47
  408.9 28.9 %collective-permute-start.48 = (bf16[192,1024]{1,0:T(8,128)(2,1)}, bf16[192,1024]{1,0:T(8,128)(2,1)S(1)}, u32[]{:S(2)}, u32[]{:S(2)}) collective-permute-start(bf16[192,1024]{1,0:T(8,128)(2,1)} %get-tuple-element.235.rest_23_), channel_id=1, source_target_pairs={{0,3},{1,2},{2,1},{3,0},{4,7},{5,6},{6,5},{7,4},{8,11},{9,10},{10,... | collective-permute-start | bytes 1179656 | tf_op jit(solution)/shard_map/ppermute | solution.py:49
  436.2 48.3 %collective-permute-start.50 = (bf16[128,1024]{1,0:T(8,128)(2,1)}, bf16[128,1024]{1,0:T(8,128)(2,1)S(1)}, u32[]{:S(2)}, u32[]{:S(2)}) collective-permute-start(bf16[128,1024]{1,0:T(8,128)(2,1)} %get-tuple-element.254.rest_27_), channel_id=1, source_target_pairs={{0,1},{1,0},{2,3},{3,2},{4,5},{5,4},{6,7},{7,6},{8,9},{9,8},{10,11... | collective-permute-start | bytes 786440 | tf_op jit(solution)/shard_map/ppermute | solution.py:45
  436.8 50.7 %collective-permute-start.54 = (bf16[128,1024]{1,0:T(8,128)(2,1)}, bf16[128,1024]{1,0:T(8,128)(2,1)S(1)}, u32[]{:S(2)}, u32[]{:S(2)}) collective-permute-start(bf16[128,1024]{1,0:T(8,128)(2,1)} %get-tuple-element.258.rest_31_), channel_id=1, source_target_pairs={{0,3},{1,2},{2,1},{3,0},{4,7},{5,6},{6,5},{7,4},{8,11},{9,10},{10,... | collective-permute-start | bytes 786440 | tf_op jit(solution)/shard_map/ppermute | solution.py:49
  473.1 16.8 %collective-permute-start.52 = (bf16[128,1024]{1,0:T(8,128)(2,1)}, bf16[128,1024]{1,0:T(8,128)(2,1)S(1)}, u32[]{:S(2)}, u32[]{:S(2)}) collective-permute-start(bf16[128,1024]{1,0:T(8,128)(2,1)} %get-tuple-element.256.rest_29_), channel_id=1, source_target_pairs={{0,2},{2,0},{4,6},{6,4},{8,10},{10,8},{12,14},{14,12},{1,3},{3,1},... | collective-permute-start | bytes 786440 | tf_op jit(solution)/shard_map/ppermute | solution.py:47
  473.8 13.8 %collective-permute-start.49 = (bf16[64,1024]{1,0:T(8,128)(2,1)}, bf16[64,1024]{1,0:T(8,128)(2,1)S(1)}, u32[]{:S(2)}, u32[]{:S(2)}) collective-permute-start(bf16[64,1024]{1,0:T(8,128)(2,1)} %get-tuple-element.253.rest_26_), channel_id=1, source_target_pairs={{0,1},{1,0},{2,3},{3,2},{4,5},{5,4},{6,7},{7,6},{8,9},{9,8},{10,11... | collective-permute-start | bytes 393224 | tf_op jit(solution)/shard_map/ppermute | solution.py:45
  474.4 13.2 %collective-permute-start.51 = (bf16[64,1024]{1,0:T(8,128)(2,1)}, bf16[64,1024]{1,0:T(8,128)(2,1)S(1)}, u32[]{:S(2)}, u32[]{:S(2)}) collective-permute-start(bf16[64,1024]{1,0:T(8,128)(2,1)} %get-tuple-element.255.rest_28_), channel_id=1, source_target_pairs={{0,2},{2,0},{4,6},{6,4},{8,10},{10,8},{12,14},{14,12},{1,3},{3,1},... | collective-permute-start | bytes 393224 | tf_op jit(solution)/shard_map/ppermute | solution.py:47
  497.0 15.3 %collective-permute-start.56 = (bf16[4,112,576]{2,1,0:T(8,128)(2,1)S(1)}, bf16[4,112,576]{2,1,0:T(8,128)(2,1)S(1)}, u32[]{:S(2)}, u32[]{:S(2)}) collective-permute-start(bf16[4,112,576]{2,1,0:T(8,128)(2,1)S(1)} %get-tuple-element.266), channel_id=1, source_target_pairs={{0,16},{16,0},{1,17},{17,1},{2,18},{18,2},{3,19},{19,3},{4,20},{20... | collective-permute-start | bytes 1548296 | tf_op jit(solution)/shard_map/ppermute | solution.py:39
  498.4 13.7 %collective-permute-start.55 = (bf16[256,768]{1,0:T(8,128)(2,1)}, bf16[256,768]{1,0:T(8,128)(2,1)S(1)}, u32[]{:S(2)}, u32[]{:S(2)}) collective-permute-start(bf16[256,768]{1,0:T(8,128)(2,1)} %get-tuple-element.265), channel_id=1, source_target_pairs={{0,12},{2,14},{4,0},{6,2},{8,4},{10,6},{12,8},{14,10},{1,13},{3,15... | collective-permute-start | bytes 1179656 | tf_op jit(solution)/shard_map/ppermute | solution.py:34
  502.3 42.1 %collective-permute-start.57 = (bf16[256,768]{1,0:T(8,128)(2,1)}, bf16[256,768]{1,0:T(8,128)(2,1)S(1)}, u32[]{:S(2)}, u32[]{:S(2)}) collective-permute-start(bf16[256,768]{1,0:T(8,128)(2,1)} %get-tuple-element.268), channel_id=1, source_target_pairs={{0,8},{2,10},{4,12},{6,14},{8,0},{10,2},{12,4},{14,6},{1,9},{3,11}... | collective-permute-start | bytes 1179656 | tf_op jit(solution)/shard_map/ppermute | solution.py:34
  513.0 31.4 %collective-permute-start.58 = (bf16[112,576]{1,0:T(8,128)(2,1)S(1)}, bf16[112,576]{1,0:T(8,128)(2,1)S(1)}, u32[]{:S(2)}, u32[]{:S(2)}) collective-permute-start(bf16[112,576]{1,0:T(8,128)(2,1)S(1)} %get-tuple-element.310), channel_id=1, source_target_pairs={{0,4},{2,6},{4,8},{6,10},{8,12},{10,14},{12,0},{14,2},{1,5},{3,7},... | collective-permute-start | bytes 387080 | tf_op jit(solution)/shard_map/ppermute | solution.py:34
  527.4 20.0 %collective-permute-start.59 = (bf16[112,576]{1,0:T(8,128)(2,1)S(1)}, bf16[112,576]{1,0:T(8,128)(2,1)S(1)}, u32[]{:S(2)}, u32[]{:S(2)}) collective-permute-start(bf16[112,576]{1,0:T(8,128)(2,1)S(1)} %get-tuple-element.309), channel_id=1, source_target_pairs={{0,8},{2,10},{4,12},{6,14},{8,0},{10,2},{12,4},{14,6},{1,9},{3,11}... | collective-permute-start | bytes 387080 | tf_op jit(solution)/shard_map/ppermute | solution.py:34
  527.4 20.0 %collective-permute-start.60 = (bf16[112,576]{1,0:T(8,128)(2,1)S(1)}, bf16[112,576]{1,0:T(8,128)(2,1)S(1)}, u32[]{:S(2)}, u32[]{:S(2)}) collective-permute-start(bf16[112,576]{1,0:T(8,128)(2,1)S(1)} %get-tuple-element.308), channel_id=1, source_target_pairs={{0,12},{2,14},{4,0},{6,2},{8,4},{10,6},{12,8},{14,10},{1,13},{3,15... | collective-permute-start | bytes 387080 | tf_op jit(solution)/shard_map/ppermute | solution.py:34
  529.9 22.9 %collective-permute-start.61 = (bf16[256,768]{1,0:T(8,128)(2,1)S(1)}, bf16[256,768]{1,0:T(8,128)(2,1)S(1)}, u32[]{:S(2)}, u32[]{:S(2)}) collective-permute-start(bf16[256,768]{1,0:T(8,128)(2,1)S(1)} %copy-done.50), channel_id=1, source_target_pairs={{0,4},{2,6},{4,8},{6,10},{8,12},{10,14},{12,0},{14,2},{1,5},{3,7},... | collective-permute-start | bytes 1179656 | tf_op jit(solution)/shard_map/ppermute | solution.py:34
  (105 other events, 1244.9 us)
Sparse Core Ops, SparseCore 0:
  84.8 102.4 all-gather.4
  190.3 68.5 all-gather.6
  308.3 148.7 reduce-scatter.1

commit v6 on v5

--- a/solution.py
+++ b/solution.py
@@ -32,6 +32,12 @@
     size = lax.axis_size("blk")
     route = [(i, (i + CORES * distance) % size) for i in range(size)]
     return lax.ppermute(array, "blk", route)
+
+
+def exchange_planes(stack):
+    size = lax.axis_size("blk")
+    groups = [list(range(core, size, CORES)) for core in range(CORES)]
+    return lax.all_to_all(stack, "blk", 0, 0, axis_index_groups=groups, tiled=True)
 
 
 def shift_batch(array, distance):
@@ -300,13 +306,19 @@
 
 
 def project_kernel(weight_ref, bias_ref, *rest):
-    piece_refs, out_ref = rest[:-1], rest[-1]
-    weight = weight_ref[...].astype(F32).T.astype(BF16)
-    step = out_ref.shape[1] // MEMBERS
+    piece_refs, (out_ref, weight) = rest[:-2], rest[-2:]
+    step = pl.program_id(0)
+
+    @pl.when(step == 0)
+    def _():
+        weight[...] = weight_ref[...].astype(F32).T.astype(BF16)
+
     for member in range(MEMBERS):
-        lanes = slice(member * step, (member + 1) * step)
-        rows = joined_rows(piece_refs, member)
-        out_ref[:, lanes] = (dot(weight, rows, 1, 1) + bias_ref[...]).astype(BF16)
+
+        @pl.when(step == member)
+        def _(member=member):
+            rows = joined_rows(piece_refs, member)
+            out_ref[...] = (dot(weight[...], rows, 1, 1) + bias_ref[...]).astype(BF16)
 
 
 def project(weight, bias_column, pieces):
@@ -314,10 +326,11 @@
     columns = weight.shape[1]
     return pl.pallas_call(
         project_kernel,
-        grid=(1,),
+        grid=(MEMBERS,),
         in_specs=[whole(weight.shape), whole(bias_column.shape)] + [whole((rows, width))] * count,
-        out_specs=whole((columns, count * rows)),
+        out_specs=pl.BlockSpec((columns, count * rows // MEMBERS), lambda i: (0, i)),
         out_shape=jax.ShapeDtypeStruct((columns, count * rows), BF16),
+        scratch_shapes=[pltpu.VMEM((columns, width), BF16)],
         compiler_params=pltpu.CompilerParams(vmem_limit_bytes=VMEM_LIMIT),
         cost_estimate=pl.CostEstimate(
             flops=2 * count * rows * width * columns,
@@ -391,9 +404,16 @@
     slots = len(counts)
     weight_refs, rest = rest[:slots], rest[slots:]
     grads = regroup(rest[: sum(map(sum, counts))], counts)
-    out_refs, joined = rest[sum(map(sum, counts)) : -1], rest[-1]
+    out_refs, (joined, weights) = rest[sum(map(sum, counts)) : -2], rest[-2:]
+    width = acc_ref.shape[1]
+    step = pl.program_id(0)
+
+    @pl.when(step == 0)
+    def _():
+        for slot in range(slots):
+            weights[slot] = weight_refs[slot][...].reshape(width, width)
+
     total = acc_ref[...]
-    width = total.shape[1]
     for slot, members in enumerate(grads):
         for member, refs in enumerate(members):
             start = info_ref[member]
@@ -401,28 +421,40 @@
                 height = ref.shape[0]
                 joined[slot, pl.ds(pl.multiple_of(start, HEAD_DIM), height), :] = ref[...]
                 start = start + height
-        weight = weight_refs[slot][...].reshape(width, width)
-        total = total + dot(joined[slot], weight, 0, 1)
-    rows = acc_ref.shape[0] // len(out_refs)
+        total = total + dot(joined[slot], weights[slot], 0, 1)
+    if len(out_refs) == 1:
+        out_refs[0][...] = total
+        return
+    each = len(out_refs) // MEMBERS
+    rows = acc_ref.shape[0] // each
     for index, out_ref in enumerate(out_refs):
-        out_ref[...] = total[index * rows : (index + 1) * rows].astype(out_ref.dtype)
+
+        @pl.when(step == index // each)
+        def _(index=index, out_ref=out_ref):
+            start = index % each * rows
+            out_ref[...] = total[start : start + rows].astype(out_ref.dtype)
 
 
 def input_grad_step(info, acc, weights, slots, out_count, dtype):
     arrays = flatten(slots)
     rows, width = acc.shape
+    block = rows // MEMBERS
     out = (rows // out_count, width)
+    row_spec = pl.BlockSpec((block, width), lambda i, info: (i, 0))
     return pl.pallas_call(
         functools.partial(input_grad_kernel, counts_of(slots)),
         grid_spec=pltpu.PrefetchScalarGridSpec(
             num_scalar_prefetch=1,
-            grid=(1,),
-            in_specs=[whole(acc.shape)]
+            grid=(MEMBERS,),
+            in_specs=[row_spec]
             + [pl.BlockSpec(dims, functools.partial(lambda at, i, info: at, place))
                for array, dims, place in weights]
-            + [whole(array.shape) for array in arrays],
-            out_specs=[whole(out)] * out_count,
-            scratch_shapes=[pltpu.VMEM((len(slots), width, rows), BF16)],
+            + [pl.BlockSpec((array.shape[0], block), lambda i, info: (0, i)) for array in arrays],
+            out_specs=[row_spec] if out_count == 1 else [whole(out)] * out_count,
+            scratch_shapes=[
+                pltpu.VMEM((len(slots), width, block), BF16),
+                pltpu.VMEM((len(slots), width, width), BF16),
+            ],
         ),
         out_shape=[jax.ShapeDtypeStruct(out, dtype)] * out_count,
         compiler_params=pltpu.CompilerParams(vmem_limit_bytes=VMEM_LIMIT),
@@ -456,16 +488,15 @@
 
 
 def gelu_parts(value):
-    size = jnp.abs(value) * math.sqrt(0.5)
-    t = 1.0 / (1.0 + 0.3275911 * size)
-    bell = jnp.exp(-0.5 * value * value)
-    poly = 1.061405429 * t - 1.453152027
-    poly = poly * t + 1.421413741
-    poly = poly * t - 0.284496736
-    poly = poly * t + 0.254829592
-    tail = 0.5 * poly * t * bell
+    t = 1.0 / (1.0 + (0.3275911 * math.sqrt(0.5)) * jnp.abs(value))
+    bell = jnp.exp2(value * value * (-0.5 * math.log2(math.e)))
+    poly = (0.5 * 1.061405429) * t - 0.5 * 1.453152027
+    poly = poly * t + 0.5 * 1.421413741
+    poly = poly * t - 0.5 * 0.284496736
+    poly = poly * t + 0.5 * 0.254829592
+    tail = poly * t * bell
     share = jnp.where(value < 0, tail, 1.0 - tail)
-    return value * share, share + value * bell * (1.0 / math.sqrt(2.0 * math.pi))
+    return value * share, share + value * (bell * (1.0 / math.sqrt(2.0 * math.pi)))
 
 
 def row_mean(array):
@@ -523,8 +554,11 @@
         bias = inner_bias_ref[pl.ds(block, 1), :]
         weight_inner = packed_inner[...].reshape(width, width)
         weight_outer = packed_outer[...].reshape(width, width)
+        ahead = dot(low[pieces[0], :], weight_inner, 1, 0)
         for k in range(planes):
-            inner = dot(low[pieces[k], :], weight_inner, 1, 0) + bias
+            inner = ahead + bias
+            if k + 1 < planes:
+                ahead = dot(low[pieces[k + 1], :], weight_inner, 1, 0)
             value, derivative = gelu_parts(inner)
             value = value.astype(BF16)
             active[block, pieces[k], :] = value
@@ -561,8 +595,11 @@
         bias_sum = 0.0
         weight_inner = packed_inner[...].reshape(width, width)
         weight_outer = packed_outer[...].reshape(width, width)
+        ahead = dot(grad_low[pieces[0], :], weight_outer, 1, 1)
         for k in range(planes):
-            moved = dot(grad_low[pieces[k], :], weight_outer, 1, 1)
+            moved = ahead
+            if k + 1 < planes:
+                ahead = dot(grad_low[pieces[k + 1], :], weight_outer, 1, 1)
             grad = (moved * slope[block, pieces[k], :]).astype(BF16)
             grad_hidden[pieces[k], :] = grad
             bias_sum += column_sum(grad.astype(F32))
@@ -755,26 +792,49 @@
     by_group = jnp.concatenate([by_group, tail_rows], axis=1)
     by_member = reorder_members(by_group, core, head_place)
 
+    valid_own = places(plane) < seq_length
+    row_starts = (own_group ^ jnp.arange(MEMBERS, dtype=jnp.int32)) * group
+    kept_rows = seq_length - places(plane)[:row_count:piece]
+    info = jnp.concatenate([row_starts, kept_rows])
+
+    def other_plane(distance):
+        return (plane // spread_planes) * spread_planes + (part - distance) % spread_planes
+
+    small = jnp.concatenate(
+        [b_attn_out, norm1_gain, norm1_bias, b_outer, norm2_gain, norm2_bias, b_inner]
+    )
+    small_row = jnp.pad(small, (0, width - small.shape[0]))[None]
+    inner_rows = jnp.swapaxes(w_inner.reshape(share, folds, width), 0, 1).reshape(-1, width)
+    second_pack = jnp.concatenate([w_outer, inner_rows, w_attn_out, small_row])
+    second_pack = pad_rows(second_pack, -second_pack.shape[0] % 8)
+    valid = [valid_own]
+    for distance in range(1, spread_planes):
+        valid.append(places(other_plane(distance)) < seq_length)
+    mask_row = jnp.where(jnp.concatenate(valid), 0.0, NEG_BIG).astype(BF16)[None]
+    mask_rows = pad_rows(mask_row, EXTRA - 1)
+
     chunks = chunks_for_planes(layer_input)
     own_pieces = chunks[:1] + [shift_planes(chunks[k], k) for k in range(1, planes - 1)]
     head_pieces = [swap_member(own_pieces[0], 1)]
     gathered = [by_member[0]] + [
         swap_member(by_member[member], member) for member in range(1, MEMBERS)
     ]
-    own_pieces, head_pieces, gathered, chunks = stage((own_pieces, head_pieces, gathered, chunks))
+    own_pieces, head_pieces, gathered, chunks, info, mask_rows, row_starts = stage(
+        (own_pieces, head_pieces, gathered, chunks, info, mask_rows, row_starts)
+    )
     own_pieces = own_pieces + [shift_planes(chunks[-1], planes - 1)]
     head_pieces = head_pieces + [swap_member(own_pieces[k], 1) for k in range(1, planes - 1)]
     core_pieces = [swap_member(own_pieces[0], 2)]
     both_pieces = [swap_member(head_pieces[0], 2)]
     gathered = reorder_members(jnp.stack(gathered), core, head_place)
-    gathered = [gathered] + [shift_planes(gathered, distance) for distance in range(1, planes)]
-    own_pieces, head_pieces, core_pieces, both_pieces, gathered = stage(
-        (own_pieces, head_pieces, core_pieces, both_pieces, gathered)
+    gathered = exchange_planes(jnp.broadcast_to(gathered[None], (planes,) + gathered.shape))
+    own_pieces, head_pieces, core_pieces, both_pieces, gathered, second_pack = stage(
+        (own_pieces, head_pieces, core_pieces, both_pieces, gathered, second_pack)
     )
+    second = lax.all_gather(second_pack, ALL_AXES, axis=0, tiled=False)
     core_pieces = core_pieces + [swap_member(own_pieces[k], 2) for k in range(1, planes)]
     both_pieces = both_pieces + [swap_member(head_pieces[k], 2) for k in range(1, planes - 1)]
     head_pieces = head_pieces + [swap_member(own_pieces[-1], 1)]
-    gathered = in_order(gathered, plane)
     gathered = [gathered] + [shift_batch(gathered, distance) for distance in range(1, batches)]
     core_pieces, both_pieces, head_pieces, gathered = stage(
         (core_pieces, both_pieces, head_pieces, gathered)
@@ -794,14 +854,6 @@
     ).astype(F32)
 
     all_pieces = own_pieces + head_pieces + core_pieces + both_pieces
-    valid_own = places(plane) < seq_length
-    row_starts = (own_group ^ jnp.arange(MEMBERS, dtype=jnp.int32)) * group
-    kept_rows = seq_length - places(plane)[:row_count:piece]
-    info = jnp.concatenate([row_starts, kept_rows])
-
-    def other_plane(distance):
-        return (plane // spread_planes) * spread_planes + (part - distance) % spread_planes
-
     def shift_parts(array, distance):
         size = lax.axis_size("blk")
         route = []
@@ -815,15 +867,6 @@
     late_cotangent, qkv = lax.optimization_barrier((cotangent, qkv))
     cot_pieces = to_planes(late_cotangent)
 
-    small = jnp.concatenate(
-        [b_attn_out, norm1_gain, norm1_bias, b_outer, norm2_gain, norm2_bias, b_inner]
-    )
-    small_row = jnp.pad(small, (0, width - small.shape[0]))[None]
-    inner_rows = jnp.swapaxes(w_inner.reshape(share, folds, width), 0, 1).reshape(-1, width)
-    second_pack = jnp.concatenate([w_outer, inner_rows, w_attn_out, small_row])
-    second_pack = pad_rows(second_pack, -second_pack.shape[0] % 8)
-    second_pack, gate = lax.optimization_barrier((second_pack, head_pieces[-1]))
-    second = lax.all_gather(second_pack, ALL_AXES, axis=0, tiled=False)
     slots = jnp.stack([w_query, w_key, w_value], axis=1)
     slots = slots.reshape(share, 3, MEMBERS, heads_here, HEAD_DIM)
     slots = jnp.transpose(slots, (3, 0, 2, 1, 4)).reshape(heads_here * share, width)
@@ -864,17 +907,12 @@
 
     queries = keys = values = qkv
     starts = (0, heads_here, 2 * heads_here)
-    valid_keys = [valid_own]
     if spread_planes > 1:
         sides = [qkv[group:]]
         for distance in range(1, spread_planes):
             sides.append(shift_parts(qkv[group:], distance))
-            valid_keys.append(places(other_plane(distance)) < seq_length)
         keys = values = jnp.concatenate(sides, axis=1)
         starts = (0, 0, heads_here)
-    valid = jnp.concatenate(valid_keys)
-    mask_row = jnp.where(valid, 0.0, NEG_BIG).astype(BF16)[None]
-    mask_rows = pad_rows(mask_row, EXTRA - 1)
 
     def to_members(pieces):
         return [pieces[0]] + [
@@ -886,6 +924,8 @@
     for slot in range(heads_here):
         slot_at = tuple(start + slot for start in starts)
         chosen = [range(MEMBERS)] if slot < heads_here - 1 else [far, near]
+        if slot == heads_here - 1:
+            cot_pieces, mask_rows = stage((cot_pieces, mask_rows))
         out, total, moved = {}, {}, {}
         for members in chosen:
             found = attention_forward(queries, keys, values, slot_at, mask_rows, members)
@@ -967,7 +1007,8 @@
             kept_slots.append([[own[member]] for member in range(MEMBERS)])
             sent_slots.append([[send(member, own[member])] for member in range(MEMBERS)])
             continue
-        sent_slots[:-1], grad_sent = lax.optimization_barrier((sent_slots[:-1], grad_sent))
+        output = collect(output_pieces, plane)
+        sent_slots[:-1], grad_sent, output = stage((sent_slots[:-1], grad_sent, output))
         grad_side = [(array, place) for array in grad_sent]
         chosen = range(1, pieces_here, 2)
         found, (partial,) = attention_backward(*given, grad_side, chosen, last=False)
@@ -1005,20 +1046,19 @@
     arrived = arrived + move(2, planes - 1)
     moved = [shift_planes(sending[k - 1], k) for k in range(1, planes)]
     arrived, moved, total = stage((arrived, moved, total))
+    arrived = arrived + move(planes - 1, planes)
     total = pick(total, plane) + sum([part_in.astype(F32) for part_in in moved])
     columns = total.shape[-1]
     member_rows = total[:chunk_rows].reshape(MEMBERS, share, columns)
     member_rows = reorder_members(member_rows, core, head_place)
     tail = jnp.broadcast_to(total[chunk_rows], (MEMBERS, piece_rows - share, columns))
     sending = jnp.concatenate([member_rows, tail], axis=1)
-    arrived = arrived + move(planes - 1, planes)
     got = [sending[0]] + [
         swap_member(sending[member], member) for member in range(1, MEMBERS)
     ]
     got = reorder_members(jnp.stack(got), core, head_place)
     got = got.reshape(MEMBERS, piece_rows, heads_here, 3, HEAD_DIM)
-    input_grad = collect([input_pieces[0]] + arrived, plane).reshape(seqs, part_rows, width)
-    output = collect(output_pieces, plane).reshape(seqs, part_rows, width)
+    output = output.reshape(seqs, part_rows, width)
     matrices = [
         jnp.swapaxes(got[:, :share, :, i], 0, 1).reshape(share, width) for i in range(3)
     ]
@@ -1026,6 +1066,9 @@
         lax.dynamic_slice_in_dim(got[:, share, :, i].reshape(width), device * share, share)
         for i in (0, 2)
     ]
+
+    arrived, matrices, biases = stage((arrived, matrices, biases))
+    input_grad = collect([input_pieces[0]] + arrived, plane).reshape(seqs, part_rows, width)
 
     def vector(index):
         return owned_vectors[index * share : (index + 1) * share]

time: 575 us -> 557 us (0.969); the launches traced: 573 us -> 548 us
  Pallas kernels: 337 us -> 323 us
  waiting for transfers between devices: 89.1 us -> 80.1 us
  starting transfers between devices: 85.2 us -> 79.2 us
    pallas_call x1, Pallas kernels: 72.1 us -> 57.4 us  [layer_rows(): pl.pallas_call(functools.partial(layer_kernel, blocks, planes, parts), gr...]
    ppermute x18 -> x15, waiting for transfers between devices: 57.8 us -> 47.6 us  [shift_planes(): return lax.ppermute(array, 'blk', route)]
    ppermute x18 -> x15, starting transfers between devices: 53.5 us -> 44.1 us  [shift_planes(): return lax.ppermute(array, 'blk', route)]
  transfers between devices with their start and end apart: 68 -> 66, of which waited for: 17 -> 17; matrix products, arithmetic and copies ran while one was open for 6% -> 6% of each run, Pallas kernels for 59% -> 59%
where the time goes in v6:
time: 557 us; the launch traced here: 548 us
  Pallas kernels  323 us (58%)
  waiting for transfers between devices  80.1 us (14%)
  starting transfers between devices  79.2 us (14%)
  local copies, waits for them, and re-layouts  37.9 us (7%)
  between operations  15.5 us (3%)
  other arithmetic  12.5 us (2%)
    pallas_call x4, Pallas kernels, attention_backward(): pl.pallas_call(functools.partial(backward_kernel, min(1024, query_count),...  145 us
    pallas_call x4, Pallas kernels, attention_forward(): pl.pallas_call(functools.partial(forward_kernel, min(512, key_count), mem...  80.3 us
    pallas_call x1, Pallas kernels, layer_rows(): pl.pallas_call(functools.partial(layer_kernel, blocks, planes, parts), gr...  57.4 us
    ppermute x15, waiting for transfers between devices, shift_planes(): return lax.ppermute(array, 'blk', route)  47.6 us
    ppermute x15, starting transfers between devices, shift_planes(): return lax.ppermute(array, 'blk', route)  44.1 us
    ppermute x15, waiting for transfers between devices, swap_member(): return lax.ppermute(array, 'head', [(0, 1), (1, 0)])  19.9 us
    ppermute x15, starting transfers between devices, swap_member(): return lax.ppermute(array, 'head', [(0, 1), (1, 0)])  16.1 us
    pallas_call x2, Pallas kernels, input_grad_step(): pl.pallas_call(functools.partial(input_grad_kernel, counts_of(slots)), gr...  15.1 us
  transfers between devices with their start and end apart: 66, of which 17 were waited for; matrix products, arithmetic and copies ran while one was open for 6% of the time, Pallas kernels for 59%

profile of v6, /device:TPU:0, one launch (start us, length us, event | category | flops | bytes accessed | tf_op | source)
XLA Modules:
  0.0 548.1 jit_solution(248692219921923126)
XLA Ops:
  8.8 3.1 collective-permute-start
  11.9 2.6 collective-permute-start.1
  14.5 1.5 collective-permute-start.2
  20.5 5.2 collective-permute-done.3
  26.9 2.6 collective-permute-done.5
  29.5 10.4 %collective-permute-done.1.rest_2_ = bf16[256,768]{1,0:T(8,128)(2,1)S(1)} collective-permute-done((bf16[256,768]{1,0:T(8,128)(2,1)S(1)}, bf16[256,768]{1,0:T(8,128)(2,1)S(1)}, u32[]{:S(2)}, u32[]{:S(2)}) %collective-permute-start.1) | collective-permute-done | bytes 393248 | tf_op jit(solution)/shard_map/ppermute | solution.py:34
  41.2 3.5 all-to-all-start
  44.7 3.7 collective-permute-start.6
  48.5 1.5 collective-permute-start.7
  51.2 2.6 concatenate.100
  53.8 12.7 %collective-permute-done.6.rest_3_ = bf16[256,768]{1,0:T(8,128)(2,1)} collective-permute-done((bf16[256,768]{1,0:T(8,128)(2,1)S(1)}, bf16[256,768]{1,0:T(8,128)(2,1)}, u32[]{:S(2)}, u32[]{:S(2)}) %collective-permute-start.6) | collective-permute-done | bytes 393248 | tf_op jit(solution)/shard_map/ppermute | solution.py:34
  68.2 1.6 collective-permute-start.17
  71.9 1.5 collective-permute-start.16
  75.4 10.2 %collective-permute-done.16.rest_7_ = bf16[256,768]{1,0:T(8,128)(2,1)S(1)} collective-permute-done((bf16[256,768]{1,0:T(8,128)(2,1)}, bf16[256,768]{1,0:T(8,128)(2,1)S(1)}, u32[]{:S(2)}, u32[]{:S(2)}) %collective-permute-start.16) | collective-permute-done | bytes 393248 | tf_op jit(solution)/shard_map/ppermute | solution.py:51
  85.5 1.9 collective-permute-done.17
  91.8 9.1 %shard_map.305.q_ref.k_ref.v_ref = bf16[576,4096]{1,0:T(8,128)(2,1)} custom-call(bf16[768,576]{1,0:T(8,128)(2,1)} %bitcast.151, f32[576,1]{1,0:T(8,128)} %copy.138.bias_ref, bf16[256,768]{1,0:T(8,128)(2,1)} %copy-done.2, bf16[256,768]{1,0:T(8,128)(2,1)} %copy-done.37, bf16[256,768]{1,0:T(8,128)(2,1)} %copy-done.38, ...), custom_call_target="tpu_custom_call" | custom-call | flops 3623878656 | bytes 12582912 | tf_op jit(solution)/shard_map/pallas_call | solution.py:327
  101.8 4.0 collective-permute-start.19
  108.2 26.1 %shard_map.306 = (bf16[64,1024]{1,0:T(8,128)(2,1)}, bf16[64,1024]{1,0:T(8,128)(2,1)}, bf16[64,1024]{1,0:T(8,128)(2,1)}, bf16[64,1024]{1,0:T(8,128)(2,1)}, f32[1,...) custom-call(bf16[576,4096]{1,0:T(8,128)(2,1)} %shard_map.305.q_ref.k_ref.v_ref, ...), custom_call_target="tpu_custom_call" | custom-call | flops 17179869184 | bytes 2097152 | tf_op jit(solution)/shard_map/pallas_call | solution.py:140
  134.3 25.7 %shard_map.307 = (bf16[64,1024]{1,0:T(8,128)(2,1)}, bf16[64,1024]{1,0:T(8,128)(2,1)}, bf16[64,1024]{1,0:T(8,128)(2,1)}, bf16[64,1024]{1,0:T(8,128)(2,1)}, f32[1,...) custom-call(bf16[576,4096]{1,0:T(8,128)(2,1)} %shard_map.305.q_ref.k_ref.v_ref, ...), custom_call_target="tpu_custom_call" | custom-call | flops 17179869184 | bytes 2097152 | tf_op jit(solution)/shard_map/pallas_call | solution.py:140
  159.9 1.6 collective-permute-start.22
  163.9 14.3 %shard_map.308 = (bf16[64,1024]{1,0:T(8,128)(2,1)}, bf16[64,1024]{1,0:T(8,128)(2,1)}, f32[1,1024]{1,0:T(1,128)}, f32[1,1024]{1,0:T(1,128)}) custom-call(bf16[576,4096]{1,0:T(8,128)(2,1)} %shard_map.305.q_ref.k_ref.v_ref, bf16[576,4096]{1,0:T(8,128)(2,1)} %shard_map.305.q_ref.k_ref.v_ref, bf16[576,4096]{1,0:T(8,128)(2,1)} %shard_map.305.q_ref.k_ref.v_ref, ...), custom_call_target="tpu_custom_call" | custom-call | flops 8589934592 | bytes 2097152 | tf_op jit(solution)/shard_map/pallas_call | solution.py:140
  178.2 14.3 %shard_map.309 = (bf16[64,1024]{1,0:T(8,128)(2,1)}, bf16[64,1024]{1,0:T(8,128)(2,1)}, f32[1,1024]{1,0:T(1,128)}, f32[1,1024]{1,0:T(1,128)}) custom-call(bf16[576,4096]{1,0:T(8,128)(2,1)} %shard_map.305.q_ref.k_ref.v_ref, bf16[576,4096]{1,0:T(8,128)(2,1)} %shard_map.305.q_ref.k_ref.v_ref, bf16[576,4096]{1,0:T(8,128)(2,1)} %shard_map.305.q_ref.k_ref.v_ref, ...), custom_call_target="tpu_custom_call" | custom-call | flops 8589934592 | bytes 2097152 | tf_op jit(solution)/shard_map/pallas_call | solution.py:140
  199.7 3.5 collective-permute-done.24.rest_12_
  203.2 2.1 collective-permute-done.30.rest_18_
  206.0 57.4 %shard_map.310 = (bf16[256,768]{1,0:T(8,128)(2,1)}, bf16[256,768]{1,0:T(8,128)(2,1)}, bf16[256,768]{1,0:T(8,128)(2,1)}, bf16[256,768]{1,0:T(8,128)(2,1)}, bf16[6...) custom-call(s32[8]{0:T(128)} %pad_add_fusion.info_ref, ...), custom_call_target="tpu_custom_call" | custom-call | flops 28991029248 | bytes 18874368 | tf_op jit(solution)/shard_map/pallas_call | solution.py:664
  264.1 1.5 collective-permute-start.33
  265.7 4.4 collective-permute-start.37
  272.5 3.1 copy.148
  276.6 5.2 fusion.1
  285.5 46.8 %shard_map.311 = (bf16[192,1024]{1,0:T(8,128)(2,1)}, bf16[192,1024]{1,0:T(8,128)(2,1)}, bf16[192,1024]{1,0:T(8,128)(2,1)}, bf16[192,1024]{1,0:T(8,128)(2,1)}) custom-call(bf16[576,4096]{1,0:T(8,128)(2,1)} %shard_map.305.q_ref.k_ref.v_ref, bf16[576,4096]{1,0:T(8,128)(2,1)} %shard_map.305.q_ref.k_ref.v_ref, bf16[576,4096]{1,0:T(8,128)(2,1)} %shard_map.305.q_ref.k_ref.v_ref, ...), custom_call_target="tpu_custom_call" | custom-call | flops 42949672960 | bytes 4194304 | tf_op jit(solution)/shard_map/pallas_call | solution.py:272
  334.6 47.0 %shard_map.313 = (bf16[192,1024]{1,0:T(8,128)(2,1)}, bf16[192,1024]{1,0:T(8,128)(2,1)}, bf16[192,1024]{1,0:T(8,128)(2,1)}, bf16[192,1024]{1,0:T(8,128)(2,1)}) custom-call(bf16[576,4096]{1,0:T(8,128)(2,1)} %shard_map.305.q_ref.k_ref.v_ref, bf16[576,4096]{1,0:T(8,128)(2,1)} %shard_map.305.q_ref.k_ref.v_ref, bf16[576,4096]{1,0:T(8,128)(2,1)} %shard_map.305.q_ref.k_ref.v_ref, ...), custom_call_target="tpu_custom_call" | custom-call | flops 42949672960 | bytes 4194304 | tf_op jit(solution)/shard_map/pallas_call | solution.py:272
  383.0 2.6 shard_map.312
  386.5 26.0 %shard_map.314 = (bf16[128,1024]{1,0:T(8,128)(2,1)}, bf16[128,1024]{1,0:T(8,128)(2,1)}, f32[64,4096]{1,0:T(8,128)}) custom-call(bf16[576,4096]{1,0:T(8,128)(2,1)} %shard_map.305.q_ref.k_ref.v_ref, bf16[576,4096]{1,0:T(8,128)(2,1)} %shard_map.305.q_ref.k_ref.v_ref, bf16[576,4096]{1,0:T(8,128)(2,1)} %shard_map.305.q_ref.k_ref.v_ref, ...), custom_call_target="tpu_custom_call" | custom-call | flops 21474836480 | bytes 4194304 | tf_op jit(solution)/shard_map/pallas_call | solution.py:272
  412.6 1.6 collective-permute-start.47
  415.2 8.3 %shard_map.315.acc_ref = f32[1024,768]{1,0:T(8,128)} custom-call(s32[4]{0:T(128)} %copy-done.27, f32[1024,768]{1,0:T(8,128)} %get-tuple-element.265.acc_ref, bf16[32,72,768]{2,1,0:T(8,128)(2,1)} %bitcast.137, bf16[32,72,768]{2,1,0:T(8,128)(2,1)} %bitcast.138, bf16[192,1024]{1,0:T(8,128)(2,1)} %get-tuple-element.266.rest_2_.rest_16_, ...), custom_call_target="tpu_custom_call" | custom-call | flops 2415919104 | bytes 6291456 | tf_op jit(solution)/shard_map/pallas_call | solution.py:444
  423.5 25.7 %shard_map.316 = (bf16[128,1024]{1,0:T(8,128)(2,1)}, bf16[128,1024]{1,0:T(8,128)(2,1)}, bf16[64,1024]{1,0:T(8,128)(2,1)}, bf16[64,1024]{1,0:T(8,128)(2,1)}, bf16...) custom-call(bf16[576,4096]{1,0:T(8,128)(2,1)} %shard_map.305.q_ref.k_ref.v_ref, ...), custom_call_target="tpu_custom_call" | custom-call | flops 21474836480 | bytes 4194304 | tf_op jit(solution)/shard_map/pallas_call | solution.py:272
  451.0 10.2 %shard_map.317 = bf16[8,112,576]{2,1,0:T(8,128)(2,1)} custom-call(bf16[256,768]{1,0:T(8,128)(2,1)} %copy-done.2, bf16[256,768]{1,0:T(8,128)(2,1)} %copy-done.37, bf16[256,768]{1,0:T(8,128)(2,1)} %copy-done.38, bf16[256,768]{1,0:T(8,128)(2,1)} %collective-permute-done.6.rest_3_, bf16[256,768]{1,0:T(8,128)(2,1)} %collective-permute-done.2.rest_4_, ...), custom_call_target="tpu_custom_call" | custom-call | flops 3623878656 | bytes 6291456 | tf_op jit(solution)/shard_map/pallas_call | solution.py:388
  463.4 3.1 collective-permute-done.50.rest_7_
  467.8 6.8 %shard_map.318 = (bf16[256,768]{1,0:T(8,128)(2,1)}, bf16[256,768]{1,0:T(8,128)(2,1)}, bf16[256,768]{1,0:T(8,128)(2,1)}, bf16[256,768]{1,0:T(8,128)(2,1)}) custom-call(s32[4]{0:T(128)} %copy-done.27, f32[1024,768]{1,0:T(8,128)} %shard_map.315.acc_ref, bf16[32,72,768]{2,1,0:T(8,128)(2,1)} %bitcast.139, bf16[64,1024]{1,0:T(8,128)(2,1)} %get-tuple-element.271.rest_24_.rest_1_, ...), custom_call_target="tpu_custom_call" | custom-call | flops 1207959552 | bytes 6291456 | tf_op jit(solution)/shard_map/pallas_call | solution.py:444
  475.9 3.6 collective-permute-start.52
  479.6 9.6 %collective-permute-done.52.rest_1_ = bf16[256,768]{1,0:T(8,128)(2,1)S(1)} collective-permute-done((bf16[256,768]{1,0:T(8,128)(2,1)}, bf16[256,768]{1,0:T(8,128)(2,1)S(1)}, u32[]{:S(2)}, u32[]{:S(2)}) %collective-permute-start.52) | collective-permute-done | bytes 393248 | tf_op jit(solution)/shard_map/ppermute | solution.py:34
  490.2 13.5 %collective-permute-start.55 = (bf16[112,576]{1,0:T(8,128)(2,1)S(1)}, bf16[112,576]{1,0:T(8,128)(2,1)S(1)}, u32[]{:S(2)}, u32[]{:S(2)}) collective-permute-start(bf16[112,576]{1,0:T(8,128)(2,1)S(1)} %get-tuple-element.338), channel_id=1, source_target_pairs={{0,4},{2,6},{4,8},{6,10},{8,12},{10,14},{12,0},{14,2},{1,5},{3,7},... | collective-permute-start | bytes 387080 | tf_op jit(solution)/shard_map/ppermute | solution.py:34
  503.7 2.4 collective-permute-start.57
  506.1 6.7 %collective-permute-done.54.rest_2_ = bf16[256,768]{1,0:T(8,128)(2,1)S(1)} collective-permute-done((bf16[256,768]{1,0:T(8,128)(2,1)}, bf16[256,768]{1,0:T(8,128)(2,1)S(1)}, u32[]{:S(2)}, u32[]{:S(2)}) %collective-permute-start.54) | collective-permute-done | bytes 393248 | tf_op jit(solution)/shard_map/ppermute | solution.py:34
  512.8 3.1 collective-permute-done.56
  518.4 2.7 collective-permute-start.58
  527.6 5.1 collective-permute-done.58.rest_3_
  533.5 2.6 shard_map.319
  (384 shorter events, 68.3 us)
Async XLA Ops:
  8.8 20.7 %collective-permute-start = (bf16[256,768]{1,0:T(8,128)(2,1)S(1)}, bf16[256,768]{1,0:T(8,128)(2,1)S(1)}, u32[]{:S(2)}, u32[]{:S(2)}) collective-permute-start(bf16[256,768]{1,0:T(8,128)(2,1)S(1)} %get-tuple-element.320), channel_id=1, source_target_pairs={{0,4},{2,6},{4,8},{6,10},{8,12},{10,14},{12,0},{14,2},{1,5},{3,7},... | collective-permute-start | bytes 1179656 | tf_op jit(solution)/shard_map/ppermute | solution.py:34
  11.9 28.0 %collective-permute-start.1 = (bf16[256,768]{1,0:T(8,128)(2,1)S(1)}, bf16[256,768]{1,0:T(8,128)(2,1)S(1)}, u32[]{:S(2)}, u32[]{:S(2)}) collective-permute-start(bf16[256,768]{1,0:T(8,128)(2,1)S(1)} %get-tuple-element.322), channel_id=1, source_target_pairs={{0,8},{2,10},{4,12},{6,14},{8,0},{10,2},{12,4},{14,6},{1,9},{3,11}... | collective-permute-start | bytes 1179656 | tf_op jit(solution)/shard_map/ppermute | solution.py:34
  14.5 25.4 %collective-permute-start.2 = (bf16[256,768]{1,0:T(8,128)(2,1)S(1)}, bf16[256,768]{1,0:T(8,128)(2,1)}, u32[]{:S(2)}, u32[]{:S(2)}) collective-permute-start(bf16[256,768]{1,0:T(8,128)(2,1)S(1)} %get-tuple-element.184.rest_0_), channel_id=1, source_target_pairs={{0,1},{1,0},{2,3},{3,2},{4,5},{5,4},{6,7},{7,6},{8,9},{9,8},{10,11... | collective-permute-start | bytes 1179656 | tf_op jit(solution)/shard_map/ppermute | solution.py:51
  41.2 26.3 %all-to-all-start = ((bf16[4,4,32,576]{3,1,2,0:T(4,128)(2,1)}), bf16[4,4,32,576]{3,1,2,0:T(4,128)(2,1)S(1)}, u32[]{:S(2)}, u32[]{:S(2)}) async-start(bf16[4,4,32,576]{3,1,2,0:T(4,128)(2,1)} %broadcast_in_dim.30), calls=%async_computation | async-start | bytes 1310720 | tf_op jit(solution)/shard_map/all_to_all | solution.py:40
  44.7 147.8 %all-gather.5.cloned.1.call-start = ((), (), s32[]{:S(2)}) async-start(), calls=%async_computation.3 | async-start | bytes 11354112 | tf_op jit(solution)/shard_map/all_gather | solution.py:834
  44.7 21.8 %collective-permute-start.6 = (bf16[256,768]{1,0:T(8,128)(2,1)S(1)}, bf16[256,768]{1,0:T(8,128)(2,1)}, u32[]{:S(2)}, u32[]{:S(2)}) collective-permute-start(bf16[256,768]{1,0:T(8,128)(2,1)S(1)} %get-tuple-element.167), channel_id=1, source_target_pairs={{0,12},{2,14},{4,0},{6,2},{8,4},{10,6},{12,8},{14,10},{1,13},{3,15... | collective-permute-start | bytes 1179656 | tf_op jit(solution)/shard_map/ppermute | solution.py:34
  48.5 18.1 %collective-permute-start.7 = (bf16[256,768]{1,0:T(8,128)(2,1)S(1)}, bf16[256,768]{1,0:T(8,128)(2,1)}, u32[]{:S(2)}, u32[]{:S(2)}) collective-permute-start(bf16[256,768]{1,0:T(8,128)(2,1)S(1)} %collective-permute-done.rest_1_), channel_id=1, source_target_pairs={{0,1},{1,0},{2,3},{3,2},{4,5},{5,4},{6,7},{7,6},{8,9},{9,8},{10,11... | collective-permute-start | bytes 1179656 | tf_op jit(solution)/shard_map/ppermute | solution.py:51
  50.0 17.5 %collective-permute-start.8 = (bf16[256,768]{1,0:T(8,128)(2,1)S(1)}, bf16[256,768]{1,0:T(8,128)(2,1)}, u32[]{:S(2)}, u32[]{:S(2)}) collective-permute-start(bf16[256,768]{1,0:T(8,128)(2,1)S(1)} %collective-permute-done.1.rest_2_), channel_id=1, source_target_pairs={{0,1},{1,0},{2,3},{3,2},{4,5},{5,4},{6,7},{7,6},{8,9},{9,8},{10,11... | collective-permute-start | bytes 1179656 | tf_op jit(solution)/shard_map/ppermute | solution.py:51
  50.5 17.0 %collective-permute-start.9 = (bf16[256,768]{1,0:T(8,128)(2,1)S(1)}, bf16[256,768]{1,0:T(8,128)(2,1)}, u32[]{:S(2)}, u32[]{:S(2)}) collective-permute-start(bf16[256,768]{1,0:T(8,128)(2,1)S(1)} %get-tuple-element.184.rest_0_), channel_id=1, source_target_pairs={{0,2},{2,0},{4,6},{6,4},{8,10},{10,8},{12,14},{14,12},{1,3},{3,1},... | collective-permute-start | bytes 1179656 | tf_op jit(solution)/shard_map/ppermute | solution.py:53
  50.5 17.0 %collective-permute-start.10 = (bf16[256,768]{1,0:T(8,128)(2,1)}, bf16[256,768]{1,0:T(8,128)(2,1)}, u32[]{:S(2)}, u32[]{:S(2)}) collective-permute-start(bf16[256,768]{1,0:T(8,128)(2,1)} %collective-permute-done.2.rest_4_), channel_id=1, source_target_pairs={{0,2},{2,0},{4,6},{6,4},{8,10},{10,8},{12,14},{14,12},{1,3},{3,1},... | collective-permute-start | bytes 1179656 | tf_op jit(solution)/shard_map/ppermute | solution.py:53
  67.5 346.6 %all-gather.7.cloned.1.call-start = ((), (), s32[]{:S(2)}) async-start(), calls=%async_computation.4 | async-start | bytes 3649536 | tf_op jit(solution)/shard_map/all_gather | solution.py:874
  68.2 19.2 %collective-permute-start.17 = (bf16[4,4,32,576]{3,2,1,0:T(8,128)(2,1)S(1)}, bf16[4,4,32,576]{3,2,1,0:T(8,128)(2,1)S(1)}, u32[]{:S(2)}, u32[]{:S(2)}) collective-permute-start(bf16[4,4,32,576]{3,2,1,0:T(8,128)(2,1)S(1)} %copy.136), channel_id=1, source_target_pairs={{0,16},{16,0},{1,17},{17,1},{2,18},{18,2},{3,19},{19,3},{4,20},{20... | collective-permute-start | bytes 1769480 | tf_op jit(solution)/shard_map/ppermute | solution.py:45
  71.9 13.7 %collective-permute-start.16 = (bf16[256,768]{1,0:T(8,128)(2,1)}, bf16[256,768]{1,0:T(8,128)(2,1)S(1)}, u32[]{:S(2)}, u32[]{:S(2)}) collective-permute-start(bf16[256,768]{1,0:T(8,128)(2,1)} %collective-permute-done.6.rest_3_), channel_id=1, source_target_pairs={{0,1},{1,0},{2,3},{3,2},{4,5},{5,4},{6,7},{7,6},{8,9},{9,8},{10,11... | collective-permute-start | bytes 1179656 | tf_op jit(solution)/shard_map/ppermute | solution.py:51
  75.2 460.9 %reduce-scatter.2.cloned.1.call-start = ((), (), s32[]{:S(2)}) async-start(), calls=%async_computation.2 | async-start | bytes 11354112 | tf_op jit(solution)/shard_map/reduce_scatter | solution.py:970
  101.8 60.2 %collective-permute-start.19 = (bf16[256,768]{1,0:T(8,128)(2,1)S(1)}, bf16[256,768]{1,0:T(8,128)(2,1)S(1)}, u32[]{:S(2)}, u32[]{:S(2)}) collective-permute-start(bf16[256,768]{1,0:T(8,128)(2,1)S(1)} %get-tuple-element.317), channel_id=1, source_target_pairs={{0,4},{2,6},{4,8},{6,10},{8,12},{10,14},{12,0},{14,2},{1,5},{3,7},... | collective-permute-start | bytes 1179656 | tf_op jit(solution)/shard_map/ppermute | solution.py:34
  105.8 56.3 %collective-permute-start.20 = (bf16[256,768]{1,0:T(8,128)(2,1)S(1)}, bf16[256,768]{1,0:T(8,128)(2,1)S(1)}, u32[]{:S(2)}, u32[]{:S(2)}) collective-permute-start(bf16[256,768]{1,0:T(8,128)(2,1)S(1)} %get-tuple-element.316), channel_id=1, source_target_pairs={{0,8},{2,10},{4,12},{6,14},{8,0},{10,2},{12,4},{14,6},{1,9},{3,11}... | collective-permute-start | bytes 1179656 | tf_op jit(solution)/shard_map/ppermute | solution.py:34
  107.1 55.5 %collective-permute-start.21 = (bf16[256,768]{1,0:T(8,128)(2,1)S(1)}, bf16[256,768]{1,0:T(8,128)(2,1)S(1)}, u32[]{:S(2)}, u32[]{:S(2)}) collective-permute-start(bf16[256,768]{1,0:T(8,128)(2,1)S(1)} %get-tuple-element.315), channel_id=1, source_target_pairs={{0,12},{2,14},{4,0},{6,2},{8,4},{10,6},{12,8},{14,10},{1,13},{3,15... | collective-permute-start | bytes 1179656 | tf_op jit(solution)/shard_map/ppermute | solution.py:34
  159.9 34.0 %collective-permute-start.22 = (bf16[64,1024]{1,0:T(8,128)(2,1)S(1)}, bf16[64,1024]{1,0:T(8,128)(2,1)S(1)}, u32[]{:S(2)}, u32[]{:S(2)}) collective-permute-start(bf16[64,1024]{1,0:T(8,128)(2,1)S(1)} %copy-done.58), channel_id=1, source_target_pairs={{0,1},{1,0},{2,3},{3,2},{4,5},{5,4},{6,7},{7,6},{8,9},{9,8},{10,11... | collective-permute-start | bytes 393224 | tf_op jit(solution)/shard_map/ppermute | solution.py:51
  161.5 33.2 %collective-permute-start.23 = (bf16[64,1024]{1,0:T(8,128)(2,1)}, bf16[64,1024]{1,0:T(8,128)(2,1)S(1)}, u32[]{:S(2)}, u32[]{:S(2)}) collective-permute-start(bf16[64,1024]{1,0:T(8,128)(2,1)} %get-tuple-element.212.rest_5_), channel_id=1, source_target_pairs={{0,1},{1,0},{2,3},{3,2},{4,5},{5,4},{6,7},{7,6},{8,9},{9,8},{10,11... | collective-permute-start | bytes 393224 | tf_op jit(solution)/shard_map/ppermute | solution.py:51
  162.0 34.1 %collective-permute-start.25 = (bf16[64,1024]{1,0:T(8,128)(2,1)S(1)}, bf16[64,1024]{1,0:T(8,128)(2,1)S(1)}, u32[]{:S(2)}, u32[]{:S(2)}) collective-permute-start(bf16[64,1024]{1,0:T(8,128)(2,1)S(1)} %copy-done.59), channel_id=1, source_target_pairs={{0,2},{2,0},{4,6},{6,4},{8,10},{10,8},{12,14},{14,12},{1,3},{3,1},... | collective-permute-start | bytes 393224 | tf_op jit(solution)/shard_map/ppermute | solution.py:53
  162.1 34.1 %collective-permute-start.26 = (bf16[64,1024]{1,0:T(8,128)(2,1)}, bf16[64,1024]{1,0:T(8,128)(2,1)S(1)}, u32[]{:S(2)}, u32[]{:S(2)}) collective-permute-start(bf16[64,1024]{1,0:T(8,128)(2,1)} %get-tuple-element.214.rest_6_), channel_id=1, source_target_pairs={{0,2},{2,0},{4,6},{6,4},{8,10},{10,8},{12,14},{14,12},{1,3},{3,1},... | collective-permute-start | bytes 393224 | tf_op jit(solution)/shard_map/ppermute | solution.py:53
  162.6 35.8 %collective-permute-start.28 = (bf16[64,1024]{1,0:T(8,128)(2,1)S(1)}, bf16[64,1024]{1,0:T(8,128)(2,1)S(1)}, u32[]{:S(2)}, u32[]{:S(2)}) collective-permute-start(bf16[64,1024]{1,0:T(8,128)(2,1)S(1)} %copy-done.60), channel_id=1, source_target_pairs={{0,3},{1,2},{2,1},{3,0},{4,7},{5,6},{6,5},{7,4},{8,11},{9,10},{10,... | collective-permute-start | bytes 393224 | tf_op jit(solution)/shard_map/ppermute | solution.py:55
  263.4 18.4 %collective-permute-start.31 = (bf16[64,1024]{1,0:T(8,128)(2,1)}, bf16[64,1024]{1,0:T(8,128)(2,1)S(1)}, u32[]{:S(2)}, u32[]{:S(2)}) collective-permute-start(bf16[64,1024]{1,0:T(8,128)(2,1)} %get-tuple-element.223), channel_id=1, source_target_pairs={{0,1},{1,0},{2,3},{3,2},{4,5},{5,4},{6,7},{7,6},{8,9},{9,8},{10,11... | collective-permute-start | bytes 393224 | tf_op jit(solution)/shard_map/ppermute | solution.py:51
  263.5 20.7 %collective-permute-start.32 = (bf16[64,1024]{1,0:T(8,128)(2,1)}, bf16[64,1024]{1,0:T(8,128)(2,1)S(1)}, u32[]{:S(2)}, u32[]{:S(2)}) collective-permute-start(bf16[64,1024]{1,0:T(8,128)(2,1)} %get-tuple-element.224), channel_id=1, source_target_pairs={{0,2},{2,0},{4,6},{6,4},{8,10},{10,8},{12,14},{14,12},{1,3},{3,1},... | collective-permute-start | bytes 393224 | tf_op jit(solution)/shard_map/ppermute | solution.py:53
  264.1 20.2 %collective-permute-start.33 = (bf16[64,1024]{1,0:T(8,128)(2,1)}, bf16[64,1024]{1,0:T(8,128)(2,1)S(1)}, u32[]{:S(2)}, u32[]{:S(2)}) collective-permute-start(bf16[64,1024]{1,0:T(8,128)(2,1)} %get-tuple-element.225), channel_id=1, source_target_pairs={{0,3},{1,2},{2,1},{3,0},{4,7},{5,6},{6,5},{7,4},{8,11},{9,10},{10,... | collective-permute-start | bytes 393224 | tf_op jit(solution)/shard_map/ppermute | solution.py:55
  265.7 68.1 %collective-permute-start.37 = (bf16[256,768]{1,0:T(8,128)(2,1)}, bf16[256,768]{1,0:T(8,128)(2,1)S(1)}, u32[]{:S(2)}, u32[]{:S(2)}) collective-permute-start(bf16[256,768]{1,0:T(8,128)(2,1)} %get-tuple-element.231), channel_id=1, source_target_pairs={{0,12},{2,14},{4,0},{6,2},{8,4},{10,6},{12,8},{14,10},{1,13},{3,15... | collective-permute-start | bytes 1179656 | tf_op jit(solution)/shard_map/ppermute | solution.py:34
  270.1 14.3 %collective-permute-start.40 = (bf16[128,1024]{1,0:T(8,128)(2,1)}, bf16[128,1024]{1,0:T(8,128)(2,1)S(1)}, u32[]{:S(2)}, u32[]{:S(2)}) collective-permute-start(bf16[128,1024]{1,0:T(8,128)(2,1)} %get-tuple-element.235), channel_id=1, source_target_pairs={{0,1},{1,0},{2,3},{3,2},{4,5},{5,4},{6,7},{7,6},{8,9},{9,8},{10,11... | collective-permute-start | bytes 786440 | tf_op jit(solution)/shard_map/ppermute | solution.py:51
  282.9 51.7 %collective-permute-start.38 = (bf16[256,768]{1,0:T(8,128)(2,1)S(1)}, bf16[256,768]{1,0:T(8,128)(2,1)S(1)}, u32[]{:S(2)}, u32[]{:S(2)}) collective-permute-start(bf16[256,768]{1,0:T(8,128)(2,1)S(1)} %copy-done.49), channel_id=1, source_target_pairs={{0,8},{2,10},{4,12},{6,14},{8,0},{10,2},{12,4},{14,6},{1,9},{3,11}... | collective-permute-start | bytes 1179656 | tf_op jit(solution)/shard_map/ppermute | solution.py:34
  284.3 50.3 %collective-permute-start.39 = (bf16[256,768]{1,0:T(8,128)(2,1)S(1)}, bf16[256,768]{1,0:T(8,128)(2,1)S(1)}, u32[]{:S(2)}, u32[]{:S(2)}) collective-permute-start(bf16[256,768]{1,0:T(8,128)(2,1)S(1)} %copy-done.47), channel_id=1, source_target_pairs={{0,4},{2,6},{4,8},{6,10},{8,12},{10,14},{12,0},{14,2},{1,5},{3,7},... | collective-permute-start | bytes 1179656 | tf_op jit(solution)/shard_map/ppermute | solution.py:34
  284.4 47.9 %collective-permute-start.41 = (bf16[128,1024]{1,0:T(8,128)(2,1)S(1)}, bf16[128,1024]{1,0:T(8,128)(2,1)S(1)}, u32[]{:S(2)}, u32[]{:S(2)}) collective-permute-start(bf16[128,1024]{1,0:T(8,128)(2,1)S(1)} %copy-done.55), channel_id=1, source_target_pairs={{0,2},{2,0},{4,6},{6,4},{8,10},{10,8},{12,14},{14,12},{1,3},{3,1},... | collective-permute-start | bytes 786440 | tf_op jit(solution)/shard_map/ppermute | solution.py:53
  284.5 49.3 %collective-permute-start.42 = (bf16[128,1024]{1,0:T(8,128)(2,1)S(1)}, bf16[128,1024]{1,0:T(8,128)(2,1)S(1)}, u32[]{:S(2)}, u32[]{:S(2)}) collective-permute-start(bf16[128,1024]{1,0:T(8,128)(2,1)S(1)} %copy-done.54), channel_id=1, source_target_pairs={{0,3},{1,2},{2,1},{3,0},{4,7},{5,6},{6,5},{7,4},{8,11},{9,10},{10,... | collective-permute-start | bytes 786440 | tf_op jit(solution)/shard_map/ppermute | solution.py:55
  332.3 53.3 %collective-permute-start.34 = (bf16[192,1024]{1,0:T(8,128)(2,1)}, bf16[192,1024]{1,0:T(8,128)(2,1)S(1)}, u32[]{:S(2)}, u32[]{:S(2)}) collective-permute-start(bf16[192,1024]{1,0:T(8,128)(2,1)} %get-tuple-element.227.rest_17_), channel_id=1, source_target_pairs={{0,1},{1,0},{2,3},{3,2},{4,5},{5,4},{6,7},{7,6},{8,9},{9,8},{10,11... | collective-permute-start | bytes 1179656 | tf_op jit(solution)/shard_map/ppermute | solution.py:51
  333.7 52.8 %collective-permute-start.35 = (bf16[192,1024]{1,0:T(8,128)(2,1)}, bf16[192,1024]{1,0:T(8,128)(2,1)S(1)}, u32[]{:S(2)}, u32[]{:S(2)}) collective-permute-start(bf16[192,1024]{1,0:T(8,128)(2,1)} %get-tuple-element.228.rest_18_), channel_id=1, source_target_pairs={{0,2},{2,0},{4,6},{6,4},{8,10},{10,8},{12,14},{14,12},{1,3},{3,1},... | collective-permute-start | bytes 1179656 | tf_op jit(solution)/shard_map/ppermute | solution.py:53
  333.8 52.8 %collective-permute-start.36 = (bf16[192,1024]{1,0:T(8,128)(2,1)}, bf16[192,1024]{1,0:T(8,128)(2,1)S(1)}, u32[]{:S(2)}, u32[]{:S(2)}) collective-permute-start(bf16[192,1024]{1,0:T(8,128)(2,1)} %get-tuple-element.229.rest_19_), channel_id=1, source_target_pairs={{0,3},{1,2},{2,1},{3,0},{4,7},{5,6},{6,5},{7,4},{8,11},{9,10},{10,... | collective-permute-start | bytes 1179656 | tf_op jit(solution)/shard_map/ppermute | solution.py:55
  381.6 32.5 %collective-permute-start.43 = (bf16[192,1024]{1,0:T(8,128)(2,1)}, bf16[192,1024]{1,0:T(8,128)(2,1)S(1)}, u32[]{:S(2)}, u32[]{:S(2)}) collective-permute-start(bf16[192,1024]{1,0:T(8,128)(2,1)} %get-tuple-element.252.rest_21_), channel_id=1, source_target_pairs={{0,1},{1,0},{2,3},{3,2},{4,5},{5,4},{6,7},{7,6},{8,9},{9,8},{10,11... | collective-permute-start | bytes 1179656 | tf_op jit(solution)/shard_map/ppermute | solution.py:51
  383.0 31.1 %collective-permute-start.44 = (bf16[192,1024]{1,0:T(8,128)(2,1)}, bf16[192,1024]{1,0:T(8,128)(2,1)S(1)}, u32[]{:S(2)}, u32[]{:S(2)}) collective-permute-start(bf16[192,1024]{1,0:T(8,128)(2,1)} %get-tuple-element.253.rest_22_), channel_id=1, source_target_pairs={{0,2},{2,0},{4,6},{6,4},{8,10},{10,8},{12,14},{14,12},{1,3},{3,1},... | collective-permute-start | bytes 1179656 | tf_op jit(solution)/shard_map/ppermute | solution.py:53
  385.7 28.5 %collective-permute-start.45 = (bf16[192,1024]{1,0:T(8,128)(2,1)S(1)}, bf16[192,1024]{1,0:T(8,128)(2,1)S(1)}, u32[]{:S(2)}, u32[]{:S(2)}) collective-permute-start(bf16[192,1024]{1,0:T(8,128)(2,1)S(1)} %copy-done.50), channel_id=1, source_target_pairs={{0,3},{1,2},{2,1},{3,0},{4,7},{5,6},{6,5},{7,4},{8,11},{9,10},{10,... | collective-permute-start | bytes 1179656 | tf_op jit(solution)/shard_map/ppermute | solution.py:55
  412.6 48.7 %collective-permute-start.47 = (bf16[128,1024]{1,0:T(8,128)(2,1)}, bf16[128,1024]{1,0:T(8,128)(2,1)S(1)}, u32[]{:S(2)}, u32[]{:S(2)}) collective-permute-start(bf16[128,1024]{1,0:T(8,128)(2,1)} %get-tuple-element.274.rest_27_), channel_id=1, source_target_pairs={{0,1},{1,0},{2,3},{3,2},{4,5},{5,4},{6,7},{7,6},{8,9},{9,8},{10,11... | collective-permute-start | bytes 786440 | tf_op jit(solution)/shard_map/ppermute | solution.py:51
  414.1 49.2 %collective-permute-start.51 = (bf16[128,1024]{1,0:T(8,128)(2,1)}, bf16[128,1024]{1,0:T(8,128)(2,1)S(1)}, u32[]{:S(2)}, u32[]{:S(2)}) collective-permute-start(bf16[128,1024]{1,0:T(8,128)(2,1)} %get-tuple-element.278.rest_31_), channel_id=1, source_target_pairs={{0,3},{1,2},{2,1},{3,0},{4,7},{5,6},{6,5},{7,4},{8,11},{9,10},{10,... | collective-permute-start | bytes 786440 | tf_op jit(solution)/shard_map/ppermute | solution.py:55
  449.2 14.2 %collective-permute-start.46 = (bf16[64,1024]{1,0:T(8,128)(2,1)}, bf16[64,1024]{1,0:T(8,128)(2,1)S(1)}, u32[]{:S(2)}, u32[]{:S(2)}) collective-permute-start(bf16[64,1024]{1,0:T(8,128)(2,1)} %get-tuple-element.273.rest_26_), channel_id=1, source_target_pairs={{0,1},{1,0},{2,3},{3,2},{4,5},{5,4},{6,7},{7,6},{8,9},{9,8},{10,11... | collective-permute-start | bytes 393224 | tf_op jit(solution)/shard_map/ppermute | solution.py:51
  450.3 13.0 %collective-permute-start.48 = (bf16[64,1024]{1,0:T(8,128)(2,1)}, bf16[64,1024]{1,0:T(8,128)(2,1)S(1)}, u32[]{:S(2)}, u32[]{:S(2)}) collective-permute-start(bf16[64,1024]{1,0:T(8,128)(2,1)} %get-tuple-element.275.rest_28_), channel_id=1, source_target_pairs={{0,2},{2,0},{4,6},{6,4},{8,10},{10,8},{12,14},{14,12},{1,3},{3,1},... | collective-permute-start | bytes 393224 | tf_op jit(solution)/shard_map/ppermute | solution.py:53
  451.0 15.5 %collective-permute-start.49 = (bf16[128,1024]{1,0:T(8,128)(2,1)}, bf16[128,1024]{1,0:T(8,128)(2,1)S(1)}, u32[]{:S(2)}, u32[]{:S(2)}) collective-permute-start(bf16[128,1024]{1,0:T(8,128)(2,1)} %get-tuple-element.276.rest_29_), channel_id=1, source_target_pairs={{0,2},{2,0},{4,6},{6,4},{8,10},{10,8},{12,14},{14,12},{1,3},{3,1},... | collective-permute-start | bytes 786440 | tf_op jit(solution)/shard_map/ppermute | solution.py:53
  474.6 15.3 %collective-permute-start.53 = (bf16[4,112,576]{2,1,0:T(8,128)(2,1)S(1)}, bf16[4,112,576]{2,1,0:T(8,128)(2,1)S(1)}, u32[]{:S(2)}, u32[]{:S(2)}) collective-permute-start(bf16[4,112,576]{2,1,0:T(8,128)(2,1)S(1)} %get-tuple-element.286), channel_id=1, source_target_pairs={{0,16},{16,0},{1,17},{17,1},{2,18},{18,2},{3,19},{19,3},{4,20},{20... | collective-permute-start | bytes 1548296 | tf_op jit(solution)/shard_map/ppermute | solution.py:45
  475.9 13.4 %collective-permute-start.52 = (bf16[256,768]{1,0:T(8,128)(2,1)}, bf16[256,768]{1,0:T(8,128)(2,1)S(1)}, u32[]{:S(2)}, u32[]{:S(2)}) collective-permute-start(bf16[256,768]{1,0:T(8,128)(2,1)} %get-tuple-element.285), channel_id=1, source_target_pairs={{0,12},{2,14},{4,0},{6,2},{8,4},{10,6},{12,8},{14,10},{1,13},{3,15... | collective-permute-start | bytes 1179656 | tf_op jit(solution)/shard_map/ppermute | solution.py:34
  479.4 33.4 %collective-permute-start.54 = (bf16[256,768]{1,0:T(8,128)(2,1)}, bf16[256,768]{1,0:T(8,128)(2,1)S(1)}, u32[]{:S(2)}, u32[]{:S(2)}) collective-permute-start(bf16[256,768]{1,0:T(8,128)(2,1)} %get-tuple-element.288), channel_id=1, source_target_pairs={{0,8},{2,10},{4,12},{6,14},{8,0},{10,2},{12,4},{14,6},{1,9},{3,11}... | collective-permute-start | bytes 1179656 | tf_op jit(solution)/shard_map/ppermute | solution.py:34
  490.2 22.6 %collective-permute-start.55 = (bf16[112,576]{1,0:T(8,128)(2,1)S(1)}, bf16[112,576]{1,0:T(8,128)(2,1)S(1)}, u32[]{:S(2)}, u32[]{:S(2)}) collective-permute-start(bf16[112,576]{1,0:T(8,128)(2,1)S(1)} %get-tuple-element.338), channel_id=1, source_target_pairs={{0,4},{2,6},{4,8},{6,10},{8,12},{10,14},{12,0},{14,2},{1,5},{3,7},... | collective-permute-start | bytes 387080 | tf_op jit(solution)/shard_map/ppermute | solution.py:34
  503.7 12.2 %collective-permute-start.56 = (bf16[112,576]{1,0:T(8,128)(2,1)S(1)}, bf16[112,576]{1,0:T(8,128)(2,1)S(1)}, u32[]{:S(2)}, u32[]{:S(2)}) collective-permute-start(bf16[112,576]{1,0:T(8,128)(2,1)S(1)} %get-tuple-element.337), channel_id=1, source_target_pairs={{0,8},{2,10},{4,12},{6,14},{8,0},{10,2},{12,4},{14,6},{1,9},{3,11}... | collective-permute-start | bytes 387080 | tf_op jit(solution)/shard_map/ppermute | solution.py:34
  518.4 14.3 %collective-permute-start.58 = (bf16[256,768]{1,0:T(8,128)(2,1)S(1)}, bf16[256,768]{1,0:T(8,128)(2,1)S(1)}, u32[]{:S(2)}, u32[]{:S(2)}) collective-permute-start(bf16[256,768]{1,0:T(8,128)(2,1)S(1)} %copy-done.44), channel_id=1, source_target_pairs={{0,4},{2,6},{4,8},{6,10},{8,12},{10,14},{12,0},{14,2},{1,5},{3,7},... | collective-permute-start | bytes 1179656 | tf_op jit(solution)/shard_map/ppermute | solution.py:34
  (95 other events, 1308.3 us)
Sparse Core Ops, SparseCore 0:
  67.6 115.1 all-gather.4
  185.7 59.4 all-gather.6
  282.0 149.0 reduce-scatter.1

commit v7 on v6

--- a/solution.py
+++ b/solution.py
@@ -270,7 +270,7 @@
         results += [((HEAD_DIM, part), BF16)] * MEMBERS
     extra = [] if first else [start]
     found = pl.pallas_call(
-        functools.partial(backward_kernel, min(1024, query_count), chosen, first, last),
+        functools.partial(backward_kernel, min(2048, query_count), chosen, first, last),
         grid=(1,),
         in_specs=head_specs((queries, keys, values), places)
         + [whole((EXTRA, key_count))]
@@ -422,9 +422,6 @@
                 joined[slot, pl.ds(pl.multiple_of(start, HEAD_DIM), height), :] = ref[...]
                 start = start + height
         total = total + dot(joined[slot], weights[slot], 0, 1)
-    if len(out_refs) == 1:
-        out_refs[0][...] = total
-        return
     each = len(out_refs) // MEMBERS
     rows = acc_ref.shape[0] // each
     for index, out_ref in enumerate(out_refs):
@@ -435,7 +432,7 @@
             out_ref[...] = total[start : start + rows].astype(out_ref.dtype)
 
 
-def input_grad_step(info, acc, weights, slots, out_count, dtype):
+def input_grad_step(info, acc, weights, slots, out_count):
     arrays = flatten(slots)
     rows, width = acc.shape
     block = rows // MEMBERS
@@ -450,13 +447,13 @@
             + [pl.BlockSpec(dims, functools.partial(lambda at, i, info: at, place))
                for array, dims, place in weights]
             + [pl.BlockSpec((array.shape[0], block), lambda i, info: (0, i)) for array in arrays],
-            out_specs=[row_spec] if out_count == 1 else [whole(out)] * out_count,
+            out_specs=[whole(out)] * out_count,
             scratch_shapes=[
                 pltpu.VMEM((len(slots), width, block), BF16),
                 pltpu.VMEM((len(slots), width, width), BF16),
             ],
         ),
-        out_shape=[jax.ShapeDtypeStruct(out, dtype)] * out_count,
+        out_shape=[jax.ShapeDtypeStruct(out, BF16)] * out_count,
         compiler_params=pltpu.CompilerParams(vmem_limit_bytes=VMEM_LIMIT),
         cost_estimate=pl.CostEstimate(
             flops=2 * rows * width * width * len(slots),
@@ -1014,10 +1011,7 @@
         found, (partial,) = attention_backward(*given, grad_side, chosen, last=False)
         own = own_places(dict(zip(chosen, found)))
         sent = {member: send(member, own[member]) for member in far}
-        grad_input = input_grad_step(
-            row_starts, grad_input, slot_weights[:-1], sent_slots, 1, F32
-        )[0]
-        partial, grad_input = lax.optimization_barrier((partial, grad_input))
+        partial, sent_slots = stage((partial, sent_slots))
         chosen = range(0, pieces_here, 2)
         found, query_grads = attention_backward(*given, grad_side, chosen, start=partial)
         own.update(own_places(dict(zip(chosen, found))))
@@ -1027,7 +1021,7 @@
             [send(member, query_grads[member]), sent[member]] for member in range(MEMBERS)
         ]
     input_pieces = input_grad_step(
-        row_starts, grad_input, slot_weights[-1:], [last_sent], planes, BF16
+        row_starts, grad_input, slot_weights, sent_slots + [last_sent], planes
     )
     chunks = weight_grad(all_pieces, kept_slots, batches * planes, chunk_rows, block_rows)
     chunks = chunks.reshape((batches, planes) + chunks.shape[1:])

time: 557 us -> 551 us (0.989); the launches traced: 548 us -> 548 us
    pallas_call x1, Pallas kernels: 57.4 us -> 69.7 us  [layer_rows(): pl.pallas_call(functools.partial(layer_kernel, blocks, planes, parts), gr...]
    pallas_call x2 -> x1, Pallas kernels: 15.1 us -> 10.2 us  [input_grad_step(): pl.pallas_call(functools.partial(input_grad_kernel, counts_of(slots)), gr...]
where the time goes in v7:
time: 551 us; the launch traced here: 548 us
  Pallas kernels  325 us (59%)
  waiting for transfers between devices  81 us (15%)
  starting transfers between devices  78.5 us (14%)
  local copies, waits for them, and re-layouts  35.5 us (6%)
  between operations  15.6 us (3%)
  other arithmetic  12.6 us (2%)
    pallas_call x4, Pallas kernels, attention_backward(): pl.pallas_call(functools.partial(backward_kernel, min(2048, query_count),...  141 us
    pallas_call x4, Pallas kernels, attention_forward(): pl.pallas_call(functools.partial(forward_kernel, min(512, key_count), mem...  80.1 us
    pallas_call x1, Pallas kernels, layer_rows(): pl.pallas_call(functools.partial(layer_kernel, blocks, planes, parts), gr...  69.7 us
    ppermute x15, waiting for transfers between devices, shift_planes(): return lax.ppermute(array, 'blk', route)  47.9 us
    ppermute x15, starting transfers between devices, shift_planes(): return lax.ppermute(array, 'blk', route)  43.5 us
    ppermute x15, waiting for transfers between devices, swap_member(): return lax.ppermute(array, 'head', [(0, 1), (1, 0)])  19.9 us
    ppermute x15, starting transfers between devices, swap_member(): return lax.ppermute(array, 'head', [(0, 1), (1, 0)])  18.5 us
  transfers between devices with their start and end apart: 66, of which 17 were waited for; matrix products, arithmetic and copies ran while one was open for 6% of the time, Pallas kernels for 59%

profile of v7, /device:TPU:0, one launch (start us, length us, event | category | flops | bytes accessed | tf_op | source)
XLA Modules:
  0.0 548.3 jit_solution(6828149591712547469)
XLA Ops:
  8.8 3.1 collective-permute-start
  11.9 2.6 collective-permute-start.1
  20.5 5.2 collective-permute-done.3
  26.9 2.5 collective-permute-done.5
  29.5 10.4 %collective-permute-done.1.rest_2_ = bf16[256,768]{1,0:T(8,128)(2,1)S(1)} collective-permute-done((bf16[256,768]{1,0:T(8,128)(2,1)S(1)}, bf16[256,768]{1,0:T(8,128)(2,1)S(1)}, u32[]{:S(2)}, u32[]{:S(2)}) %collective-permute-start.1) | collective-permute-done | bytes 393248 | tf_op jit(solution)/shard_map/ppermute | solution.py:34
  41.2 3.5 all-to-all-start
  44.7 3.7 collective-permute-start.6
  51.2 2.6 concatenate.100
  53.8 12.7 %collective-permute-done.6.rest_3_ = bf16[256,768]{1,0:T(8,128)(2,1)} collective-permute-done((bf16[256,768]{1,0:T(8,128)(2,1)S(1)}, bf16[256,768]{1,0:T(8,128)(2,1)}, u32[]{:S(2)}, u32[]{:S(2)}) %collective-permute-start.6) | collective-permute-done | bytes 393248 | tf_op jit(solution)/shard_map/ppermute | solution.py:34
  68.2 1.6 collective-permute-start.17
  75.4 10.2 %collective-permute-done.16.rest_7_ = bf16[256,768]{1,0:T(8,128)(2,1)S(1)} collective-permute-done((bf16[256,768]{1,0:T(8,128)(2,1)}, bf16[256,768]{1,0:T(8,128)(2,1)S(1)}, u32[]{:S(2)}, u32[]{:S(2)}) %collective-permute-start.16) | collective-permute-done | bytes 393248 | tf_op jit(solution)/shard_map/ppermute | solution.py:51
  85.5 1.9 collective-permute-done.17
  91.8 9.1 %shard_map.305.q_ref.k_ref.v_ref = bf16[576,4096]{1,0:T(8,128)(2,1)} custom-call(bf16[768,576]{1,0:T(8,128)(2,1)} %bitcast.151, f32[576,1]{1,0:T(8,128)} %copy.138.bias_ref, bf16[256,768]{1,0:T(8,128)(2,1)} %copy-done.3, bf16[256,768]{1,0:T(8,128)(2,1)} %copy-done.38, bf16[256,768]{1,0:T(8,128)(2,1)} %copy-done.39, ...), custom_call_target="tpu_custom_call" | custom-call | flops 3623878656 | bytes 12582912 | tf_op jit(solution)/shard_map/pallas_call | solution.py:327
  101.8 4.0 collective-permute-start.19
  108.2 25.9 %shard_map.306 = (bf16[64,1024]{1,0:T(8,128)(2,1)}, bf16[64,1024]{1,0:T(8,128)(2,1)}, bf16[64,1024]{1,0:T(8,128)(2,1)}, bf16[64,1024]{1,0:T(8,128)(2,1)}, f32[1,...) custom-call(bf16[576,4096]{1,0:T(8,128)(2,1)} %shard_map.305.q_ref.k_ref.v_ref, ...), custom_call_target="tpu_custom_call" | custom-call | flops 17179869184 | bytes 2097152 | tf_op jit(solution)/shard_map/pallas_call | solution.py:140
  134.0 25.7 %shard_map.307 = (bf16[64,1024]{1,0:T(8,128)(2,1)}, bf16[64,1024]{1,0:T(8,128)(2,1)}, bf16[64,1024]{1,0:T(8,128)(2,1)}, bf16[64,1024]{1,0:T(8,128)(2,1)}, f32[1,...) custom-call(bf16[576,4096]{1,0:T(8,128)(2,1)} %shard_map.305.q_ref.k_ref.v_ref, ...), custom_call_target="tpu_custom_call" | custom-call | flops 17179869184 | bytes 2097152 | tf_op jit(solution)/shard_map/pallas_call | solution.py:140
  159.7 1.6 collective-permute-start.22
  163.7 14.2 %shard_map.308 = (bf16[64,1024]{1,0:T(8,128)(2,1)}, bf16[64,1024]{1,0:T(8,128)(2,1)}, f32[1,1024]{1,0:T(1,128)}, f32[1,1024]{1,0:T(1,128)}) custom-call(bf16[576,4096]{1,0:T(8,128)(2,1)} %shard_map.305.q_ref.k_ref.v_ref, bf16[576,4096]{1,0:T(8,128)(2,1)} %shard_map.305.q_ref.k_ref.v_ref, bf16[576,4096]{1,0:T(8,128)(2,1)} %shard_map.305.q_ref.k_ref.v_ref, ...), custom_call_target="tpu_custom_call" | custom-call | flops 8589934592 | bytes 2097152 | tf_op jit(solution)/shard_map/pallas_call | solution.py:140
  177.9 14.3 %shard_map.309 = (bf16[64,1024]{1,0:T(8,128)(2,1)}, bf16[64,1024]{1,0:T(8,128)(2,1)}, f32[1,1024]{1,0:T(1,128)}, f32[1,1024]{1,0:T(1,128)}) custom-call(bf16[576,4096]{1,0:T(8,128)(2,1)} %shard_map.305.q_ref.k_ref.v_ref, bf16[576,4096]{1,0:T(8,128)(2,1)} %shard_map.305.q_ref.k_ref.v_ref, bf16[576,4096]{1,0:T(8,128)(2,1)} %shard_map.305.q_ref.k_ref.v_ref, ...), custom_call_target="tpu_custom_call" | custom-call | flops 8589934592 | bytes 2097152 | tf_op jit(solution)/shard_map/pallas_call | solution.py:140
  194.4 1.7 collective-permute-start.24
  198.0 1.6 collective-permute-done.29.rest_17_
  199.6 3.5 collective-permute-done.24.rest_12_
  203.2 2.1 collective-permute-done.30.rest_18_
  205.9 69.7 %shard_map.310 = (bf16[256,768]{1,0:T(8,128)(2,1)}, bf16[256,768]{1,0:T(8,128)(2,1)}, bf16[256,768]{1,0:T(8,128)(2,1)}, bf16[256,768]{1,0:T(8,128)(2,1)}, bf16[6...) custom-call(s32[8]{0:T(128)} %pad_add_fusion.info_ref, ...), custom_call_target="tpu_custom_call" | custom-call | flops 28991029248 | bytes 18874368 | tf_op jit(solution)/shard_map/pallas_call | solution.py:661
  276.2 1.6 collective-permute-start.33
  277.8 4.3 collective-permute-start.37
  284.8 3.1 copy.148
  288.8 5.2 fusion.1
  297.4 45.0 %shard_map.311 = (bf16[192,1024]{1,0:T(8,128)(2,1)}, bf16[192,1024]{1,0:T(8,128)(2,1)}, bf16[192,1024]{1,0:T(8,128)(2,1)}, bf16[192,1024]{1,0:T(8,128)(2,1)}) custom-call(bf16[576,4096]{1,0:T(8,128)(2,1)} %shard_map.305.q_ref.k_ref.v_ref, bf16[576,4096]{1,0:T(8,128)(2,1)} %shard_map.305.q_ref.k_ref.v_ref, bf16[576,4096]{1,0:T(8,128)(2,1)} %shard_map.305.q_ref.k_ref.v_ref, ...), custom_call_target="tpu_custom_call" | custom-call | flops 42949672960 | bytes 4194304 | tf_op jit(solution)/shard_map/pallas_call | solution.py:272
  342.4 1.6 collective-permute-start.34
  344.7 45.5 %shard_map.313 = (bf16[192,1024]{1,0:T(8,128)(2,1)}, bf16[192,1024]{1,0:T(8,128)(2,1)}, bf16[192,1024]{1,0:T(8,128)(2,1)}, bf16[192,1024]{1,0:T(8,128)(2,1)}) custom-call(bf16[576,4096]{1,0:T(8,128)(2,1)} %shard_map.305.q_ref.k_ref.v_ref, bf16[576,4096]{1,0:T(8,128)(2,1)} %shard_map.305.q_ref.k_ref.v_ref, bf16[576,4096]{1,0:T(8,128)(2,1)} %shard_map.305.q_ref.k_ref.v_ref, ...), custom_call_target="tpu_custom_call" | custom-call | flops 42949672960 | bytes 4194304 | tf_op jit(solution)/shard_map/pallas_call | solution.py:272
  390.3 1.9 collective-permute-start.43
  392.2 2.6 shard_map.312
  395.2 24.8 %shard_map.314 = (bf16[128,1024]{1,0:T(8,128)(2,1)}, bf16[128,1024]{1,0:T(8,128)(2,1)}, f32[64,4096]{1,0:T(8,128)}) custom-call(bf16[576,4096]{1,0:T(8,128)(2,1)} %shard_map.305.q_ref.k_ref.v_ref, bf16[576,4096]{1,0:T(8,128)(2,1)} %shard_map.305.q_ref.k_ref.v_ref, bf16[576,4096]{1,0:T(8,128)(2,1)} %shard_map.305.q_ref.k_ref.v_ref, ...), custom_call_target="tpu_custom_call" | custom-call | flops 21474836480 | bytes 4194304 | tf_op jit(solution)/shard_map/pallas_call | solution.py:272
  420.1 1.9 collective-permute-start.47
  422.0 25.2 %shard_map.315 = (bf16[128,1024]{1,0:T(8,128)(2,1)}, bf16[128,1024]{1,0:T(8,128)(2,1)}, bf16[64,1024]{1,0:T(8,128)(2,1)}, bf16[64,1024]{1,0:T(8,128)(2,1)}, bf16...) custom-call(bf16[576,4096]{1,0:T(8,128)(2,1)} %shard_map.305.q_ref.k_ref.v_ref, ...), custom_call_target="tpu_custom_call" | custom-call | flops 21474836480 | bytes 4194304 | tf_op jit(solution)/shard_map/pallas_call | solution.py:272
  449.2 10.2 %shard_map.316 = bf16[8,112,576]{2,1,0:T(8,128)(2,1)} custom-call(bf16[256,768]{1,0:T(8,128)(2,1)} %copy-done.3, bf16[256,768]{1,0:T(8,128)(2,1)} %copy-done.38, bf16[256,768]{1,0:T(8,128)(2,1)} %copy-done.39, bf16[256,768]{1,0:T(8,128)(2,1)} %collective-permute-done.6.rest_3_, bf16[256,768]{1,0:T(8,128)(2,1)} %collective-permute-done.2.rest_4_, ...), custom_call_target="tpu_custom_call" | custom-call | flops 3623878656 | bytes 6291456 | tf_op jit(solution)/shard_map/pallas_call | solution.py:388
  461.3 3.4 collective-permute-done.50.rest_17_
  465.5 10.2 %shard_map.317 = (bf16[256,768]{1,0:T(8,128)(2,1)}, bf16[256,768]{1,0:T(8,128)(2,1)}, bf16[256,768]{1,0:T(8,128)(2,1)}, bf16[256,768]{1,0:T(8,128)(2,1)}) custom-call(s32[4]{0:T(128)} %copy-done.28, f32[1024,768]{1,0:T(8,128)} %get-tuple-element.285.acc_ref, bf16[32,72,768]{2,1,0:T(8,128)(2,1)} %bitcast.137, bf16[32,72,768]{2,1,0:T(8,128)(2,1)} %bitcast.138, ...), custom_call_target="tpu_custom_call" | custom-call | flops 3623878656 | bytes 6291456 | tf_op jit(solution)/shard_map/pallas_call | solution.py:441
  476.9 3.5 collective-permute-start.52
  480.4 9.8 %collective-permute-done.52.rest_1_ = bf16[256,768]{1,0:T(8,128)(2,1)S(1)} collective-permute-done((bf16[256,768]{1,0:T(8,128)(2,1)}, bf16[256,768]{1,0:T(8,128)(2,1)S(1)}, u32[]{:S(2)}, u32[]{:S(2)}) %collective-permute-start.52) | collective-permute-done | bytes 393248 | tf_op jit(solution)/shard_map/ppermute | solution.py:34
  491.2 13.1 %collective-permute-start.55 = (bf16[112,576]{1,0:T(8,128)(2,1)S(1)}, bf16[112,576]{1,0:T(8,128)(2,1)S(1)}, u32[]{:S(2)}, u32[]{:S(2)}) collective-permute-start(bf16[112,576]{1,0:T(8,128)(2,1)S(1)} %get-tuple-element.352), channel_id=1, source_target_pairs={{0,4},{2,6},{4,8},{6,10},{8,12},{10,14},{12,0},{14,2},{1,5},{3,7},... | collective-permute-start | bytes 387080 | tf_op jit(solution)/shard_map/ppermute | solution.py:34
  504.3 2.4 collective-permute-start.57
  506.8 6.7 %collective-permute-done.54.rest_2_ = bf16[256,768]{1,0:T(8,128)(2,1)S(1)} collective-permute-done((bf16[256,768]{1,0:T(8,128)(2,1)}, bf16[256,768]{1,0:T(8,128)(2,1)S(1)}, u32[]{:S(2)}, u32[]{:S(2)}) %collective-permute-start.54) | collective-permute-done | bytes 393248 | tf_op jit(solution)/shard_map/ppermute | solution.py:34
  513.5 3.1 collective-permute-done.56
  519.0 2.9 collective-permute-start.58
  528.5 5.2 collective-permute-done.58.rest_3_
  534.4 2.6 shard_map.318
  (385 shorter events, 63.5 us)
Async XLA Ops:
  8.8 20.7 %collective-permute-start = (bf16[256,768]{1,0:T(8,128)(2,1)S(1)}, bf16[256,768]{1,0:T(8,128)(2,1)S(1)}, u32[]{:S(2)}, u32[]{:S(2)}) collective-permute-start(bf16[256,768]{1,0:T(8,128)(2,1)S(1)} %get-tuple-element.334), channel_id=1, source_target_pairs={{0,4},{2,6},{4,8},{6,10},{8,12},{10,14},{12,0},{14,2},{1,5},{3,7},... | collective-permute-start | bytes 1179656 | tf_op jit(solution)/shard_map/ppermute | solution.py:34
  11.9 28.0 %collective-permute-start.1 = (bf16[256,768]{1,0:T(8,128)(2,1)S(1)}, bf16[256,768]{1,0:T(8,128)(2,1)S(1)}, u32[]{:S(2)}, u32[]{:S(2)}) collective-permute-start(bf16[256,768]{1,0:T(8,128)(2,1)S(1)} %get-tuple-element.336), channel_id=1, source_target_pairs={{0,8},{2,10},{4,12},{6,14},{8,0},{10,2},{12,4},{14,6},{1,9},{3,11}... | collective-permute-start | bytes 1179656 | tf_op jit(solution)/shard_map/ppermute | solution.py:34
  14.5 25.4 %collective-permute-start.2 = (bf16[256,768]{1,0:T(8,128)(2,1)S(1)}, bf16[256,768]{1,0:T(8,128)(2,1)}, u32[]{:S(2)}, u32[]{:S(2)}) collective-permute-start(bf16[256,768]{1,0:T(8,128)(2,1)S(1)} %get-tuple-element.191.rest_0_), channel_id=1, source_target_pairs={{0,1},{1,0},{2,3},{3,2},{4,5},{5,4},{6,7},{7,6},{8,9},{9,8},{10,11... | collective-permute-start | bytes 1179656 | tf_op jit(solution)/shard_map/ppermute | solution.py:51
  41.2 26.3 %all-to-all-start = ((bf16[4,4,32,576]{3,1,2,0:T(4,128)(2,1)}), bf16[4,4,32,576]{3,1,2,0:T(4,128)(2,1)S(1)}, u32[]{:S(2)}, u32[]{:S(2)}) async-start(bf16[4,4,32,576]{3,1,2,0:T(4,128)(2,1)} %broadcast_in_dim.30), calls=%async_computation | async-start | bytes 1310720 | tf_op jit(solution)/shard_map/all_to_all | solution.py:40
  44.7 147.6 %all-gather.5.cloned.1.call-start = ((), (), s32[]{:S(2)}) async-start(), calls=%async_computation.3 | async-start | bytes 11354112 | tf_op jit(solution)/shard_map/all_gather | solution.py:831
  44.7 21.8 %collective-permute-start.6 = (bf16[256,768]{1,0:T(8,128)(2,1)S(1)}, bf16[256,768]{1,0:T(8,128)(2,1)}, u32[]{:S(2)}, u32[]{:S(2)}) collective-permute-start(bf16[256,768]{1,0:T(8,128)(2,1)S(1)} %get-tuple-element.174), channel_id=1, source_target_pairs={{0,12},{2,14},{4,0},{6,2},{8,4},{10,6},{12,8},{14,10},{1,13},{3,15... | collective-permute-start | bytes 1179656 | tf_op jit(solution)/shard_map/ppermute | solution.py:34
  48.5 18.1 %collective-permute-start.7 = (bf16[256,768]{1,0:T(8,128)(2,1)S(1)}, bf16[256,768]{1,0:T(8,128)(2,1)}, u32[]{:S(2)}, u32[]{:S(2)}) collective-permute-start(bf16[256,768]{1,0:T(8,128)(2,1)S(1)} %collective-permute-done.rest_1_), channel_id=1, source_target_pairs={{0,1},{1,0},{2,3},{3,2},{4,5},{5,4},{6,7},{7,6},{8,9},{9,8},{10,11... | collective-permute-start | bytes 1179656 | tf_op jit(solution)/shard_map/ppermute | solution.py:51
  50.0 17.5 %collective-permute-start.8 = (bf16[256,768]{1,0:T(8,128)(2,1)S(1)}, bf16[256,768]{1,0:T(8,128)(2,1)}, u32[]{:S(2)}, u32[]{:S(2)}) collective-permute-start(bf16[256,768]{1,0:T(8,128)(2,1)S(1)} %collective-permute-done.1.rest_2_), channel_id=1, source_target_pairs={{0,1},{1,0},{2,3},{3,2},{4,5},{5,4},{6,7},{7,6},{8,9},{9,8},{10,11... | collective-permute-start | bytes 1179656 | tf_op jit(solution)/shard_map/ppermute | solution.py:51
  50.5 17.0 %collective-permute-start.9 = (bf16[256,768]{1,0:T(8,128)(2,1)S(1)}, bf16[256,768]{1,0:T(8,128)(2,1)}, u32[]{:S(2)}, u32[]{:S(2)}) collective-permute-start(bf16[256,768]{1,0:T(8,128)(2,1)S(1)} %get-tuple-element.191.rest_0_), channel_id=1, source_target_pairs={{0,2},{2,0},{4,6},{6,4},{8,10},{10,8},{12,14},{14,12},{1,3},{3,1},... | collective-permute-start | bytes 1179656 | tf_op jit(solution)/shard_map/ppermute | solution.py:53
  50.5 17.0 %collective-permute-start.10 = (bf16[256,768]{1,0:T(8,128)(2,1)}, bf16[256,768]{1,0:T(8,128)(2,1)}, u32[]{:S(2)}, u32[]{:S(2)}) collective-permute-start(bf16[256,768]{1,0:T(8,128)(2,1)} %collective-permute-done.2.rest_4_), channel_id=1, source_target_pairs={{0,2},{2,0},{4,6},{6,4},{8,10},{10,8},{12,14},{14,12},{1,3},{3,1},... | collective-permute-start | bytes 1179656 | tf_op jit(solution)/shard_map/ppermute | solution.py:53
  67.5 393.8 %all-gather.7.cloned.1.call-start = ((), (), s32[]{:S(2)}) async-start(), calls=%async_computation.4 | async-start | bytes 3649536 | tf_op jit(solution)/shard_map/all_gather | solution.py:871
  68.2 19.2 %collective-permute-start.17 = (bf16[4,4,32,576]{3,2,1,0:T(8,128)(2,1)S(1)}, bf16[4,4,32,576]{3,2,1,0:T(8,128)(2,1)S(1)}, u32[]{:S(2)}, u32[]{:S(2)}) collective-permute-start(bf16[4,4,32,576]{3,2,1,0:T(8,128)(2,1)S(1)} %copy.136), channel_id=1, source_target_pairs={{0,16},{16,0},{1,17},{17,1},{2,18},{18,2},{3,19},{19,3},{4,20},{20... | collective-permute-start | bytes 1769480 | tf_op jit(solution)/shard_map/ppermute | solution.py:45
  71.8 13.7 %collective-permute-start.16 = (bf16[256,768]{1,0:T(8,128)(2,1)}, bf16[256,768]{1,0:T(8,128)(2,1)S(1)}, u32[]{:S(2)}, u32[]{:S(2)}) collective-permute-start(bf16[256,768]{1,0:T(8,128)(2,1)} %collective-permute-done.6.rest_3_), channel_id=1, source_target_pairs={{0,1},{1,0},{2,3},{3,2},{4,5},{5,4},{6,7},{7,6},{8,9},{9,8},{10,11... | collective-permute-start | bytes 1179656 | tf_op jit(solution)/shard_map/ppermute | solution.py:51
  75.2 461.9 %reduce-scatter.2.cloned.1.call-start = ((), (), s32[]{:S(2)}) async-start(), calls=%async_computation.2 | async-start | bytes 11354112 | tf_op jit(solution)/shard_map/reduce_scatter | solution.py:967
  101.8 60.0 %collective-permute-start.19 = (bf16[256,768]{1,0:T(8,128)(2,1)S(1)}, bf16[256,768]{1,0:T(8,128)(2,1)S(1)}, u32[]{:S(2)}, u32[]{:S(2)}) collective-permute-start(bf16[256,768]{1,0:T(8,128)(2,1)S(1)} %get-tuple-element.331), channel_id=1, source_target_pairs={{0,4},{2,6},{4,8},{6,10},{8,12},{10,14},{12,0},{14,2},{1,5},{3,7},... | collective-permute-start | bytes 1179656 | tf_op jit(solution)/shard_map/ppermute | solution.py:34
  105.8 56.1 %collective-permute-start.20 = (bf16[256,768]{1,0:T(8,128)(2,1)S(1)}, bf16[256,768]{1,0:T(8,128)(2,1)S(1)}, u32[]{:S(2)}, u32[]{:S(2)}) collective-permute-start(bf16[256,768]{1,0:T(8,128)(2,1)S(1)} %get-tuple-element.330), channel_id=1, source_target_pairs={{0,8},{2,10},{4,12},{6,14},{8,0},{10,2},{12,4},{14,6},{1,9},{3,11}... | collective-permute-start | bytes 1179656 | tf_op jit(solution)/shard_map/ppermute | solution.py:34
  107.1 55.3 %collective-permute-start.21 = (bf16[256,768]{1,0:T(8,128)(2,1)S(1)}, bf16[256,768]{1,0:T(8,128)(2,1)S(1)}, u32[]{:S(2)}, u32[]{:S(2)}) collective-permute-start(bf16[256,768]{1,0:T(8,128)(2,1)S(1)} %get-tuple-element.329), channel_id=1, source_target_pairs={{0,12},{2,14},{4,0},{6,2},{8,4},{10,6},{12,8},{14,10},{1,13},{3,15... | collective-permute-start | bytes 1179656 | tf_op jit(solution)/shard_map/ppermute | solution.py:34
  159.7 34.0 %collective-permute-start.22 = (bf16[64,1024]{1,0:T(8,128)(2,1)S(1)}, bf16[64,1024]{1,0:T(8,128)(2,1)S(1)}, u32[]{:S(2)}, u32[]{:S(2)}) collective-permute-start(bf16[64,1024]{1,0:T(8,128)(2,1)S(1)} %copy-done.59), channel_id=1, source_target_pairs={{0,1},{1,0},{2,3},{3,2},{4,5},{5,4},{6,7},{7,6},{8,9},{9,8},{10,11... | collective-permute-start | bytes 393224 | tf_op jit(solution)/shard_map/ppermute | solution.py:51
  161.3 33.1 %collective-permute-start.23 = (bf16[64,1024]{1,0:T(8,128)(2,1)}, bf16[64,1024]{1,0:T(8,128)(2,1)S(1)}, u32[]{:S(2)}, u32[]{:S(2)}) collective-permute-start(bf16[64,1024]{1,0:T(8,128)(2,1)} %get-tuple-element.219.rest_5_), channel_id=1, source_target_pairs={{0,1},{1,0},{2,3},{3,2},{4,5},{5,4},{6,7},{7,6},{8,9},{9,8},{10,11... | collective-permute-start | bytes 393224 | tf_op jit(solution)/shard_map/ppermute | solution.py:51
  161.8 34.2 %collective-permute-start.25 = (bf16[64,1024]{1,0:T(8,128)(2,1)S(1)}, bf16[64,1024]{1,0:T(8,128)(2,1)S(1)}, u32[]{:S(2)}, u32[]{:S(2)}) collective-permute-start(bf16[64,1024]{1,0:T(8,128)(2,1)S(1)} %copy-done.60), channel_id=1, source_target_pairs={{0,2},{2,0},{4,6},{6,4},{8,10},{10,8},{12,14},{14,12},{1,3},{3,1},... | collective-permute-start | bytes 393224 | tf_op jit(solution)/shard_map/ppermute | solution.py:53
  161.9 34.2 %collective-permute-start.26 = (bf16[64,1024]{1,0:T(8,128)(2,1)}, bf16[64,1024]{1,0:T(8,128)(2,1)S(1)}, u32[]{:S(2)}, u32[]{:S(2)}) collective-permute-start(bf16[64,1024]{1,0:T(8,128)(2,1)} %get-tuple-element.221.rest_6_), channel_id=1, source_target_pairs={{0,2},{2,0},{4,6},{6,4},{8,10},{10,8},{12,14},{14,12},{1,3},{3,1},... | collective-permute-start | bytes 393224 | tf_op jit(solution)/shard_map/ppermute | solution.py:53
  162.4 35.6 %collective-permute-start.28 = (bf16[64,1024]{1,0:T(8,128)(2,1)S(1)}, bf16[64,1024]{1,0:T(8,128)(2,1)S(1)}, u32[]{:S(2)}, u32[]{:S(2)}) collective-permute-start(bf16[64,1024]{1,0:T(8,128)(2,1)S(1)} %copy-done.61), channel_id=1, source_target_pairs={{0,3},{1,2},{2,1},{3,0},{4,7},{5,6},{6,5},{7,4},{8,11},{9,10},{10,... | collective-permute-start | bytes 393224 | tf_op jit(solution)/shard_map/ppermute | solution.py:55
  275.6 18.5 %collective-permute-start.31 = (bf16[64,1024]{1,0:T(8,128)(2,1)}, bf16[64,1024]{1,0:T(8,128)(2,1)S(1)}, u32[]{:S(2)}, u32[]{:S(2)}) collective-permute-start(bf16[64,1024]{1,0:T(8,128)(2,1)} %get-tuple-element.230), channel_id=1, source_target_pairs={{0,1},{1,0},{2,3},{3,2},{4,5},{5,4},{6,7},{7,6},{8,9},{9,8},{10,11... | collective-permute-start | bytes 393224 | tf_op jit(solution)/shard_map/ppermute | solution.py:51
  276.0 20.4 %collective-permute-start.32 = (bf16[64,1024]{1,0:T(8,128)(2,1)}, bf16[64,1024]{1,0:T(8,128)(2,1)S(1)}, u32[]{:S(2)}, u32[]{:S(2)}) collective-permute-start(bf16[64,1024]{1,0:T(8,128)(2,1)} %get-tuple-element.231), channel_id=1, source_target_pairs={{0,2},{2,0},{4,6},{6,4},{8,10},{10,8},{12,14},{14,12},{1,3},{3,1},... | collective-permute-start | bytes 393224 | tf_op jit(solution)/shard_map/ppermute | solution.py:53
  276.2 20.2 %collective-permute-start.33 = (bf16[64,1024]{1,0:T(8,128)(2,1)}, bf16[64,1024]{1,0:T(8,128)(2,1)S(1)}, u32[]{:S(2)}, u32[]{:S(2)}) collective-permute-start(bf16[64,1024]{1,0:T(8,128)(2,1)} %get-tuple-element.232), channel_id=1, source_target_pairs={{0,3},{1,2},{2,1},{3,0},{4,7},{5,6},{6,5},{7,4},{8,11},{9,10},{10,... | collective-permute-start | bytes 393224 | tf_op jit(solution)/shard_map/ppermute | solution.py:55
  277.8 66.3 %collective-permute-start.37 = (bf16[256,768]{1,0:T(8,128)(2,1)}, bf16[256,768]{1,0:T(8,128)(2,1)S(1)}, u32[]{:S(2)}, u32[]{:S(2)}) collective-permute-start(bf16[256,768]{1,0:T(8,128)(2,1)} %get-tuple-element.238), channel_id=1, source_target_pairs={{0,12},{2,14},{4,0},{6,2},{8,4},{10,6},{12,8},{14,10},{1,13},{3,15... | collective-permute-start | bytes 1179656 | tf_op jit(solution)/shard_map/ppermute | solution.py:34
  282.1 14.5 %collective-permute-start.40 = (bf16[128,1024]{1,0:T(8,128)(2,1)}, bf16[128,1024]{1,0:T(8,128)(2,1)S(1)}, u32[]{:S(2)}, u32[]{:S(2)}) collective-permute-start(bf16[128,1024]{1,0:T(8,128)(2,1)} %get-tuple-element.242), channel_id=1, source_target_pairs={{0,1},{1,0},{2,3},{3,2},{4,5},{5,4},{6,7},{7,6},{8,9},{9,8},{10,11... | collective-permute-start | bytes 786440 | tf_op jit(solution)/shard_map/ppermute | solution.py:51
  295.0 49.6 %collective-permute-start.38 = (bf16[256,768]{1,0:T(8,128)(2,1)S(1)}, bf16[256,768]{1,0:T(8,128)(2,1)S(1)}, u32[]{:S(2)}, u32[]{:S(2)}) collective-permute-start(bf16[256,768]{1,0:T(8,128)(2,1)S(1)} %copy-done.50), channel_id=1, source_target_pairs={{0,8},{2,10},{4,12},{6,14},{8,0},{10,2},{12,4},{14,6},{1,9},{3,11}... | collective-permute-start | bytes 1179656 | tf_op jit(solution)/shard_map/ppermute | solution.py:34
  296.4 48.2 %collective-permute-start.39 = (bf16[256,768]{1,0:T(8,128)(2,1)S(1)}, bf16[256,768]{1,0:T(8,128)(2,1)S(1)}, u32[]{:S(2)}, u32[]{:S(2)}) collective-permute-start(bf16[256,768]{1,0:T(8,128)(2,1)S(1)} %copy-done.48), channel_id=1, source_target_pairs={{0,4},{2,6},{4,8},{6,10},{8,12},{10,14},{12,0},{14,2},{1,5},{3,7},... | collective-permute-start | bytes 1179656 | tf_op jit(solution)/shard_map/ppermute | solution.py:34
  296.5 45.9 %collective-permute-start.41 = (bf16[128,1024]{1,0:T(8,128)(2,1)S(1)}, bf16[128,1024]{1,0:T(8,128)(2,1)S(1)}, u32[]{:S(2)}, u32[]{:S(2)}) collective-permute-start(bf16[128,1024]{1,0:T(8,128)(2,1)S(1)} %copy-done.56), channel_id=1, source_target_pairs={{0,2},{2,0},{4,6},{6,4},{8,10},{10,8},{12,14},{14,12},{1,3},{3,1},... | collective-permute-start | bytes 786440 | tf_op jit(solution)/shard_map/ppermute | solution.py:53
  296.6 47.4 %collective-permute-start.42 = (bf16[128,1024]{1,0:T(8,128)(2,1)S(1)}, bf16[128,1024]{1,0:T(8,128)(2,1)S(1)}, u32[]{:S(2)}, u32[]{:S(2)}) collective-permute-start(bf16[128,1024]{1,0:T(8,128)(2,1)S(1)} %copy-done.55), channel_id=1, source_target_pairs={{0,3},{1,2},{2,1},{3,0},{4,7},{5,6},{6,5},{7,4},{8,11},{9,10},{10,... | collective-permute-start | bytes 786440 | tf_op jit(solution)/shard_map/ppermute | solution.py:55
  342.4 52.4 %collective-permute-start.34 = (bf16[192,1024]{1,0:T(8,128)(2,1)}, bf16[192,1024]{1,0:T(8,128)(2,1)S(1)}, u32[]{:S(2)}, u32[]{:S(2)}) collective-permute-start(bf16[192,1024]{1,0:T(8,128)(2,1)} %get-tuple-element.234.rest_17_), channel_id=1, source_target_pairs={{0,1},{1,0},{2,3},{3,2},{4,5},{5,4},{6,7},{7,6},{8,9},{9,8},{10,11... | collective-permute-start | bytes 1179656 | tf_op jit(solution)/shard_map/ppermute | solution.py:51
  344.1 51.1 %collective-permute-start.35 = (bf16[192,1024]{1,0:T(8,128)(2,1)}, bf16[192,1024]{1,0:T(8,128)(2,1)S(1)}, u32[]{:S(2)}, u32[]{:S(2)}) collective-permute-start(bf16[192,1024]{1,0:T(8,128)(2,1)} %get-tuple-element.235.rest_18_), channel_id=1, source_target_pairs={{0,2},{2,0},{4,6},{6,4},{8,10},{10,8},{12,14},{14,12},{1,3},{3,1},... | collective-permute-start | bytes 1179656 | tf_op jit(solution)/shard_map/ppermute | solution.py:53
  344.1 51.1 %collective-permute-start.36 = (bf16[192,1024]{1,0:T(8,128)(2,1)}, bf16[192,1024]{1,0:T(8,128)(2,1)S(1)}, u32[]{:S(2)}, u32[]{:S(2)}) collective-permute-start(bf16[192,1024]{1,0:T(8,128)(2,1)} %get-tuple-element.236.rest_19_), channel_id=1, source_target_pairs={{0,3},{1,2},{2,1},{3,0},{4,7},{5,6},{6,5},{7,4},{8,11},{9,10},{10,... | collective-permute-start | bytes 1179656 | tf_op jit(solution)/shard_map/ppermute | solution.py:55
  390.3 31.6 %collective-permute-start.43 = (bf16[192,1024]{1,0:T(8,128)(2,1)}, bf16[192,1024]{1,0:T(8,128)(2,1)S(1)}, u32[]{:S(2)}, u32[]{:S(2)}) collective-permute-start(bf16[192,1024]{1,0:T(8,128)(2,1)} %get-tuple-element.259.rest_21_), channel_id=1, source_target_pairs={{0,1},{1,0},{2,3},{3,2},{4,5},{5,4},{6,7},{7,6},{8,9},{9,8},{10,11... | collective-permute-start | bytes 1179656 | tf_op jit(solution)/shard_map/ppermute | solution.py:51
  392.2 29.7 %collective-permute-start.44 = (bf16[192,1024]{1,0:T(8,128)(2,1)}, bf16[192,1024]{1,0:T(8,128)(2,1)S(1)}, u32[]{:S(2)}, u32[]{:S(2)}) collective-permute-start(bf16[192,1024]{1,0:T(8,128)(2,1)} %get-tuple-element.260.rest_22_), channel_id=1, source_target_pairs={{0,2},{2,0},{4,6},{6,4},{8,10},{10,8},{12,14},{14,12},{1,3},{3,1},... | collective-permute-start | bytes 1179656 | tf_op jit(solution)/shard_map/ppermute | solution.py:53
  394.9 27.1 %collective-permute-start.45 = (bf16[192,1024]{1,0:T(8,128)(2,1)S(1)}, bf16[192,1024]{1,0:T(8,128)(2,1)S(1)}, u32[]{:S(2)}, u32[]{:S(2)}) collective-permute-start(bf16[192,1024]{1,0:T(8,128)(2,1)S(1)} %copy-done.51), channel_id=1, source_target_pairs={{0,3},{1,2},{2,1},{3,0},{4,7},{5,6},{6,5},{7,4},{8,11},{9,10},{10,... | collective-permute-start | bytes 1179656 | tf_op jit(solution)/shard_map/ppermute | solution.py:55
  420.1 39.4 %collective-permute-start.47 = (bf16[128,1024]{1,0:T(8,128)(2,1)}, bf16[128,1024]{1,0:T(8,128)(2,1)S(1)}, u32[]{:S(2)}, u32[]{:S(2)}) collective-permute-start(bf16[128,1024]{1,0:T(8,128)(2,1)} %get-tuple-element.279.rest_27_), channel_id=1, source_target_pairs={{0,1},{1,0},{2,3},{3,2},{4,5},{5,4},{6,7},{7,6},{8,9},{9,8},{10,11... | collective-permute-start | bytes 786440 | tf_op jit(solution)/shard_map/ppermute | solution.py:51
  421.9 39.4 %collective-permute-start.51 = (bf16[128,1024]{1,0:T(8,128)(2,1)}, bf16[128,1024]{1,0:T(8,128)(2,1)S(1)}, u32[]{:S(2)}, u32[]{:S(2)}) collective-permute-start(bf16[128,1024]{1,0:T(8,128)(2,1)} %get-tuple-element.283.rest_31_), channel_id=1, source_target_pairs={{0,3},{1,2},{2,1},{3,0},{4,7},{5,6},{6,5},{7,4},{8,11},{9,10},{10,... | collective-permute-start | bytes 786440 | tf_op jit(solution)/shard_map/ppermute | solution.py:55
  447.2 14.1 %collective-permute-start.46 = (bf16[64,1024]{1,0:T(8,128)(2,1)}, bf16[64,1024]{1,0:T(8,128)(2,1)S(1)}, u32[]{:S(2)}, u32[]{:S(2)}) collective-permute-start(bf16[64,1024]{1,0:T(8,128)(2,1)} %get-tuple-element.278.rest_26_), channel_id=1, source_target_pairs={{0,1},{1,0},{2,3},{3,2},{4,5},{5,4},{6,7},{7,6},{8,9},{9,8},{10,11... | collective-permute-start | bytes 393224 | tf_op jit(solution)/shard_map/ppermute | solution.py:51
  448.7 12.6 %collective-permute-start.48 = (bf16[64,1024]{1,0:T(8,128)(2,1)}, bf16[64,1024]{1,0:T(8,128)(2,1)S(1)}, u32[]{:S(2)}, u32[]{:S(2)}) collective-permute-start(bf16[64,1024]{1,0:T(8,128)(2,1)} %get-tuple-element.280.rest_28_), channel_id=1, source_target_pairs={{0,2},{2,0},{4,6},{6,4},{8,10},{10,8},{12,14},{14,12},{1,3},{3,1},... | collective-permute-start | bytes 393224 | tf_op jit(solution)/shard_map/ppermute | solution.py:53
  449.2 15.6 %collective-permute-start.49 = (bf16[128,1024]{1,0:T(8,128)(2,1)}, bf16[128,1024]{1,0:T(8,128)(2,1)S(1)}, u32[]{:S(2)}, u32[]{:S(2)}) collective-permute-start(bf16[128,1024]{1,0:T(8,128)(2,1)} %get-tuple-element.281.rest_29_), channel_id=1, source_target_pairs={{0,2},{2,0},{4,6},{6,4},{8,10},{10,8},{12,14},{14,12},{1,3},{3,1},... | collective-permute-start | bytes 786440 | tf_op jit(solution)/shard_map/ppermute | solution.py:53
  475.7 15.3 %collective-permute-start.53 = (bf16[4,112,576]{2,1,0:T(8,128)(2,1)S(1)}, bf16[4,112,576]{2,1,0:T(8,128)(2,1)S(1)}, u32[]{:S(2)}, u32[]{:S(2)}) collective-permute-start(bf16[4,112,576]{2,1,0:T(8,128)(2,1)S(1)} %get-tuple-element.300), channel_id=1, source_target_pairs={{0,16},{16,0},{1,17},{17,1},{2,18},{18,2},{3,19},{19,3},{4,20},{20... | collective-permute-start | bytes 1548296 | tf_op jit(solution)/shard_map/ppermute | solution.py:45
  476.9 13.4 %collective-permute-start.52 = (bf16[256,768]{1,0:T(8,128)(2,1)}, bf16[256,768]{1,0:T(8,128)(2,1)S(1)}, u32[]{:S(2)}, u32[]{:S(2)}) collective-permute-start(bf16[256,768]{1,0:T(8,128)(2,1)} %get-tuple-element.299), channel_id=1, source_target_pairs={{0,12},{2,14},{4,0},{6,2},{8,4},{10,6},{12,8},{14,10},{1,13},{3,15... | collective-permute-start | bytes 1179656 | tf_op jit(solution)/shard_map/ppermute | solution.py:34
  480.4 33.0 %collective-permute-start.54 = (bf16[256,768]{1,0:T(8,128)(2,1)}, bf16[256,768]{1,0:T(8,128)(2,1)S(1)}, u32[]{:S(2)}, u32[]{:S(2)}) collective-permute-start(bf16[256,768]{1,0:T(8,128)(2,1)} %get-tuple-element.302), channel_id=1, source_target_pairs={{0,8},{2,10},{4,12},{6,14},{8,0},{10,2},{12,4},{14,6},{1,9},{3,11}... | collective-permute-start | bytes 1179656 | tf_op jit(solution)/shard_map/ppermute | solution.py:34
  491.2 22.2 %collective-permute-start.55 = (bf16[112,576]{1,0:T(8,128)(2,1)S(1)}, bf16[112,576]{1,0:T(8,128)(2,1)S(1)}, u32[]{:S(2)}, u32[]{:S(2)}) collective-permute-start(bf16[112,576]{1,0:T(8,128)(2,1)S(1)} %get-tuple-element.352), channel_id=1, source_target_pairs={{0,4},{2,6},{4,8},{6,10},{8,12},{10,14},{12,0},{14,2},{1,5},{3,7},... | collective-permute-start | bytes 387080 | tf_op jit(solution)/shard_map/ppermute | solution.py:34
  504.3 12.2 %collective-permute-start.56 = (bf16[112,576]{1,0:T(8,128)(2,1)S(1)}, bf16[112,576]{1,0:T(8,128)(2,1)S(1)}, u32[]{:S(2)}, u32[]{:S(2)}) collective-permute-start(bf16[112,576]{1,0:T(8,128)(2,1)S(1)} %get-tuple-element.351), channel_id=1, source_target_pairs={{0,8},{2,10},{4,12},{6,14},{8,0},{10,2},{12,4},{14,6},{1,9},{3,11}... | collective-permute-start | bytes 387080 | tf_op jit(solution)/shard_map/ppermute | solution.py:34
  519.0 14.6 %collective-permute-start.58 = (bf16[256,768]{1,0:T(8,128)(2,1)S(1)}, bf16[256,768]{1,0:T(8,128)(2,1)S(1)}, u32[]{:S(2)}, u32[]{:S(2)}) collective-permute-start(bf16[256,768]{1,0:T(8,128)(2,1)S(1)} %copy-done.45), channel_id=1, source_target_pairs={{0,4},{2,6},{4,8},{6,10},{8,12},{10,14},{12,0},{14,2},{1,5},{3,7},... | collective-permute-start | bytes 1179656 | tf_op jit(solution)/shard_map/ppermute | solution.py:34
  (96 other events, 1345.1 us)
Sparse Core Ops, SparseCore 0:
  67.6 115.1 all-gather.4
  185.7 59.4 all-gather.6
  294.1 149.9 reduce-scatter.1

commit v8 on v7

--- a/solution.py
+++ b/solution.py
@@ -972,7 +972,7 @@
     owned_vectors = owned[out_start + share]
 
     chunk_rows = width // (batches * planes)
-    block_rows = chunk_rows + -chunk_rows % 16 + 16
+    block_rows = chunk_rows + -chunk_rows % 8 + 8
 
     def own_places(found):
         own = {index: array for index, array in found.items() if index < MEMBERS}
@@ -1004,8 +1004,7 @@
             kept_slots.append([[own[member]] for member in range(MEMBERS)])
             sent_slots.append([[send(member, own[member])] for member in range(MEMBERS)])
             continue
-        output = collect(output_pieces, plane)
-        sent_slots[:-1], grad_sent, output = stage((sent_slots[:-1], grad_sent, output))
+        sent_slots[:-1], grad_sent = stage((sent_slots[:-1], grad_sent))
         grad_side = [(array, place) for array in grad_sent]
         chosen = range(1, pieces_here, 2)
         found, (partial,) = attention_backward(*given, grad_side, chosen, last=False)
@@ -1052,7 +1051,6 @@
     ]
     got = reorder_members(jnp.stack(got), core, head_place)
     got = got.reshape(MEMBERS, piece_rows, heads_here, 3, HEAD_DIM)
-    output = output.reshape(seqs, part_rows, width)
     matrices = [
         jnp.swapaxes(got[:, :share, :, i], 0, 1).reshape(share, width) for i in range(3)
     ]
@@ -1061,7 +1059,8 @@
         for i in (0, 2)
     ]
 
-    arrived, matrices, biases = stage((arrived, matrices, biases))
+    output = collect(output_pieces, plane).reshape(seqs, part_rows, width)
+    arrived, matrices, biases, output = stage((arrived, matrices, biases, output))
     input_grad = collect([input_pieces[0]] + arrived, plane).reshape(seqs, part_rows, width)
 
     def vector(index):

time: 551 us -> 550 us (level)
  transfers between devices with their start and end apart: 66 -> 66, of which waited for: 17 -> 15; matrix products, arithmetic and copies ran while one was open for 6% -> 6% of each run, Pallas kernels for 59% -> 59%
where the time goes in v8:
time: 550 us; the launch traced here: 547 us
  Pallas kernels  325 us (59%)
  waiting for transfers between devices  80.1 us (15%)
  starting transfers between devices  78.6 us (14%)
  local copies, waits for them, and re-layouts  35.5 us (6%)
  between operations  15.6 us (3%)
  other arithmetic  12.6 us (2%)
    pallas_call x4, Pallas kernels, attention_backward(): pl.pallas_call(functools.partial(backward_kernel, min(2048, query_count),...  141 us
    pallas_call x4, Pallas kernels, attention_forward(): pl.pallas_call(functools.partial(forward_kernel, min(512, key_count), mem...  80.1 us
    pallas_call x1, Pallas kernels, layer_rows(): pl.pallas_call(functools.partial(layer_kernel, blocks, planes, parts), gr...  69.7 us
    ppermute x15, waiting for transfers between devices, shift_planes(): return lax.ppermute(array, 'blk', route)  48.3 us
    ppermute x15, starting transfers between devices, shift_planes(): return lax.ppermute(array, 'blk', route)  43.6 us
    ppermute x15, waiting for transfers between devices, swap_member(): return lax.ppermute(array, 'head', [(0, 1), (1, 0)])  19.9 us
    ppermute x15, starting transfers between devices, swap_member(): return lax.ppermute(array, 'head', [(0, 1), (1, 0)])  18.4 us
  transfers between devices with their start and end apart: 66, of which 15 were waited for; matrix products, arithmetic and copies ran while one was open for 6% of the time, Pallas kernels for 59%

profile of v8, /device:TPU:0, one launch (start us, length us, event | category | flops | bytes accessed | tf_op | source)
XLA Modules:
  0.0 547.4 jit_solution(925210944243679829)
XLA Ops:
  8.8 3.1 collective-permute-start
  11.9 2.6 collective-permute-start.1
  20.5 5.2 collective-permute-done.3
  26.9 2.6 collective-permute-done.5
  29.5 10.4 %collective-permute-done.1.rest_2_ = bf16[256,768]{1,0:T(8,128)(2,1)S(1)} collective-permute-done((bf16[256,768]{1,0:T(8,128)(2,1)S(1)}, bf16[256,768]{1,0:T(8,128)(2,1)S(1)}, u32[]{:S(2)}, u32[]{:S(2)}) %collective-permute-start.1) | collective-permute-done | bytes 393248 | tf_op jit(solution)/shard_map/ppermute | solution.py:34
  41.2 3.5 all-to-all-start
  44.7 3.7 collective-permute-start.6
  51.2 2.6 concatenate.100
  53.8 12.7 %collective-permute-done.6.rest_3_ = bf16[256,768]{1,0:T(8,128)(2,1)} collective-permute-done((bf16[256,768]{1,0:T(8,128)(2,1)S(1)}, bf16[256,768]{1,0:T(8,128)(2,1)}, u32[]{:S(2)}, u32[]{:S(2)}) %collective-permute-start.6) | collective-permute-done | bytes 393248 | tf_op jit(solution)/shard_map/ppermute | solution.py:34
  68.2 1.6 collective-permute-start.17
  75.4 10.2 %collective-permute-done.16.rest_7_ = bf16[256,768]{1,0:T(8,128)(2,1)S(1)} collective-permute-done((bf16[256,768]{1,0:T(8,128)(2,1)}, bf16[256,768]{1,0:T(8,128)(2,1)S(1)}, u32[]{:S(2)}, u32[]{:S(2)}) %collective-permute-start.16) | collective-permute-done | bytes 393248 | tf_op jit(solution)/shard_map/ppermute | solution.py:51
  85.6 1.9 collective-permute-done.17
  91.7 9.1 %shard_map.305.q_ref.k_ref.v_ref = bf16[576,4096]{1,0:T(8,128)(2,1)} custom-call(bf16[768,576]{1,0:T(8,128)(2,1)} %bitcast.151, f32[576,1]{1,0:T(8,128)} %copy.138.bias_ref, bf16[256,768]{1,0:T(8,128)(2,1)} %copy-done.3, bf16[256,768]{1,0:T(8,128)(2,1)} %copy-done.38, bf16[256,768]{1,0:T(8,128)(2,1)} %copy-done.39, ...), custom_call_target="tpu_custom_call" | custom-call | flops 3623878656 | bytes 12582912 | tf_op jit(solution)/shard_map/pallas_call | solution.py:327
  101.7 4.0 collective-permute-start.19
  108.1 25.9 %shard_map.306 = (bf16[64,1024]{1,0:T(8,128)(2,1)}, bf16[64,1024]{1,0:T(8,128)(2,1)}, bf16[64,1024]{1,0:T(8,128)(2,1)}, bf16[64,1024]{1,0:T(8,128)(2,1)}, f32[1,...) custom-call(bf16[576,4096]{1,0:T(8,128)(2,1)} %shard_map.305.q_ref.k_ref.v_ref, ...), custom_call_target="tpu_custom_call" | custom-call | flops 17179869184 | bytes 2097152 | tf_op jit(solution)/shard_map/pallas_call | solution.py:140
  134.0 25.7 %shard_map.307 = (bf16[64,1024]{1,0:T(8,128)(2,1)}, bf16[64,1024]{1,0:T(8,128)(2,1)}, bf16[64,1024]{1,0:T(8,128)(2,1)}, bf16[64,1024]{1,0:T(8,128)(2,1)}, f32[1,...) custom-call(bf16[576,4096]{1,0:T(8,128)(2,1)} %shard_map.305.q_ref.k_ref.v_ref, ...), custom_call_target="tpu_custom_call" | custom-call | flops 17179869184 | bytes 2097152 | tf_op jit(solution)/shard_map/pallas_call | solution.py:140
  159.7 1.6 collective-permute-start.22
  163.7 14.3 %shard_map.308 = (bf16[64,1024]{1,0:T(8,128)(2,1)}, bf16[64,1024]{1,0:T(8,128)(2,1)}, f32[1,1024]{1,0:T(1,128)}, f32[1,1024]{1,0:T(1,128)}) custom-call(bf16[576,4096]{1,0:T(8,128)(2,1)} %shard_map.305.q_ref.k_ref.v_ref, bf16[576,4096]{1,0:T(8,128)(2,1)} %shard_map.305.q_ref.k_ref.v_ref, bf16[576,4096]{1,0:T(8,128)(2,1)} %shard_map.305.q_ref.k_ref.v_ref, ...), custom_call_target="tpu_custom_call" | custom-call | flops 8589934592 | bytes 2097152 | tf_op jit(solution)/shard_map/pallas_call | solution.py:140
  178.0 14.3 %shard_map.309 = (bf16[64,1024]{1,0:T(8,128)(2,1)}, bf16[64,1024]{1,0:T(8,128)(2,1)}, f32[1,1024]{1,0:T(1,128)}, f32[1,1024]{1,0:T(1,128)}) custom-call(bf16[576,4096]{1,0:T(8,128)(2,1)} %shard_map.305.q_ref.k_ref.v_ref, bf16[576,4096]{1,0:T(8,128)(2,1)} %shard_map.305.q_ref.k_ref.v_ref, bf16[576,4096]{1,0:T(8,128)(2,1)} %shard_map.305.q_ref.k_ref.v_ref, ...), custom_call_target="tpu_custom_call" | custom-call | flops 8589934592 | bytes 2097152 | tf_op jit(solution)/shard_map/pallas_call | solution.py:140
  194.4 1.7 collective-permute-start.24
  198.0 1.7 collective-permute-done.29.rest_17_
  199.6 3.5 collective-permute-done.24.rest_12_
  203.2 2.1 collective-permute-done.30.rest_18_
  205.9 69.7 %shard_map.310 = (bf16[256,768]{1,0:T(8,128)(2,1)}, bf16[256,768]{1,0:T(8,128)(2,1)}, bf16[256,768]{1,0:T(8,128)(2,1)}, bf16[256,768]{1,0:T(8,128)(2,1)}, bf16[6...) custom-call(s32[8]{0:T(128)} %pad_add_fusion.info_ref, ...), custom_call_target="tpu_custom_call" | custom-call | flops 28991029248 | bytes 18874368 | tf_op jit(solution)/shard_map/pallas_call | solution.py:661
  276.2 1.5 collective-permute-start.33
  277.8 4.3 collective-permute-start.34
  284.7 3.1 copy.148
  288.8 5.2 fusion.1
  297.4 45.0 %shard_map.311 = (bf16[192,1024]{1,0:T(8,128)(2,1)}, bf16[192,1024]{1,0:T(8,128)(2,1)}, bf16[192,1024]{1,0:T(8,128)(2,1)}, bf16[192,1024]{1,0:T(8,128)(2,1)}) custom-call(bf16[576,4096]{1,0:T(8,128)(2,1)} %shard_map.305.q_ref.k_ref.v_ref, bf16[576,4096]{1,0:T(8,128)(2,1)} %shard_map.305.q_ref.k_ref.v_ref, bf16[576,4096]{1,0:T(8,128)(2,1)} %shard_map.305.q_ref.k_ref.v_ref, ...), custom_call_target="tpu_custom_call" | custom-call | flops 42949672960 | bytes 4194304 | tf_op jit(solution)/shard_map/pallas_call | solution.py:272
  342.5 1.6 collective-permute-start.40
  344.8 45.5 %shard_map.312 = (bf16[192,1024]{1,0:T(8,128)(2,1)}, bf16[192,1024]{1,0:T(8,128)(2,1)}, bf16[192,1024]{1,0:T(8,128)(2,1)}, bf16[192,1024]{1,0:T(8,128)(2,1)}) custom-call(bf16[576,4096]{1,0:T(8,128)(2,1)} %shard_map.305.q_ref.k_ref.v_ref, bf16[576,4096]{1,0:T(8,128)(2,1)} %shard_map.305.q_ref.k_ref.v_ref, bf16[576,4096]{1,0:T(8,128)(2,1)} %shard_map.305.q_ref.k_ref.v_ref, ...), custom_call_target="tpu_custom_call" | custom-call | flops 42949672960 | bytes 4194304 | tf_op jit(solution)/shard_map/pallas_call | solution.py:272
  390.4 1.8 collective-permute-start.43
  392.6 24.8 %shard_map.313 = (bf16[128,1024]{1,0:T(8,128)(2,1)}, bf16[128,1024]{1,0:T(8,128)(2,1)}, f32[64,4096]{1,0:T(8,128)}) custom-call(bf16[576,4096]{1,0:T(8,128)(2,1)} %shard_map.305.q_ref.k_ref.v_ref, bf16[576,4096]{1,0:T(8,128)(2,1)} %shard_map.305.q_ref.k_ref.v_ref, bf16[576,4096]{1,0:T(8,128)(2,1)} %shard_map.305.q_ref.k_ref.v_ref, ...), custom_call_target="tpu_custom_call" | custom-call | flops 21474836480 | bytes 4194304 | tf_op jit(solution)/shard_map/pallas_call | solution.py:272
  417.5 1.8 collective-permute-start.47
  419.3 25.2 %shard_map.314 = (bf16[128,1024]{1,0:T(8,128)(2,1)}, bf16[128,1024]{1,0:T(8,128)(2,1)}, bf16[64,1024]{1,0:T(8,128)(2,1)}, bf16[64,1024]{1,0:T(8,128)(2,1)}, bf16...) custom-call(bf16[576,4096]{1,0:T(8,128)(2,1)} %shard_map.305.q_ref.k_ref.v_ref, ...), custom_call_target="tpu_custom_call" | custom-call | flops 21474836480 | bytes 4194304 | tf_op jit(solution)/shard_map/pallas_call | solution.py:272
  446.6 10.2 %shard_map.315 = bf16[8,104,576]{2,1,0:T(8,128)(2,1)} custom-call(bf16[256,768]{1,0:T(8,128)(2,1)} %copy-done.3, bf16[256,768]{1,0:T(8,128)(2,1)} %copy-done.38, bf16[256,768]{1,0:T(8,128)(2,1)} %copy-done.39, bf16[256,768]{1,0:T(8,128)(2,1)} %collective-permute-done.6.rest_3_, bf16[256,768]{1,0:T(8,128)(2,1)} %collective-permute-done.2.rest_4_, ...), custom_call_target="tpu_custom_call" | custom-call | flops 3623878656 | bytes 6291456 | tf_op jit(solution)/shard_map/pallas_call | solution.py:388
  458.7 3.4 collective-permute-done.50.rest_17_
  462.8 10.2 %shard_map.316 = (bf16[256,768]{1,0:T(8,128)(2,1)}, bf16[256,768]{1,0:T(8,128)(2,1)}, bf16[256,768]{1,0:T(8,128)(2,1)}, bf16[256,768]{1,0:T(8,128)(2,1)}) custom-call(s32[4]{0:T(128)} %copy-done.28, f32[1024,768]{1,0:T(8,128)} %get-tuple-element.280.acc_ref, bf16[32,72,768]{2,1,0:T(8,128)(2,1)} %bitcast.137, bf16[32,72,768]{2,1,0:T(8,128)(2,1)} %bitcast.138, ...), custom_call_target="tpu_custom_call" | custom-call | flops 3623878656 | bytes 6291456 | tf_op jit(solution)/shard_map/pallas_call | solution.py:441
  474.4 3.5 collective-permute-start.52
  477.9 9.8 %collective-permute-done.52.rest_1_ = bf16[256,768]{1,0:T(8,128)(2,1)S(1)} collective-permute-done((bf16[256,768]{1,0:T(8,128)(2,1)}, bf16[256,768]{1,0:T(8,128)(2,1)S(1)}, u32[]{:S(2)}, u32[]{:S(2)}) %collective-permute-start.52) | collective-permute-done | bytes 393248 | tf_op jit(solution)/shard_map/ppermute | solution.py:34
  487.9 13.5 %collective-permute-start.55 = (bf16[104,576]{1,0:T(8,128)(2,1)S(1)}, bf16[104,576]{1,0:T(8,128)(2,1)S(1)}, u32[]{:S(2)}, u32[]{:S(2)}) collective-permute-start(bf16[104,576]{1,0:T(8,128)(2,1)S(1)} %get-tuple-element.352), channel_id=1, source_target_pairs={{0,4},{2,6},{4,8},{6,10},{8,12},{10,14},{12,0},{14,2},{1,5},{3,7},... | collective-permute-start | bytes 359432 | tf_op jit(solution)/shard_map/ppermute | solution.py:34
  501.5 2.4 collective-permute-start.57
  503.9 6.6 %collective-permute-done.54.rest_2_ = bf16[256,768]{1,0:T(8,128)(2,1)S(1)} collective-permute-done((bf16[256,768]{1,0:T(8,128)(2,1)}, bf16[256,768]{1,0:T(8,128)(2,1)S(1)}, u32[]{:S(2)}, u32[]{:S(2)}) %collective-permute-start.54) | collective-permute-done | bytes 393248 | tf_op jit(solution)/shard_map/ppermute | solution.py:34
  510.5 2.8 collective-permute-done.56
  515.9 2.6 shard_map.317
  518.5 2.5 collective-permute-start.58
  526.9 5.9 %collective-permute-done.58.rest_3_ = bf16[256,768]{1,0:T(8,128)(2,1)S(1)} collective-permute-done((bf16[256,768]{1,0:T(8,128)(2,1)S(1)}, bf16[256,768]{1,0:T(8,128)(2,1)S(1)}, u32[]{:S(2)}, u32[]{:S(2)}) %collective-permute-start.58) | collective-permute-done | bytes 393248 | tf_op jit(solution)/shard_map/ppermute | solution.py:34
  533.6 2.6 shard_map.318
  (383 shorter events, 62.1 us)
Async XLA Ops:
  8.8 20.7 %collective-permute-start = (bf16[256,768]{1,0:T(8,128)(2,1)S(1)}, bf16[256,768]{1,0:T(8,128)(2,1)S(1)}, u32[]{:S(2)}, u32[]{:S(2)}) collective-permute-start(bf16[256,768]{1,0:T(8,128)(2,1)S(1)} %get-tuple-element.334), channel_id=1, source_target_pairs={{0,4},{2,6},{4,8},{6,10},{8,12},{10,14},{12,0},{14,2},{1,5},{3,7},... | collective-permute-start | bytes 1179656 | tf_op jit(solution)/shard_map/ppermute | solution.py:34
  11.9 28.0 %collective-permute-start.1 = (bf16[256,768]{1,0:T(8,128)(2,1)S(1)}, bf16[256,768]{1,0:T(8,128)(2,1)S(1)}, u32[]{:S(2)}, u32[]{:S(2)}) collective-permute-start(bf16[256,768]{1,0:T(8,128)(2,1)S(1)} %get-tuple-element.336), channel_id=1, source_target_pairs={{0,8},{2,10},{4,12},{6,14},{8,0},{10,2},{12,4},{14,6},{1,9},{3,11}... | collective-permute-start | bytes 1179656 | tf_op jit(solution)/shard_map/ppermute | solution.py:34
  14.5 25.4 %collective-permute-start.2 = (bf16[256,768]{1,0:T(8,128)(2,1)S(1)}, bf16[256,768]{1,0:T(8,128)(2,1)}, u32[]{:S(2)}, u32[]{:S(2)}) collective-permute-start(bf16[256,768]{1,0:T(8,128)(2,1)S(1)} %get-tuple-element.180.rest_0_), channel_id=1, source_target_pairs={{0,1},{1,0},{2,3},{3,2},{4,5},{5,4},{6,7},{7,6},{8,9},{9,8},{10,11... | collective-permute-start | bytes 1179656 | tf_op jit(solution)/shard_map/ppermute | solution.py:51
  41.2 26.3 %all-to-all-start = ((bf16[4,4,32,576]{3,1,2,0:T(4,128)(2,1)}), bf16[4,4,32,576]{3,1,2,0:T(4,128)(2,1)S(1)}, u32[]{:S(2)}, u32[]{:S(2)}) async-start(bf16[4,4,32,576]{3,1,2,0:T(4,128)(2,1)} %broadcast_in_dim.30), calls=%async_computation | async-start | bytes 1310720 | tf_op jit(solution)/shard_map/all_to_all | solution.py:40
  44.7 147.6 %all-gather.5.cloned.1.call-start = ((), (), s32[]{:S(2)}) async-start(), calls=%async_computation.3 | async-start | bytes 11354112 | tf_op jit(solution)/shard_map/all_gather | solution.py:831
  44.7 21.8 %collective-permute-start.6 = (bf16[256,768]{1,0:T(8,128)(2,1)S(1)}, bf16[256,768]{1,0:T(8,128)(2,1)}, u32[]{:S(2)}, u32[]{:S(2)}) collective-permute-start(bf16[256,768]{1,0:T(8,128)(2,1)S(1)} %get-tuple-element.174), channel_id=1, source_target_pairs={{0,12},{2,14},{4,0},{6,2},{8,4},{10,6},{12,8},{14,10},{1,13},{3,15... | collective-permute-start | bytes 1179656 | tf_op jit(solution)/shard_map/ppermute | solution.py:34
  48.5 18.1 %collective-permute-start.7 = (bf16[256,768]{1,0:T(8,128)(2,1)S(1)}, bf16[256,768]{1,0:T(8,128)(2,1)}, u32[]{:S(2)}, u32[]{:S(2)}) collective-permute-start(bf16[256,768]{1,0:T(8,128)(2,1)S(1)} %collective-permute-done.rest_1_), channel_id=1, source_target_pairs={{0,1},{1,0},{2,3},{3,2},{4,5},{5,4},{6,7},{7,6},{8,9},{9,8},{10,11... | collective-permute-start | bytes 1179656 | tf_op jit(solution)/shard_map/ppermute | solution.py:51
  50.0 17.5 %collective-permute-start.8 = (bf16[256,768]{1,0:T(8,128)(2,1)S(1)}, bf16[256,768]{1,0:T(8,128)(2,1)}, u32[]{:S(2)}, u32[]{:S(2)}) collective-permute-start(bf16[256,768]{1,0:T(8,128)(2,1)S(1)} %collective-permute-done.1.rest_2_), channel_id=1, source_target_pairs={{0,1},{1,0},{2,3},{3,2},{4,5},{5,4},{6,7},{7,6},{8,9},{9,8},{10,11... | collective-permute-start | bytes 1179656 | tf_op jit(solution)/shard_map/ppermute | solution.py:51
  50.5 17.0 %collective-permute-start.9 = (bf16[256,768]{1,0:T(8,128)(2,1)S(1)}, bf16[256,768]{1,0:T(8,128)(2,1)}, u32[]{:S(2)}, u32[]{:S(2)}) collective-permute-start(bf16[256,768]{1,0:T(8,128)(2,1)S(1)} %get-tuple-element.180.rest_0_), channel_id=1, source_target_pairs={{0,2},{2,0},{4,6},{6,4},{8,10},{10,8},{12,14},{14,12},{1,3},{3,1},... | collective-permute-start | bytes 1179656 | tf_op jit(solution)/shard_map/ppermute | solution.py:53
  50.5 17.0 %collective-permute-start.10 = (bf16[256,768]{1,0:T(8,128)(2,1)}, bf16[256,768]{1,0:T(8,128)(2,1)}, u32[]{:S(2)}, u32[]{:S(2)}) collective-permute-start(bf16[256,768]{1,0:T(8,128)(2,1)} %collective-permute-done.2.rest_4_), channel_id=1, source_target_pairs={{0,2},{2,0},{4,6},{6,4},{8,10},{10,8},{12,14},{14,12},{1,3},{3,1},... | collective-permute-start | bytes 1179656 | tf_op jit(solution)/shard_map/ppermute | solution.py:53
  67.5 391.1 %all-gather.7.cloned.1.call-start = ((), (), s32[]{:S(2)}) async-start(), calls=%async_computation.4 | async-start | bytes 3649536 | tf_op jit(solution)/shard_map/all_gather | solution.py:871
  68.2 19.2 %collective-permute-start.17 = (bf16[4,4,32,576]{3,2,1,0:T(8,128)(2,1)S(1)}, bf16[4,4,32,576]{3,2,1,0:T(8,128)(2,1)S(1)}, u32[]{:S(2)}, u32[]{:S(2)}) collective-permute-start(bf16[4,4,32,576]{3,2,1,0:T(8,128)(2,1)S(1)} %copy.136), channel_id=1, source_target_pairs={{0,16},{16,0},{1,17},{17,1},{2,18},{18,2},{3,19},{19,3},{4,20},{20... | collective-permute-start | bytes 1769480 | tf_op jit(solution)/shard_map/ppermute | solution.py:45
  71.9 13.7 %collective-permute-start.16 = (bf16[256,768]{1,0:T(8,128)(2,1)}, bf16[256,768]{1,0:T(8,128)(2,1)S(1)}, u32[]{:S(2)}, u32[]{:S(2)}) collective-permute-start(bf16[256,768]{1,0:T(8,128)(2,1)} %collective-permute-done.6.rest_3_), channel_id=1, source_target_pairs={{0,1},{1,0},{2,3},{3,2},{4,5},{5,4},{6,7},{7,6},{8,9},{9,8},{10,11... | collective-permute-start | bytes 1179656 | tf_op jit(solution)/shard_map/ppermute | solution.py:51
  75.2 461.0 %reduce-scatter.2.cloned.1.call-start = ((), (), s32[]{:S(2)}) async-start(), calls=%async_computation.2 | async-start | bytes 11354112 | tf_op jit(solution)/shard_map/reduce_scatter | solution.py:967
  101.7 60.1 %collective-permute-start.19 = (bf16[256,768]{1,0:T(8,128)(2,1)S(1)}, bf16[256,768]{1,0:T(8,128)(2,1)S(1)}, u32[]{:S(2)}, u32[]{:S(2)}) collective-permute-start(bf16[256,768]{1,0:T(8,128)(2,1)S(1)} %get-tuple-element.331), channel_id=1, source_target_pairs={{0,4},{2,6},{4,8},{6,10},{8,12},{10,14},{12,0},{14,2},{1,5},{3,7},... | collective-permute-start | bytes 1179656 | tf_op jit(solution)/shard_map/ppermute | solution.py:34
  105.8 56.1 %collective-permute-start.20 = (bf16[256,768]{1,0:T(8,128)(2,1)S(1)}, bf16[256,768]{1,0:T(8,128)(2,1)S(1)}, u32[]{:S(2)}, u32[]{:S(2)}) collective-permute-start(bf16[256,768]{1,0:T(8,128)(2,1)S(1)} %get-tuple-element.330), channel_id=1, source_target_pairs={{0,8},{2,10},{4,12},{6,14},{8,0},{10,2},{12,4},{14,6},{1,9},{3,11}... | collective-permute-start | bytes 1179656 | tf_op jit(solution)/shard_map/ppermute | solution.py:34
  107.1 55.3 %collective-permute-start.21 = (bf16[256,768]{1,0:T(8,128)(2,1)S(1)}, bf16[256,768]{1,0:T(8,128)(2,1)S(1)}, u32[]{:S(2)}, u32[]{:S(2)}) collective-permute-start(bf16[256,768]{1,0:T(8,128)(2,1)S(1)} %get-tuple-element.329), channel_id=1, source_target_pairs={{0,12},{2,14},{4,0},{6,2},{8,4},{10,6},{12,8},{14,10},{1,13},{3,15... | collective-permute-start | bytes 1179656 | tf_op jit(solution)/shard_map/ppermute | solution.py:34
  159.7 34.0 %collective-permute-start.22 = (bf16[64,1024]{1,0:T(8,128)(2,1)S(1)}, bf16[64,1024]{1,0:T(8,128)(2,1)S(1)}, u32[]{:S(2)}, u32[]{:S(2)}) collective-permute-start(bf16[64,1024]{1,0:T(8,128)(2,1)S(1)} %copy-done.58), channel_id=1, source_target_pairs={{0,1},{1,0},{2,3},{3,2},{4,5},{5,4},{6,7},{7,6},{8,9},{9,8},{10,11... | collective-permute-start | bytes 393224 | tf_op jit(solution)/shard_map/ppermute | solution.py:51
  161.3 33.1 %collective-permute-start.23 = (bf16[64,1024]{1,0:T(8,128)(2,1)}, bf16[64,1024]{1,0:T(8,128)(2,1)S(1)}, u32[]{:S(2)}, u32[]{:S(2)}) collective-permute-start(bf16[64,1024]{1,0:T(8,128)(2,1)} %get-tuple-element.219.rest_5_), channel_id=1, source_target_pairs={{0,1},{1,0},{2,3},{3,2},{4,5},{5,4},{6,7},{7,6},{8,9},{9,8},{10,11... | collective-permute-start | bytes 393224 | tf_op jit(solution)/shard_map/ppermute | solution.py:51
  161.8 34.2 %collective-permute-start.25 = (bf16[64,1024]{1,0:T(8,128)(2,1)S(1)}, bf16[64,1024]{1,0:T(8,128)(2,1)S(1)}, u32[]{:S(2)}, u32[]{:S(2)}) collective-permute-start(bf16[64,1024]{1,0:T(8,128)(2,1)S(1)} %copy-done.59), channel_id=1, source_target_pairs={{0,2},{2,0},{4,6},{6,4},{8,10},{10,8},{12,14},{14,12},{1,3},{3,1},... | collective-permute-start | bytes 393224 | tf_op jit(solution)/shard_map/ppermute | solution.py:53
  161.9 34.2 %collective-permute-start.26 = (bf16[64,1024]{1,0:T(8,128)(2,1)}, bf16[64,1024]{1,0:T(8,128)(2,1)S(1)}, u32[]{:S(2)}, u32[]{:S(2)}) collective-permute-start(bf16[64,1024]{1,0:T(8,128)(2,1)} %get-tuple-element.221.rest_6_), channel_id=1, source_target_pairs={{0,2},{2,0},{4,6},{6,4},{8,10},{10,8},{12,14},{14,12},{1,3},{3,1},... | collective-permute-start | bytes 393224 | tf_op jit(solution)/shard_map/ppermute | solution.py:53
  162.4 35.6 %collective-permute-start.28 = (bf16[64,1024]{1,0:T(8,128)(2,1)S(1)}, bf16[64,1024]{1,0:T(8,128)(2,1)S(1)}, u32[]{:S(2)}, u32[]{:S(2)}) collective-permute-start(bf16[64,1024]{1,0:T(8,128)(2,1)S(1)} %copy-done.60), channel_id=1, source_target_pairs={{0,3},{1,2},{2,1},{3,0},{4,7},{5,6},{6,5},{7,4},{8,11},{9,10},{10,... | collective-permute-start | bytes 393224 | tf_op jit(solution)/shard_map/ppermute | solution.py:55
  275.6 18.5 %collective-permute-start.31 = (bf16[64,1024]{1,0:T(8,128)(2,1)}, bf16[64,1024]{1,0:T(8,128)(2,1)S(1)}, u32[]{:S(2)}, u32[]{:S(2)}) collective-permute-start(bf16[64,1024]{1,0:T(8,128)(2,1)} %get-tuple-element.230), channel_id=1, source_target_pairs={{0,1},{1,0},{2,3},{3,2},{4,5},{5,4},{6,7},{7,6},{8,9},{9,8},{10,11... | collective-permute-start | bytes 393224 | tf_op jit(solution)/shard_map/ppermute | solution.py:51
  275.9 20.5 %collective-permute-start.32 = (bf16[64,1024]{1,0:T(8,128)(2,1)}, bf16[64,1024]{1,0:T(8,128)(2,1)S(1)}, u32[]{:S(2)}, u32[]{:S(2)}) collective-permute-start(bf16[64,1024]{1,0:T(8,128)(2,1)} %get-tuple-element.231), channel_id=1, source_target_pairs={{0,2},{2,0},{4,6},{6,4},{8,10},{10,8},{12,14},{14,12},{1,3},{3,1},... | collective-permute-start | bytes 393224 | tf_op jit(solution)/shard_map/ppermute | solution.py:53
  276.2 20.3 %collective-permute-start.33 = (bf16[64,1024]{1,0:T(8,128)(2,1)}, bf16[64,1024]{1,0:T(8,128)(2,1)S(1)}, u32[]{:S(2)}, u32[]{:S(2)}) collective-permute-start(bf16[64,1024]{1,0:T(8,128)(2,1)} %get-tuple-element.232), channel_id=1, source_target_pairs={{0,3},{1,2},{2,1},{3,0},{4,7},{5,6},{6,5},{7,4},{8,11},{9,10},{10,... | collective-permute-start | bytes 393224 | tf_op jit(solution)/shard_map/ppermute | solution.py:55
  277.8 66.4 %collective-permute-start.34 = (bf16[256,768]{1,0:T(8,128)(2,1)}, bf16[256,768]{1,0:T(8,128)(2,1)S(1)}, u32[]{:S(2)}, u32[]{:S(2)}) collective-permute-start(bf16[256,768]{1,0:T(8,128)(2,1)} %get-tuple-element.242), channel_id=1, source_target_pairs={{0,12},{2,14},{4,0},{6,2},{8,4},{10,6},{12,8},{14,10},{1,13},{3,15... | collective-permute-start | bytes 1179656 | tf_op jit(solution)/shard_map/ppermute | solution.py:34
  282.1 14.6 %collective-permute-start.37 = (bf16[128,1024]{1,0:T(8,128)(2,1)}, bf16[128,1024]{1,0:T(8,128)(2,1)S(1)}, u32[]{:S(2)}, u32[]{:S(2)}) collective-permute-start(bf16[128,1024]{1,0:T(8,128)(2,1)} %get-tuple-element.246), channel_id=1, source_target_pairs={{0,1},{1,0},{2,3},{3,2},{4,5},{5,4},{6,7},{7,6},{8,9},{9,8},{10,11... | collective-permute-start | bytes 786440 | tf_op jit(solution)/shard_map/ppermute | solution.py:51
  295.1 49.7 %collective-permute-start.35 = (bf16[256,768]{1,0:T(8,128)(2,1)S(1)}, bf16[256,768]{1,0:T(8,128)(2,1)S(1)}, u32[]{:S(2)}, u32[]{:S(2)}) collective-permute-start(bf16[256,768]{1,0:T(8,128)(2,1)S(1)} %copy-done.50), channel_id=1, source_target_pairs={{0,8},{2,10},{4,12},{6,14},{8,0},{10,2},{12,4},{14,6},{1,9},{3,11}... | collective-permute-start | bytes 1179656 | tf_op jit(solution)/shard_map/ppermute | solution.py:34
  296.5 48.3 %collective-permute-start.36 = (bf16[256,768]{1,0:T(8,128)(2,1)S(1)}, bf16[256,768]{1,0:T(8,128)(2,1)S(1)}, u32[]{:S(2)}, u32[]{:S(2)}) collective-permute-start(bf16[256,768]{1,0:T(8,128)(2,1)S(1)} %copy-done.48), channel_id=1, source_target_pairs={{0,4},{2,6},{4,8},{6,10},{8,12},{10,14},{12,0},{14,2},{1,5},{3,7},... | collective-permute-start | bytes 1179656 | tf_op jit(solution)/shard_map/ppermute | solution.py:34
  296.6 45.9 %collective-permute-start.38 = (bf16[128,1024]{1,0:T(8,128)(2,1)S(1)}, bf16[128,1024]{1,0:T(8,128)(2,1)S(1)}, u32[]{:S(2)}, u32[]{:S(2)}) collective-permute-start(bf16[128,1024]{1,0:T(8,128)(2,1)S(1)} %copy-done.55), channel_id=1, source_target_pairs={{0,2},{2,0},{4,6},{6,4},{8,10},{10,8},{12,14},{14,12},{1,3},{3,1},... | collective-permute-start | bytes 786440 | tf_op jit(solution)/shard_map/ppermute | solution.py:53
  296.7 47.5 %collective-permute-start.39 = (bf16[128,1024]{1,0:T(8,128)(2,1)S(1)}, bf16[128,1024]{1,0:T(8,128)(2,1)S(1)}, u32[]{:S(2)}, u32[]{:S(2)}) collective-permute-start(bf16[128,1024]{1,0:T(8,128)(2,1)S(1)} %copy-done.53), channel_id=1, source_target_pairs={{0,3},{1,2},{2,1},{3,0},{4,7},{5,6},{6,5},{7,4},{8,11},{9,10},{10,... | collective-permute-start | bytes 786440 | tf_op jit(solution)/shard_map/ppermute | solution.py:55
  342.5 49.7 %collective-permute-start.40 = (bf16[192,1024]{1,0:T(8,128)(2,1)}, bf16[192,1024]{1,0:T(8,128)(2,1)S(1)}, u32[]{:S(2)}, u32[]{:S(2)}) collective-permute-start(bf16[192,1024]{1,0:T(8,128)(2,1)} %get-tuple-element.234.rest_17_), channel_id=1, source_target_pairs={{0,1},{1,0},{2,3},{3,2},{4,5},{5,4},{6,7},{7,6},{8,9},{9,8},{10,11... | collective-permute-start | bytes 1179656 | tf_op jit(solution)/shard_map/ppermute | solution.py:51
  344.1 48.5 %collective-permute-start.41 = (bf16[192,1024]{1,0:T(8,128)(2,1)}, bf16[192,1024]{1,0:T(8,128)(2,1)S(1)}, u32[]{:S(2)}, u32[]{:S(2)}) collective-permute-start(bf16[192,1024]{1,0:T(8,128)(2,1)} %get-tuple-element.235.rest_18_), channel_id=1, source_target_pairs={{0,2},{2,0},{4,6},{6,4},{8,10},{10,8},{12,14},{14,12},{1,3},{3,1},... | collective-permute-start | bytes 1179656 | tf_op jit(solution)/shard_map/ppermute | solution.py:53
  344.2 48.4 %collective-permute-start.42 = (bf16[192,1024]{1,0:T(8,128)(2,1)}, bf16[192,1024]{1,0:T(8,128)(2,1)S(1)}, u32[]{:S(2)}, u32[]{:S(2)}) collective-permute-start(bf16[192,1024]{1,0:T(8,128)(2,1)} %get-tuple-element.236.rest_19_), channel_id=1, source_target_pairs={{0,3},{1,2},{2,1},{3,0},{4,7},{5,6},{6,5},{7,4},{8,11},{9,10},{10,... | collective-permute-start | bytes 1179656 | tf_op jit(solution)/shard_map/ppermute | solution.py:55
  390.4 28.9 %collective-permute-start.43 = (bf16[192,1024]{1,0:T(8,128)(2,1)}, bf16[192,1024]{1,0:T(8,128)(2,1)S(1)}, u32[]{:S(2)}, u32[]{:S(2)}) collective-permute-start(bf16[192,1024]{1,0:T(8,128)(2,1)} %get-tuple-element.254.rest_21_), channel_id=1, source_target_pairs={{0,1},{1,0},{2,3},{3,2},{4,5},{5,4},{6,7},{7,6},{8,9},{9,8},{10,11... | collective-permute-start | bytes 1179656 | tf_op jit(solution)/shard_map/ppermute | solution.py:51
  392.2 27.1 %collective-permute-start.44 = (bf16[192,1024]{1,0:T(8,128)(2,1)}, bf16[192,1024]{1,0:T(8,128)(2,1)S(1)}, u32[]{:S(2)}, u32[]{:S(2)}) collective-permute-start(bf16[192,1024]{1,0:T(8,128)(2,1)} %get-tuple-element.255.rest_22_), channel_id=1, source_target_pairs={{0,2},{2,0},{4,6},{6,4},{8,10},{10,8},{12,14},{14,12},{1,3},{3,1},... | collective-permute-start | bytes 1179656 | tf_op jit(solution)/shard_map/ppermute | solution.py:53
  392.2 27.1 %collective-permute-start.45 = (bf16[192,1024]{1,0:T(8,128)(2,1)}, bf16[192,1024]{1,0:T(8,128)(2,1)S(1)}, u32[]{:S(2)}, u32[]{:S(2)}) collective-permute-start(bf16[192,1024]{1,0:T(8,128)(2,1)} %get-tuple-element.256.rest_23_), channel_id=1, source_target_pairs={{0,3},{1,2},{2,1},{3,0},{4,7},{5,6},{6,5},{7,4},{8,11},{9,10},{10,... | collective-permute-start | bytes 1179656 | tf_op jit(solution)/shard_map/ppermute | solution.py:55
  417.5 39.3 %collective-permute-start.47 = (bf16[128,1024]{1,0:T(8,128)(2,1)}, bf16[128,1024]{1,0:T(8,128)(2,1)S(1)}, u32[]{:S(2)}, u32[]{:S(2)}) collective-permute-start(bf16[128,1024]{1,0:T(8,128)(2,1)} %get-tuple-element.274.rest_27_), channel_id=1, source_target_pairs={{0,1},{1,0},{2,3},{3,2},{4,5},{5,4},{6,7},{7,6},{8,9},{9,8},{10,11... | collective-permute-start | bytes 786440 | tf_op jit(solution)/shard_map/ppermute | solution.py:51
  419.3 39.3 %collective-permute-start.51 = (bf16[128,1024]{1,0:T(8,128)(2,1)}, bf16[128,1024]{1,0:T(8,128)(2,1)S(1)}, u32[]{:S(2)}, u32[]{:S(2)}) collective-permute-start(bf16[128,1024]{1,0:T(8,128)(2,1)} %get-tuple-element.278.rest_31_), channel_id=1, source_target_pairs={{0,3},{1,2},{2,1},{3,0},{4,7},{5,6},{6,5},{7,4},{8,11},{9,10},{10,... | collective-permute-start | bytes 786440 | tf_op jit(solution)/shard_map/ppermute | solution.py:55
  444.6 14.1 %collective-permute-start.46 = (bf16[64,1024]{1,0:T(8,128)(2,1)}, bf16[64,1024]{1,0:T(8,128)(2,1)S(1)}, u32[]{:S(2)}, u32[]{:S(2)}) collective-permute-start(bf16[64,1024]{1,0:T(8,128)(2,1)} %get-tuple-element.273.rest_26_), channel_id=1, source_target_pairs={{0,1},{1,0},{2,3},{3,2},{4,5},{5,4},{6,7},{7,6},{8,9},{9,8},{10,11... | collective-permute-start | bytes 393224 | tf_op jit(solution)/shard_map/ppermute | solution.py:51
  446.1 12.6 %collective-permute-start.48 = (bf16[64,1024]{1,0:T(8,128)(2,1)}, bf16[64,1024]{1,0:T(8,128)(2,1)S(1)}, u32[]{:S(2)}, u32[]{:S(2)}) collective-permute-start(bf16[64,1024]{1,0:T(8,128)(2,1)} %get-tuple-element.275.rest_28_), channel_id=1, source_target_pairs={{0,2},{2,0},{4,6},{6,4},{8,10},{10,8},{12,14},{14,12},{1,3},{3,1},... | collective-permute-start | bytes 393224 | tf_op jit(solution)/shard_map/ppermute | solution.py:53
  446.5 15.6 %collective-permute-start.49 = (bf16[128,1024]{1,0:T(8,128)(2,1)}, bf16[128,1024]{1,0:T(8,128)(2,1)S(1)}, u32[]{:S(2)}, u32[]{:S(2)}) collective-permute-start(bf16[128,1024]{1,0:T(8,128)(2,1)} %get-tuple-element.276.rest_29_), channel_id=1, source_target_pairs={{0,2},{2,0},{4,6},{6,4},{8,10},{10,8},{12,14},{14,12},{1,3},{3,1},... | collective-permute-start | bytes 786440 | tf_op jit(solution)/shard_map/ppermute | solution.py:53
  473.0 14.7 %collective-permute-start.53 = (bf16[4,104,576]{2,1,0:T(8,128)(2,1)S(1)}, bf16[4,104,576]{2,1,0:T(8,128)(2,1)S(1)}, u32[]{:S(2)}, u32[]{:S(2)}) collective-permute-start(bf16[4,104,576]{2,1,0:T(8,128)(2,1)S(1)} %get-tuple-element.294), channel_id=1, source_target_pairs={{0,16},{16,0},{1,17},{17,1},{2,18},{18,2},{3,19},{19,3},{4,20},{20... | collective-permute-start | bytes 1437704 | tf_op jit(solution)/shard_map/ppermute | solution.py:45
  474.4 13.3 %collective-permute-start.52 = (bf16[256,768]{1,0:T(8,128)(2,1)}, bf16[256,768]{1,0:T(8,128)(2,1)S(1)}, u32[]{:S(2)}, u32[]{:S(2)}) collective-permute-start(bf16[256,768]{1,0:T(8,128)(2,1)} %get-tuple-element.293), channel_id=1, source_target_pairs={{0,12},{2,14},{4,0},{6,2},{8,4},{10,6},{12,8},{14,10},{1,13},{3,15... | collective-permute-start | bytes 1179656 | tf_op jit(solution)/shard_map/ppermute | solution.py:34
  477.9 32.6 %collective-permute-start.54 = (bf16[256,768]{1,0:T(8,128)(2,1)}, bf16[256,768]{1,0:T(8,128)(2,1)S(1)}, u32[]{:S(2)}, u32[]{:S(2)}) collective-permute-start(bf16[256,768]{1,0:T(8,128)(2,1)} %get-tuple-element.296), channel_id=1, source_target_pairs={{0,8},{2,10},{4,12},{6,14},{8,0},{10,2},{12,4},{14,6},{1,9},{3,11}... | collective-permute-start | bytes 1179656 | tf_op jit(solution)/shard_map/ppermute | solution.py:34
  487.9 22.6 %collective-permute-start.55 = (bf16[104,576]{1,0:T(8,128)(2,1)S(1)}, bf16[104,576]{1,0:T(8,128)(2,1)S(1)}, u32[]{:S(2)}, u32[]{:S(2)}) collective-permute-start(bf16[104,576]{1,0:T(8,128)(2,1)S(1)} %get-tuple-element.352), channel_id=1, source_target_pairs={{0,4},{2,6},{4,8},{6,10},{8,12},{10,14},{12,0},{14,2},{1,5},{3,7},... | collective-permute-start | bytes 359432 | tf_op jit(solution)/shard_map/ppermute | solution.py:34
  501.5 11.9 %collective-permute-start.56 = (bf16[104,576]{1,0:T(8,128)(2,1)S(1)}, bf16[104,576]{1,0:T(8,128)(2,1)S(1)}, u32[]{:S(2)}, u32[]{:S(2)}) collective-permute-start(bf16[104,576]{1,0:T(8,128)(2,1)S(1)} %get-tuple-element.351), channel_id=1, source_target_pairs={{0,8},{2,10},{4,12},{6,14},{8,0},{10,2},{12,4},{14,6},{1,9},{3,11}... | collective-permute-start | bytes 359432 | tf_op jit(solution)/shard_map/ppermute | solution.py:34
  518.5 14.3 %collective-permute-start.58 = (bf16[256,768]{1,0:T(8,128)(2,1)S(1)}, bf16[256,768]{1,0:T(8,128)(2,1)S(1)}, u32[]{:S(2)}, u32[]{:S(2)}) collective-permute-start(bf16[256,768]{1,0:T(8,128)(2,1)S(1)} %copy-done.45), channel_id=1, source_target_pairs={{0,4},{2,6},{4,8},{6,10},{8,12},{10,14},{12,0},{14,2},{1,5},{3,7},... | collective-permute-start | bytes 1179656 | tf_op jit(solution)/shard_map/ppermute | solution.py:34
  (95 other events, 1320.9 us)
Sparse Core Ops, SparseCore 0:
  67.6 115.1 all-gather.4
  185.7 59.3 all-gather.6
  294.2 149.1 reduce-scatter.1
